TPU v7x, 32 devices: a whole 2x2x4 slice. The times are simulated.
32 devices in a mesh: row: 8 (over y, x, core), col: 4 (over z).
Axes of the slice: x: 2, y: 2, z: 4, core: 2. Of those that a mesh axis runs over, the one named last changes fastest.
Arguments:
- resid: float32 [32, 960, 1024], P('row', 'col'), may hold values from -6 to 6
- cotangent: float32 [32, 960, 1024], P('row', 'col'), may hold values from -6 to 6
- prefix: int32 [32], P('row'), may hold values from 102 to 512, as said below
- slot: int32 [32], P('row'), may hold values from 0 to 3, as said below
- chosen: int32 [4, 8, 768], P(None, 'row'), may hold values from 0 to 1023, as said below
- norm1_gain: float32 [960], replicated, may hold values from 0.25 to 1.75
- norm2_gain: float32 [960], replicated, may hold values from 0.25 to 1.75
- router: float32 [960], replicated, may hold values from -0.125 to 0.125
- w_query: bfloat16 [960, 960], P('row', 'col'), may hold values from -0.1875 to 0.1875
- w_key: bfloat16 [960, 320], P('row', 'col'), may hold values from -0.1875 to 0.1875
- w_value: bfloat16 [960, 320], P('row', 'col'), may hold values from -0.1875 to 0.1875
- w_out: bfloat16 [960, 960], P('row', 'col'), may hold values from -2 to 2
- w_gate: bfloat16 [960, 2560], P('row', 'col'), may hold values from -0.1875 to 0.1875
- w_up: bfloat16 [960, 2560], P('row', 'col'), may hold values from -0.1875 to 0.1875
- w_down: bfloat16 [2560, 960], P('row', 'col'), may hold values from -0.25 to 0.25
Outputs:
- block_out: float32 [32, 960, 1024], P('row', 'col')
- resid_grad: float32 [32, 960, 1024], P('row', 'col')
- norm1_gain_grad: float32 [960], P('col')
- norm2_gain_grad: float32 [960], P('col')
- router_grad: float32 [960], P('col')
- w_query_grad: float32 [960, 960], P('row', 'col')
- w_key_grad: float32 [960, 320], P('row', 'col')
- w_value_grad: float32 [960, 320], P('row', 'col')
- w_out_grad: float32 [960, 960], P('row', 'col')
- w_gate_grad: float32 [960, 2560], P('row', 'col')
- w_up_grad: float32 [960, 2560], P('row', 'col')
- w_down_grad: float32 [2560, 960], P('row', 'col')
Inputs may be any that keep to these rules, and one draw needn't show every extreme that they name: Some sequence has a prefix of exactly 512 tokens and some one of exactly 102. `slot`: the 4 sequences stored on one index of row take the micro-batches 0 to 3, one each. `chosen`: for each micro-batch and row index the 768 positions are distinct.
All inputs are finite; a program needn't handle non-finite values.
Results may differ from a plain program's by a relative error of at most 0.039.
Values may be sent and summed in bfloat16 or wider, within the bound.
No kernel may reach another device: no remote copies, remote signals or barrier semaphores. Data moves between devices by JAX's collectives and lax.ppermute only.
A program may use at most 256 MiB of HBM per device.

v0:
```python
import math

import jax
import jax.numpy as jnp
from jax import lax
from jax.sharding import PartitionSpec as P

H = 15
KVH = 5
HD = 64
KEYB = 128


EPSILON = 1e-05
ROPE_BASE = 10000.0


def rope_tables(positions, head_size):
    half_width = head_size // 2
    frequency = jnp.exp(
        jnp.arange(half_width, dtype=jnp.float32) * (-2.0 * math.log(ROPE_BASE) / head_size)
    )
    angles = positions.astype(jnp.float32)[:, None] * frequency[None, :]
    return (jnp.cos(angles)[:, None, :], jnp.sin(angles)[:, None, :])


def rotate(values, tables, direction):
    cosine_table, sine_table = tables
    half_width = values.shape[-1] // 2
    first_half = values[..., :half_width]
    second = values[..., half_width:]
    sine_signed = sine_table * direction
    return jnp.concatenate(
        [
            first_half * cosine_table - second * sine_signed,
            second * cosine_table + first_half * sine_signed,
        ],
        axis=-1,
    )


def full_features(values_major):
    gathered = lax.all_gather(values_major.astype(jnp.bfloat16), "col", axis=0, tiled=True).astype(
        values_major.dtype
    )
    token_major = gathered.T
    return [token_major]


def split_sums(partial_value, row_stats, col_count):
    spread = jnp.broadcast_to(
        row_stats[:, None, :], (row_stats.shape[0], col_count, row_stats.shape[1])
    )
    own_share, stat_sum = (
        lax.psum_scatter(
            partial_value.astype(jnp.bfloat16), "col", scatter_dimension=1, tiled=True
        ).astype(jnp.float32),
        lax.psum_scatter(
            spread.astype(jnp.bfloat16), "col", scatter_dimension=1, tiled=True
        ).astype(jnp.float32),
    )
    return (own_share, stat_sum[:, 0, :])


def row_share(gradients):
    return (
        lax.psum_scatter(
            gradients[0].astype(jnp.bfloat16), "row", scatter_dimension=0, tiled=True
        ).astype(jnp.float32),
        lax.psum_scatter(
            gradients[1].astype(jnp.bfloat16), "row", scatter_dimension=0, tiled=True
        ).astype(jnp.float32),
        lax.psum_scatter(
            gradients[2].astype(jnp.bfloat16), "row", scatter_dimension=0, tiled=True
        ).astype(jnp.float32),
        lax.psum_scatter(
            gradients[3].astype(jnp.bfloat16), "row", scatter_dimension=0, tiled=True
        ).astype(jnp.float32),
        lax.psum_scatter(
            gradients[4].astype(jnp.bfloat16), "row", scatter_dimension=0, tiled=True
        ).astype(jnp.float32),
        lax.psum_scatter(
            gradients[5].astype(jnp.bfloat16), "row", scatter_dimension=0, tiled=True
        ).astype(jnp.float32),
        lax.psum_scatter(
            gradients[6].astype(jnp.bfloat16), "row", scatter_dimension=0, tiled=True
        ).astype(jnp.float32),
    )


def add_rows(target, update, row_start):
    current = lax.dynamic_slice_in_dim(target, row_start, update.shape[0], 0)
    return lax.dynamic_update_slice_in_dim(target, current + update, row_start, 0)


def block_count(positions, prefix_len):
    key_reach = jnp.maximum(positions[-1] + 1, prefix_len)
    return (key_reach + KEYB - 1) // KEYB


def masked_scores(queries, key_rows, positions, prefix_len, key_start, score_scale):
    key_block = lax.dynamic_slice_in_dim(key_rows, key_start, KEYB, 0)
    scores = (
        jnp.einsum("pkgd,tkd->kgpt", queries, key_block, preferred_element_type=jnp.float32)
        * score_scale
    )
    key_pos = key_start + jnp.arange(KEYB, dtype=jnp.int32)
    allowed = (key_pos[None, :] <= positions[:, None]) | (key_pos[None, :] < prefix_len)
    return jnp.where(allowed, scores, -1e30)


def attend_forward(queries, key_rows, value_rows, positions, prefix_len, score_scale):
    blocks = block_count(positions, prefix_len)
    stat_shape = (queries.shape[1], queries.shape[2], queries.shape[0])

    def first_pass(key_index, running_state):
        running_max, row_total = running_state
        scores = masked_scores(
            queries, key_rows, positions, prefix_len, key_index * KEYB, score_scale
        )
        new_max = jnp.maximum(running_max, jnp.max(scores, axis=-1))
        row_total = row_total * jnp.exp(running_max - new_max) + jnp.sum(
            jnp.exp(scores - new_max[..., None]), axis=-1
        )
        return (new_max, row_total)

    start_state = (jnp.full(stat_shape, -1e30, jnp.float32), jnp.zeros(stat_shape, jnp.float32))
    running_max, row_total = lax.fori_loop(0, blocks, first_pass, start_state)
    log_total = running_max + jnp.log(row_total)

    def second_pass(key_index, output):
        key_start = key_index * KEYB
        scores = masked_scores(queries, key_rows, positions, prefix_len, key_start, score_scale)
        weights_low = jnp.exp(scores - log_total[..., None]).astype(jnp.bfloat16)
        value_block = lax.dynamic_slice_in_dim(value_rows, key_start, KEYB, 0)
        return output + jnp.einsum(
            "kgpt,tkd->pkgd", weights_low, value_block, preferred_element_type=jnp.float32
        )

    output = lax.fori_loop(0, blocks, second_pass, jnp.zeros(queries.shape, jnp.float32))
    return (output, log_total)


def attend_backward(
    queries,
    key_rows,
    value_rows,
    positions,
    prefix_len,
    score_scale,
    grad_out,
    output,
    log_total,
    grad_sums,
):
    blocks = block_count(positions, prefix_len)
    delta_rows = jnp.einsum("pkgd,pkgd->kgp", grad_out.astype(jnp.float32), output)

    def back_pass(key_index, running_state):
        grad_query, grad_keys, grad_values = running_state
        key_start = key_index * KEYB
        scores = masked_scores(queries, key_rows, positions, prefix_len, key_start, score_scale)
        probs = jnp.exp(scores - log_total[..., None])
        weights_low = probs.astype(jnp.bfloat16)
        key_block = lax.dynamic_slice_in_dim(key_rows, key_start, KEYB, 0)
        value_block = lax.dynamic_slice_in_dim(value_rows, key_start, KEYB, 0)
        grad_probs = jnp.einsum(
            "pkgd,tkd->kgpt", grad_out, value_block, preferred_element_type=jnp.float32
        )
        grad_scores = (probs * (grad_probs - delta_rows[..., None])).astype(jnp.bfloat16)
        grad_query = (
            grad_query
            + jnp.einsum(
                "kgpt,tkd->pkgd", grad_scores, key_block, preferred_element_type=jnp.float32
            )
            * score_scale
        )
        key_term = (
            jnp.einsum("kgpt,pkgd->tkd", grad_scores, queries, preferred_element_type=jnp.float32)
            * score_scale
        )
        value_term = jnp.einsum(
            "kgpt,pkgd->tkd", weights_low, grad_out, preferred_element_type=jnp.float32
        )
        return (
            grad_query,
            add_rows(grad_keys, key_term, key_start),
            add_rows(grad_values, value_term, key_start),
        )

    return lax.fori_loop(0, blocks, back_pass, (jnp.zeros(queries.shape, jnp.float32),) + grad_sums)


def on_device(
    resid,
    cotangent,
    prefix,
    slot,
    chosen,
    norm1_gain,
    norm2_gain,
    router,
    w_query,
    w_key,
    w_value,
    w_out,
    w_gate,
    w_up,
    w_down,
):
    col_count = lax.axis_size("col")
    column = lax.axis_index("col")
    micro_count = resid.shape[0]
    width_col = resid.shape[1]
    length = resid.shape[2]
    model_width = width_col * col_count
    query_rows = length // col_count
    groups = H // KVH
    score_scale = HD ** (-0.5)
    gain_one = lax.dynamic_slice_in_dim(norm1_gain, column * width_col, width_col)
    gain_two = lax.dynamic_slice_in_dim(norm2_gain, column * width_col, width_col)
    router_col = lax.dynamic_slice_in_dim(router, column * width_col, width_col)
    positions = jnp.arange(length, dtype=jnp.int32)
    tables_all = rope_tables(positions, HD)
    query_pos = column * query_rows + jnp.arange(query_rows, dtype=jnp.int32)
    pieces = ((0, query_rows),)
    query_tables = rope_tables(query_pos, HD)
    full_weights = (
        lax.all_gather(w_query, "row", axis=0, tiled=True),
        lax.all_gather(w_key, "row", axis=0, tiled=True),
        lax.all_gather(w_value, "row", axis=0, tiled=True),
        lax.all_gather(w_out, "row", axis=0, tiled=True),
        lax.all_gather(w_gate, "row", axis=0, tiled=True),
        lax.all_gather(w_up, "row", axis=0, tiled=True),
        lax.all_gather(w_down, "row", axis=0, tiled=True),
    )
    query_full, key_full, value_full, out_full, gate_full, up_full, down_full = full_weights
    grad_totals = tuple(
        (
            jnp.zeros(weight.shape, jnp.float32)
            for weight in (w_query, w_key, w_value, w_out, w_gate, w_up, w_down)
        )
    )
    gain_one_acc = jnp.zeros((width_col,), jnp.float32)
    gain_two_acc = jnp.zeros((width_col,), jnp.float32)
    router_acc = jnp.zeros((width_col,), jnp.float32)
    block_out = jnp.zeros(resid.shape, jnp.float32)
    resid_grad = jnp.zeros(resid.shape, jnp.float32)
    for micro_step in range(micro_count):
        seq_pick = jnp.sum(
            jnp.arange(micro_count, dtype=jnp.int32) * (slot == micro_step).astype(jnp.int32)
        )
        resid_major = lax.dynamic_index_in_dim(resid, seq_pick, 0, keepdims=False)
        resid_seq = resid_major.T
        cot_major = lax.dynamic_index_in_dim(cotangent, seq_pick, 0, keepdims=False)
        grad_seq = cot_major.T
        prefix_len = lax.dynamic_index_in_dim(prefix, seq_pick, 0, keepdims=False)
        selected = jnp.any(positions[:, None] == chosen[micro_step, 0][None, :], axis=1).astype(
            jnp.float32
        )
        resid_full = full_features(resid_major)[0]
        inverse_one = lax.rsqrt(jnp.mean(resid_full * resid_full, axis=1, keepdims=True) + EPSILON)
        normed_one = (resid_full * inverse_one * norm1_gain).astype(jnp.bfloat16)
        router_logit = jnp.dot(resid_full, router, precision=lax.Precision.HIGHEST)
        gate_prob = jax.nn.sigmoid(router_logit)
        gate_share = selected * gate_prob
        query_part = jnp.dot(normed_one, query_full, preferred_element_type=jnp.float32).astype(
            jnp.bfloat16
        )
        key_part = jnp.dot(normed_one, key_full, preferred_element_type=jnp.float32).astype(
            jnp.bfloat16
        )
        value_part = jnp.dot(normed_one, value_full, preferred_element_type=jnp.float32).astype(
            jnp.bfloat16
        )
        query_heads = lax.all_to_all(query_part, "col", split_axis=0, concat_axis=1, tiled=True)
        queries = rotate(
            query_heads.astype(jnp.float32).reshape(query_rows, H, HD), query_tables, 1.0
        )
        queries = queries.astype(jnp.bfloat16).reshape(query_rows, KVH, groups, HD)
        key_all, value_all = (
            lax.all_gather(key_part, "col", axis=1, tiled=True),
            lax.all_gather(value_part, "col", axis=1, tiled=True),
        )
        key_rows = rotate(
            key_all.astype(jnp.float32).reshape(length, KVH, HD), tables_all, 1.0
        ).astype(jnp.bfloat16)
        value_rows = value_all.reshape(length, KVH, HD)
        out_piece, total_piece = attend_forward(
            queries, key_rows, value_rows, query_pos, prefix_len, score_scale
        )
        piece_outputs = [out_piece]
        piece_totals = [total_piece]
        attended = piece_outputs[0]
        attended_low = attended.reshape(query_rows, model_width).astype(jnp.bfloat16)
        attended_all = lax.all_gather(attended_low, "col", axis=0, tiled=True)
        branch_attn = jnp.dot(attended_all, out_full, preferred_element_type=jnp.float32)
        hidden = resid_seq + branch_attn
        hidden_full = full_features(hidden.T)[0]
        inverse_two = lax.rsqrt(
            jnp.mean(hidden_full * hidden_full, axis=1, keepdims=True) + EPSILON
        )
        normed_two = (hidden_full * inverse_two * norm2_gain).astype(jnp.bfloat16)
        gate_proj = jnp.dot(normed_two, gate_full, preferred_element_type=jnp.float32)
        up_proj = jnp.dot(normed_two, up_full, preferred_element_type=jnp.float32)
        active = (jax.nn.silu(gate_proj) * up_proj).astype(jnp.bfloat16)
        active_all = lax.all_gather(active, "col", axis=1, tiled=True)
        branch_ffn = jnp.dot(active_all, down_full, preferred_element_type=jnp.float32)
        branch_sum = branch_attn + branch_ffn
        block_seq = resid_seq + gate_share[:, None] * branch_sum
        block_out = lax.dynamic_update_index_in_dim(block_out, block_seq.T, seq_pick, 0)
        grad_branch = gate_share[:, None] * grad_seq
        logit_part = jnp.sum(grad_seq * branch_sum, axis=1)
        grad_ffn = grad_branch.astype(jnp.bfloat16)
        grad_down = jnp.einsum(
            "tf,td->fd", active_all, grad_ffn, preferred_element_type=jnp.float32
        )
        partial_ffn = jnp.einsum(
            "td,fd->tf", grad_ffn, down_full, preferred_element_type=jnp.float32
        )
        grad_active, logit_stat = split_sums(partial_ffn, logit_part[:, None], col_count)
        gate_sigmoid = jax.nn.sigmoid(gate_proj)
        grad_gate = (
            grad_active * up_proj * gate_sigmoid * (1.0 + gate_proj * (1.0 - gate_sigmoid))
        ).astype(jnp.bfloat16)
        grad_up = (grad_active * (gate_proj * gate_sigmoid)).astype(jnp.bfloat16)
        grad_gate_w = jnp.einsum(
            "td,tf->df", normed_two, grad_gate, preferred_element_type=jnp.float32
        )
        grad_up_w = jnp.einsum("td,tf->df", normed_two, grad_up, preferred_element_type=jnp.float32)
        partial_two = jnp.einsum(
            "tf,df->td", grad_gate, gate_full, preferred_element_type=jnp.float32
        ) + jnp.einsum("tf,df->td", grad_up, up_full, preferred_element_type=jnp.float32)
        stat_two = jnp.sum(partial_two * hidden_full * norm2_gain, axis=1)
        grad_norm_two, two_stats = split_sums(partial_two, stat_two[:, None], col_count)
        dot_two = two_stats[:, 0]
        logit_sum = logit_stat[:, 0]
        unit_two = grad_norm_two * gain_two
        grad_hidden = (
            inverse_two * unit_two - hidden * inverse_two**3 * dot_two[:, None] / model_width
        )
        gain_two_acc = gain_two_acc + jnp.sum(grad_norm_two * hidden * inverse_two, axis=0)
        grad_attn_low = (grad_hidden + grad_branch).astype(jnp.bfloat16)
        grad_out_w = jnp.einsum(
            "td,tc->dc", attended_all, grad_attn_low, preferred_element_type=jnp.float32
        )
        partial_out = jnp.einsum(
            "tc,dc->td", grad_attn_low, out_full, preferred_element_type=jnp.float32
        )
        grad_attended = lax.psum_scatter(
            partial_out.astype(jnp.bfloat16), "col", scatter_dimension=0, tiled=True
        )
        grad_heads = grad_attended.reshape(query_rows, KVH, groups, HD)
        grad_sums = (
            jnp.zeros((length, KVH, HD), jnp.float32),
            jnp.zeros((length, KVH, HD), jnp.float32),
        )
        query_grads = []
        for (offset, piece_rows), out_piece, total_piece in zip(
            pieces, piece_outputs, piece_totals
        ):
            grad_query, grad_keys, grad_values = attend_backward(
                queries,
                key_rows,
                value_rows,
                query_pos,
                prefix_len,
                score_scale,
                grad_heads,
                out_piece,
                total_piece,
                grad_sums,
            )
            grad_sums = (grad_keys, grad_values)
            query_grads.append(grad_query)
        grad_queries = query_grads[0].reshape(query_rows, H, HD)
        grad_q_raw = (
            rotate(grad_queries, query_tables, -1.0)
            .astype(jnp.bfloat16)
            .reshape(query_rows, model_width)
        )
        grad_query_col = lax.all_to_all(grad_q_raw, "col", split_axis=1, concat_axis=0, tiled=True)
        grad_keys_raw = rotate(grad_sums[0], tables_all, -1.0).reshape(length, KVH * HD)
        grad_key_col, grad_value_col = (
            lax.psum_scatter(
                grad_keys_raw.astype(jnp.bfloat16), "col", scatter_dimension=1, tiled=True
            ).astype(jnp.float32),
            lax.psum_scatter(
                grad_sums[1].reshape(length, KVH * HD).astype(jnp.bfloat16),
                "col",
                scatter_dimension=1,
                tiled=True,
            ).astype(jnp.float32),
        )
        grad_key_low = grad_key_col.astype(jnp.bfloat16)
        grad_value_low = grad_value_col.astype(jnp.bfloat16)
        grad_query_w = jnp.einsum(
            "td,tc->dc", normed_one, grad_query_col, preferred_element_type=jnp.float32
        )
        grad_key_w = jnp.einsum(
            "td,tc->dc", normed_one, grad_key_low, preferred_element_type=jnp.float32
        )
        grad_value_w = jnp.einsum(
            "td,tc->dc", normed_one, grad_value_low, preferred_element_type=jnp.float32
        )
        partial_one = jnp.einsum(
            "tc,dc->td", grad_query_col, query_full, preferred_element_type=jnp.float32
        )
        partial_one = partial_one + jnp.einsum(
            "tc,dc->td", grad_key_low, key_full, preferred_element_type=jnp.float32
        )
        partial_one = partial_one + jnp.einsum(
            "tc,dc->td", grad_value_low, value_full, preferred_element_type=jnp.float32
        )
        stat_one = jnp.sum(partial_one * resid_full * norm1_gain, axis=1)
        grad_norm_one, one_stats = split_sums(partial_one, stat_one[:, None], col_count)
        unit_one = grad_norm_one * gain_one
        grad_from_norm = (
            inverse_one * unit_one - resid_seq * inverse_one**3 * one_stats / model_width
        )
        gain_one_acc = gain_one_acc + jnp.sum(grad_norm_one * resid_seq * inverse_one, axis=0)
        logit_grad = logit_sum * gate_share * (1.0 - gate_prob)
        router_acc = router_acc + jnp.sum(logit_grad[:, None] * resid_seq, axis=0)
        grad_resid_seq = grad_seq + grad_hidden + grad_from_norm + logit_grad[:, None] * router_col
        resid_grad = lax.dynamic_update_index_in_dim(resid_grad, grad_resid_seq.T, seq_pick, 0)
        step_grads = (
            grad_query_w,
            grad_key_w,
            grad_value_w,
            grad_out_w,
            grad_gate_w,
            grad_up_w,
            grad_down,
        )
        grad_totals = tuple(
            (summed + owned_part for summed, owned_part in zip(grad_totals, row_share(step_grads)))
        )
    gain_one_grad, gain_two_grad, router_grad = lax.psum(
        (gain_one_acc, gain_two_acc, router_acc), "row"
    )
    return (block_out, resid_grad, gain_one_grad, gain_two_grad, router_grad) + tuple(grad_totals)


def solution(mesh):
    placed = (
        P("row", "col", None),
        P("row", "col", None),
        P("row"),
        P("row"),
        P(None, "row", None),
        P(),
        P(),
        P(),
        P("row", "col"),
        P("row", "col"),
        P("row", "col"),
        P("row", "col"),
        P("row", "col"),
        P("row", "col"),
        P("row", "col"),
    )
    return jax.shard_map(
        on_device,
        mesh=mesh,
        in_specs=placed,
        out_specs=(
            P("row", "col", None),
            P("row", "col", None),
            P("col"),
            P("col"),
            P("col"),
            P("row", "col"),
            P("row", "col"),
            P("row", "col"),
            P("row", "col"),
            P("row", "col"),
            P("row", "col"),
            P("row", "col"),
        ),
        check_vma=False,
    )
```

profile of v0, /device:TPU:0, one launch (start us, length us, event | category | flops | bytes accessed | tf_op | source)
XLA Modules:
  0.0 3412.7 jit_solution(5481615709936654314)
XLA Ops:
  68.9 41.4 %all-gather.44.cloned.1.call-done = bf16[960,1024]{1,0:T(8,128)(2,1)} async-done(((bf16[240,1024]{1,0:T(8,128)(2,1)}), bf16[960,1024]{1,0:T(8,128)(2,1)}) %all-gather.44.cloned.1.call-update) | async-done | bytes 1966096 | tf_op jit(solution)/shard_map/all_gather | solution.py:43
  112.9 42.0 %all-gather.36.cloned.1.call-done = bf16[960,1024]{1,0:T(8,128)(2,1)} async-done(((bf16[240,1024]{1,0:T(8,128)(2,1)}), bf16[960,1024]{1,0:T(8,128)(2,1)}) %all-gather.36.cloned.1.call-update) | async-done | bytes 1966096 | tf_op jit(solution)/shard_map/all_gather | solution.py:43
  157.5 41.2 %all-gather.22.cloned.1.call-done = bf16[960,1024]{1,0:T(8,128)(2,1)} async-done(((bf16[240,1024]{1,0:T(8,128)(2,1)}), bf16[960,1024]{1,0:T(8,128)(2,1)}) %all-gather.22.cloned.1.call-update) | async-done | bytes 1966096 | tf_op jit(solution)/shard_map/all_gather | solution.py:43
  216.5 25.9 all_gather.97
  511.1 82.4 %all-gather.38.cloned.1.call-done = bf16[1024,960]{0,1:T(8,128)(2,1)} async-done(((bf16[256,960]{0,1:T(8,128)(2,1)}), bf16[1024,960]{0,1:T(8,128)(2,1)}) %all-gather.38.cloned.1.call-update) | async-done | bytes 1966096 | tf_op jit(solution)/shard_map/all_gather | solution.py:296
  595.8 42.2 %all-gather.24.cloned.1.call-done = bf16[1024,960]{0,1:T(8,128)(2,1)} async-done(((bf16[256,960]{0,1:T(8,128)(2,1)}), bf16[1024,960]{0,1:T(8,128)(2,1)}) %all-gather.24.cloned.1.call-update) | async-done | bytes 1966096 | tf_op jit(solution)/shard_map/all_gather | solution.py:296
  640.4 41.6 %all-gather.54.cloned.1.call-done = bf16[1024,960]{0,1:T(8,128)(2,1)} async-done(((bf16[256,960]{0,1:T(8,128)(2,1)}), bf16[1024,960]{0,1:T(8,128)(2,1)}) %all-gather.54.cloned.1.call-update) | async-done | bytes 1966096 | tf_op jit(solution)/shard_map/all_gather | solution.py:296
  769.9 26.4 all-gather.48.cloned.1.call-done
  798.3 42.4 %all-gather.40.cloned.1.call-done = bf16[960,1024]{1,0:T(8,128)(2,1)} async-done(((bf16[240,1024]{1,0:T(8,128)(2,1)}), bf16[960,1024]{1,0:T(8,128)(2,1)}) %all-gather.40.cloned.1.call-update) | async-done | bytes 1966096 | tf_op jit(solution)/shard_map/all_gather | solution.py:43
  842.7 42.0 %all-gather.26.cloned.1.call-done = bf16[960,1024]{1,0:T(8,128)(2,1)} async-done(((bf16[240,1024]{1,0:T(8,128)(2,1)}), bf16[960,1024]{1,0:T(8,128)(2,1)}) %all-gather.26.cloned.1.call-update) | async-done | bytes 1966096 | tf_op jit(solution)/shard_map/all_gather | solution.py:43
  925.9 79.7 %reduce-scatter.147.cloned.1.call-done = bf16[640,1024]{1,0:T(8,128)(2,1)} async-done(((bf16[2560,1024]{1,0:T(8,128)(2,1)}), bf16[640,1024]{1,0:T(8,128)(2,1)}) %reduce-scatter.147.cloned.1.call-update) | async-done | bytes 1310736
  1008.2 93.8 %reduce-scatter.145.cloned.1.call-done = bf16[640,1024]{1,0:T(8,128)(2,1)} async-done(((bf16[2560,1024]{1,0:T(8,128)(2,1)}), bf16[640,1024]{1,0:T(8,128)(2,1)}) %reduce-scatter.145.cloned.1.call-update) | async-done | bytes 1310736
  1104.4 94.0 %reduce-scatter.143.cloned.1.call-done = bf16[640,1024]{1,0:T(8,128)(2,1)} async-done(((bf16[2560,1024]{1,0:T(8,128)(2,1)}), bf16[640,1024]{1,0:T(8,128)(2,1)}) %reduce-scatter.143.cloned.1.call-update) | async-done | bytes 1310736
  1200.9 94.0 %reduce-scatter.141.cloned.1.call-done = bf16[640,1024]{1,0:T(8,128)(2,1)} async-done(((bf16[2560,1024]{1,0:T(8,128)(2,1)}), bf16[640,1024]{1,0:T(8,128)(2,1)}) %reduce-scatter.141.cloned.1.call-update) | async-done | bytes 1310736
  1297.3 24.3 all-gather.30.cloned.1.call-done
  1414.8 43.7 %reduce-scatter.97.cloned.1.call-done = bf16[1024,240]{0,1:T(8,128)(2,1)} async-done(((bf16[1024,960]{0,1:T(8,128)(2,1)}), bf16[1024,240]{0,1:T(8,128)(2,1)}) %reduce-scatter.97.cloned.1.call-update) | async-done | bytes 491536 | tf_op jit(solution)/shard_map/reduce_scatter | solution.py:55
  1468.3 33.2 reduce-scatter.107.cloned.1.call-done
  1501.5 43.0 %reduce-scatter.87.cloned.1.call-done = bf16[1024,240]{0,1:T(8,128)(2,1)} async-done(((bf16[1024,960]{0,1:T(8,128)(2,1)}), bf16[1024,240]{0,1:T(8,128)(2,1)}) %reduce-scatter.87.cloned.1.call-update) | async-done | bytes 491536 | tf_op jit(solution)/shard_map/reduce_scatter | solution.py:55
  1558.0 29.4 reduce-scatter.79.cloned.1.call-done
  1590.1 29.8 while.164
  1634.5 27.0 while.167
  1722.4 40.4 %while.166 = (s32[]{:T(128)}, f32[256,5,3,64]{0,3,2,1:T(8,128)}, f32[1024,5,64]{0,2,1:T(8,128)}, f32[1024,5,64]{0,2,1:T(8,128)}, s32[]{:T(128)}, /*index=5*/bf16...) while((s32[]{:T(128)}, f32[256,5,3,64]{0,3,2,1:T(8,128)}, ...), condition=%wide.region_74.75_spmd.clone, body=%wide.region_73.74_spmd.clone.sunk | while | flops 318694016 | bytes 21649960 | solution.py:191
  1830.7 138.2 %all-to-all-start.7 = ((bf16[256,4,240]{0,2,1:T(8,128)(2,1)}), bf16[256,4,240]{0,2,1:T(8,128)(2,1)S(1)}, u32[]{:S(2)}, u32[]{:S(2)}) async-start(bf16[256,4,240]{0,2,1:T(8,128)(2,1)} %bitcast.142), calls=%async_computation.24 | async-start | bytes 983040 | tf_op jit(solution)/shard_map/all_to_all | solution.py:382
  1973.1 25.2 all-to-all-done.7
  2050.6 91.0 %all-gather.58.cloned.1.call-done = bf16[1024,2560]{1,0:T(8,128)(2,1)} async-done(((bf16[1024,640]{1,0:T(8,128)(2,1)}), bf16[1024,2560]{1,0:T(8,128)(2,1)}) %all-gather.58.cloned.1.call-update) | async-done | bytes 5242896 | tf_op jit(solution)/shard_map/all_gather | solution.py:307
  2406.1 39.9 %reduce-scatter.159.cloned.1.call-done = bf16[120,640]{1,0:T(8,128)(2,1)} async-done(((bf16[960,640]{1,0:T(8,128)(2,1)}), bf16[120,640]{1,0:T(8,128)(2,1)}) %reduce-scatter.159.cloned.1.call-update) | async-done | bytes 153616
  2446.1 39.8 %reduce-scatter.157.cloned.1.call-done = bf16[120,640]{1,0:T(8,128)(2,1)} async-done(((bf16[960,640]{1,0:T(8,128)(2,1)}), bf16[120,640]{1,0:T(8,128)(2,1)}) %reduce-scatter.157.cloned.1.call-update) | async-done | bytes 153616
  2487.8 38.0 %reduce-scatter.155.cloned.1.call-done = bf16[120,640]{1,0:T(8,128)(2,1)} async-done(((bf16[960,640]{1,0:T(8,128)(2,1)}), bf16[120,640]{1,0:T(8,128)(2,1)}) %reduce-scatter.155.cloned.1.call-update) | async-done | bytes 153616
  2525.9 39.8 %reduce-scatter.153.cloned.1.call-done = bf16[120,640]{1,0:T(8,128)(2,1)} async-done(((bf16[960,640]{1,0:T(8,128)(2,1)}), bf16[120,640]{1,0:T(8,128)(2,1)}) %reduce-scatter.153.cloned.1.call-update) | async-done | bytes 153616
  2565.7 39.8 %reduce-scatter.151.cloned.1.call-done = bf16[120,640]{1,0:T(8,128)(2,1)} async-done(((bf16[960,640]{1,0:T(8,128)(2,1)}), bf16[120,640]{1,0:T(8,128)(2,1)}) %reduce-scatter.151.cloned.1.call-update) | async-done | bytes 153616
  2605.5 39.8 %reduce-scatter.149.cloned.1.call-done = bf16[120,640]{1,0:T(8,128)(2,1)} async-done(((bf16[960,640]{1,0:T(8,128)(2,1)}), bf16[120,640]{1,0:T(8,128)(2,1)}) %reduce-scatter.149.cloned.1.call-update) | async-done | bytes 153616
  2647.3 34.5 %reduce-scatter.131.cloned.1.call-done = bf16[120,240]{1,0:T(8,128)(2,1)} async-done(((bf16[960,240]{1,0:T(8,128)(2,1)}), bf16[120,240]{1,0:T(8,128)(2,1)}) %reduce-scatter.131.cloned.1.call-update) | async-done | bytes 57616 | tf_op jit(solution)/shard_map/reduce_scatter | solution.py:76
  2681.8 36.4 %reduce-scatter.127.cloned.1.call-done = bf16[120,240]{1,0:T(8,128)(2,1)} async-done(((bf16[960,240]{1,0:T(8,128)(2,1)}), bf16[120,240]{1,0:T(8,128)(2,1)}) %reduce-scatter.127.cloned.1.call-update) | async-done | bytes 57616 | tf_op jit(solution)/shard_map/reduce_scatter | solution.py:76
  2718.2 36.6 %reduce-scatter.129.cloned.1.call-done = bf16[120,240]{1,0:T(8,128)(2,1)} async-done(((bf16[960,240]{1,0:T(8,128)(2,1)}), bf16[120,240]{1,0:T(8,128)(2,1)}) %reduce-scatter.129.cloned.1.call-update) | async-done | bytes 57616 | tf_op jit(solution)/shard_map/reduce_scatter | solution.py:76
  2754.8 36.4 %reduce-scatter.125.cloned.1.call-done = bf16[120,240]{1,0:T(8,128)(2,1)} async-done(((bf16[960,240]{1,0:T(8,128)(2,1)}), bf16[120,240]{1,0:T(8,128)(2,1)}) %reduce-scatter.125.cloned.1.call-update) | async-done | bytes 57616 | tf_op jit(solution)/shard_map/reduce_scatter | solution.py:76
  2792.8 37.6 %all-reduce.37.cloned.1.call-done = (bf16[1024,4,1]{0,2,1:T(2,128)(2,1)}, bf16[1024,4,1]{0,2,1:T(2,128)(2,1)}, bf16[1024,4,1]{0,2,1:T(2,128)(2,1)}, bf16[1024,4,...) async-done(((bf16[1024,4,1]{0,2,1:T(2,128)(2,1)}, ...) | async-done | bytes 65552
  2867.0 36.9 %reduce-scatter.121.cloned.1.call-done = bf16[120,240]{1,0:T(8,128)(2,1)} async-done(((bf16[960,240]{1,0:T(8,128)(2,1)}), bf16[120,240]{1,0:T(8,128)(2,1)}) %reduce-scatter.121.cloned.1.call-update) | async-done | bytes 57616 | tf_op jit(solution)/shard_map/reduce_scatter | solution.py:67
  2904.0 36.9 %reduce-scatter.119.cloned.1.call-done = bf16[120,240]{1,0:T(8,128)(2,1)} async-done(((bf16[960,240]{1,0:T(8,128)(2,1)}), bf16[120,240]{1,0:T(8,128)(2,1)}) %reduce-scatter.119.cloned.1.call-update) | async-done | bytes 57616 | tf_op jit(solution)/shard_map/reduce_scatter | solution.py:67
  2940.9 36.9 %reduce-scatter.117.cloned.1.call-done = bf16[120,240]{1,0:T(8,128)(2,1)} async-done(((bf16[960,240]{1,0:T(8,128)(2,1)}), bf16[120,240]{1,0:T(8,128)(2,1)}) %reduce-scatter.117.cloned.1.call-update) | async-done | bytes 57616 | tf_op jit(solution)/shard_map/reduce_scatter | solution.py:67
  2979.4 39.9 %reduce-scatter.139.cloned.1.call-done = bf16[320,240]{1,0:T(8,128)(2,1)} async-done(((bf16[2560,240]{1,0:T(8,128)(2,1)}), bf16[320,240]{1,0:T(8,128)(2,1)}) %reduce-scatter.139.cloned.1.call-update) | async-done | bytes 153616 | tf_op jit(solution)/shard_map/reduce_scatter | solution.py:85
  3019.3 40.8 %reduce-scatter.137.cloned.1.call-done = bf16[320,240]{1,0:T(8,128)(2,1)} async-done(((bf16[2560,240]{1,0:T(8,128)(2,1)}), bf16[320,240]{1,0:T(8,128)(2,1)}) %reduce-scatter.137.cloned.1.call-update) | async-done | bytes 153616 | tf_op jit(solution)/shard_map/reduce_scatter | solution.py:85
  3060.1 40.8 %reduce-scatter.135.cloned.1.call-done = bf16[320,240]{1,0:T(8,128)(2,1)} async-done(((bf16[2560,240]{1,0:T(8,128)(2,1)}), bf16[320,240]{1,0:T(8,128)(2,1)}) %reduce-scatter.135.cloned.1.call-update) | async-done | bytes 153616 | tf_op jit(solution)/shard_map/reduce_scatter | solution.py:85
  3100.9 41.0 %reduce-scatter.133.cloned.1.call-done = bf16[320,240]{1,0:T(8,128)(2,1)} async-done(((bf16[2560,240]{1,0:T(8,128)(2,1)}), bf16[320,240]{1,0:T(8,128)(2,1)}) %reduce-scatter.133.cloned.1.call-update) | async-done | bytes 153616 | tf_op jit(solution)/shard_map/reduce_scatter | solution.py:85
  3143.8 61.8 %all-reduce.35.cloned.1.call-done = (bf16[960,80]{0,1:T(8,128)(2,1)}, bf16[960,80]{0,1:T(8,128)(2,1)}, bf16[960,80]{0,1:T(8,128)(2,1)}, bf16[960,80]{0,1:T(8,128...) async-done(((bf16[960,80]{0,1:T(8,128)(2,1)}, bf16[960,80]{0,1:T(8,128)(2,1)}, ...) | async-done | bytes 1228816
  3208.8 39.8 %reduce-scatter.105.cloned.1.call-done = bf16[1024,240]{0,1:T(8,128)(2,1)} async-done(((bf16[1024,960]{0,1:T(8,128)(2,1)}), bf16[1024,240]{0,1:T(8,128)(2,1)}) %reduce-scatter.105.cloned.1.call-update) | async-done | bytes 491536 | tf_op jit(solution)/shard_map/reduce_scatter | solution.py:55
  3248.6 42.9 %reduce-scatter.115.cloned.1.call-done = bf16[1024,240]{0,1:T(8,128)(2,1)} async-done(((bf16[1024,960]{0,1:T(8,128)(2,1)}), bf16[1024,240]{0,1:T(8,128)(2,1)}) %reduce-scatter.115.cloned.1.call-update) | async-done | bytes 491536 | tf_op jit(solution)/shard_map/reduce_scatter | solution.py:55
  3291.5 42.9 %reduce-scatter.85.cloned.1.call-done = bf16[1024,240]{0,1:T(8,128)(2,1)} async-done(((bf16[1024,960]{0,1:T(8,128)(2,1)}), bf16[1024,240]{0,1:T(8,128)(2,1)}) %reduce-scatter.85.cloned.1.call-update) | async-done | bytes 491536 | tf_op jit(solution)/shard_map/reduce_scatter | solution.py:55
  3334.3 43.0 %reduce-scatter.95.cloned.1.call-done = bf16[1024,240]{0,1:T(8,128)(2,1)} async-done(((bf16[1024,960]{0,1:T(8,128)(2,1)}), bf16[1024,240]{0,1:T(8,128)(2,1)}) %reduce-scatter.95.cloned.1.call-update) | async-done | bytes 491536 | tf_op jit(solution)/shard_map/reduce_scatter | solution.py:55
  (1199 shorter events, 1329.6 us)
Async XLA Ops:
  493.0 213.7 %all-gather.34.cloned.1.call-start = ((), (), s32[]{:S(2)}) async-start(), calls=%async_computation.58 | async-start | bytes 1474560 | tf_op jit(solution)/shard_map/all_gather | solution.py:235
  493.8 274.1 %all-gather.56.cloned.1.call-start = ((), (), s32[]{:S(2)}) async-start(), calls=%async_computation.69 | async-start | bytes 2457600 | tf_op jit(solution)/shard_map/all_gather | solution.py:43
  689.3 220.3 %all-gather.28.cloned.1.call-start = ((), (), s32[]{:S(2)}) async-start(), calls=%async_computation.55 | async-start | bytes 1382400 | tf_op jit(solution)/shard_map/all_gather | solution.py:233
  689.9 315.7 %reduce-scatter.147.cloned.1.call-start = ((), (), s32[]{:S(2)}) async-start(), calls=%async_computation.106 | async-start | bytes 6553600
  720.3 381.7 %reduce-scatter.145.cloned.1.call-start = ((), (), s32[]{:S(2)}) async-start(), calls=%async_computation.105 | async-start | bytes 6553600
  735.6 462.8 %reduce-scatter.143.cloned.1.call-start = ((), (), s32[]{:S(2)}) async-start(), calls=%async_computation.104 | async-start | bytes 6553600
  751.3 543.6 %reduce-scatter.141.cloned.1.call-start = ((), (), s32[]{:S(2)}) async-start(), calls=%async_computation.103 | async-start | bytes 6553600
  766.9 554.7 %all-gather.30.cloned.1.call-start = ((), (), s32[]{:S(2)}) async-start(), calls=%async_computation.56 | async-start | bytes 1382400 | tf_op jit(solution)/shard_map/all_gather | solution.py:234
  767.6 647.2 %reduce-scatter.77.cloned.1.call-start = ((), (), s32[]{:S(2)}) async-start(), calls=%async_computation.71 | async-start | bytes 2457600 | tf_op jit(solution)/shard_map/reduce_scatter | solution.py:55
  1373.5 213.9 %reduce-scatter.79.cloned.1.call-start = ((), (), s32[]{:S(2)}) async-start(), calls=%async_computation.72 | async-start | bytes 2457600 | tf_op jit(solution)/shard_map/reduce_scatter | solution.py:350
  1555.2 451.1 %all-gather.32.cloned.1.call-start = ((), (), s32[]{:S(2)}) async-start(), calls=%async_computation.57 | async-start | bytes 6553600 | tf_op jit(solution)/shard_map/all_gather | solution.py:307
  1555.9 475.7 %all-gather.42.cloned.1.call-start = ((), (), s32[]{:S(2)}) async-start(), calls=%async_computation.62 | async-start | bytes 6553600 | tf_op jit(solution)/shard_map/all_gather | solution.py:307
  1556.7 481.9 %all-gather.50.cloned.1.call-start = ((), (), s32[]{:S(2)}) async-start(), calls=%async_computation.66 | async-start | bytes 6553600 | tf_op jit(solution)/shard_map/all_gather | solution.py:307
  1557.3 584.3 %all-gather.58.cloned.1.call-start = ((), (), s32[]{:S(2)}) async-start(), calls=%async_computation.70 | async-start | bytes 6553600 | tf_op jit(solution)/shard_map/all_gather | solution.py:307
  1558.0 606.3 %reduce-scatter.111.cloned.1.call-start = ((), (), s32[]{:S(2)}) async-start(), calls=%async_computation.88 | async-start | bytes 819200 | tf_op jit(solution)/shard_map/reduce_scatter | solution.py:385
  1768.0 419.5 %reduce-scatter.101.cloned.1.call-start = ((), (), s32[]{:S(2)}) async-start(), calls=%async_computation.83 | async-start | bytes 819200 | tf_op jit(solution)/shard_map/reduce_scatter | solution.py:385
  1770.1 440.8 %reduce-scatter.91.cloned.1.call-start = ((), (), s32[]{:S(2)}) async-start(), calls=%async_computation.78 | async-start | bytes 819200 | tf_op jit(solution)/shard_map/reduce_scatter | solution.py:385
  1771.1 463.2 %reduce-scatter.81.cloned.1.call-start = ((), (), s32[]{:S(2)}) async-start(), calls=%async_computation.73 | async-start | bytes 819200 | tf_op jit(solution)/shard_map/reduce_scatter | solution.py:385
  1772.1 485.4 %reduce-scatter.103.cloned.1.call-start = ((), (), s32[]{:S(2)}) async-start(), calls=%async_computation.84 | async-start | bytes 819200 | tf_op jit(solution)/shard_map/reduce_scatter | solution.py:388
  1774.5 506.2 %reduce-scatter.93.cloned.1.call-start = ((), (), s32[]{:S(2)}) async-start(), calls=%async_computation.79 | async-start | bytes 819200 | tf_op jit(solution)/shard_map/reduce_scatter | solution.py:388
  1776.8 527.2 %reduce-scatter.83.cloned.1.call-start = ((), (), s32[]{:S(2)}) async-start(), calls=%async_computation.74 | async-start | bytes 819200 | tf_op jit(solution)/shard_map/reduce_scatter | solution.py:388
  1779.4 547.8 %reduce-scatter.113.cloned.1.call-start = ((), (), s32[]{:S(2)}) async-start(), calls=%async_computation.89 | async-start | bytes 819200 | tf_op jit(solution)/shard_map/reduce_scatter | solution.py:388
  1781.7 621.0 %reduce-scatter.163.cloned.1.call-start = ((), (), s32[]{:S(2)}) async-start(), calls=%async_computation.114 | async-start | bytes 1382400
  1786.5 619.6 %reduce-scatter.161.cloned.1.call-start = ((), (), s32[]{:S(2)}) async-start(), calls=%async_computation.113 | async-start | bytes 1382400
  1791.4 654.7 %reduce-scatter.159.cloned.1.call-start = ((), (), s32[]{:S(2)}) async-start(), calls=%async_computation.112 | async-start | bytes 1382400
  1796.2 689.7 %reduce-scatter.157.cloned.1.call-start = ((), (), s32[]{:S(2)}) async-start(), calls=%async_computation.111 | async-start | bytes 1382400
  1801.0 724.9 %reduce-scatter.155.cloned.1.call-start = ((), (), s32[]{:S(2)}) async-start(), calls=%async_computation.110 | async-start | bytes 1382400
  1805.8 759.9 %reduce-scatter.153.cloned.1.call-start = ((), (), s32[]{:S(2)}) async-start(), calls=%async_computation.109 | async-start | bytes 1382400
  1810.5 795.0 %reduce-scatter.151.cloned.1.call-start = ((), (), s32[]{:S(2)}) async-start(), calls=%async_computation.108 | async-start | bytes 1382400
  1815.3 830.0 %reduce-scatter.149.cloned.1.call-start = ((), (), s32[]{:S(2)}) async-start(), calls=%async_computation.107 | async-start | bytes 1382400
  1820.2 861.6 %reduce-scatter.131.cloned.1.call-start = ((), (), s32[]{:S(2)}) async-start(), calls=%async_computation.98 | async-start | bytes 552960 | tf_op jit(solution)/shard_map/reduce_scatter | solution.py:76
  1823.4 894.8 %reduce-scatter.127.cloned.1.call-start = ((), (), s32[]{:S(2)}) async-start(), calls=%async_computation.96 | async-start | bytes 552960 | tf_op jit(solution)/shard_map/reduce_scatter | solution.py:76
  1969.0 785.8 %reduce-scatter.129.cloned.1.call-start = ((), (), s32[]{:S(2)}) async-start(), calls=%async_computation.97 | async-start | bytes 552960 | tf_op jit(solution)/shard_map/reduce_scatter | solution.py:76
  2002.4 788.9 %reduce-scatter.125.cloned.1.call-start = ((), (), s32[]{:S(2)}) async-start(), calls=%async_computation.95 | async-start | bytes 552960 | tf_op jit(solution)/shard_map/reduce_scatter | solution.py:76
  2050.4 780.1 %all-reduce.37.cloned.1.call-start = ((), (), s32[]{:S(2)}) async-start(), calls=%async_computation.116 | async-start | bytes 262144
  2350.6 516.4 %reduce-scatter.123.cloned.1.call-start = ((), (), s32[]{:S(2)}) async-start(), calls=%async_computation.94 | async-start | bytes 552960 | tf_op jit(solution)/shard_map/reduce_scatter | solution.py:67
  2354.2 549.8 %reduce-scatter.121.cloned.1.call-start = ((), (), s32[]{:S(2)}) async-start(), calls=%async_computation.93 | async-start | bytes 552960 | tf_op jit(solution)/shard_map/reduce_scatter | solution.py:67
  2355.8 585.1 %reduce-scatter.119.cloned.1.call-start = ((), (), s32[]{:S(2)}) async-start(), calls=%async_computation.92 | async-start | bytes 552960 | tf_op jit(solution)/shard_map/reduce_scatter | solution.py:67
  2359.0 618.8 %reduce-scatter.117.cloned.1.call-start = ((), (), s32[]{:S(2)}) async-start(), calls=%async_computation.91 | async-start | bytes 552960 | tf_op jit(solution)/shard_map/reduce_scatter | solution.py:67
  2362.2 657.1 %reduce-scatter.139.cloned.1.call-start = ((), (), s32[]{:S(2)}) async-start(), calls=%async_computation.102 | async-start | bytes 1474560 | tf_op jit(solution)/shard_map/reduce_scatter | solution.py:85
  2367.7 692.4 %reduce-scatter.137.cloned.1.call-start = ((), (), s32[]{:S(2)}) async-start(), calls=%async_computation.101 | async-start | bytes 1474560 | tf_op jit(solution)/shard_map/reduce_scatter | solution.py:85
  2373.1 727.8 %reduce-scatter.135.cloned.1.call-start = ((), (), s32[]{:S(2)}) async-start(), calls=%async_computation.100 | async-start | bytes 1474560 | tf_op jit(solution)/shard_map/reduce_scatter | solution.py:85
  2378.8 763.1 %reduce-scatter.133.cloned.1.call-start = ((), (), s32[]{:S(2)}) async-start(), calls=%async_computation.99 | async-start | bytes 1474560 | tf_op jit(solution)/shard_map/reduce_scatter | solution.py:85
  2384.5 821.2 %all-reduce.35.cloned.1.call-start = ((), (), s32[]{:S(2)}) async-start(), calls=%async_computation.115 | async-start | bytes 2621440
  2397.9 850.7 %reduce-scatter.105.cloned.1.call-start = ((), (), s32[]{:S(2)}) async-start(), calls=%async_computation.85 | async-start | bytes 2457600 | tf_op jit(solution)/shard_map/reduce_scatter | solution.py:55
  2398.6 892.8 %reduce-scatter.115.cloned.1.call-start = ((), (), s32[]{:S(2)}) async-start(), calls=%async_computation.90 | async-start | bytes 2457600 | tf_op jit(solution)/shard_map/reduce_scatter | solution.py:55
  2399.2 935.1 %reduce-scatter.85.cloned.1.call-start = ((), (), s32[]{:S(2)}) async-start(), calls=%async_computation.75 | async-start | bytes 2457600 | tf_op jit(solution)/shard_map/reduce_scatter | solution.py:55
  2399.8 977.6 %reduce-scatter.95.cloned.1.call-start = ((), (), s32[]{:S(2)}) async-start(), calls=%async_computation.80 | async-start | bytes 2457600 | tf_op jit(solution)/shard_map/reduce_scatter | solution.py:55
  (248 other events, 18293.9 us)
Sparse Core Ops, SparseCore 0:
  20.0 46.2 all-gather.51
  67.9 42.3 all-gather.43
  112.4 42.3 all-gather.35
  156.3 42.3 all-gather.21
  440.1 65.1 all-gather.45
  507.3 86.2 all-gather.37
  595.6 42.3 all-gather.23
  639.6 42.3 all-gather.53
  708.7 43.5 all-gather.55
  753.9 42.3 all-gather.47
  798.3 42.3 all-gather.39
  842.3 42.3 all-gather.25
  911.8 93.7 reduce-scatter.146
  1007.7 94.2 reduce-scatter.144
  1104.1 94.2 reduce-scatter.142
  1200.6 94.2 reduce-scatter.140
  1371.4 43.3 reduce-scatter.76
  1417.7 40.7 reduce-scatter.96
  1460.8 40.6 reduce-scatter.106
  1503.8 40.6 reduce-scatter.86
  1546.7 40.6 reduce-scatter.78
  1589.7 40.6 reduce-scatter.108
  1633.2 40.6 reduce-scatter.88
  1676.6 40.6 reduce-scatter.98
  1718.9 97.2 all-gather.31
  1817.9 96.4 all-gather.41
  1915.8 117.3 all-gather.49
  2034.8 106.7 all-gather.57
  2330.6 35.5 reduce-scatter.162
  2369.4 36.6 reduce-scatter.160
  2409.5 36.5 reduce-scatter.158
  2449.3 36.5 reduce-scatter.156
  2489.2 36.5 reduce-scatter.154
  2529.1 36.5 reduce-scatter.152
  2568.9 36.5 reduce-scatter.150
  2608.7 36.5 reduce-scatter.148
  2795.2 35.1 all-reduce.36
  2870.5 33.4 reduce-scatter.120
  2907.4 33.4 reduce-scatter.118
  2982.0 37.2 reduce-scatter.138
  3022.8 37.2 reduce-scatter.136
  3063.5 37.3 reduce-scatter.134
  3104.5 37.3 reduce-scatter.132
  3146.4 59.2 all-reduce.34
  3208.0 40.5 reduce-scatter.104
  3250.7 40.6 reduce-scatter.114
  3293.6 40.6 reduce-scatter.84
  3336.6 40.6 reduce-scatter.94
  (17 shorter events, 437.7 us)
where the time goes:
time: 3430 us; the launch traced here: 3410 us
  waiting for transfers between devices  2270 us (66%)
  matrix products  441 us (13%)
  blocking collectives  235 us (7%)
  starting transfers between devices  173 us (5%)
  other arithmetic  161 us (5%)
  local copies, waits for them, and re-layouts  100 us (3%)
    unnamed x79, waiting for transfers between devices  715 us
    reduce_scatter x8, waiting for transfers between devices, split_sums(): lax.psum_scatter(partial_value.astype(jnp.bfloat16), 'col', scatter_dimen...  305 us
    all_gather x8, waiting for transfers between devices, full_features(): lax.all_gather(values_major.astype(jnp.bfloat16), 'col', axis=0, tiled=True)  244 us
    all_gather x4, waiting for transfers between devices, on_device(): attended_all = lax.all_gather(attended_low, 'col', axis=0, tiled=True)  166 us
    reduce_scatter x4, waiting for transfers between devices, row_share(): lax.psum_scatter(gradients[6].astype(jnp.bfloat16), 'row', scatter_dimens...  162 us
    all_to_all x4, starting transfers between devices, on_device(): lax.all_to_all(grad_q_raw, 'col', split_axis=1, concat_axis=0, tiled=True)  151 us
    reduce_scatter x4, waiting for transfers between devices, row_share(): lax.psum_scatter(gradients[3].astype(jnp.bfloat16), 'row', scatter_dimens...  144 us
    reduce_scatter x4, waiting for transfers between devices, row_share(): lax.psum_scatter(gradients[0].astype(jnp.bfloat16), 'row', scatter_dimens...  132 us
  transfers between devices with their start and end apart: 73, of which 62 were waited for; matrix products, arithmetic and copies ran while one was open for 17% of the time, Pallas kernels for 0%

commit v1 on v0

v1 whole, which is shorter than its diff:
```python
import functools
import math

import jax
import jax.numpy as jnp
from jax import lax
from jax.experimental import pallas as pl
from jax.experimental.pallas import tpu as pltpu
from jax.sharding import PartitionSpec as P

H = 15
KVH = 5
HD = 64
GROUP = H // KVH
QBLOCK = 256

EPSILON = 1e-05
ROPE_BASE = 10000.0
NEG = -1e30

BF = jnp.bfloat16
F32 = jnp.float32
MIB = 1 << 20


def dot_nn(a, b):
    return lax.dot_general(a, b, (((1,), (0,)), ((), ())), preferred_element_type=F32)


def dot_tn(a, b):
    return lax.dot_general(a, b, (((0,), (0,)), ((), ())), preferred_element_type=F32)


def dot_nt(a, b):
    return lax.dot_general(a, b, (((1,), (1,)), ((), ())), preferred_element_type=F32)


def params(limit=56):
    return pltpu.CompilerParams(
        dimension_semantics=("arbitrary",), vmem_limit_bytes=limit * MIB
    )


def cost(flops, nbytes, exps=0):
    return pl.CostEstimate(
        flops=int(flops), bytes_accessed=int(nbytes), transcendentals=int(exps)
    )


def struct(shape, dtype):
    return jax.ShapeDtypeStruct(shape, dtype)


def whole(shape):
    return pl.BlockSpec(shape, lambda i: (0,) * len(shape))


def pick_columns(rank_column, picks):
    place = lax.broadcasted_iota(jnp.int32, (rank_column.shape[0], picks), 1)
    return jnp.where(rank_column == place, 1.0, 0.0).astype(BF)


def pick_rows(rank_row, picks):
    place = lax.broadcasted_iota(jnp.int32, (picks, rank_row.shape[1]), 0)
    return jnp.where(rank_row == place, 1.0, 0.0).astype(BF)


def turn(first, second, cosine, sine, direction):
    signed = sine * direction
    return first * cosine - second * signed, second * cosine + first * signed


def gather_body(values, rank, out):
    chosen = pick_columns(rank[0], out.shape[2])
    out[0] = dot_nn(values[0].astype(BF), chosen).astype(BF)


def gather_tokens(values, rank_column, picks):
    count, width, length = values.shape
    return pl.pallas_call(
        gather_body,
        grid=(count,),
        in_specs=[
            pl.BlockSpec((1, width, length), lambda i: (i, 0, 0)),
            pl.BlockSpec((1, length, 1), lambda i: (i, 0, 0)),
        ],
        out_specs=pl.BlockSpec((1, width, picks), lambda i: (i, 0, 0)),
        out_shape=struct((count, width, picks), BF),
        compiler_params=params(),
        cost_estimate=cost(2 * count * width * length * picks, 6 * values.size),
        name="gather_tokens",
    )(values, rank_column)


def scatter_body(base, values, rank, out):
    chosen = pick_rows(rank[0], values.shape[2])
    out[0] = base[0] + dot_nn(values[0], chosen)


def scatter_tokens(base, values, rank_row):
    count, width, length = base.shape
    picks = values.shape[2]
    return pl.pallas_call(
        scatter_body,
        grid=(count,),
        in_specs=[
            pl.BlockSpec((1, width, length), lambda i: (i, 0, 0)),
            pl.BlockSpec((1, width, picks), lambda i: (i, 0, 0)),
            pl.BlockSpec((1, 1, length), lambda i: (i, 0, 0)),
        ],
        out_specs=pl.BlockSpec((1, width, length), lambda i: (i, 0, 0)),
        out_shape=struct(base.shape, F32),
        compiler_params=params(),
        cost_estimate=cost(2 * count * width * length * picks, 10 * base.size),
        name="scatter_tokens",
    )(base, values, rank_row)


def project_body(
    x, rank, gain, router, cos_k, sin_k, cos_q, sin_q, w,
    picked, prob, q_out, kt_out, k_out, vt_out, v_out,
    normed, normed_picked, q_raw, kv_raw,
):
    step = pl.program_id(0)
    width = x.shape[0]
    q_part = q_raw.shape[0] // w_count(w, width)
    kv_part = (w.shape[2] - q_part) // 2

    @pl.when(step == 0)
    def _():
        full = x[...].astype(F32)
        inverse = lax.rsqrt(jnp.sum(full * full, axis=0, keepdims=True) / width + EPSILON)
        normed[...] = (full * inverse * gain[...]).astype(BF)
        chosen = pick_columns(rank[...], picked.shape[1])
        part = dot_nn(x[...], chosen)
        picked[...] = part.astype(BF)
        inverse = lax.rsqrt(jnp.sum(part * part, axis=0, keepdims=True) / width + EPSILON)
        normed_picked[...] = (part * inverse * gain[...]).astype(BF)
        logit = jnp.sum(part * router[...], axis=0, keepdims=True)
        prob[...] = jax.nn.sigmoid(logit)

    q_raw[pl.ds(pl.multiple_of(step * q_part, 8), q_part)] = dot_tn(
        w[0, :, :q_part], normed_picked[...]
    ).astype(BF)
    kv = dot_tn(w[0, :, q_part:], normed[...]).astype(BF)
    kv_raw[0, pl.ds(pl.multiple_of(step * kv_part, 8), kv_part)] = kv[:kv_part]
    kv_raw[1, pl.ds(pl.multiple_of(step * kv_part, 8), kv_part)] = kv[kv_part:]

    @pl.when(step == pl.num_programs(0) - 1)
    def _():
        half = HD // 2
        for head in range(H):
            at = head * HD
            a, b = turn(
                q_raw[at : at + half].astype(F32),
                q_raw[at + half : at + HD].astype(F32),
                cos_q[...], sin_q[...], 1.0,
            )
            scale = HD ** (-0.5)
            q_out[at : at + half] = (a.astype(BF).astype(F32) * scale).astype(BF)
            q_out[at + half : at + HD] = (b.astype(BF).astype(F32) * scale).astype(BF)
        for head in range(KVH):
            at = head * HD
            a, b = turn(
                kv_raw[0, at : at + half].astype(F32),
                kv_raw[0, at + half : at + HD].astype(F32),
                cos_k[...], sin_k[...], 1.0,
            )
            turned = jnp.concatenate([a, b], axis=0)
            kt_out[at : at + HD] = turned.astype(BF)
            k_out[head] = turned.T.astype(BF)
            value = kv_raw[1, at : at + HD]
            vt_out[at : at + HD] = value
            v_out[head] = value.astype(F32).T.astype(BF)


def w_count(w, width):
    whole_width = width + 2 * (width * KVH // H)
    return whole_width // w.shape[2]


def project(x, rank_column, gain, router, tables_k, tables_q, w):
    width, length = x.shape
    picks = tables_q[0].shape[1]
    blocks, _, part = w.shape
    kv = KVH * HD
    half = HD // 2
    return pl.pallas_call(
        project_body,
        grid=(blocks,),
        in_specs=[
            whole((width, length)),
            whole((length, 1)),
            whole((width, 1)),
            whole((width, 1)),
            whole((half, length)),
            whole((half, length)),
            whole((half, picks)),
            whole((half, picks)),
            pl.BlockSpec((1, width, part), lambda i: (i, 0, 0)),
        ],
        out_specs=[
            whole((width, picks)),
            whole((1, picks)),
            whole((width, picks)),
            whole((kv, length)),
            whole((KVH, length, HD)),
            whole((kv, length)),
            whole((KVH, length, HD)),
        ],
        out_shape=[
            struct((width, picks), BF),
            struct((1, picks), F32),
            struct((width, picks), BF),
            struct((kv, length), BF),
            struct((KVH, length, HD), BF),
            struct((kv, length), BF),
            struct((KVH, length, HD), BF),
        ],
        scratch_shapes=[
            pltpu.VMEM((width, length), BF),
            pltpu.VMEM((width, picks), BF),
            pltpu.VMEM((width, picks), BF),
            pltpu.VMEM((2, kv, length), BF),
        ],
        compiler_params=params(),
        cost_estimate=cost(
            2 * width * (length * picks + picks * width + length * 2 * kv),
            2 * (w.size + 4 * x.size),
        ),
        name="project",
    )(x, rank_column, gain, router, *tables_k, *tables_q, w)


def reach_of(block, length, picks):
    return max((block + 1) * QBLOCK + length - picks, length // 2)


def clear_of(block):
    return block * QBLOCK


def block_scores(q, k, limit, block, reach):
    scores = dot_nn(k[:reach], q)
    clear = clear_of(block)
    tail = scores[clear:] if clear else scores
    key = lax.broadcasted_iota(jnp.int32, tail.shape, 0) + clear
    tail = jnp.where(key <= limit, tail, NEG)
    return jnp.concatenate([scores[:clear], tail], axis=0) if clear else tail


def attend_body(q, k, vt, limit, out, total):
    length = k.shape[1]
    picks = q.shape[1]
    for block in range(picks // QBLOCK):
        at = block * QBLOCK
        reach = reach_of(block, length, picks)
        for head in range(GROUP):
            rows = slice(head * HD, (head + 1) * HD)
            scores = block_scores(
                q[rows, at : at + QBLOCK], k[0], limit[:, at : at + QBLOCK], block, reach
            )
            top = jnp.max(scores, axis=0, keepdims=True)
            weight = jnp.exp(scores - top)
            mass = jnp.sum(weight, axis=0, keepdims=True)
            mixed = dot_nn(vt[:, :reach], weight.astype(BF))
            out[rows, at : at + QBLOCK] = (mixed / mass).astype(BF)
            total[0, head : head + 1, at : at + QBLOCK] = top + jnp.log(mass)


def attend(q, k, vt, limit):
    width, picks = q.shape
    length = k.shape[1]
    part = GROUP * HD
    return pl.pallas_call(
        attend_body,
        grid=(KVH,),
        in_specs=[
            pl.BlockSpec((part, picks), lambda i: (i, 0)),
            pl.BlockSpec((1, length, HD), lambda i: (i, 0, 0)),
            pl.BlockSpec((HD, length), lambda i: (i, 0)),
            whole((1, picks)),
        ],
        out_specs=[
            pl.BlockSpec((part, picks), lambda i: (i, 0)),
            pl.BlockSpec((1, GROUP, picks), lambda i: (i, 0, 0)),
        ],
        out_shape=[struct((width, picks), BF), struct((KVH, GROUP, picks), F32)],
        compiler_params=params(),
        cost_estimate=cost(
            16 * width * length * picks, 4 * width * picks, H * length * picks
        ),
        name="attend",
    )(q, k, vt, limit)


def attend_back_body(
    q, k, kt, v, limit, total, grad, mixed, cos_k, sin_k, cos_q, sin_q,
    gq_out, gk_out, gv_out, gk, gv,
):
    length = k.shape[1]
    picks = q.shape[1]
    half = HD // 2
    gk[...] = jnp.zeros_like(gk)
    gv[...] = jnp.zeros_like(gv)
    for block in range(picks // QBLOCK):
        at = block * QBLOCK
        cols = slice(at, at + QBLOCK)
        reach = reach_of(block, length, picks)
        for head in range(GROUP):
            rows = slice(head * HD, (head + 1) * HD)
            q_part = q[rows, cols]
            g_part = grad[rows, cols]
            scores = block_scores(q_part, k[0], limit[:, cols], block, reach)
            weight = jnp.exp(scores - total[0, head : head + 1, cols])
            delta = jnp.sum(
                g_part.astype(F32) * mixed[rows, cols].astype(F32), axis=0, keepdims=True
            )
            pull = dot_nn(v[0, :reach], g_part)
            back = (weight * (pull - delta)).astype(BF)
            gq = dot_nn(kt[:, :reach], back) * HD ** (-0.5)
            a, b = turn(gq[:half], gq[half:], cos_q[:, cols], sin_q[:, cols], -1.0)
            gq_out[head * HD : head * HD + half, cols] = a.astype(BF)
            gq_out[head * HD + half : (head + 1) * HD, cols] = b.astype(BF)
            gk[:reach] += dot_nt(back, q_part)
            gv[:reach] += dot_nt(weight.astype(BF), g_part)
    turned = gk[...].T
    a, b = turn(turned[:half], turned[half:], cos_k[...], sin_k[...], -1.0)
    gk_out[:half] = a.astype(BF)
    gk_out[half:] = b.astype(BF)
    gv_out[...] = gv[...].T.astype(BF)


def attend_back(q, k, kt, v, limit, total, grad, mixed, tables_k, tables_q):
    width, picks = q.shape
    length = k.shape[1]
    part = GROUP * HD
    half = HD // 2
    wide = pl.BlockSpec((part, picks), lambda i: (i, 0))
    tall = pl.BlockSpec((1, length, HD), lambda i: (i, 0, 0))
    flat = pl.BlockSpec((HD, length), lambda i: (i, 0))
    return pl.pallas_call(
        attend_back_body,
        grid=(KVH,),
        in_specs=[
            wide, tall, flat, tall, whole((1, picks)),
            pl.BlockSpec((1, GROUP, picks), lambda i: (i, 0, 0)),
            wide, wide,
            whole((half, length)), whole((half, length)),
            whole((half, picks)), whole((half, picks)),
        ],
        out_specs=[wide, flat, flat],
        out_shape=[
            struct((width, picks), BF),
            struct((KVH * HD, length), BF),
            struct((KVH * HD, length), BF),
        ],
        scratch_shapes=[pltpu.VMEM((length, HD), F32), pltpu.VMEM((length, HD), F32)],
        compiler_params=params(),
        cost_estimate=cost(
            40 * width * length * picks, 8 * width * picks, H * length * picks
        ),
        name="attend_back",
    )(q, k, kt, v, limit, total, grad, mixed, *tables_k, *tables_q)


def merge_body(mixed, picked, cot, prob, gain, w, branch, inverse_out, normed, grad_ffn, hidden, square):
    step = pl.program_id(0)
    width = mixed.shape[0]
    part = w.shape[2]
    rows = pl.ds(pl.multiple_of(step * part, 8), part)

    @pl.when(step == 0)
    def _():
        square[...] = jnp.zeros_like(square)
        grad_ffn[...] = (prob[...] * cot[...].astype(F32)).astype(BF)

    value = dot_tn(w[0], mixed[...])
    branch[...] = value
    total = picked[rows, :].astype(F32) + value
    hidden[rows, :] = total
    square[...] += jnp.sum(total * total, axis=0, keepdims=True)

    @pl.when(step == pl.num_programs(0) - 1)
    def _():
        inverse = lax.rsqrt(square[...] / width + EPSILON)
        inverse_out[...] = inverse
        normed[...] = (hidden[...] * inverse * gain[...]).astype(BF)


def merge(mixed, picked, cot, prob, gain, w):
    width, picks = mixed.shape
    blocks, _, part = w.shape
    return pl.pallas_call(
        merge_body,
        grid=(blocks,),
        in_specs=[
            whole((width, picks)),
            whole((width, picks)),
            whole((width, picks)),
            whole((1, picks)),
            whole((width, 1)),
            pl.BlockSpec((1, width, part), lambda i: (i, 0, 0)),
        ],
        out_specs=[
            pl.BlockSpec((part, picks), lambda i: (i, 0)),
            whole((1, picks)),
            whole((width, picks)),
            whole((width, picks)),
        ],
        out_shape=[
            struct((width, picks), F32),
            struct((1, picks), F32),
            struct((width, picks), BF),
            struct((width, picks), BF),
        ],
        scratch_shapes=[pltpu.VMEM((width, picks), F32), pltpu.VMEM((1, picks), F32)],
        compiler_params=params(),
        cost_estimate=cost(2 * width * width * picks, 14 * width * picks + 2 * w.size),
        name="merge",
    )(mixed, picked, cot, prob, gain, w)


def ffn_body(
    normed, grad_ffn, branch, picked, cot, prob, inverse, gain, router, w_gate, w_up, w_down,
    delta_out, grad_attn, rest_out, logit_out, gain_out, router_out, gw_gate, gw_up, gw_down,
    forward, backward,
):
    step = pl.program_id(0)
    width = normed.shape[0]
    columns, _, part = w_down.shape

    @pl.when(step == 0)
    def _():
        forward[...] = jnp.zeros_like(forward)
        backward[...] = jnp.zeros_like(backward)

    tokens = normed[...]
    gate = dot_tn(w_gate[0], tokens)
    up = dot_tn(w_up[0], tokens)
    pull = dot_nn(w_down[0], grad_ffn[:part])
    for c in range(1, columns):
        pull += dot_nn(w_down[c], grad_ffn[c * part : (c + 1) * part])
    sigmoid = jax.nn.sigmoid(gate)
    silu = gate * sigmoid
    active = (silu * up).astype(BF)
    grad_gate = (pull * up * sigmoid * (1.0 + gate * (1.0 - sigmoid))).astype(BF)
    grad_up = (pull * silu).astype(BF)
    for c in range(columns):
        rows = slice(c * part, (c + 1) * part)
        forward[rows] += dot_tn(w_down[c], active)
        gw_down[c] = dot_nt(active, grad_ffn[rows]).astype(BF)
    backward[...] += dot_nn(w_gate[0], grad_gate) + dot_nn(w_up[0], grad_up)
    gw_gate[0] = dot_nt(tokens, grad_gate).astype(BF)
    gw_up[0] = dot_nt(tokens, grad_up).astype(BF)

    @pl.when(step == pl.num_programs(0) - 1)
    def _():
        share = prob[...]
        both = branch[...] + forward[...]
        delta_out[...] = (share * both).astype(BF)
        cot_full = cot[...].astype(F32)
        slope = share * (1.0 - share) * jnp.sum(cot_full * both, axis=0, keepdims=True)
        logit_out[...] = slope
        token = picked[...].astype(F32)
        router_out[...] = jnp.sum(slope * token, axis=1, keepdims=True)
        hidden = token + branch[...]
        inv = inverse[...]
        grad_norm = backward[...]
        gain_out[...] = jnp.sum(grad_norm * hidden * inv, axis=1, keepdims=True)
        unit = grad_norm * gain[...]
        along = jnp.sum(unit * hidden, axis=0, keepdims=True) / width
        grad_hidden = inv * unit - hidden * (inv * inv * inv * along)
        grad_attn[...] = (grad_hidden + share * cot_full).astype(BF)
        rest_out[...] = (grad_hidden + slope * router[...]).astype(BF)


def ffn(normed, grad_ffn, branch, picked, cot, prob, inverse, gain, router, w_gate, w_up, w_down):
    width, picks = normed.shape
    blocks, _, hidden = w_gate.shape
    columns, _, part = w_down.shape
    tall = pl.BlockSpec((1, width, hidden), lambda i: (i, 0, 0))
    flat = pl.BlockSpec((columns, hidden, part), lambda i: (0, i, 0))
    full = whole((width, picks))
    row = whole((1, picks))
    column = whole((width, 1))
    return pl.pallas_call(
        ffn_body,
        grid=(blocks,),
        in_specs=[full, full, full, full, full, row, row, column, column, tall, tall, flat],
        out_specs=[full, full, full, row, column, column, tall, tall, flat],
        out_shape=[
            struct((width, picks), BF),
            struct((width, picks), BF),
            struct((width, picks), BF),
            struct((1, picks), F32),
            struct((width, 1), F32),
            struct((width, 1), F32),
            struct(w_gate.shape, BF),
            struct(w_up.shape, BF),
            struct(w_down.shape, BF),
        ],
        scratch_shapes=[pltpu.VMEM((width, picks), F32), pltpu.VMEM((width, picks), F32)],
        compiler_params=params(60),
        cost_estimate=cost(
            18 * width * w_gate.size // width * picks, 12 * w_gate.size + 20 * width * picks
        ),
        name="ffn",
    )(normed, grad_ffn, branch, picked, cot, prob, inverse, gain, router, w_gate, w_up, w_down)


def merge_back_body(mixed, grad, w, gw, grad_mixed, total):
    step = pl.program_id(0)
    part = w.shape[2]
    rows = pl.ds(pl.multiple_of(step * part, 8), part)
    piece = grad[rows, :]
    gw[0] = dot_nt(mixed[...], piece).astype(BF)
    value = dot_nn(w[0], piece)

    @pl.when(step == 0)
    def _():
        total[...] = value

    @pl.when(step > 0)
    def _():
        total[...] += value

    @pl.when(step == pl.num_programs(0) - 1)
    def _():
        grad_mixed[...] = total[...].astype(BF)


def merge_back(mixed, grad, w):
    width, picks = mixed.shape
    blocks, _, part = w.shape
    block = pl.BlockSpec((1, width, part), lambda i: (i, 0, 0))
    return pl.pallas_call(
        merge_back_body,
        grid=(blocks,),
        in_specs=[whole((width, picks)), whole((width, picks)), block],
        out_specs=[block, whole((width, picks))],
        out_shape=[struct(w.shape, BF), struct((width, picks), BF)],
        scratch_shapes=[pltpu.VMEM((width, picks), F32)],
        compiler_params=params(),
        cost_estimate=cost(4 * width * width * picks, 6 * width * picks + 4 * w.size),
        name="merge_back",
    )(mixed, grad, w)


def project_back_body(
    x, rank, gain, gq, gk, gv, rest, w,
    gw, out, gain_out,
    normed, gq_full, total,
):
    step = pl.program_id(0)
    width = x.shape[0]
    count = w_count(w, width)
    q_part = width // count
    kv_part = (w.shape[2] - q_part) // 2

    def inverse():
        full = x[...].astype(F32)
        return lax.rsqrt(jnp.sum(full * full, axis=0, keepdims=True) / width + EPSILON)

    @pl.when(step == 0)
    def _():
        normed[...] = (x[...].astype(F32) * inverse() * gain[...]).astype(BF)
        chosen = pick_rows(rank[...], gq.shape[1])
        gq_full[...] = dot_nn(gq[...], chosen).astype(BF)
        total[...] = jnp.zeros_like(total)

    q_rows = pl.ds(pl.multiple_of(step * q_part, 8), q_part)
    kv_rows = pl.ds(pl.multiple_of(step * kv_part, 8), kv_part)
    grads = jnp.concatenate([gq_full[q_rows, :], gk[kv_rows, :], gv[kv_rows, :]], axis=0)
    total[...] += dot_nn(w[0], grads)
    gw[0] = dot_nt(normed[...], grads).astype(BF)

    @pl.when(step == pl.num_programs(0) - 1)
    def _():
        full = x[...].astype(F32)
        inv = inverse()
        grad_norm = total[...]
        gain_out[...] = jnp.sum(grad_norm * full * inv, axis=1, keepdims=True)
        unit = grad_norm * gain[...]
        along = jnp.sum(unit * full, axis=0, keepdims=True) / width
        chosen = pick_rows(rank[...], gq.shape[1])
        out[...] = (
            inv * unit - full * (inv * inv * inv * along) + dot_nn(rest[...], chosen)
        ).astype(BF)


def project_back(x, rank_row, gain, gq, gk, gv, rest, w):
    width, length = x.shape
    picks = gq.shape[1]
    blocks, _, part = w.shape
    kv = KVH * HD
    block = pl.BlockSpec((1, width, part), lambda i: (i, 0, 0))
    return pl.pallas_call(
        project_back_body,
        grid=(blocks,),
        in_specs=[
            whole((width, length)),
            whole((1, length)),
            whole((width, 1)),
            whole((width, picks)),
            whole((kv, length)),
            whole((kv, length)),
            whole((width, picks)),
            block,
        ],
        out_specs=[block, whole((width, length)), whole((width, 1))],
        out_shape=[
            struct(w.shape, BF),
            struct((width, length), BF),
            struct((width, 1), F32),
        ],
        scratch_shapes=[
            pltpu.VMEM((width, length), BF),
            pltpu.VMEM((width, length), BF),
            pltpu.VMEM((width, length), F32),
        ],
        compiler_params=params(),
        cost_estimate=cost(
            4 * width * length * (picks + width + 2 * kv), 10 * x.size + 4 * w.size
        ),
        name="project_back",
    )(x, rank_row, gain, gq, gk, gv, rest, w)


def rope_tables(positions):
    half = HD // 2
    frequency = jnp.exp(jnp.arange(half, dtype=F32) * (-2.0 * math.log(ROPE_BASE) / HD))
    angles = frequency[:, None] * positions.astype(F32)[None, :]
    return jnp.cos(angles), jnp.sin(angles)


def sequence_step(x, cot, rank, prefix_len, gain_one, gain_two, router, w_qkv, w_out, w_gate, w_up, w_down):
    width, length = x.shape
    picks = cot.shape[1]
    place = jnp.arange(picks, dtype=jnp.int32)
    every = jnp.arange(length, dtype=jnp.int32)
    spot = jnp.sum(jnp.where(rank[None, :] == place[:, None], every[None, :], 0), axis=1)
    limit = jnp.maximum(spot, prefix_len - 1)[None, :]
    tables_k = rope_tables(every)
    tables_q = rope_tables(spot)
    gain_one, gain_two, router = gain_one[:, None], gain_two[:, None], router[:, None]
    picked, prob, q, kt, k, vt, v = project(
        x, rank[:, None], gain_one, router, tables_k, tables_q, w_qkv
    )
    mixed, total = attend(q, k, vt, limit)
    branch, inverse, normed, grad_ffn = merge(mixed, picked, cot, prob, gain_two, w_out)
    delta, grad_attn, rest, _, gain_two_grad, router_grad, gw_gate, gw_up, gw_down = ffn(
        normed, grad_ffn, branch, picked, cot, prob, inverse, gain_two, router, w_gate, w_up, w_down
    )
    gw_out, grad_mixed = merge_back(mixed, grad_attn, w_out)
    gq, gk, gv = attend_back(q, k, kt, v, limit, total, grad_mixed, mixed, tables_k, tables_q)
    gw_qkv, back, gain_one_grad = project_back(
        x, rank[None, :], gain_one, gq, gk, gv, rest, w_qkv
    )
    vectors = jnp.concatenate([gain_one_grad, gain_two_grad, router_grad], axis=1)
    return delta, back, vectors, (gw_qkv, gw_out, gw_gate, gw_up, gw_down)


def bits_of(count):
    return count.bit_length() - 1


def swap(value, axis, bit):
    count = lax.axis_size(axis)
    return lax.ppermute(value, axis, [(i, i ^ (1 << bit)) for i in range(count)])


def own_bit(axis, bit):
    return (lax.axis_index(axis) >> bit) & 1


def join_bit(value, axis, bit, at):
    other = swap(value, axis, bit)
    mine = own_bit(axis, bit) == 0
    return jnp.stack([jnp.where(mine, value, other), jnp.where(mine, other, value)], axis=at)


def route(flip):
    bits = list(range(1, bits_of(lax.axis_size("row"))))
    return bits if flip else bits[::-1]


def gather_weight(value, flip):
    col_bits = bits_of(lax.axis_size("col"))
    row_bits = bits_of(lax.axis_size("row"))
    rows, cols = value.shape
    for done, bit in enumerate(range(col_bits)[::-1]):
        value = join_bit(value, "col", bit, done)
    taken = []
    for bit in route(flip) + [0]:
        at = col_bits + sum(1 for other in taken if other > bit)
        value = join_bit(value, "row", bit, at)
        taken.append(bit)
    return value.reshape(1 << col_bits, rows << row_bits, cols)


def halve_bit(value, axis, bit, at):
    mine = own_bit(axis, bit)
    keep = lax.dynamic_index_in_dim(value, mine, at, keepdims=False)
    send = lax.dynamic_index_in_dim(value, 1 - mine, at, keepdims=False)
    other = swap(send, axis, bit)
    return (keep.astype(F32) + other.astype(F32)).astype(BF)


def scatter_weight(value, flip):
    col_bits = bits_of(lax.axis_size("col"))
    row_bits = bits_of(lax.axis_size("row"))
    columns, rows, cols = value.shape
    value = value.reshape((2,) * (col_bits + row_bits) + (rows >> row_bits, cols))
    left = list(range(row_bits))[::-1]
    for bit in [0] + route(flip)[::-1]:
        value = halve_bit(value, "row", bit, col_bits + left.index(bit))
        left.remove(bit)
    for done, bit in enumerate(range(col_bits)):
        value = halve_bit(value, "col", bit, col_bits - 1 - done)
    return value.astype(F32)


def to_owner(value):
    count = lax.axis_size("col")
    copies = count // value.shape[0]
    if copies > 1:
        value = jnp.concatenate([value] * copies, axis=0)
    moved = lax.all_to_all(value, "col", split_axis=0, concat_axis=1, tiled=True)
    return moved[0]


def from_owner(value, sequences):
    count = lax.axis_size("col")
    value = value.reshape(count, value.shape[0] // count, value.shape[1])
    moved = lax.all_to_all(value, "col", split_axis=0, concat_axis=0, tiled=True)
    return moved[:sequences]


def on_device(
    resid, cotangent, prefix, slot, chosen, norm1_gain, norm2_gain, router,
    w_query, w_key, w_value, w_out, w_gate, w_up, w_down,
):
    col_count = lax.axis_size("col")
    column = lax.axis_index("col")
    sequences, part, length = resid.shape
    picks = chosen.shape[2]
    copies = col_count // sequences
    own = lax.rem(column, sequences)

    x = to_owner(resid.astype(BF))
    w_qkv = gather_weight(jnp.concatenate([w_query, w_key, w_value], axis=1), False)
    w_out_all = gather_weight(w_out, True)
    w_gate_all = gather_weight(w_gate, False)
    w_up_all = gather_weight(w_up, True)
    w_down_all = gather_weight(w_down, False)

    every = jnp.arange(length, dtype=jnp.int32)
    chosen_of = chosen[:, 0][slot]
    selected = jnp.any(every[None, :, None] == chosen_of[:, None, :], axis=2)
    before = (every[:, None] < every[None, :]).astype(BF)
    places = jnp.dot(selected.astype(BF), before, preferred_element_type=F32)
    rank = jnp.where(selected, places.astype(jnp.int32), -1)

    cot = to_owner(gather_tokens(cotangent, rank[:, :, None], picks))

    delta, back, vectors, grads = sequence_step(
        x, cot,
        lax.dynamic_index_in_dim(rank, own, 0, keepdims=False),
        lax.dynamic_index_in_dim(prefix, own, 0, keepdims=False),
        norm1_gain, norm2_gain, router,
        w_qkv, w_out_all, w_gate_all, w_up_all, w_down_all,
    )
    if copies > 1:
        vectors = vectors / copies
        grads = tuple((g.astype(F32) / copies).astype(BF) for g in grads)
    gw_qkv, gw_out, gw_gate, gw_up, gw_down = grads

    block_out = scatter_tokens(resid, from_owner(delta, sequences), rank[:, None, :])
    gw_gate = scatter_weight(gw_gate, False)
    gw_up = scatter_weight(gw_up, True)
    gw_down = scatter_weight(gw_down, False)
    gw_out = scatter_weight(gw_out, True)
    resid_grad = cotangent + from_owner(back, sequences).astype(F32)
    gw_qkv = scatter_weight(gw_qkv, False)
    vectors = lax.psum(vectors.T, ("row", "col"))
    vectors = lax.dynamic_slice_in_dim(vectors, column * part, part, 1)
    kv_part = w_key.shape[1]
    return (
        block_out, resid_grad, vectors[0], vectors[1], vectors[2],
        gw_qkv[:, :part], gw_qkv[:, part : part + kv_part], gw_qkv[:, part + kv_part :],
        gw_out, gw_gate, gw_up, gw_down,
    )


def solution(mesh):
    block = P("row", "col")
    placed = (
        P("row", "col", None), P("row", "col", None), P("row"), P("row"), P(None, "row", None),
        P(), P(), P(),
        block, block, block, block, block, block, block,
    )
    given = (
        P("row", "col", None), P("row", "col", None), P("col"), P("col"), P("col"),
        block, block, block, block, block, block, block,
    )
    return jax.shard_map(
        on_device, mesh=mesh, in_specs=placed, out_specs=given, check_vma=False
    )
```

time: 3430 us -> 585 us (0.17)
  waiting for transfers between devices: 2270 us -> 148 us
  matrix products: 441 us -> 0.32 us
  blocking collectives: 235 us -> 40.1 us
  Pallas kernels: 0 us -> 174 us
  other arithmetic: 161 us -> 57.8 us
  starting transfers between devices: 173 us -> 93.6 us
  local copies, waits for them, and re-layouts: 100 us -> 63.1 us
    reduce_scatter x32 -> x0, waiting for transfers between devices: 945 us -> none  [the longest x8 305 us: split_sums(): lax.psum_scatter(partial_value.astype(jnp.bfloat16), 'col', scatter_dimen...]
    unnamed x79 -> x0, waiting for transfers between devices: 715 us -> none
    all_gather x19 -> x0, waiting for transfers between devices: 562 us -> none  [the longest x8 244 us: full_features(): lax.all_gather(values_major.astype(jnp.bfloat16), 'col', axis=0, tiled=True)]
    dot_general x179 -> x1, matrix products: 441 us -> 0.32 us  [on_device(): places = jnp.dot(selected.astype(BF), before, preferred_element_type=F32)]
    all_gather x12 -> x0, blocking collectives: 198 us -> none  [the longest x4 78.9 us: on_device(): lax.all_gather(value_part, 'col', axis=1, tiled=True)]
    pallas_call x0 -> x9, Pallas kernels: none -> 174 us  [the longest x1 53.3 us: ffn(): pl.pallas_call(ffn_body, grid=(blocks,), in_specs=[full, full, full, full...]
    all_to_all x8 -> x4, starting transfers between devices: 168 us -> 19 us  [the longest x2 9.5 us: from_owner(): lax.all_to_all(value, 'col', split_axis=0, concat_axis=0, tiled=True)]
    ppermute x0 -> x50, waiting for transfers between devices: none -> 142 us  [swap(): return lax.ppermute(value, axis, [(i, i ^ 1 << bit) for i in range(count)])]
  transfers between devices with their start and end apart: 73 -> 54, of which waited for: 62 -> 26; matrix products, arithmetic and copies ran while one was open for 17% -> 19% of each run, Pallas kernels for 0% -> 19%
where the time goes in v1:
time: 585 us; the launch traced here: 580 us
  Pallas kernels  174 us (30%)
  waiting for transfers between devices  148 us (25%)
  starting transfers between devices  93.6 us (16%)
  local copies, waits for them, and re-layouts  63.1 us (11%)
  other arithmetic  57.8 us (10%)
  blocking collectives  40.1 us (7%)
    ppermute x50, waiting for transfers between devices, swap(): return lax.ppermute(value, axis, [(i, i ^ 1 << bit) for i in range(count)])  142 us
    ppermute x50, starting transfers between devices, swap(): return lax.ppermute(value, axis, [(i, i ^ 1 << bit) for i in range(count)])  74.6 us
    pallas_call x1, Pallas kernels, ffn(): pl.pallas_call(ffn_body, grid=(blocks,), in_specs=[full, full, full, full...  53.3 us
    psum x1, blocking collectives, on_device(): vectors = lax.psum(vectors.T, ('row', 'col'))  40.1 us
    pallas_call x1, Pallas kernels, attend_back(): pl.pallas_call(attend_back_body, grid=(KVH,), in_specs=[wide, tall, flat,...  29.9 us
    pallas_call x1, Pallas kernels, attend(): pl.pallas_call(attend_body, grid=(KVH,), in_specs=[pl.BlockSpec((part, pi...  26.1 us
    another operation x49, other arithmetic, join_bit(): jnp.stack([jnp.where(mine, value, other), jnp.where(mine, other, value)],...  22.4 us
    pallas_call x1, Pallas kernels, project_back(): pl.pallas_call(project_back_body, grid=(blocks,), in_specs=[whole((width,...  20.2 us
  transfers between devices with their start and end apart: 54, of which 26 were waited for; matrix products, arithmetic and copies ran while one was open for 19% of the time, Pallas kernels for 19%

profile of v1, /device:TPU:0, one launch (start us, length us, event | category | flops | bytes accessed | tf_op | source)
XLA Modules:
  0.0 579.7 jit_solution(8670211212343849972)
XLA Ops:
  0.6 4.1 collective-permute-start.20
  4.8 2.8 collective-permute-start.15
  9.5 2.9 collective-permute-start
  12.4 3.7 convert_element_type.346
  16.1 4.6 all-to-all-start
  29.1 6.2 %gather_tokens.1 = bf16[4,240,768]{2,1,0:T(8,128)(2,1)} custom-call(f32[4,240,1024]{2,1,0:T(8,128)} %values.1, s32[4,1024,1]{2,1,0:T(8,128)} %copy.121.rank), custom_call_target="tpu_custom_call" | custom-call | flops 1509949440 | bytes 5898240 | tf_op jit(solution)/shard_map/gather_tokens/pallas_call | solution.py:80
  42.8 3.5 collective-permute-done
  46.4 8.5 %collective-permute-start.1 = (bf16[2,120,400]{1,2,0:T(8,128)(2,1)S(1)}, bf16[2,120,400]{1,2,0:T(8,128)(2,1)S(1)}, u32[]{:S(2)}, u32[]{:S(2)}) collective-permute-start(bf16[2,120,400]{1,2,0:T(8,128)(2,1)S(1)} %pad_maximum_fusion.23), channel_id=1, source_target_pairs={{0,1},{1,0},{2,3},{3,2},{4,5},{5,4},{6,7},{7,6},{8,9},{9,8},{10,11... | collective-permute-start | bytes 576008 | tf_op jit(solution)/shard_map/ppermute | solution.py:670
  66.4 12.2 %collective-permute-done.21 = bf16[2,320,240]{2,1,0:T(8,128)(2,1)S(1)} collective-permute-done((bf16[2,320,240]{2,1,0:T(8,128)(2,1)S(1)}, bf16[2,320,240]{2,1,0:T(8,128)(2,1)S(1)}, u32[]{:S(2)}, u32[]{:S(2)}) %collective-permute-start.21) | collective-permute-done | bytes 307232 | tf_op jit(solution)/shard_map/ppermute | solution.py:670
  80.4 4.7 collective-permute-done.16
  86.9 4.7 collective-permute-done.11
  95.7 2.5 collective-permute-done.22
  104.0 7.3 %collective-permute-done.12 = bf16[2,2,120,640]{3,2,0,1:T(8,128)(2,1)S(1)} collective-permute-done((bf16[2,2,120,640]{3,2,0,1:T(8,128)(2,1)S(1)}, bf16[2,2,120,640]{3,2,0,1:T(8,128)(2,1)S(1)}, u32[]{:S(2)}, u32[]{:S(2)}) %collective-permute-start.12) | collective-permute-done | bytes 614432 | tf_op jit(solution)/shard_map/ppermute | solution.py:670
  113.2 6.5 %collective-permute-done.3 = bf16[2,2,2,120,400]{3,4,2,1,0:T(8,128)(2,1)S(1)} collective-permute-done((bf16[2,2,2,120,400]{3,4,2,1,0:T(8,128)(2,1)S(1)}, bf16[2,2,2,120,400]{3,4,2,1,0:T(8,128)(2,1)S(1)}, u32[]{:S(2)}, u32[]{:S(2)}) %collective-permute-start.3) | collective-permute-done | bytes 768032 | tf_op jit(solution)/shard_map/ppermute | solution.py:670
  123.7 24.1 %collective-permute-done.23 = bf16[2,2,2,320,240]{4,3,0,1,2:T(8,128)(2,1)S(1)} collective-permute-done((bf16[2,2,2,320,240]{4,3,0,1,2:T(8,128)(2,1)S(1)}, bf16[2,2,2,320,240]{4,3,0,1,2:T(8,128)(2,1)S(1)}, u32[]{:S(2)}, u32[]{:S(2)}) %collective-permute-start.23) | collective-permute-done | bytes 1228832 | tf_op jit(solution)/shard_map/ppermute | solution.py:670
  153.4 19.6 %collective-permute-done.13 = bf16[2,2,2,120,640]{4,3,0,1,2:T(8,128)(2,1)S(1)} collective-permute-done((bf16[2,2,2,120,640]{4,3,0,1,2:T(8,128)(2,1)S(1)}, bf16[2,2,2,120,640]{4,3,0,1,2:T(8,128)(2,1)S(1)}, u32[]{:S(2)}, u32[]{:S(2)}) %collective-permute-start.13) | collective-permute-done | bytes 1228832 | tf_op jit(solution)/shard_map/ppermute | solution.py:670
  173.4 4.9 all-to-all-start.1
  182.7 4.3 copy.117
  187.0 15.1 %project.1 = (bf16[960,768]{1,0:T(8,128)(2,1)}, f32[1,768]{1,0:T(1,128)}, bf16[960,768]{1,0:T(8,128)(2,1)}, bf16[320,1024]{1,0:T(8,128)(2,1)}, bf16[5,1024,64]{2...) custom-call(bf16[960,1024]{1,0:T(8,128)(2,1)} %bitcast.x, s32[1024,1]{1,0:T(8,128)} %copy.118.rank, ...), custom_call_target="tpu_custom_call" | custom-call | flops 4183818240 | bytes 10936320 | tf_op jit(solution)/shard_map/project/pallas_call | solution.py:188
  202.1 26.1 %attend.1 = (bf16[960,768]{1,0:T(8,128)(2,1)}, f32[5,3,768]{2,1,0:T(4,128)}) custom-call(bf16[960,768]{1,0:T(8,128)(2,1)} %get-tuple-element.41.q, bf16[5,1024,64]{2,1,0:T(8,128)(2,1)} %get-tuple-element.42.k, bf16[320,1024]{1,0:T(8,128)(2,1)} %get-tuple-element.43.vt, s32[1,768]{1,0:T(1,128)} %max.18.limit), custom_call_target="tpu_custom_call" | custom-call | flops 12079595520 | bytes 2949120 | tf_op jit(solution)/shard_map/attend/pallas_call | solution.py:275
  228.3 8.5 %merge.1 = (f32[960,768]{1,0:T(8,128)}, f32[1,768]{1,0:T(1,128)}, bf16[960,768]{1,0:T(8,128)(2,1)}, bf16[960,768]{1,0:T(8,128)(2,1)}) custom-call(bf16[960,768]{1,0:T(8,128)(2,1)} %get-tuple-element.44.mixed, bf16[960,768]{1,0:T(8,128)(2,1)} %get-tuple-element.45.picked, bf16[960,768]{1,0:T(8,128)(2,1)} %bitcast.20.cot, f32[1,768]{1,0:T(1,128)} %get-tuple-element.46.prob, ...), custom_call_target="tpu_custom_call" | custom-call | flops 1415577600 | bytes 12165120 | tf_op jit(solution)/shard_map/merge/pallas_call | solution.py:394
  236.8 2.4 select_bitcast_fusion.1
  240.2 2.8 copy.127
  245.8 2.7 copy.126
  251.2 2.7 copy.125
  253.9 53.3 %ffn.1 = (bf16[960,768]{1,0:T(8,128)(2,1)}, bf16[960,768]{1,0:T(8,128)(2,1)}, bf16[960,768]{1,0:T(8,128)(2,1)}, f32[1,768]{1,0:T(1,128)}, f32[960,1]{1,0:T(8,128...) custom-call(bf16[960,768]{1,0:T(8,128)(2,1)} %get-tuple-element.47.n, ...), custom_call_target="tpu_custom_call" | custom-call | flops 33973862400 | bytes 44236800 | tf_op jit(solution)/shard_map/ffn/pallas_call | solution.py:487
  307.2 8.4 %merge_back.1 = (bf16[4,960,240]{2,1,0:T(8,128)(2,1)}, bf16[960,768]{1,0:T(8,128)(2,1)}) custom-call(bf16[960,768]{1,0:T(8,128)(2,1)} %get-tuple-element.44.mixed, bf16[960,768]{1,0:T(8,128)(2,1)} %get-tuple-element.55.grad, bf16[4,960,240]{2,1,0:T(8,128)(2,1)} %bitcast.275), custom_call_target="tpu_custom_call" | custom-call | flops 2831155200 | bytes 8110080 | tf_op jit(solution)/shard_map/merge_back/pallas_call | solution.py:537
  318.8 29.9 %attend_back.1 = (bf16[960,768]{1,0:T(8,128)(2,1)}, bf16[320,1024]{1,0:T(8,128)(2,1)}, bf16[320,1024]{1,0:T(8,128)(2,1)}) custom-call(bf16[960,768]{1,0:T(8,128)(2,1)} %get-tuple-element.41.q, bf16[5,1024,64]{2,1,0:T(8,128)(2,1)} %get-tuple-element.42.k, bf16[320,1024]{1,0:T(8,128)(2,1)} %get-tuple-element.52.kt, bf16[5,1024,64]{2,1,0:T(8,128)(2,1)} %get-tuple-element.53.v, ...), custom_call_target="tpu_custom_call" | custom-call | flops 30198988800 | bytes 5898240 | tf_op jit(solution)/shard_map/attend_back/pallas_call | solution.py:342
  348.7 20.2 %project_back.1 = (bf16[4,960,400]{2,1,0:T(8,128)(2,1)}, bf16[960,1024]{1,0:T(8,128)(2,1)}, f32[960,1]{1,0:T(8,128)}) custom-call(bf16[960,1024]{1,0:T(8,128)(2,1)} %bitcast.x, s32[1,1024]{1,0:T(1,128)} %copy-done.36, f32[960,1]{1,0:T(8,128)} %copy.119.gain, bf16[960,768]{1,0:T(8,128)(2,1)} %get-tuple-element.57.gq, bf16[320,1024]{1,0:T(8,128)(2,1)} %get-tuple-element.58.gk, ...), custom_call_target="tpu_custom_call" | custom-call | flops 9311354880 | bytes 15974400 | tf_op jit(solution)/shard_map/project_back/pallas_call | solution.py:598
  368.9 3.8 constant_dynamic-slice_fusion.10
  372.7 4.0 copy.136
  376.8 4.6 constant_dynamic-slice_fusion.2
  383.5 5.1 all-to-all-start.2
  392.5 4.4 constant_dynamic-slice_fusion.4
  406.0 40.1 %psum.7 = f32[3,960]{1,0:T(4,128)S(1)} all-reduce(f32[3,960]{1,0:T(4,128)S(1)} %maximum_bitcast_fusion), channel_id=1, replica_groups=mesh['row'=8,'col'=4] {'row','col'}, use_global_device_ids=true, to_apply=%region_2.3 | all-reduce | flops 2880 | bytes 23040 | tf_op jit(solution)/shard_map/psum | solution.py:786
  451.6 3.2 collective-permute-done.32
  463.0 4.4 all-to-all-start.3
  468.1 6.0 %scatter_tokens.1 = f32[4,240,1024]{2,1,0:T(8,128)} custom-call(f32[4,240,1024]{2,1,0:T(8,128)} %base.1, bf16[4,240,768]{2,1,0:T(8,128)(2,1)} %all-to-all-done.2.values, s32[4,1,1024]{2,1,0:T(1,128)} %copy.130.rank), custom_call_target="tpu_custom_call" | custom-call | flops 1509949440 | bytes 9830400 | tf_op jit(solution)/shard_map/scatter_tokens/pallas_call | solution.py:103
  476.7 2.6 fusion.1
  488.5 2.4 fusion.3
  494.5 6.5 %collective-permute-done.28 = bf16[2,120,400]{1,2,0:T(8,128)(2,1)S(1)} collective-permute-done((bf16[2,120,400]{1,2,0:T(8,128)(2,1)S(1)}, bf16[2,120,400]{1,2,0:T(8,128)(2,1)S(1)}, u32[]{:S(2)}, u32[]{:S(2)}) %collective-permute-start.28) | collective-permute-done | bytes 192032 | tf_op jit(solution)/shard_map/ppermute | solution.py:670
  501.1 5.8 collective-permute-start.29
  506.9 6.7 %all-to-all-done.3 = bf16[4,240,1024]{2,1,0:T(8,128)(2,1)} async-done(((bf16[4,240,1024]{2,1,0:T(8,128)(2,1)}), bf16[4,240,1024]{2,1,0:T(8,128)(2,1)}, u32[]{:S(2)}, u32[]{:S(2)}) %all-to-all-start.3) | async-done | bytes 1966112 | tf_op jit(solution)/shard_map/all_to_all | solution.py:736
  513.6 5.7 convert_add_fusion.3
  526.1 12.7 %collective-permute-done.36 = bf16[2,2,2,120,640]{4,3,0,1,2:T(8,128)(2,1)} collective-permute-done((bf16[2,2,2,120,640]{4,3,0,1,2:T(8,128)(2,1)}, bf16[2,2,2,120,640]{4,3,0,1,2:T(8,128)(2,1)}, u32[]{:S(2)}, u32[]{:S(2)}) %collective-permute-start.36) | collective-permute-done | bytes 1228832 | tf_op jit(solution)/shard_map/ppermute | solution.py:670
  544.0 3.5 collective-permute-done.42
  556.3 7.6 %collective-permute-done.43 = bf16[2,120,640]{2,1,0:T(8,128)(2,1)S(1)} collective-permute-done((bf16[2,120,640]{2,1,0:T(8,128)(2,1)S(1)}, bf16[2,120,640]{2,1,0:T(8,128)(2,1)S(1)}, u32[]{:S(2)}, u32[]{:S(2)}) %collective-permute-start.43) | collective-permute-done | bytes 307232 | tf_op jit(solution)/shard_map/ppermute | solution.py:670
  569.5 7.6 %collective-permute-done.44 = bf16[120,640]{1,0:T(8,128)(2,1)S(1)} collective-permute-done((bf16[120,640]{1,0:T(8,128)(2,1)S(1)}, bf16[120,640]{1,0:T(8,128)(2,1)S(1)}, u32[]{:S(2)}, u32[]{:S(2)}) %collective-permute-start.44) | collective-permute-done | bytes 153632 | tf_op jit(solution)/shard_map/ppermute | solution.py:670
  (298 shorter events, 141.0 us)
Async XLA Ops:
  0.6 54.3 %collective-permute-start.20 = (bf16[320,240]{1,0:T(8,128)(2,1)}, bf16[320,240]{1,0:T(8,128)(2,1)S(1)}, u32[]{:S(2)}, u32[]{:S(2)}) collective-permute-start(bf16[320,240]{1,0:T(8,128)(2,1)} %param.29), channel_id=1, source_target_pairs={{0,2},{1,3},{2,0},{3,1},{4,6},{5,7},{6,4},{7,5},{8,10},{9,11},{10,... | collective-permute-start | bytes 460808 | tf_op jit(solution)/shard_map/ppermute | solution.py:670
  4.7 50.4 %collective-permute-start.10 = (bf16[120,640]{1,0:T(8,128)(2,1)}, bf16[120,640]{1,0:T(8,128)(2,1)S(1)}, u32[]{:S(2)}, u32[]{:S(2)}) collective-permute-start(bf16[120,640]{1,0:T(8,128)(2,1)} %param.27), channel_id=1, source_target_pairs={{0,2},{1,3},{2,0},{3,1},{4,6},{5,7},{6,4},{7,5},{8,10},{9,11},{10,... | collective-permute-start | bytes 460808 | tf_op jit(solution)/shard_map/ppermute | solution.py:670
  4.8 50.3 %collective-permute-start.15 = (bf16[120,640]{1,0:T(8,128)(2,1)}, bf16[120,640]{1,0:T(8,128)(2,1)S(1)}, u32[]{:S(2)}, u32[]{:S(2)}) collective-permute-start(bf16[120,640]{1,0:T(8,128)(2,1)} %param.28), channel_id=1, source_target_pairs={{0,2},{1,3},{2,0},{3,1},{4,6},{5,7},{6,4},{7,5},{8,10},{9,11},{10,... | collective-permute-start | bytes 460808 | tf_op jit(solution)/shard_map/ppermute | solution.py:670
  7.7 34.5 %collective-permute-start.5 = (bf16[120,240]{1,0:T(8,128)(2,1)}, bf16[120,240]{1,0:T(8,128)(2,1)S(1)}, u32[]{:S(2)}, u32[]{:S(2)}) collective-permute-start(bf16[120,240]{1,0:T(8,128)(2,1)} %param.26), channel_id=1, source_target_pairs={{0,2},{1,3},{2,0},{3,1},{4,6},{5,7},{6,4},{7,5},{8,10},{9,11},{10,... | collective-permute-start | bytes 172808 | tf_op jit(solution)/shard_map/ppermute | solution.py:670
  9.5 36.8 %collective-permute-start = (bf16[120,400]{0,1:T(8,128)(2,1)S(1)}, bf16[120,400]{0,1:T(8,128)(2,1)S(1)}, u32[]{:S(2)}, u32[]{:S(2)}) collective-permute-start(bf16[120,400]{0,1:T(8,128)(2,1)S(1)} %pad_maximum_fusion.25), channel_id=1, source_target_pairs={{0,2},{1,3},{2,0},{3,1},{4,6},{5,7},{6,4},{7,5},{8,10},{9,11},{10,... | collective-permute-start | bytes 288008 | tf_op jit(solution)/shard_map/ppermute | solution.py:670
  16.1 157.3 %all-to-all-start = ((bf16[4,240,1024]{2,1,0:T(8,128)(2,1)}), bf16[4,240,1024]{2,1,0:T(8,128)(2,1)}, u32[]{:S(2)}, u32[]{:S(2)}) async-start(bf16[4,240,1024]{2,1,0:T(8,128)(2,1)} %convert_element_type.346), calls=%async_computation | async-start | bytes 3932160 | tf_op jit(solution)/shard_map/all_to_all | solution.py:729
  42.2 15.3 %collective-permute-start.6 = (bf16[2,120,240]{2,1,0:T(8,128)(2,1)S(1)}, bf16[2,120,240]{2,1,0:T(8,128)(2,1)S(1)}, u32[]{:S(2)}, u32[]{:S(2)}) collective-permute-start(bf16[2,120,240]{2,1,0:T(8,128)(2,1)S(1)} %pad_maximum_fusion.24), channel_id=1, source_target_pairs={{0,1},{1,0},{2,3},{3,2},{4,5},{5,4},{6,7},{7,6},{8,9},{9,8},{10,11... | collective-permute-start | bytes 345608 | tf_op jit(solution)/shard_map/ppermute | solution.py:670
  46.4 14.6 %collective-permute-start.1 = (bf16[2,120,400]{1,2,0:T(8,128)(2,1)S(1)}, bf16[2,120,400]{1,2,0:T(8,128)(2,1)S(1)}, u32[]{:S(2)}, u32[]{:S(2)}) collective-permute-start(bf16[2,120,400]{1,2,0:T(8,128)(2,1)S(1)} %pad_maximum_fusion.23), channel_id=1, source_target_pairs={{0,1},{1,0},{2,3},{3,2},{4,5},{5,4},{6,7},{7,6},{8,9},{9,8},{10,11... | collective-permute-start | bytes 576008 | tf_op jit(solution)/shard_map/ppermute | solution.py:670
  55.0 23.6 %collective-permute-start.21 = (bf16[2,320,240]{2,1,0:T(8,128)(2,1)S(1)}, bf16[2,320,240]{2,1,0:T(8,128)(2,1)S(1)}, u32[]{:S(2)}, u32[]{:S(2)}) collective-permute-start(bf16[2,320,240]{2,1,0:T(8,128)(2,1)S(1)} %pad_maximum_fusion.19), channel_id=1, source_target_pairs={{0,1},{1,0},{2,3},{3,2},{4,5},{5,4},{6,7},{7,6},{8,9},{9,8},{10,11... | collective-permute-start | bytes 921608 | tf_op jit(solution)/shard_map/ppermute | solution.py:670
  55.2 29.9 %collective-permute-start.16 = (bf16[2,120,640]{2,1,0:T(8,128)(2,1)S(1)}, bf16[2,120,640]{2,1,0:T(8,128)(2,1)S(1)}, u32[]{:S(2)}, u32[]{:S(2)}) collective-permute-start(bf16[2,120,640]{2,1,0:T(8,128)(2,1)S(1)} %pad_maximum_fusion.21), channel_id=1, source_target_pairs={{0,1},{1,0},{2,3},{3,2},{4,5},{5,4},{6,7},{7,6},{8,9},{9,8},{10,11... | collective-permute-start | bytes 921608 | tf_op jit(solution)/shard_map/ppermute | solution.py:670
  57.3 34.3 %collective-permute-start.11 = (bf16[2,120,640]{2,1,0:T(8,128)(2,1)S(1)}, bf16[2,120,640]{2,1,0:T(8,128)(2,1)S(1)}, u32[]{:S(2)}, u32[]{:S(2)}) collective-permute-start(bf16[2,120,640]{2,1,0:T(8,128)(2,1)S(1)} %pad_maximum_fusion.20), channel_id=1, source_target_pairs={{0,1},{1,0},{2,3},{3,2},{4,5},{5,4},{6,7},{7,6},{8,9},{9,8},{10,11... | collective-permute-start | bytes 921608 | tf_op jit(solution)/shard_map/ppermute | solution.py:670
  61.2 32.3 %collective-permute-start.2 = (bf16[2,2,120,400]{2,3,1,0:T(8,128)(2,1)S(1)}, bf16[2,2,120,400]{2,3,1,0:T(8,128)(2,1)S(1)}, u32[]{:S(2)}, u32[]{:S(2)}) collective-permute-start(bf16[2,2,120,400]{2,3,1,0:T(8,128)(2,1)S(1)} %pad_maximum_fusion.18), channel_id=1, source_target_pairs={{0,16},{4,20},{8,24},{12,28},{16,0},{20,4},{24,8},{28,12},{1,17},{... | collective-permute-start | bytes 1152008 | tf_op jit(solution)/shard_map/ppermute | solution.py:670
  64.8 30.5 %collective-permute-start.8 = (bf16[2,2,2,120,240]{4,3,0,1,2:T(8,128)(2,1)S(1)}, bf16[2,2,2,120,240]{4,3,0,1,2:T(8,128)(2,1)S(1)}, u32[]{:S(2)}, u32[]{:S(2)}) collective-permute-start(bf16[2,2,2,120,240]{4,3,0,1,2:T(8,128)(2,1)S(1)} %pad_maximum_fusion.17), channel_id=1, source_target_pairs={{0,16},{4,20},{8,24},{12,28},{16,0},{20,4},{24,8},{28,12},{1,17},{... | collective-permute-start | bytes 1382408 | tf_op jit(solution)/shard_map/ppermute | solution.py:670
  78.8 19.4 %collective-permute-start.22 = (bf16[2,2,320,240]{3,2,0,1:T(8,128)(2,1)S(1)}, bf16[2,2,320,240]{3,2,0,1:T(8,128)(2,1)S(1)}, u32[]{:S(2)}, u32[]{:S(2)}) collective-permute-start(bf16[2,2,320,240]{3,2,0,1:T(8,128)(2,1)S(1)} %pad_maximum_fusion.14), channel_id=1, source_target_pairs={{0,16},{4,20},{8,24},{12,28},{16,0},{20,4},{24,8},{28,12},{1,17},{... | collective-permute-start | bytes 1843208 | tf_op jit(solution)/shard_map/ppermute | solution.py:670
  85.3 16.8 %collective-permute-start.17 = (bf16[2,2,120,640]{3,2,0,1:T(8,128)(2,1)S(1)}, bf16[2,2,120,640]{3,2,0,1:T(8,128)(2,1)S(1)}, u32[]{:S(2)}, u32[]{:S(2)}) collective-permute-start(bf16[2,2,120,640]{3,2,0,1:T(8,128)(2,1)S(1)} %pad_maximum_fusion.16), channel_id=1, source_target_pairs={{0,8},{4,12},{8,0},{12,4},{16,24},{20,28},{24,16},{28,20},{1,9},{5... | collective-permute-start | bytes 1843208 | tf_op jit(solution)/shard_map/ppermute | solution.py:670
  91.8 19.5 %collective-permute-start.12 = (bf16[2,2,120,640]{3,2,0,1:T(8,128)(2,1)S(1)}, bf16[2,2,120,640]{3,2,0,1:T(8,128)(2,1)S(1)}, u32[]{:S(2)}, u32[]{:S(2)}) collective-permute-start(bf16[2,2,120,640]{3,2,0,1:T(8,128)(2,1)S(1)} %pad_maximum_fusion.15), channel_id=1, source_target_pairs={{0,16},{4,20},{8,24},{12,28},{16,0},{20,4},{24,8},{28,12},{1,17},{... | collective-permute-start | bytes 1843208 | tf_op jit(solution)/shard_map/ppermute | solution.py:670
  93.7 25.9 %collective-permute-start.3 = (bf16[2,2,2,120,400]{3,4,2,1,0:T(8,128)(2,1)S(1)}, bf16[2,2,2,120,400]{3,4,2,1,0:T(8,128)(2,1)S(1)}, u32[]{:S(2)}, u32[]{:S(2)}) collective-permute-start(bf16[2,2,2,120,400]{3,4,2,1,0:T(8,128)(2,1)S(1)} %pad_maximum_fusion.13), channel_id=1, source_target_pairs={{0,8},{4,12},{8,0},{12,4},{16,24},{20,28},{24,16},{28,20},{1,9},{5... | collective-permute-start | bytes 2304008 | tf_op jit(solution)/shard_map/ppermute | solution.py:670
  95.6 25.9 %collective-permute-start.9 = (bf16[2,2,2,2,120,240]{5,4,0,1,3,2:T(8,128)(2,1)S(1)}, bf16[2,2,2,2,120,240]{5,4,0,1,3,2:T(8,128)(2,1)S(1)}, u32[]{:S(2)}, u32[]{:S(2)}) collective-permute-start(bf16[2,2,2,2,120,240]{5,4,0,1,3,2:T(8,128)(2,1)S(1)} %pad_maximum_fusion.12), channel_id=1, source_target_pairs={{0,4},{4,0},{8,12},{12,8},{16,20},{20,16},{24,28},{28,24},{1,5},{5... | collective-permute-start | bytes 2764808 | tf_op jit(solution)/shard_map/ppermute | solution.py:670
  98.6 49.2 %collective-permute-start.23 = (bf16[2,2,2,320,240]{4,3,0,1,2:T(8,128)(2,1)S(1)}, bf16[2,2,2,320,240]{4,3,0,1,2:T(8,128)(2,1)S(1)}, u32[]{:S(2)}, u32[]{:S(2)}) collective-permute-start(bf16[2,2,2,320,240]{4,3,0,1,2:T(8,128)(2,1)S(1)} %pad_maximum_fusion.9), channel_id=1, source_target_pairs={{0,8},{4,12},{8,0},{12,4},{16,24},{20,28},{24,16},{28,20},{1,9},{5... | collective-permute-start | bytes 3686408 | tf_op jit(solution)/shard_map/ppermute | solution.py:670
  102.4 48.0 %collective-permute-start.18 = (bf16[2,2,2,120,640]{4,3,0,1,2:T(8,128)(2,1)S(1)}, bf16[2,2,2,120,640]{4,3,0,1,2:T(8,128)(2,1)S(1)}, u32[]{:S(2)}, u32[]{:S(2)}) collective-permute-start(bf16[2,2,2,120,640]{4,3,0,1,2:T(8,128)(2,1)S(1)} %pad_maximum_fusion.11), channel_id=1, source_target_pairs={{0,16},{4,20},{8,24},{12,28},{16,0},{20,4},{24,8},{28,12},{1,17},{... | collective-permute-start | bytes 3686408 | tf_op jit(solution)/shard_map/ppermute | solution.py:670
  111.6 61.4 %collective-permute-start.13 = (bf16[2,2,2,120,640]{4,3,0,1,2:T(8,128)(2,1)S(1)}, bf16[2,2,2,120,640]{4,3,0,1,2:T(8,128)(2,1)S(1)}, u32[]{:S(2)}, u32[]{:S(2)}) collective-permute-start(bf16[2,2,2,120,640]{4,3,0,1,2:T(8,128)(2,1)S(1)} %pad_maximum_fusion.10), channel_id=1, source_target_pairs={{0,8},{4,12},{8,0},{12,4},{16,24},{20,28},{24,16},{28,20},{1,9},{5... | collective-permute-start | bytes 3686408 | tf_op jit(solution)/shard_map/ppermute | solution.py:670
  121.6 58.4 %collective-permute-start.4 = (bf16[2,2,2,2,120,400]{4,5,3,2,1,0:T(8,128)(2,1)}, bf16[2,2,2,2,120,400]{4,5,3,2,1,0:T(8,128)(2,1)}, u32[]{:S(2)}, u32[]{:S(2)}) collective-permute-start(bf16[2,2,2,2,120,400]{4,5,3,2,1,0:T(8,128)(2,1)} %copy.114), channel_id=1, source_target_pairs={{0,4},{4,0},{8,12},{12,8},{16,20},{20,16},{24,28},{28,24},{1,5},{5... | collective-permute-start | bytes 4608008 | tf_op jit(solution)/shard_map/ppermute | solution.py:670
  150.4 86.3 %collective-permute-start.24 = (bf16[2,2,2,2,320,240]{5,4,0,1,2,3:T(8,128)(2,1)}, bf16[2,2,2,2,320,240]{5,4,0,1,2,3:T(8,128)(2,1)}, u32[]{:S(2)}, u32[]{:S(2)}) collective-permute-start(bf16[2,2,2,2,320,240]{5,4,0,1,2,3:T(8,128)(2,1)} %pad_maximum_fusion.4), channel_id=1, source_target_pairs={{0,4},{4,0},{8,12},{12,8},{16,20},{20,16},{24,28},{28,24},{1,5},{5... | collective-permute-start | bytes 7372808 | tf_op jit(solution)/shard_map/ppermute | solution.py:670
  152.9 90.1 %collective-permute-start.19 = (bf16[2,2,2,2,120,640]{5,4,0,1,3,2:T(8,128)(2,1)}, bf16[2,2,2,2,120,640]{5,4,0,1,3,2:T(8,128)(2,1)}, u32[]{:S(2)}, u32[]{:S(2)}) collective-permute-start(bf16[2,2,2,2,120,640]{5,4,0,1,3,2:T(8,128)(2,1)} %pad_maximum_fusion.6), channel_id=1, source_target_pairs={{0,4},{4,0},{8,12},{12,8},{16,20},{20,16},{24,28},{28,24},{1,5},{5... | collective-permute-start | bytes 7372808 | tf_op jit(solution)/shard_map/ppermute | solution.py:670
  173.4 54.9 %all-to-all-start.1 = ((bf16[4,240,768]{2,1,0:T(8,128)(2,1)}), bf16[4,240,768]{2,1,0:T(8,128)(2,1)}, u32[]{:S(2)}, u32[]{:S(2)}) async-start(bf16[4,240,768]{2,1,0:T(8,128)(2,1)} %gather_tokens.1), calls=%async_computation.1 | async-start | bytes 2949120 | tf_op jit(solution)/shard_map/all_to_all | solution.py:729
  180.0 68.5 %collective-permute-start.14 = (bf16[2,2,2,2,120,640]{5,4,0,1,3,2:T(8,128)(2,1)}, bf16[2,2,2,2,120,640]{5,4,0,1,3,2:T(8,128)(2,1)}, u32[]{:S(2)}, u32[]{:S(2)}) collective-permute-start(bf16[2,2,2,2,120,640]{5,4,0,1,3,2:T(8,128)(2,1)} %pad_maximum_fusion.5), channel_id=1, source_target_pairs={{0,4},{4,0},{8,12},{12,8},{16,20},{20,16},{24,28},{28,24},{1,5},{5... | collective-permute-start | bytes 7372808 | tf_op jit(solution)/shard_map/ppermute | solution.py:670
  318.3 70.3 %collective-permute-start.30 = (bf16[2,2,2,2,120,240]{5,4,0,1,3,2:T(8,128)(2,1)}, bf16[2,2,2,2,120,240]{5,4,0,1,3,2:T(8,128)(2,1)}, u32[]{:S(2)}, u32[]{:S(2)}) collective-permute-start(bf16[2,2,2,2,120,240]{5,4,0,1,3,2:T(8,128)(2,1)} %bitcast.272), channel_id=1, source_target_pairs={{0,4},{4,0},{8,12},{12,8},{16,20},{20,16},{24,28},{28,24},{1,5},{5... | collective-permute-start | bytes 2764808 | tf_op jit(solution)/shard_map/ppermute | solution.py:670
  376.7 73.0 %collective-permute-start.25 = (bf16[2,2,2,2,120,400]{4,5,0,1,2,3:T(8,128)(2,1)}, bf16[2,2,2,2,120,400]{4,5,0,1,2,3:T(8,128)(2,1)}, u32[]{:S(2)}, u32[]{:S(2)}) collective-permute-start(bf16[2,2,2,2,120,400]{4,5,0,1,2,3:T(8,128)(2,1)} %bitcast.289), channel_id=1, source_target_pairs={{0,4},{4,0},{8,12},{12,8},{16,20},{20,16},{24,28},{28,24},{1,5},{5... | collective-permute-start | bytes 4608008 | tf_op jit(solution)/shard_map/ppermute | solution.py:670
  383.0 93.6 %collective-permute-start.45 = (bf16[2,2,2,2,320,240]{5,4,0,1,2,3:T(8,128)(2,1)}, bf16[2,2,2,2,320,240]{5,4,0,1,2,3:T(8,128)(2,1)}, u32[]{:S(2)}, u32[]{:S(2)}) collective-permute-start(bf16[2,2,2,2,320,240]{5,4,0,1,2,3:T(8,128)(2,1)} %bitcast.269), channel_id=1, source_target_pairs={{0,4},{4,0},{8,12},{12,8},{16,20},{20,16},{24,28},{28,24},{1,5},{5... | collective-permute-start | bytes 7372808 | tf_op jit(solution)/shard_map/ppermute | solution.py:670
  383.5 79.5 %all-to-all-start.2 = ((bf16[4,240,768]{2,1,0:T(8,128)(2,1)}), bf16[4,240,768]{2,1,0:T(8,128)(2,1)}, u32[]{:S(2)}, u32[]{:S(2)}) async-start(bf16[4,240,768]{2,1,0:T(8,128)(2,1)} %bitcast.290), calls=%async_computation.2 | async-start | bytes 2949120 | tf_op jit(solution)/shard_map/all_to_all | solution.py:736
  391.0 55.1 %collective-permute-start.31 = (bf16[2,2,2,120,240]{4,3,0,1,2:T(8,128)(2,1)}, bf16[2,2,2,120,240]{4,3,0,1,2:T(8,128)(2,1)}, u32[]{:S(2)}, u32[]{:S(2)}) collective-permute-start(bf16[2,2,2,120,240]{4,3,0,1,2:T(8,128)(2,1)} %dynamic-slice_bitcast_fusion.7), channel_id=1, source_target_pairs={{0,16},{4,20},{8,24},{12,28},{16,0},{20,4},{24,8},{28,12},{1,17},{... | collective-permute-start | bytes 1382408 | tf_op jit(solution)/shard_map/ppermute | solution.py:670
  398.7 82.9 %collective-permute-start.40 = (bf16[2,2,2,2,120,640]{5,4,0,1,3,2:T(8,128)(2,1)}, bf16[2,2,2,2,120,640]{5,4,0,1,3,2:T(8,128)(2,1)}, u32[]{:S(2)}, u32[]{:S(2)}) collective-permute-start(bf16[2,2,2,2,120,640]{5,4,0,1,3,2:T(8,128)(2,1)} %bitcast.270), channel_id=1, source_target_pairs={{0,4},{4,0},{8,12},{12,8},{16,20},{20,16},{24,28},{28,24},{1,5},{5... | collective-permute-start | bytes 7372808 | tf_op jit(solution)/shard_map/ppermute | solution.py:670
  402.6 85.9 %collective-permute-start.35 = (bf16[2,2,2,2,120,640]{5,4,0,1,2,3:T(8,128)(2,1)}, bf16[2,2,2,2,120,640]{5,4,0,1,2,3:T(8,128)(2,1)}, u32[]{:S(2)}, u32[]{:S(2)}) collective-permute-start(bf16[2,2,2,2,120,640]{5,4,0,1,2,3:T(8,128)(2,1)} %bitcast.271), channel_id=1, source_target_pairs={{0,4},{4,0},{8,12},{12,8},{16,20},{20,16},{24,28},{28,24},{1,5},{5... | collective-permute-start | bytes 7372808 | tf_op jit(solution)/shard_map/ppermute | solution.py:670
  456.6 18.3 %collective-permute-start.26 = (bf16[2,2,2,120,400]{3,4,0,1,2:T(8,128)(2,1)S(1)}, bf16[2,2,2,120,400]{3,4,0,1,2:T(8,128)(2,1)S(1)}, u32[]{:S(2)}, u32[]{:S(2)}) collective-permute-start(bf16[2,2,2,120,400]{3,4,0,1,2:T(8,128)(2,1)S(1)} %dynamic-slice_bitcast_fusion.3), channel_id=1, source_target_pairs={{0,8},{4,12},{8,0},{12,4},{16,24},{20,28},{24,16},{28,20},{1,9},{5... | collective-permute-start | bytes 2304008 | tf_op jit(solution)/shard_map/ppermute | solution.py:670
  463.0 50.6 %all-to-all-start.3 = ((bf16[4,240,1024]{2,1,0:T(8,128)(2,1)}), bf16[4,240,1024]{2,1,0:T(8,128)(2,1)}, u32[]{:S(2)}, u32[]{:S(2)}) async-start(bf16[4,240,1024]{2,1,0:T(8,128)(2,1)} %bitcast.287), calls=%async_computation.3 | async-start | bytes 3932160 | tf_op jit(solution)/shard_map/all_to_all | solution.py:736
  480.4 40.2 %collective-permute-start.46 = (bf16[2,2,2,320,240]{4,3,0,1,2:T(8,128)(2,1)}, bf16[2,2,2,320,240]{4,3,0,1,2:T(8,128)(2,1)}, u32[]{:S(2)}, u32[]{:S(2)}) collective-permute-start(bf16[2,2,2,320,240]{4,3,0,1,2:T(8,128)(2,1)} %dynamic-slice_bitcast_fusion), channel_id=1, source_target_pairs={{0,8},{4,12},{8,0},{12,4},{16,24},{20,28},{24,16},{28,20},{1,9},{5... | collective-permute-start | bytes 3686408 | tf_op jit(solution)/shard_map/ppermute | solution.py:670
  485.1 38.9 %collective-permute-start.41 = (bf16[2,2,2,120,640]{4,3,0,1,2:T(8,128)(2,1)}, bf16[2,2,2,120,640]{4,3,0,1,2:T(8,128)(2,1)}, u32[]{:S(2)}, u32[]{:S(2)}) collective-permute-start(bf16[2,2,2,120,640]{4,3,0,1,2:T(8,128)(2,1)} %dynamic-slice_bitcast_fusion.1), channel_id=1, source_target_pairs={{0,16},{4,20},{8,24},{12,28},{16,0},{20,4},{24,8},{28,12},{1,17},{... | collective-permute-start | bytes 3686408 | tf_op jit(solution)/shard_map/ppermute | solution.py:670
  486.4 14.6 %collective-permute-start.28 = (bf16[2,120,400]{1,2,0:T(8,128)(2,1)S(1)}, bf16[2,120,400]{1,2,0:T(8,128)(2,1)S(1)}, u32[]{:S(2)}, u32[]{:S(2)}) collective-permute-start(bf16[2,120,400]{1,2,0:T(8,128)(2,1)S(1)} %dynamic-slice_bitcast_fusion.13), channel_id=1, source_target_pairs={{0,1},{1,0},{2,3},{3,2},{4,5},{5,4},{6,7},{7,6},{8,9},{9,8},{10,11... | collective-permute-start | bytes 576008 | tf_op jit(solution)/shard_map/ppermute | solution.py:670
  493.5 45.3 %collective-permute-start.36 = (bf16[2,2,2,120,640]{4,3,0,1,2:T(8,128)(2,1)}, bf16[2,2,2,120,640]{4,3,0,1,2:T(8,128)(2,1)}, u32[]{:S(2)}, u32[]{:S(2)}) collective-permute-start(bf16[2,2,2,120,640]{4,3,0,1,2:T(8,128)(2,1)} %dynamic-slice_bitcast_fusion.2), channel_id=1, source_target_pairs={{0,8},{4,12},{8,0},{12,4},{16,24},{20,28},{24,16},{28,20},{1,9},{5... | collective-permute-start | bytes 3686408 | tf_op jit(solution)/shard_map/ppermute | solution.py:670
  501.1 18.1 %collective-permute-start.29 = (bf16[120,400]{0,1:T(8,128)(2,1)S(1)}, bf16[120,400]{0,1:T(8,128)(2,1)S(1)}, u32[]{:S(2)}, u32[]{:S(2)}) collective-permute-start(bf16[120,400]{0,1:T(8,128)(2,1)S(1)} %dynamic-slice_bitcast_fusion.18), channel_id=1, source_target_pairs={{0,2},{1,3},{2,0},{3,1},{4,6},{5,7},{6,4},{7,5},{8,10},{9,11},{10,... | collective-permute-start | bytes 288008 | tf_op jit(solution)/shard_map/ppermute | solution.py:670
  522.5 19.2 %collective-permute-start.47 = (bf16[2,2,320,240]{3,2,0,1:T(8,128)(2,1)S(1)}, bf16[2,2,320,240]{3,2,0,1:T(8,128)(2,1)S(1)}, u32[]{:S(2)}, u32[]{:S(2)}) collective-permute-start(bf16[2,2,320,240]{3,2,0,1:T(8,128)(2,1)S(1)} %dynamic-slice_bitcast_fusion.4), channel_id=1, source_target_pairs={{0,16},{4,20},{8,24},{12,28},{16,0},{20,4},{24,8},{28,12},{1,17},{... | collective-permute-start | bytes 1843208 | tf_op jit(solution)/shard_map/ppermute | solution.py:670
  525.7 21.7 %collective-permute-start.42 = (bf16[2,2,120,640]{3,2,0,1:T(8,128)(2,1)S(1)}, bf16[2,2,120,640]{3,2,0,1:T(8,128)(2,1)S(1)}, u32[]{:S(2)}, u32[]{:S(2)}) collective-permute-start(bf16[2,2,120,640]{3,2,0,1:T(8,128)(2,1)S(1)} %dynamic-slice_bitcast_fusion.5), channel_id=1, source_target_pairs={{0,8},{4,12},{8,0},{12,4},{16,24},{20,28},{24,16},{28,20},{1,9},{5... | collective-permute-start | bytes 1843208 | tf_op jit(solution)/shard_map/ppermute | solution.py:670
  541.9 12.1 %collective-permute-start.48 = (bf16[2,320,240]{2,1,0:T(8,128)(2,1)S(1)}, bf16[2,320,240]{2,1,0:T(8,128)(2,1)S(1)}, u32[]{:S(2)}, u32[]{:S(2)}) collective-permute-start(bf16[2,320,240]{2,1,0:T(8,128)(2,1)S(1)} %dynamic-slice_bitcast_fusion.9), channel_id=1, source_target_pairs={{0,1},{1,0},{2,3},{3,2},{4,5},{5,4},{6,7},{7,6},{8,9},{9,8},{10,11... | collective-permute-start | bytes 921608 | tf_op jit(solution)/shard_map/ppermute | solution.py:670
  547.6 16.4 %collective-permute-start.43 = (bf16[2,120,640]{2,1,0:T(8,128)(2,1)S(1)}, bf16[2,120,640]{2,1,0:T(8,128)(2,1)S(1)}, u32[]{:S(2)}, u32[]{:S(2)}) collective-permute-start(bf16[2,120,640]{2,1,0:T(8,128)(2,1)S(1)} %dynamic-slice_bitcast_fusion.10), channel_id=1, source_target_pairs={{0,1},{1,0},{2,3},{3,2},{4,5},{5,4},{6,7},{7,6},{8,9},{9,8},{10,11... | collective-permute-start | bytes 921608 | tf_op jit(solution)/shard_map/ppermute | solution.py:670
  550.9 16.5 %collective-permute-start.38 = (bf16[2,120,640]{2,1,0:T(8,128)(2,1)S(1)}, bf16[2,120,640]{2,1,0:T(8,128)(2,1)S(1)}, u32[]{:S(2)}, u32[]{:S(2)}) collective-permute-start(bf16[2,120,640]{2,1,0:T(8,128)(2,1)S(1)} %dynamic-slice_bitcast_fusion.11), channel_id=1, source_target_pairs={{0,1},{1,0},{2,3},{3,2},{4,5},{5,4},{6,7},{7,6},{8,9},{9,8},{10,11... | collective-permute-start | bytes 921608 | tf_op jit(solution)/shard_map/ppermute | solution.py:670
  554.1 14.6 %collective-permute-start.49 = (bf16[320,240]{1,0:T(8,128)(2,1)S(1)}, bf16[320,240]{1,0:T(8,128)(2,1)S(1)}, u32[]{:S(2)}, u32[]{:S(2)}) collective-permute-start(bf16[320,240]{1,0:T(8,128)(2,1)S(1)} %dynamic-slice_bitcast_fusion.14), channel_id=1, source_target_pairs={{0,2},{1,3},{2,0},{3,1},{4,6},{5,7},{6,4},{7,5},{8,10},{9,11},{10,... | collective-permute-start | bytes 460808 | tf_op jit(solution)/shard_map/ppermute | solution.py:670
  564.1 13.0 %collective-permute-start.44 = (bf16[120,640]{1,0:T(8,128)(2,1)S(1)}, bf16[120,640]{1,0:T(8,128)(2,1)S(1)}, u32[]{:S(2)}, u32[]{:S(2)}) collective-permute-start(bf16[120,640]{1,0:T(8,128)(2,1)S(1)} %dynamic-slice_bitcast_fusion.15), channel_id=1, source_target_pairs={{0,2},{1,3},{2,0},{3,1},{4,6},{5,7},{6,4},{7,5},{8,10},{9,11},{10,... | collective-permute-start | bytes 460808 | tf_op jit(solution)/shard_map/ppermute | solution.py:670
  567.5 11.3 %collective-permute-start.39 = (bf16[120,640]{1,0:T(8,128)(2,1)S(1)}, bf16[120,640]{1,0:T(8,128)(2,1)S(1)}, u32[]{:S(2)}, u32[]{:S(2)}) collective-permute-start(bf16[120,640]{1,0:T(8,128)(2,1)S(1)} %dynamic-slice_bitcast_fusion.16), channel_id=1, source_target_pairs={{0,2},{1,3},{2,0},{3,1},{4,6},{5,7},{6,4},{7,5},{8,10},{9,11},{10,... | collective-permute-start | bytes 460808 | tf_op jit(solution)/shard_map/ppermute | solution.py:670
  (47 other events, 327.9 us)

commit v2 on v1

v2 whole, which is shorter than its diff:
```python
import functools
import math

import jax
import jax.numpy as jnp
from jax import lax
from jax.experimental import pallas as pl
from jax.experimental.pallas import tpu as pltpu
from jax.sharding import PartitionSpec as P

H = 15
KVH = 5
HD = 64
GROUP = H // KVH
QBLOCK = 256

EPSILON = 1e-05
ROPE_BASE = 10000.0
NEG = -1e30
VECTOR_ROWS = 8

BF = jnp.bfloat16
F32 = jnp.float32
MIB = 1 << 20


def dot_nn(a, b):
    return lax.dot_general(a, b, (((1,), (0,)), ((), ())), preferred_element_type=F32)


def dot_tn(a, b):
    return lax.dot_general(a, b, (((0,), (0,)), ((), ())), preferred_element_type=F32)


def dot_nt(a, b):
    return lax.dot_general(a, b, (((1,), (1,)), ((), ())), preferred_element_type=F32)


def params(limit=56):
    return pltpu.CompilerParams(
        dimension_semantics=("arbitrary",), vmem_limit_bytes=limit * MIB
    )


def cost(flops, nbytes, exps=0):
    return pl.CostEstimate(
        flops=int(flops) // 32,
        bytes_accessed=int(nbytes) // 32,
        transcendentals=int(exps) // 32,
    )


def struct(shape, dtype):
    return jax.ShapeDtypeStruct(shape, dtype)


def whole(shape):
    return pl.BlockSpec(shape, lambda i, *_: (0,) * len(shape))


def pick_columns(rank_column, picks):
    place = lax.broadcasted_iota(jnp.int32, (rank_column.shape[0], picks), 1)
    return jnp.where(rank_column == place, 1.0, 0.0).astype(BF)


def pick_rows(rank_row, picks):
    place = lax.broadcasted_iota(jnp.int32, (picks, rank_row.shape[1]), 0)
    return jnp.where(rank_row == place, 1.0, 0.0).astype(BF)


def turn(first, second, cosine, sine, direction):
    signed = sine * direction
    return first * cosine - second * signed, second * cosine + first * signed


def gather_body(values, rank, out):
    chosen = pick_columns(rank[0], out.shape[2])
    out[0] = dot_nn(values[0].astype(BF), chosen).astype(BF)


def gather_tokens(values, rank_column, picks):
    count, width, length = values.shape
    return pl.pallas_call(
        gather_body,
        grid=(count,),
        in_specs=[
            pl.BlockSpec((1, width, length), lambda i: (i, 0, 0)),
            pl.BlockSpec((1, length, 1), lambda i: (i, 0, 0)),
        ],
        out_specs=pl.BlockSpec((1, width, picks), lambda i: (i, 0, 0)),
        out_shape=struct((count, width, picks), BF),
        compiler_params=params(),
        cost_estimate=cost(2 * count * width * length * picks, 6 * values.size),
        name="gather_tokens",
    )(values, rank_column)


def scatter_body(base, values, rank, out):
    chosen = pick_rows(rank[0], values.shape[2])
    out[0] = base[0] + dot_nn(values[0], chosen)


def scatter_tokens(base, values, rank_row):
    count, width, length = base.shape
    picks = values.shape[2]
    return pl.pallas_call(
        scatter_body,
        grid=(count,),
        in_specs=[
            pl.BlockSpec((1, width, length), lambda i: (i, 0, 0)),
            pl.BlockSpec((1, width, picks), lambda i: (i, 0, 0)),
            pl.BlockSpec((1, 1, length), lambda i: (i, 0, 0)),
        ],
        out_specs=pl.BlockSpec((1, width, length), lambda i: (i, 0, 0)),
        out_shape=struct(base.shape, F32),
        compiler_params=params(),
        cost_estimate=cost(2 * count * width * length * picks, 10 * base.size),
        name="scatter_tokens",
    )(base, values, rank_row)


def project_body(who, x, rank, gain, router, cos_k, sin_k, cos_q, sin_q, *refs):
    pieces = refs[:-12]
    (
        picked, prob, q_out, kt_out, k_out, vt_out, v_out, w,
        normed, normed_picked, q_raw, kv_raw,
    ) = refs[-12:]
    step = pl.program_id(0)
    block = step ^ who[0]
    width = x.shape[0]
    q_part = width // pl.num_programs(0)
    kv_part = KVH * HD // pl.num_programs(0)
    if len(pieces) == 1:
        w[0] = pieces[0][0]
    else:
        even = who[2] == 0
        count = len(pieces) // 2
        for k, (own, other) in enumerate(zip(pieces[:count], pieces[count:])):
            first, second = own[0].astype(F32), other[0].astype(F32)
            both = [jnp.where(even, first, second), jnp.where(even, second, first)]
            height = 2 * first.shape[0]
            place = pl.ds(pl.multiple_of((who[1] ^ k) * height, 16), height)
            w[0, place] = jnp.concatenate(both, axis=0).astype(BF)

    @pl.when(step == 0)
    def _():
        full = x[...].astype(F32)
        inverse = lax.rsqrt(jnp.sum(full * full, axis=0, keepdims=True) / width + EPSILON)
        normed[...] = (full * inverse * gain[...]).astype(BF)
        chosen = pick_columns(rank[...], picked.shape[1])
        part = dot_nn(x[...], chosen)
        picked[...] = part.astype(BF)
        inverse = lax.rsqrt(jnp.sum(part * part, axis=0, keepdims=True) / width + EPSILON)
        normed_picked[...] = (part * inverse * gain[...]).astype(BF)
        logit = jnp.sum(part * router[...], axis=0, keepdims=True)
        prob[...] = jax.nn.sigmoid(logit)

    q_raw[pl.ds(pl.multiple_of(block * q_part, 8), q_part)] = dot_tn(
        w[0, :, :q_part], normed_picked[...]
    ).astype(BF)
    kv = dot_tn(w[0, :, q_part : q_part + 2 * kv_part], normed[...]).astype(BF)
    kv_raw[0, pl.ds(pl.multiple_of(block * kv_part, 8), kv_part)] = kv[:kv_part]
    kv_raw[1, pl.ds(pl.multiple_of(block * kv_part, 8), kv_part)] = kv[kv_part:]

    @pl.when(step == pl.num_programs(0) - 1)
    def _():
        half = HD // 2
        for head in range(H):
            at = head * HD
            a, b = turn(
                q_raw[at : at + half].astype(F32),
                q_raw[at + half : at + HD].astype(F32),
                cos_q[...], sin_q[...], 1.0,
            )
            scale = HD ** (-0.5)
            q_out[at : at + half] = (a.astype(BF).astype(F32) * scale).astype(BF)
            q_out[at + half : at + HD] = (b.astype(BF).astype(F32) * scale).astype(BF)
        for head in range(KVH):
            at = head * HD
            a, b = turn(
                kv_raw[0, at : at + half].astype(F32),
                kv_raw[0, at + half : at + HD].astype(F32),
                cos_k[...], sin_k[...], 1.0,
            )
            turned = jnp.concatenate([a, b], axis=0)
            kt_out[at : at + HD] = turned.astype(BF)
            k_out[head] = turned.T.astype(BF)
            value = kv_raw[1, at : at + HD]
            vt_out[at : at + HD] = value
            v_out[head] = value.astype(F32).T.astype(BF)


def project(who, x, rank_column, gain, router, tables_k, tables_q, pieces):
    width, length = x.shape
    picks = tables_q[0].shape[1]
    blocks, height, part = pieces[0].shape
    kv = KVH * HD
    half = HD // 2
    return pl.pallas_call(
        project_body,
        grid_spec=pltpu.PrefetchScalarGridSpec(
        num_scalar_prefetch=1,
        grid=(blocks,),
        in_specs=[
            whole((width, length)),
            whole((length, 1)),
            whole((width, 1)),
            whole((width, 1)),
            whole((half, length)),
            whole((half, length)),
            whole((half, picks)),
            whole((half, picks)),
        ]
        + [pl.BlockSpec((1, height, part), lambda i, who: (i, 0, 0))] * len(pieces),
        out_specs=[
            whole((width, picks)),
            whole((1, picks)),
            whole((width, picks)),
            whole((kv, length)),
            whole((KVH, length, HD)),
            whole((kv, length)),
            whole((KVH, length, HD)),
            pl.BlockSpec((1, width, part), lambda i, who: (i ^ who[0], 0, 0)),
        ],
        scratch_shapes=[
            pltpu.VMEM((width, length), BF),
            pltpu.VMEM((width, picks), BF),
            pltpu.VMEM((width, picks), BF),
            pltpu.VMEM((2, kv, length), BF),
        ],
        ),
        out_shape=[
            struct((width, picks), BF),
            struct((1, picks), F32),
            struct((width, picks), BF),
            struct((kv, length), BF),
            struct((KVH, length, HD), BF),
            struct((kv, length), BF),
            struct((KVH, length, HD), BF),
            struct((blocks, width, part), BF),
        ],
        compiler_params=params(),
        cost_estimate=cost(
            2 * width * (length * picks + picks * width + length * 2 * kv),
            2 * (2 * blocks * width * part + 4 * x.size),
        ),
        name="project",
    )(who, x, rank_column, gain, router, *tables_k, *tables_q, *pieces)


def reach_of(block, length, picks):
    return max((block + 1) * QBLOCK + length - picks, length // 2)


def clear_of(block):
    return block * QBLOCK


def block_scores(q, k, limit, block, reach):
    scores = dot_nn(k[:reach], q)
    clear = clear_of(block)
    tail = scores[clear:] if clear else scores
    key = lax.broadcasted_iota(jnp.int32, tail.shape, 0) + clear
    tail = jnp.where(key <= limit, tail, NEG)
    return jnp.concatenate([scores[:clear], tail], axis=0) if clear else tail


def attend_body(q, k, vt, limit, out, total):
    length = k.shape[1]
    picks = q.shape[1]
    for block in range(picks // QBLOCK):
        at = block * QBLOCK
        reach = reach_of(block, length, picks)
        for head in range(GROUP):
            rows = slice(head * HD, (head + 1) * HD)
            scores = block_scores(
                q[rows, at : at + QBLOCK], k[0], limit[:, at : at + QBLOCK], block, reach
            )
            top = jnp.max(scores, axis=0, keepdims=True)
            weight = jnp.exp(scores - top)
            mass = jnp.sum(weight, axis=0, keepdims=True)
            mixed = dot_nn(vt[:, :reach], weight.astype(BF))
            out[rows, at : at + QBLOCK] = (mixed / mass).astype(BF)
            total[0, head : head + 1, at : at + QBLOCK] = top + jnp.log(mass)


def attend(q, k, vt, limit):
    width, picks = q.shape
    length = k.shape[1]
    part = GROUP * HD
    return pl.pallas_call(
        attend_body,
        grid=(KVH,),
        in_specs=[
            pl.BlockSpec((part, picks), lambda i: (i, 0)),
            pl.BlockSpec((1, length, HD), lambda i: (i, 0, 0)),
            pl.BlockSpec((HD, length), lambda i: (i, 0)),
            whole((1, picks)),
        ],
        out_specs=[
            pl.BlockSpec((part, picks), lambda i: (i, 0)),
            pl.BlockSpec((1, GROUP, picks), lambda i: (i, 0, 0)),
        ],
        out_shape=[struct((width, picks), BF), struct((KVH, GROUP, picks), F32)],
        compiler_params=params(),
        cost_estimate=cost(
            16 * width * length * picks, 4 * width * picks, H * length * picks
        ),
        name="attend",
    )(q, k, vt, limit)


def attend_back_body(
    q, k, kt, v, limit, total, grad, mixed, cos_k, sin_k, cos_q, sin_q,
    gq_out, gk_out, gv_out, gk, gv,
):
    length = k.shape[1]
    picks = q.shape[1]
    half = HD // 2
    gk[...] = jnp.zeros_like(gk)
    gv[...] = jnp.zeros_like(gv)
    for block in range(picks // QBLOCK):
        at = block * QBLOCK
        cols = slice(at, at + QBLOCK)
        reach = reach_of(block, length, picks)
        for head in range(GROUP):
            rows = slice(head * HD, (head + 1) * HD)
            q_part = q[rows, cols]
            g_part = grad[rows, cols]
            scores = block_scores(q_part, k[0], limit[:, cols], block, reach)
            weight = jnp.exp(scores - total[0, head : head + 1, cols])
            delta = jnp.sum(
                g_part.astype(F32) * mixed[rows, cols].astype(F32), axis=0, keepdims=True
            )
            pull = dot_nn(v[0, :reach], g_part)
            back = (weight * (pull - delta)).astype(BF)
            gq = dot_nn(kt[:, :reach], back) * HD ** (-0.5)
            a, b = turn(gq[:half], gq[half:], cos_q[:, cols], sin_q[:, cols], -1.0)
            gq_out[head * HD : head * HD + half, cols] = a.astype(BF)
            gq_out[head * HD + half : (head + 1) * HD, cols] = b.astype(BF)
            gk[:reach] += dot_nt(back, q_part)
            gv[:reach] += dot_nt(weight.astype(BF), g_part)
    turned = gk[...].T
    a, b = turn(turned[:half], turned[half:], cos_k[...], sin_k[...], -1.0)
    gk_out[:half] = a.astype(BF)
    gk_out[half:] = b.astype(BF)
    gv_out[...] = gv[...].T.astype(BF)


def attend_back(q, k, kt, v, limit, total, grad, mixed, tables_k, tables_q):
    width, picks = q.shape
    length = k.shape[1]
    part = GROUP * HD
    half = HD // 2
    wide = pl.BlockSpec((part, picks), lambda i: (i, 0))
    tall = pl.BlockSpec((1, length, HD), lambda i: (i, 0, 0))
    flat = pl.BlockSpec((HD, length), lambda i: (i, 0))
    return pl.pallas_call(
        attend_back_body,
        grid=(KVH,),
        in_specs=[
            wide, tall, flat, tall, whole((1, picks)),
            pl.BlockSpec((1, GROUP, picks), lambda i: (i, 0, 0)),
            wide, wide,
            whole((half, length)), whole((half, length)),
            whole((half, picks)), whole((half, picks)),
        ],
        out_specs=[wide, flat, flat],
        out_shape=[
            struct((width, picks), BF),
            struct((KVH * HD, length), BF),
            struct((KVH * HD, length), BF),
        ],
        scratch_shapes=[pltpu.VMEM((length, HD), F32), pltpu.VMEM((length, HD), F32)],
        compiler_params=params(),
        cost_estimate=cost(
            40 * width * length * picks, 8 * width * picks, H * length * picks
        ),
        name="attend_back",
    )(q, k, kt, v, limit, total, grad, mixed, *tables_k, *tables_q)


def merge_body(mixed, picked, gain, w, branch, inverse_out, normed, hidden, square):
    step = pl.program_id(0)
    width = mixed.shape[0]
    part = width // pl.num_programs(0)
    rows = pl.ds(pl.multiple_of(step * part, 8), part)

    @pl.when(step == 0)
    def _():
        square[...] = jnp.zeros_like(square)

    value = dot_tn(w[0, :, w.shape[2] - part :], mixed[...])
    branch[...] = value
    total = picked[rows, :].astype(F32) + value
    hidden[rows, :] = total
    square[...] += jnp.sum(total * total, axis=0, keepdims=True)

    @pl.when(step == pl.num_programs(0) - 1)
    def _():
        inverse = lax.rsqrt(square[...] / width + EPSILON)
        inverse_out[...] = inverse
        normed[...] = (hidden[...] * inverse * gain[...]).astype(BF)


def merge(mixed, picked, gain, w):
    width, picks = mixed.shape
    blocks, _, wide = w.shape
    part = width // blocks
    return pl.pallas_call(
        merge_body,
        grid=(blocks,),
        in_specs=[
            whole((width, picks)),
            whole((width, picks)),
            whole((width, 1)),
            pl.BlockSpec((1, width, wide), lambda i: (i, 0, 0)),
        ],
        out_specs=[
            pl.BlockSpec((part, picks), lambda i: (i, 0)),
            whole((1, picks)),
            whole((width, picks)),
        ],
        out_shape=[
            struct((width, picks), F32),
            struct((1, picks), F32),
            struct((width, picks), BF),
        ],
        scratch_shapes=[pltpu.VMEM((width, picks), F32), pltpu.VMEM((1, picks), F32)],
        compiler_params=params(),
        cost_estimate=cost(2 * width * width * picks, 14 * width * picks + 2 * w.size),
        name="merge",
    )(mixed, picked, gain, w)


def down_half(part):
    return -(-part // 32) * 16


def ffn_weights(who, first, sources, w_gate, w_up, w_down, done):
    step, steps = pl.program_id(0), pl.num_programs(0)
    slot = lax.rem(step, 2)
    width = w_gate.shape[1]

    def copies(step, at):
        block = (step + first) ^ who[0]
        if len(sources) == 2:
            some = [
                (sources[0].at[0, block], w_gate.at[at]),
                (sources[0].at[1, block], w_up.at[at]),
                (sources[1].at[block], w_down.at[at]),
            ]
        else:
            (source,) = sources
            pairs, _, columns, _, _ = source.shape
            height, part = width // pairs, width // columns
            half = down_half(part)
            some = []
            for i in range(pairs):
                place = slice(i * height, (i + 1) * height)
                some.append((source.at[i, 0, block, :height], w_gate.at[at, place]))
                some.append((source.at[i, 1, block, :height], w_up.at[at, place]))
            for c in range(columns):
                top = slice(c * part, c * part + half)
                some.append((source.at[block, 0, c, height : height + half], w_down.at[at, top]))
                end = slice(c * part + half, (c + 1) * part)
                rest = slice(height + 2 * half - part, height + half)
                some.append((source.at[block, 1, c, rest], w_down.at[at, end]))
        return [
            pltpu.make_async_copy(source, target, done.at[at, i])
            for i, (source, target) in enumerate(some)
        ]

    @pl.when(step == 0)
    def _():
        for copy in copies(step, slot):
            copy.start()

    @pl.when(step + 1 < steps)
    def _():
        for copy in copies(step + 1, 1 - slot):
            copy.start()

    for copy in copies(step, slot):
        copy.wait()
    return slot


def ffn_scratch(width, sources):
    hidden = sources[0].shape[-1]
    count = 3
    if len(sources) == 1:
        count = 2 * (sources[0].shape[0] + sources[0].shape[2])
    return [pltpu.VMEM((2, width, hidden), BF)] * 3 + [pltpu.SemaphoreType.DMA((2, count))]


def ffn_body(many, who, normed, branch, prob, *refs):
    sources, refs = refs[:many], refs[many:]
    gate_out, up_out, active_out, delta, both_out, forward, *buffers = refs
    w_gate, w_up, w_down, _ = buffers
    slot = ffn_weights(who, 0, sources, *buffers)

    @pl.when(pl.program_id(0) == 0)
    def _():
        forward[...] = branch[...]

    tokens = normed[...]
    gate = dot_tn(w_gate[slot], tokens)
    up = dot_tn(w_up[slot], tokens)
    active = (gate * jax.nn.sigmoid(gate) * up).astype(BF)
    gate_out[0] = gate.astype(BF)
    up_out[0] = up.astype(BF)
    active_out[0] = active
    forward[...] += dot_nn(w_down[slot], active)

    @pl.when(pl.program_id(0) == pl.num_programs(0) - 1)
    def _():
        both = forward[...]
        delta[...] = (prob[...] * both).astype(BF)
        both_out[...] = both.astype(BF)


def ffn(who, normed, branch, prob, blocks, hidden, sources):
    width, picks = normed.shape
    full, row = whole((width, picks)), whole((1, picks))
    far = pl.BlockSpec(memory_space=pl.ANY)
    kept = pl.BlockSpec((1, hidden, picks), lambda i, who: (i, 0, 0))
    kept_shape = struct((blocks, hidden, picks), BF)
    low = struct((width, picks), BF)
    return pl.pallas_call(
        functools.partial(ffn_body, len(sources)),
        grid_spec=pltpu.PrefetchScalarGridSpec(
            num_scalar_prefetch=1,
            grid=(blocks,),
            in_specs=[full, full, row] + [far] * len(sources),
            out_specs=[kept] * 3 + [full, full],
            scratch_shapes=[pltpu.VMEM((width, picks), F32)] + ffn_scratch(width, sources),
        ),
        out_shape=[kept_shape] * 3 + [low, low],
        compiler_params=params(60),
        cost_estimate=cost(
            6 * width * hidden * blocks * picks, 6 * width * hidden * blocks + 8 * width * picks
        ),
        name="ffn",
    )(who, normed, branch, prob, *sources)


def down_grad_body(who, grad_ffn, active, keep, send):
    here, columns, half, lanes = keep.shape
    part = grad_ffn.shape[0] // columns
    even = who[2] == 0
    for c in range(columns):
        value = dot_nt(grad_ffn[c * part : (c + 1) * part], active[0])
        low, high = value[:half].astype(BF), value[part - half :].astype(BF)
        mine, other = jnp.where(even, low, high), jnp.where(even, high, low)
        for i in range(here):
            at = i ^ lax.rem(who[1], here) if here > 1 else 0
            keep[at, c ^ who[0]] = mine[:, i * lanes : (i + 1) * lanes]
            send[at, c ^ who[0]] = other[:, i * lanes : (i + 1) * lanes]


def down_grad(who, grad_ffn, active, pairs, columns):
    width, picks = grad_ffn.shape
    blocks, hidden, _ = active.shape
    here = pairs // blocks
    tile = (columns, down_half(width // columns), hidden // here)
    block = pl.BlockSpec(
        (here,) + tile, lambda i, who: (i ^ who[0] ^ lax.div(who[1], here), 0, 0, 0)
    )
    return pl.pallas_call(
        down_grad_body,
        grid_spec=pltpu.PrefetchScalarGridSpec(
            num_scalar_prefetch=1,
            grid=(blocks,),
            in_specs=[
                whole((width, picks)),
                pl.BlockSpec((1, hidden, picks), lambda i, who: (i, 0, 0)),
            ],
            out_specs=[block, block],
        ),
        out_shape=[struct((pairs,) + tile, BF)] * 2,
        compiler_params=params(),
        cost_estimate=cost(2 * blocks * hidden * width * picks, 6 * blocks * hidden * width),
        name="down_grad",
    )(who, grad_ffn, active)


def ffn_back_body(first, last, many, who, normed, grad_ffn, gate_in, up_in, *refs):
    sources, refs = refs[:many], refs[many:]
    if first:
        carried, refs = refs[0], refs[1:]
    if last:
        (branch, both_in, picked, cot, prob, inverse, gain, router), refs = refs[:8], refs[8:]
    keep_pair, send_pair, refs = refs[0], refs[1], refs[2:]
    outs, backward, buffers = refs[:-5], refs[-5], refs[-4:]
    w_gate, w_up, w_down, _ = buffers
    slot = ffn_weights(who, first, sources, *buffers)
    width = normed.shape[0]
    even = who[2] == 0

    @pl.when(pl.program_id(0) == 0)
    def _():
        backward[...] = carried[...] if first else jnp.zeros_like(backward)

    pull = dot_tn(w_down[slot], grad_ffn[...])
    gate = gate_in[0].astype(F32)
    sigmoid = jax.nn.sigmoid(gate)
    silu = gate * sigmoid
    grad_gate = (pull * up_in[0].astype(F32) * (sigmoid + silu * (1.0 - sigmoid))).astype(BF)
    grad_up = (pull * silu).astype(BF)
    backward[...] += dot_nn(w_gate[slot], grad_gate) + dot_nn(w_up[slot], grad_up)
    tokens = normed[...]
    for_gate = dot_nt(tokens, grad_gate).astype(BF)
    for_up = dot_nt(tokens, grad_up).astype(BF)
    pieces, _, height, _ = keep_pair.shape
    for i in range(pieces):
        place = slice(i * height, (i + 1) * height)
        at = i ^ who[1] if pieces > 1 else 0
        keep_pair[at, 0] = jnp.where(even, for_gate[place], for_up[place])
        send_pair[at, 0] = jnp.where(even, for_up[place], for_gate[place])

    @pl.when(pl.program_id(0) == pl.num_programs(0) - 1)
    def _():
        if not last:
            outs[0][...] = backward[...]
            return
        grad_attn, rest_out, gain_out, router_out = outs
        share = prob[...]
        cot_full = cot[...].astype(F32)
        slope = share * (1.0 - share) * jnp.sum(
            cot_full * both_in[...].astype(F32), axis=0, keepdims=True
        )
        token = picked[...].astype(F32)
        router_out[...] = jnp.sum(slope * token, axis=1, keepdims=True)
        hidden = token + branch[...]
        inv = inverse[...]
        grad_norm = backward[...]
        gain_out[...] = jnp.sum(grad_norm * hidden * inv, axis=1, keepdims=True)
        unit = grad_norm * gain[...]
        along = jnp.sum(unit * hidden, axis=0, keepdims=True) / width
        grad_hidden = inv * unit - hidden * (inv * inv * inv * along)
        grad_attn[...] = (grad_hidden + share * cot_full).astype(BF)
        rest_out[...] = (grad_hidden + slope * router[...]).astype(BF)


def ffn_back(who, first, count, last, pieces, normed, grad_ffn, gate, up, sources, carried, tail):
    width, picks = normed.shape
    hidden = gate.shape[1]
    height = width // pieces
    full, row, column = whole((width, picks)), whole((1, picks)), whole((width, 1))
    far = pl.BlockSpec(memory_space=pl.ANY)
    kept = pl.BlockSpec((1, hidden, picks), lambda i, who: (i + first, 0, 0))
    tall = pl.BlockSpec((pieces, 1, height, hidden), lambda i, who: (0, i, 0, 0))
    tall_shape = struct((pieces, count, height, hidden), BF)
    low, thin = struct((width, picks), BF), struct((width, 1), F32)
    extra = ([carried] if first else []) + (list(tail) if last else [])
    extra_specs = ([full] if first else []) + ([full] * 4 + [row] * 2 + [column] * 2 if last else [])
    return pl.pallas_call(
        functools.partial(ffn_back_body, first, last, len(sources)),
        grid_spec=pltpu.PrefetchScalarGridSpec(
            num_scalar_prefetch=1,
            grid=(count,),
            in_specs=[full, full, kept, kept] + [far] * len(sources) + extra_specs,
            out_specs=[tall, tall] + ([full, full, column, column] if last else [full]),
            scratch_shapes=[pltpu.VMEM((width, picks), F32)] + ffn_scratch(width, sources),
        ),
        out_shape=[tall_shape, tall_shape]
        + ([low, low, thin, thin] if last else [struct((width, picks), F32)]),
        compiler_params=params(60),
        cost_estimate=cost(
            10 * width * hidden * count * picks, 10 * width * hidden * count + 12 * width * picks
        ),
        name="ffn_back",
    )(who, normed, grad_ffn, gate, up, *sources, *extra)


def merge_back_body(mixed, grad, w, gw, grad_mixed, total):
    step = pl.program_id(0)
    part = gw.shape[2]
    rows = pl.ds(pl.multiple_of(step * part, 8), part)
    piece = grad[rows, :]
    gw[0] = dot_nt(mixed[...], piece).astype(BF)
    value = dot_nn(w[0, :, w.shape[2] - part :], piece)

    @pl.when(step == 0)
    def _():
        total[...] = value

    @pl.when(step > 0)
    def _():
        total[...] += value

    @pl.when(step == pl.num_programs(0) - 1)
    def _():
        grad_mixed[...] = total[...].astype(BF)


def merge_back(mixed, grad, w):
    width, picks = mixed.shape
    blocks, _, wide = w.shape
    part = width // blocks
    block = pl.BlockSpec((1, width, part), lambda i: (i, 0, 0))
    wide_block = pl.BlockSpec((1, width, wide), lambda i: (i, 0, 0))
    return pl.pallas_call(
        merge_back_body,
        grid=(blocks,),
        in_specs=[whole((width, picks)), whole((width, picks)), wide_block],
        out_specs=[block, whole((width, picks))],
        out_shape=[struct((blocks, width, part), BF), struct((width, picks), BF)],
        scratch_shapes=[pltpu.VMEM((width, picks), F32)],
        compiler_params=params(),
        cost_estimate=cost(4 * width * width * picks, 6 * width * picks + 4 * w.size),
        name="merge_back",
    )(mixed, grad, w)


def mixing_grad_body(
    who, x, rank, gain, gq, gk, gv, gw_out,
    keep, send, grads_out,
    normed, gq_full,
):
    step = pl.program_id(0)
    width = x.shape[0]
    q_part = width // pl.num_programs(0)
    kv_part = KVH * HD // pl.num_programs(0)
    even = who[2] == 0

    @pl.when(step == 0)
    def _():
        full = x[...].astype(F32)
        inverse = lax.rsqrt(jnp.sum(full * full, axis=0, keepdims=True) / width + EPSILON)
        normed[...] = (full * inverse * gain[...]).astype(BF)
        gq_full[...] = dot_nn(gq[...], pick_rows(rank[...], gq.shape[1])).astype(BF)

    q_rows = pl.ds(pl.multiple_of(step * q_part, 8), q_part)
    kv_rows = pl.ds(pl.multiple_of(step * kv_part, 8), kv_part)
    grads = jnp.concatenate([gq_full[q_rows, :], gk[kv_rows, :], gv[kv_rows, :]], axis=0)
    grads_out[0] = grads
    value = dot_nt(normed[...], grads)
    value = jnp.concatenate([value, gw_out[0].astype(F32)], axis=1)
    pairs = keep.shape[0]
    rows = width // (2 * pairs)
    for pair in range(pairs):
        low = value[2 * pair * rows : (2 * pair + 1) * rows]
        high = value[(2 * pair + 1) * rows : (2 * pair + 2) * rows]
        keep[pair ^ who[1], 0, :rows] = jnp.where(even, low, high).astype(BF)
        send[pair ^ who[1], 0, :rows] = jnp.where(even, high, low).astype(BF)


def mixing_grad(who, x, rank_row, gain, gq, gk, gv, gw_out, pairs):
    width, length = x.shape
    picks = gq.shape[1]
    blocks, _, out_part = gw_out.shape
    kv = KVH * HD
    part = (width + 2 * kv) // blocks
    rows = width // (2 * pairs) + VECTOR_ROWS
    split = pl.BlockSpec((pairs, 1, rows, part + out_part), lambda i, who: (0, i ^ who[0], 0, 0))
    split_shape = struct((pairs, blocks, rows, part + out_part), BF)
    return pl.pallas_call(
        mixing_grad_body,
        grid_spec=pltpu.PrefetchScalarGridSpec(
            num_scalar_prefetch=1,
            grid=(blocks,),
            in_specs=[
                whole((width, length)),
                whole((1, length)),
                whole((width, 1)),
                whole((width, picks)),
                whole((kv, length)),
                whole((kv, length)),
                pl.BlockSpec((1, width, out_part), lambda i, who: (i, 0, 0)),
            ],
            out_specs=[split, split, pl.BlockSpec((1, part, length), lambda i, who: (i, 0, 0))],
            scratch_shapes=[pltpu.VMEM((width, length), BF), pltpu.VMEM((width, length), BF)],
        ),
        out_shape=[split_shape, split_shape, struct((blocks, part, length), BF)],
        compiler_params=params(),
        cost_estimate=cost(2 * width * length * (picks + width + 2 * kv), 10 * x.size),
        name="mixing_grad",
    )(who, x, rank_row, gain, gq, gk, gv, gw_out)


def project_back_body(x, rank, gain, grads, rest, w, out, gain_out, total):
    step = pl.program_id(0)
    width = x.shape[0]
    part = grads.shape[1]

    @pl.when(step == 0)
    def _():
        total[...] = jnp.zeros_like(total)

    total[...] += dot_nn(w[0, :, :part], grads[0])

    @pl.when(step == pl.num_programs(0) - 1)
    def _():
        full = x[...].astype(F32)
        inv = lax.rsqrt(jnp.sum(full * full, axis=0, keepdims=True) / width + EPSILON)
        grad_norm = total[...]
        gain_out[...] = jnp.sum(grad_norm * full * inv, axis=1, keepdims=True)
        unit = grad_norm * gain[...]
        along = jnp.sum(unit * full, axis=0, keepdims=True) / width
        chosen = pick_rows(rank[...], rest.shape[1])
        out[...] = (
            inv * unit - full * (inv * inv * inv * along) + dot_nn(rest[...], chosen)
        ).astype(BF)


def project_back(x, rank_row, gain, grads, rest, w):
    width, length = x.shape
    picks = rest.shape[1]
    blocks, part, _ = grads.shape
    return pl.pallas_call(
        project_back_body,
        grid=(blocks,),
        in_specs=[
            whole((width, length)),
            whole((1, length)),
            whole((width, 1)),
            pl.BlockSpec((1, part, length), lambda i: (i, 0, 0)),
            whole((width, picks)),
            pl.BlockSpec((1,) + w.shape[1:], lambda i: (i, 0, 0)),
        ],
        out_specs=[whole((width, length)), whole((width, 1))],
        out_shape=[struct((width, length), BF), struct((width, 1), F32)],
        scratch_shapes=[pltpu.VMEM((width, length), F32)],
        compiler_params=params(),
        cost_estimate=cost(2 * width * length * (picks + blocks * part), 10 * x.size + 2 * w.size),
        name="project_back",
    )(x, rank_row, gain, grads, rest, w)


def hold(*values):
    return lax.optimization_barrier(values)


def swap(value):
    count = lax.axis_size("row")
    return lax.ppermute(value, "row", [(i, i ^ 1) for i in range(count)])


def partner(value, axis, k):
    count = lax.axis_size(axis)
    far = k if axis == "col" else 2 * k
    return lax.ppermute(value, axis, [(i, i ^ far) for i in range(count)])


def collect(value, axis, partners):
    return [partner(value, axis, k) if k else value for k in partners]


def spread(values, axis):
    return [values[0]] + [partner(value, axis, k) for k, value in enumerate(values) if k]


def add_up(values):
    return sum(value.astype(F32) for value in values)


def pair_up(keep, got):
    return [add_up((a, b)).astype(BF) for a, b in zip(keep, got)]


def to_owner(value):
    copies = lax.axis_size("col") // value.shape[0]
    if copies > 1:
        value = jnp.concatenate([value] * copies, axis=0)
    moved = lax.all_to_all(value, "col", split_axis=0, concat_axis=1, tiled=True)
    return moved[0]


def from_owner(value, sequences):
    count = lax.axis_size("col")
    value = value.reshape(count, value.shape[0] // count, value.shape[1])
    moved = lax.all_to_all(value, "col", split_axis=0, concat_axis=0, tiled=True)
    return moved[:sequences]


def rope_tables(positions):
    half = HD // 2
    frequency = jnp.exp(jnp.arange(half, dtype=F32) * (-2.0 * math.log(ROPE_BASE) / HD))
    angles = frequency[:, None] * positions.astype(F32)[None, :]
    return jnp.cos(angles), jnp.sin(angles)


def on_device(
    resid, cotangent, prefix, slot, chosen, norm1_gain, norm2_gain, router,
    w_query, w_key, w_value, w_out, w_gate, w_up, w_down,
):
    col_count, row_count = lax.axis_size("col"), lax.axis_size("row")
    column = lax.axis_index("col")
    sequences, part, length = resid.shape
    width = part * col_count
    picks = chosen.shape[2]
    copies = col_count // sequences
    own = lax.rem(column, sequences)
    rows, hidden = w_gate.shape
    down_rows = w_down.shape[0]
    pairs = row_count // 2
    mixing_part = part + 2 * w_key.shape[1] + part

    own_pair_index = lax.axis_index("row") >> 1
    core = lax.axis_index("row") & 1
    even = core == 0
    who = jnp.stack([column, own_pair_index, core]).astype(jnp.int32)
    aligned = 2 * rows % 16 == 0

    half = col_count // 2

    mine = jnp.where(even, w_gate, w_up)
    other = swap(jnp.where(even, w_up, w_gate))
    pair = jnp.concatenate([jnp.where(even, mine, other), jnp.where(even, other, mine)], axis=0)
    down_rows_kept = down_half(part)
    turned = w_down.T
    low, high = turned[:down_rows_kept], turned[part - down_rows_kept :]
    mine, other = jnp.where(even, low, high), swap(jnp.where(even, high, low))
    down = jnp.concatenate([jnp.where(even, mine, other), jnp.where(even, other, mine)], axis=1)
    mixing = jnp.concatenate([w_query, w_key, w_value, w_out], axis=1)
    if aligned:
        sources = lax.all_gather(jnp.concatenate([pair, down], axis=0), ("row", "col"), axis=0)
        sources = (sources.reshape((pairs, 2, col_count) + sources.shape[1:]),)
    else:
        pair_all = lax.all_gather(pair, ("row", "col"), axis=0)
        pair_all = pair_all.reshape(pairs, 2, col_count, 2 * rows, hidden).transpose(1, 2, 0, 3, 4)
        down_all = lax.all_gather(down, ("row", "col"), axis=0)
        down_all = down_all.reshape((col_count, pairs // col_count, 2, col_count) + down.shape)
        down_all = jnp.concatenate(
            [down_all[:, :, 0], down_all[:, :, 1, :, 2 * down_rows_kept - part :]], axis=3
        )
        sources = (
            pair_all.reshape(2, col_count, width, hidden),
            down_all.transpose(0, 2, 3, 1, 4).reshape(col_count, width, hidden),
        )
    mixing, x = hold(collect(mixing, "col", range(col_count)), resid.astype(BF))
    mixing = jnp.stack(mixing)

    every = jnp.arange(length, dtype=jnp.int32)
    chosen_of = chosen[:, 0][slot]
    selected = jnp.any(every[None, :, None] == chosen_of[:, None, :], axis=2)
    before = (every[:, None] < every[None, :]).astype(BF)
    places = jnp.dot(selected.astype(BF), before, preferred_element_type=F32)
    ranks = jnp.where(selected, places.astype(jnp.int32), -1)
    rank = lax.dynamic_index_in_dim(ranks, own, 0, keepdims=False)
    prefix_len = lax.dynamic_index_in_dim(prefix, own, 0, keepdims=False)
    place = jnp.arange(picks, dtype=jnp.int32)
    spot = jnp.sum(jnp.where(rank[None, :] == place[:, None], every[None, :], 0), axis=1)
    limit = jnp.maximum(spot, prefix_len - 1)[None, :]
    tables_k = rope_tables(every)
    tables_q = rope_tables(spot)
    gain_one, gain_two, router = norm1_gain[:, None], norm2_gain[:, None], router[:, None]
    cot = gather_tokens(cotangent, ranks[:, :, None], picks)

    x, mixing, cot, limit, tables_k, tables_q = hold(
        to_owner(x), collect(mixing, "row", range(pairs)), cot, limit, tables_k, tables_q
    )
    cot = to_owner(cot)
    mixing_other, mixing = hold([swap(piece) for piece in mixing], mixing)
    if aligned:
        mixing = mixing + mixing_other
    else:
        order = jnp.arange(pairs) ^ own_pair_index
        mixing = jnp.stack([jnp.stack(mixing), jnp.stack(mixing_other)])[jnp.stack([core, 1 - core])]
        mixing = [mixing[:, order].transpose(2, 1, 0, 3, 4).reshape(col_count, width, mixing_part)]
    picked, prob, q, kt, k, vt, v, mixing = project(
        who, x, rank[:, None], gain_one, router, tables_k, tables_q, mixing
    )
    mixed, mass = attend(q, k, vt, limit)
    (branch, inverse, normed), cot = hold(merge(mixed, picked, gain_two, mixing), cot)
    gate, up, active, delta, both = ffn(who, normed, branch, prob, col_count, hidden, sources)
    grad_ffn = (prob * cot.astype(F32)).astype(BF)
    (keep_down, send_down), delta, gate = hold(
        down_grad(who, grad_ffn, active, pairs, col_count), delta, gate
    )
    delta = from_owner(delta, sequences)
    pieces = pairs if aligned else 1
    back_args = (pieces, normed, grad_ffn, gate, up, sources)
    tail = (branch, both, picked, cot, prob, inverse, gain_two, router)

    def by_pairs(value):
        if aligned:
            return value
        value = value[0].reshape(half, pairs, 2 * rows, hidden).transpose(1, 0, 2, 3)
        return value[jnp.arange(pairs) ^ own_pair_index]

    got_down, (keep_low, send_low, carried), keep_down = hold(
        swap(send_down), ffn_back(who, 0, half, False, *back_args, None, None), keep_down
    )
    sum_down = pair_up(keep_down, got_down)
    sum_down, send_low, keep_low, carried = hold(sum_down, send_low, keep_low, carried)
    sum_down = spread(sum_down, "row")
    got_low, (keep_high, send_high, grad_attn, rest, gain_two_grad, router_grad), keep_low = hold(
        swap(send_low), ffn_back(who, half, half, True, *back_args, carried, tail), keep_low
    )
    sum_low = pair_up(by_pairs(keep_low), by_pairs(got_low))
    sum_low, send_high, keep_high, grad_attn = hold(sum_low, send_high, keep_high, grad_attn)
    got_high, sum_down, (gw_out, grad_mixed), keep_high = hold(
        swap(send_high), sum_down, merge_back(mixed, grad_attn, mixing), keep_high
    )
    sum_high = pair_up(by_pairs(keep_high), by_pairs(got_high))
    sum_down = list(add_up(sum_down).astype(BF))
    sum_high, sum_down, grad_mixed = hold(sum_high, sum_down, grad_mixed)
    sum_low, delta, (gq, gk, gv), sum_high, sum_down = hold(
        spread(sum_low, "row"),
        delta,
        attend_back(q, k, kt, v, limit, mass, grad_mixed, mixed, tables_k, tables_q),
        sum_high,
        spread(sum_down, "col"),
    )
    sum_low = list(add_up(sum_low).astype(BF))
    sum_down = add_up(sum_down)
    sum_low, sum_high, gq = hold(sum_low, sum_high, gq)
    sum_high, sum_low, (keep_mixing, send_mixing, grads) = hold(
        spread(sum_high, "row"),
        spread(sum_low, "col"),
        mixing_grad(who, x, rank[None, :], gain_one, gq, gk, gv, gw_out, pairs),
    )
    sum_high = list(add_up(sum_high).astype(BF))
    sum_high, send_mixing, keep_mixing, grads = hold(sum_high, send_mixing, keep_mixing, grads)
    got_mixing, (back, gain_one_grad), keep_mixing = hold(
        swap(send_mixing),
        project_back(x, rank[None, :], gain_one, grads, rest, mixing),
        keep_mixing,
    )
    back = from_owner(back, sequences)
    sum_pair = add_up(sum_low + [partner(value, "col", half + k) for k, value in enumerate(sum_high)])

    lanes = sum_down.shape[1] // 2
    first, second = sum_down[:, :lanes], sum_down[:, lanes:]
    mine, other = jnp.where(even, first, second), jnp.where(even, second, first)
    other = swap(other.astype(BF)).astype(F32)
    top, end = jnp.where(even, mine, other), jnp.where(even, other, mine)
    gw_down = jnp.concatenate([top, end[2 * down_rows_kept - part :]], axis=0).T

    vectors = jnp.concatenate([gain_one_grad, gain_two_grad, router_grad], axis=1).T.astype(BF)
    vectors = vectors.reshape(3, col_count, part).transpose(1, 0, 2)
    vectors = vectors[jnp.arange(col_count) ^ column]
    vectors = jnp.pad(vectors, ((0, 0), (0, VECTOR_ROWS - 3), (0, mixing_part - part)))
    other = swap(vectors)
    vectors = jnp.broadcast_to(vectors[None], (pairs,) + vectors.shape)
    other = jnp.broadcast_to(other[None], vectors.shape)
    keep_mixing = lax.dynamic_update_slice(keep_mixing, vectors, (0, 0, rows, 0))
    got_mixing = lax.dynamic_update_slice(got_mixing, other, (0, 0, rows, 0))
    sum_mixing = pair_up(keep_mixing, got_mixing)
    sum_mixing, block_out = hold(
        spread(sum_mixing, "row"), scatter_tokens(resid, delta, ranks[:, None, :])
    )
    sum_mixing = add_up(sum_mixing).astype(BF)
    gw_mixing = add_up(spread(list(sum_mixing), "col"))

    sum_pair = sum_pair.reshape(2, rows, hidden)
    mine = jnp.where(even, sum_pair[0], sum_pair[1])
    other = jnp.where(even, sum_pair[1], sum_pair[0]).astype(BF)
    other = swap(other).astype(F32)
    gw_gate, gw_up = jnp.where(even, mine, other), jnp.where(even, other, mine)
    if copies > 1:
        gw_gate, gw_up, gw_down, gw_mixing = (
            a / copies for a in (gw_gate, gw_up, gw_down, gw_mixing)
        )

    resid_grad = cotangent + back.astype(F32)
    kv_part = w_key.shape[1]
    ends = (part, part + kv_part, part + 2 * kv_part)
    return (
        block_out, resid_grad,
        gw_mixing[rows, :part], gw_mixing[rows + 1, :part], gw_mixing[rows + 2, :part],
        gw_mixing[:rows, : ends[0]], gw_mixing[:rows, ends[0] : ends[1]],
        gw_mixing[:rows, ends[1] : ends[2]], gw_mixing[:rows, ends[2] :],
        gw_gate, gw_up, gw_down,
    )


def solution(mesh):
    block = P("row", "col")
    placed = (
        P("row", "col", None), P("row", "col", None), P("row"), P("row"), P(None, "row", None),
        P(), P(), P(),
        block, block, block, block, block, block, block,
    )
    given = (
        P("row", "col", None), P("row", "col", None), P("col"), P("col"), P("col"),
        block, block, block, block, block, block, block,
    )
    return jax.shard_map(
        on_device, mesh=mesh, in_specs=placed, out_specs=given, check_vma=False
    )
```

time: 585 us -> 504 us (0.86)
  local copies, waits for them, and re-layouts: 63.1 us -> 20.9 us
  blocking collectives: 40.1 us -> 0 us
  Pallas kernels: 174 us -> 207 us
  starting transfers between devices: 93.6 us -> 64.7 us
  between operations: 2.54 us -> 15.6 us
  other arithmetic: 57.8 us -> 47.1 us
  waiting for transfers between devices: 148 us -> 141 us
    pallas_call x2 -> x6, Pallas kernels: 68.4 us -> 109 us  [the longest x2 46.8 us: ffn_back(): pl.pallas_call(functools.partial(ffn_back_body, first, last, len(sources)...]
    psum x1 -> x0, blocking collectives: 40.1 us -> none  [on_device(): vectors = lax.psum(vectors.T, ('row', 'col'))]
    ppermute x50 -> x40, starting transfers between devices: 74.6 us -> 41.1 us  [the longest x27 37.9 us: partner(): return lax.ppermute(value, axis, [(i, i ^ far) for i in range(count)])]
    ppermute x50 -> x40, waiting for transfers between devices: 142 us -> 112 us  [the longest x27 110 us: partner(): return lax.ppermute(value, axis, [(i, i ^ far) for i in range(count)])]
    all_to_all x2, waiting for transfers between devices: 0.01 us -> 26.8 us  [to_owner(): lax.all_to_all(value, 'col', split_axis=0, concat_axis=1, tiled=True)]
    dynamic_slice x12 -> x2, local copies, waits for them, and re-layouts: 27.4 us -> 0.6 us  [the longest x1 0.59 us: on_device(): prefix_len = lax.dynamic_index_in_dim(prefix, own, 0, keepdims=False)]
    another operation x49 -> x5, other arithmetic: 22.4 us -> 3.26 us  [join_bit(): jnp.stack([jnp.where(mine, value, other), jnp.where(mine, other, value)],...]
    another operation x6 -> x7, local copies, waits for them, and re-layouts: 15.2 us -> 1.43 us  [the longest x1 0.87 us: on_device(): sum_high = list(add_up(sum_high).astype(BF))]
  transfers between devices with their start and end apart: 54 -> 45, of which waited for: 26 -> 18; matrix products, arithmetic and copies ran while one was open for 19% -> 9% of each run, Pallas kernels for 19% -> 35%
where the time goes in v2:
time: 504 us; the launch traced here: 496 us
  Pallas kernels  207 us (41%)
  waiting for transfers between devices  141 us (28%)
  starting transfers between devices  64.7 us (13%)
  other arithmetic  47.1 us (9%)
  local copies, waits for them, and re-layouts  20.9 us (4%)
  between operations  15.6 us (3%)
    ppermute x27, waiting for transfers between devices, partner(): return lax.ppermute(value, axis, [(i, i ^ far) for i in range(count)])  110 us
    pallas_call x2, Pallas kernels, ffn_back(): pl.pallas_call(functools.partial(ffn_back_body, first, last, len(sources)...  46.8 us
    ppermute x27, starting transfers between devices, partner(): return lax.ppermute(value, axis, [(i, i ^ far) for i in range(count)])  37.9 us
    pallas_call x1, Pallas kernels, attend_back(): pl.pallas_call(attend_back_body, grid=(KVH,), in_specs=[wide, tall, flat,...  29.9 us
    all_to_all x2, waiting for transfers between devices, to_owner(): lax.all_to_all(value, 'col', split_axis=0, concat_axis=1, tiled=True)  26.8 us
    pallas_call x1, Pallas kernels, attend(): pl.pallas_call(attend_body, grid=(KVH,), in_specs=[pl.BlockSpec((part, pi...  26.2 us
    pallas_call x1, Pallas kernels, ffn(): pl.pallas_call(functools.partial(ffn_body, len(sources)), grid_spec=pltpu...  22.4 us
    pallas_call x1, Pallas kernels, project(): pl.pallas_call(project_body, grid_spec=pltpu.PrefetchScalarGridSpec(num_s...  17.9 us
  transfers between devices with their start and end apart: 45, of which 18 were waited for; matrix products, arithmetic and copies ran while one was open for 9% of the time, Pallas kernels for 35%

profile of v2, /device:TPU:0, one launch (start us, length us, event | category | flops | bytes accessed | tf_op | source)
XLA Modules:
  0.0 496.4 jit_solution(11658475284389518155)
XLA Ops:
  12.7 2.8 collective-permute-start
  15.5 2.6 collective-permute-start.1
  18.1 3.7 convert_element_type.374
  22.8 10.2 %collective-permute-done.1 = bf16[120,640]{1,0:T(8,128)(2,1)S(1)} collective-permute-done((bf16[120,640]{1,0:T(8,128)(2,1)S(1)}, bf16[120,640]{1,0:T(8,128)(2,1)S(1)}, u32[]{:S(2)}, u32[]{:S(2)}) %collective-permute-start.1) | collective-permute-done | bytes 153632 | tf_op jit(solution)/shard_map/ppermute | solution.py:844
  32.9 12.3 %all-to-all-start = ((bf16[4,240,1024]{2,1,0:T(8,128)(2,1)}), bf16[4,240,1024]{2,1,0:T(8,128)(2,1)S(1)}, u32[]{:S(2)}, u32[]{:S(2)}) async-start(bf16[4,240,1024]{2,1,0:T(8,128)(2,1)} %convert_element_type.374), calls=%async_computation | async-start | bytes 3932160 | tf_op jit(solution)/shard_map/all_to_all | solution.py:867
  53.6 2.0 copy.110.rank
  55.5 5.9 %gather_tokens.1 = bf16[4,240,768]{2,1,0:T(8,128)(2,1)} custom-call(f32[4,240,1024]{2,1,0:T(8,128)} %values.1, s32[4,1024,1]{2,1,0:T(8,128)} %copy.110.rank), custom_call_target="tpu_custom_call" | custom-call | flops 47185920 | bytes 184320 | tf_op jit(solution)/shard_map/gather_tokens/pallas_call | solution.py:83
  63.8 13.9 %collective-permute-done.3.refs_1_ = bf16[4,120,640]{2,1,0:T(8,128)(2,1)S(1)} collective-permute-done((bf16[4,120,640]{2,1,0:T(8,128)(2,1)S(1)}, bf16[4,120,640]{2,1,0:T(8,128)(2,1)S(1)}, u32[]{:S(2)}, u32[]{:S(2)}) %collective-permute-start.3) | collective-permute-done | bytes 614432 | tf_op jit(solution)/shard_map/ppermute | solution.py:844
  77.7 11.4 %collective-permute-done.5.refs_3_ = bf16[4,120,640]{2,1,0:T(8,128)(2,1)} collective-permute-done((bf16[4,120,640]{2,1,0:T(8,128)(2,1)S(1)}, bf16[4,120,640]{2,1,0:T(8,128)(2,1)}, u32[]{:S(2)}, u32[]{:S(2)}) %collective-permute-start.5) | collective-permute-done | bytes 614432 | tf_op jit(solution)/shard_map/ppermute | solution.py:844
  89.1 18.3 %all-to-all-done = bf16[4,240,1024]{2,1,0:T(8,128)(2,1)S(1)} async-done(((bf16[4,240,1024]{2,1,0:T(8,128)(2,1)}), bf16[4,240,1024]{2,1,0:T(8,128)(2,1)S(1)}, u32[]{:S(2)}, u32[]{:S(2)}) %all-to-all-start) | async-done | bytes 1966112 | tf_op jit(solution)/shard_map/all_to_all | solution.py:867
  108.8 3.7 all-to-all-start.1
  119.6 17.9 %project.1 = (bf16[960,768]{1,0:T(8,128)(2,1)}, f32[1,768]{1,0:T(1,128)}, bf16[960,768]{1,0:T(8,128)(2,1)}, bf16[320,1024]{1,0:T(8,128)(2,1)}, bf16[5,1024,64]{2...) custom-call(s32[3]{0:T(128)} %pad_add_fusion.who, ...), custom_call_target="tpu_custom_call" | custom-call | flops 130744320 | bytes 552960 | tf_op jit(solution)/shard_map/project/pallas_call | solution.py:199
  138.2 26.2 %attend.1 = (bf16[960,768]{1,0:T(8,128)(2,1)}, f32[5,3,768]{2,1,0:T(4,128)}) custom-call(bf16[960,768]{1,0:T(8,128)(2,1)} %get-tuple-element.196.q, bf16[5,1024,64]{2,1,0:T(8,128)(2,1)} %get-tuple-element.197.k, bf16[320,1024]{1,0:T(8,128)(2,1)} %get-tuple-element.198.vt, s32[1,768]{1,0:T(1,128)} %max.18.limit), custom_call_target="tpu_custom_call" | custom-call | flops 377487360 | bytes 92160 | tf_op jit(solution)/shard_map/attend/pallas_call | solution.py:291
  164.4 8.0 %merge.1 = (f32[960,768]{1,0:T(8,128)}, f32[1,768]{1,0:T(1,128)}, bf16[960,768]{1,0:T(8,128)(2,1)}) custom-call(bf16[960,768]{1,0:T(8,128)(2,1)} %get-tuple-element.200.mixed, bf16[960,768]{1,0:T(8,128)(2,1)} %get-tuple-element.201.picked.refs_4_, f32[960,1]{1,0:T(8,128)} %copy.114.gain.refs_8_, bf16[4,960,640]{2,1,0:T(8,128)(2,1)} %get-tuple-element.202.w), custom_call_target="tpu_custom_call" | custom-call | flops 44236800 | bytes 476160 | tf_op jit(solution)/shard_map/merge/pallas_call | solution.py:410
  172.4 8.5 %all-to-all-done.1 = bf16[4,240,768]{2,1,0:T(8,128)(2,1)S(1)} async-done(((bf16[4,240,768]{2,1,0:T(8,128)(2,1)}), bf16[4,240,768]{2,1,0:T(8,128)(2,1)S(1)}, u32[]{:S(2)}, u32[]{:S(2)}) %all-to-all-start.1) | async-done | bytes 1474592 | tf_op jit(solution)/shard_map/all_to_all | solution.py:867
  182.5 2.5 all-gather.3.cloned.1.call-done
  184.9 22.4 %ffn.1 = (bf16[4,640,768]{2,1,0:T(8,128)(2,1)}, bf16[4,640,768]{2,1,0:T(8,128)(2,1)}, bf16[4,640,768]{2,1,0:T(8,128)(2,1)}, bf16[960,768]{1,0:T(8,128)(2,1)}, bf16[960,768]{1,0:T(8,128)(2,1)}) custom-call(s32[3]{0:T(128)} %pad_add_fusion.who, bf16[960,768]{1,0:T(8,128)(2,1)} %get-tuple-element.208.normed, f32[960,768]{1,0:T(8,128)} %get-tuple-element.209.branch.refs_2_, ...), custom_call_target="tpu_custom_call" | custom-call | flops 353894400 | bytes 645120 | tf_op jit(solution)/shard_map/ffn/pallas_call | solution.py:530
  207.4 9.4 %down_grad.1 = (bf16[4,4,128,640]{3,2,1,0:T(8,128)(2,1)}, bf16[4,4,128,640]{3,2,1,0:T(8,128)(2,1)}) custom-call(s32[3]{0:T(128)} %pad_add_fusion.who, bf16[960,768]{1,0:T(8,128)(2,1)} %multiply_convert_fusion.grad_ffn, bf16[4,640,768]{2,1,0:T(8,128)(2,1)} %get-tuple-element.210.active), custom_call_target="tpu_custom_call" | custom-call | flops 117964800 | bytes 460800 | tf_op jit(solution)/shard_map/down_grad/pallas_call | solution.py:570
  217.1 20.5 %ffn_back.2 = (bf16[4,2,240,640]{3,2,1,0:T(8,128)(2,1)}, bf16[4,2,240,640]{3,2,1,0:T(8,128)(2,1)}, f32[960,768]{1,0:T(8,128)}) custom-call(s32[3]{0:T(128)} %pad_add_fusion.who, bf16[960,768]{1,0:T(8,128)(2,1)} %get-tuple-element.208.normed, bf16[960,768]{1,0:T(8,128)(2,1)} %multiply_convert_fusion.grad_ffn, ...), custom_call_target="tpu_custom_call" | custom-call | flops 294912000 | bytes 660480 | tf_op jit(solution)/shard_map/ffn_back/pallas_call | solution.py:658
  237.6 3.5 fusion.7
  241.3 26.3 %ffn_back.3 = (bf16[4,2,240,640]{3,2,1,0:T(8,128)(2,1)}, bf16[4,2,240,640]{3,2,1,0:T(8,128)(2,1)}, bf16[960,768]{1,0:T(8,128)(2,1)}, bf16[960,768]{1,0:T(8,128)(...) custom-call(s32[3]{0:T(128)} %pad_add_fusion.who, bf16[960,768]{1,0:T(8,128)(2,1)} %get-tuple-element.208.normed, ...), custom_call_target="tpu_custom_call" | custom-call | flops 294912000 | bytes 660480 | tf_op jit(solution)/shard_map/ffn_back/pallas_call | solution.py:658
  267.7 3.3 fusion.15
  271.2 3.7 all-to-all-start.2
  280.0 8.8 %merge_back.1 = (bf16[4,960,240]{2,1,0:T(8,128)(2,1)}, bf16[960,768]{1,0:T(8,128)(2,1)}) custom-call(bf16[960,768]{1,0:T(8,128)(2,1)} %get-tuple-element.200.mixed, bf16[960,768]{1,0:T(8,128)(2,1)} %get-tuple-element.256.grad, bf16[4,960,640]{2,1,0:T(8,128)(2,1)} %get-tuple-element.202.w), custom_call_target="tpu_custom_call" | custom-call | flops 88473600 | bytes 445440 | tf_op jit(solution)/shard_map/merge_back/pallas_call | solution.py:704
  288.8 4.0 collective-permute-done.18
  294.3 13.1 %collective-permute-done.19 = bf16[4,128,640]{2,1,0:T(8,128)(2,1)S(1)} collective-permute-done((bf16[4,128,640]{2,1,0:T(8,128)(2,1)}, bf16[4,128,640]{2,1,0:T(8,128)(2,1)S(1)}, u32[]{:S(2)}, u32[]{:S(2)}) %collective-permute-start.19) | collective-permute-done | bytes 655392 | tf_op jit(solution)/shard_map/ppermute | solution.py:844
  310.5 3.3 fusion.19
  315.1 2.4 collective-permute-start.22
  317.5 2.6 collective-permute-done.14
  320.1 3.8 collective-permute-start.23
  323.9 29.9 %attend_back.1 = (bf16[960,768]{1,0:T(8,128)(2,1)}, bf16[320,1024]{1,0:T(8,128)(2,1)}, bf16[320,1024]{1,0:T(8,128)(2,1)}) custom-call(bf16[960,768]{1,0:T(8,128)(2,1)} %get-tuple-element.196.q, bf16[5,1024,64]{2,1,0:T(8,128)(2,1)} %get-tuple-element.197.k, bf16[320,1024]{1,0:T(8,128)(2,1)} %get-tuple-element.248.kt, ...), custom_call_target="tpu_custom_call" | custom-call | flops 943718400 | bytes 184320 | tf_op jit(solution)/shard_map/attend_back/pallas_call | solution.py:358
  354.0 2.3 add_convert_fusion.11
  359.9 12.7 %mixing_grad.1 = (bf16[4,4,128,640]{3,2,1,0:T(8,128)(2,1)}, bf16[4,4,128,640]{3,2,1,0:T(8,128)(2,1)}, bf16[4,400,1024]{2,1,0:T(8,128)(2,1)}) custom-call(s32[3]{0:T(128)} %pad_add_fusion.who, bf16[960,1024]{1,0:T(8,128)(2,1)} %bitcast.100, s32[1,1024]{1,0:T(1,128)} %copy-done.24, f32[960,1]{1,0:T(8,128)} %copy.112.gain, ...), custom_call_target="tpu_custom_call" | custom-call | flops 145489920 | bytes 307200 | tf_op jit(solution)/shard_map/mixing_grad/pallas_call | solution.py:759
  373.2 11.3 %collective-permute-done.25 = bf16[2,240,640]{2,1,0:T(8,128)(2,1)S(1)} collective-permute-done((bf16[2,240,640]{2,1,0:T(8,128)(2,1)S(1)}, bf16[2,240,640]{2,1,0:T(8,128)(2,1)S(1)}, u32[]{:S(2)}, u32[]{:S(2)}) %collective-permute-start.25) | collective-permute-done | bytes 614432 | tf_op jit(solution)/shard_map/ppermute | solution.py:844
  390.1 6.1 %scatter_tokens.1 = f32[4,240,1024]{2,1,0:T(8,128)} custom-call(f32[4,240,1024]{2,1,0:T(8,128)} %base.1, bf16[4,240,768]{2,1,0:T(8,128)(2,1)} %copy-done.2, s32[4,1,1024]{2,1,0:T(1,128)} %broadcast_in_dim.75.rank), custom_call_target="tpu_custom_call" | custom-call | flops 47185920 | bytes 307200 | tf_op jit(solution)/shard_map/scatter_tokens/pallas_call | solution.py:106
  397.7 1.7 broadcast_select_fusion.4
  399.6 1.8 collective-permute-start.37
  401.4 12.7 %project_back.1 = (bf16[960,1024]{1,0:T(8,128)(2,1)}, f32[960,1]{1,0:T(8,128)}) custom-call(bf16[960,1024]{1,0:T(8,128)(2,1)} %bitcast.101, s32[1,1024]{1,0:T(1,128)} %copy-done.24, f32[960,1]{1,0:T(8,128)} %copy.112.gain, bf16[4,400,1024]{2,1,0:T(8,128)(2,1)} %get-tuple-element.309.grads, bf16[960,768]{1,0:T(8,128)(2,1)} %get-tuple-element.310.rest, ...), custom_call_target="tpu_custom_call" | custom-call | flops 145489920 | bytes 460800 | tf_op jit(solution)/shard_map/project_back/pallas_call | solution.py:812
  417.2 3.8 all-to-all-start.3
  421.8 4.3 fusion.11
  431.9 12.0 %collective-permute-done.30 = bf16[4,128,640]{2,1,0:T(8,128)(2,1)} collective-permute-done((bf16[4,128,640]{2,1,0:T(8,128)(2,1)}, bf16[4,128,640]{2,1,0:T(8,128)(2,1)}, u32[]{:S(2)}, u32[]{:S(2)}) %collective-permute-start.30) | collective-permute-done | bytes 655392 | tf_op jit(solution)/shard_map/ppermute | solution.py:844
  443.9 13.0 %collective-permute-done.31 = bf16[4,128,640]{2,1,0:T(8,128)(2,1)} collective-permute-done((bf16[4,128,640]{2,1,0:T(8,128)(2,1)}, bf16[4,128,640]{2,1,0:T(8,128)(2,1)}, u32[]{:S(2)}, u32[]{:S(2)}) %collective-permute-start.31) | collective-permute-done | bytes 655392 | tf_op jit(solution)/shard_map/ppermute | solution.py:844
  458.4 1.8 add_convert_fusion
  460.2 1.8 collective-permute-start.33
  462.0 2.4 collective-permute-start.34
  465.6 7.4 %collective-permute-done.33 = bf16[128,640]{1,0:T(8,128)(2,1)S(1)} collective-permute-done((bf16[128,640]{1,0:T(8,128)(2,1)S(1)}, bf16[128,640]{1,0:T(8,128)(2,1)S(1)}, u32[]{:S(2)}, u32[]{:S(2)}) %collective-permute-start.33) | collective-permute-done | bytes 163872 | tf_op jit(solution)/shard_map/ppermute | solution.py:844
  473.0 8.4 %collective-permute-done.34 = bf16[128,640]{1,0:T(8,128)(2,1)S(1)} collective-permute-done((bf16[128,640]{1,0:T(8,128)(2,1)S(1)}, bf16[128,640]{1,0:T(8,128)(2,1)S(1)}, u32[]{:S(2)}, u32[]{:S(2)}) %collective-permute-start.34) | collective-permute-done | bytes 163872 | tf_op jit(solution)/shard_map/ppermute | solution.py:844
  484.3 5.0 %convert_add_fusion = f32[4,240,1024]{2,1,0:T(8,128)} fusion(f32[4,240,1024]{2,1,0:T(8,128)} %values.1, bf16[4,240,1024]{2,1,0:T(8,128)(2,1)S(1)} %all-to-all-done.3), kind=kLoop, calls=%fused_computation.6 | loop fusion | flops 1966080 | bytes 9830400 | tf_op jit(solution)/shard_map/add | solution.py:1059
  (202 shorter events, 65.6 us)
Async XLA Ops:
  7.2 177.7 %all-gather.3.cloned.1.call-start = ((), (), s32[]{:S(2)}) async-start(), calls=%async_computation.4 | async-start | bytes 15544320 | tf_op jit(solution)/shard_map/all_gather | solution.py:919
  8.4 1.6 collective-permute-start.11
  9.9 1.4 collective-permute-start.10
  12.7 10.0 %collective-permute-start = (bf16[120,640]{1,0:T(8,128)(2,1)S(1)}, bf16[120,640]{1,0:T(8,128)(2,1)S(1)}, u32[]{:S(2)}, u32[]{:S(2)}) collective-permute-start(bf16[120,640]{1,0:T(8,128)(2,1)S(1)} %pad_maximum_fusion.1), channel_id=1, source_target_pairs={{0,1},{1,0},{2,3},{3,2},{4,5},{5,4},{6,7},{7,6},{8,9},{9,8},{10,11... | collective-permute-start | bytes 460808 | tf_op jit(solution)/shard_map/ppermute | solution.py:844
  15.5 17.4 %collective-permute-start.1 = (bf16[120,640]{1,0:T(8,128)(2,1)S(1)}, bf16[120,640]{1,0:T(8,128)(2,1)S(1)}, u32[]{:S(2)}, u32[]{:S(2)}) collective-permute-start(bf16[120,640]{1,0:T(8,128)(2,1)S(1)} %pad_maximum_fusion.1), channel_id=1, source_target_pairs={{0,2},{1,3},{2,0},{3,1},{4,6},{5,7},{6,4},{7,5},{8,10},{9,11},{10,... | collective-permute-start | bytes 460808 | tf_op jit(solution)/shard_map/ppermute | solution.py:844
  18.1 14.8 %collective-permute-start.2 = (bf16[120,640]{1,0:T(8,128)(2,1)S(1)}, bf16[120,640]{1,0:T(8,128)(2,1)S(1)}, u32[]{:S(2)}, u32[]{:S(2)}) collective-permute-start(bf16[120,640]{1,0:T(8,128)(2,1)S(1)} %pad_maximum_fusion.1), channel_id=1, source_target_pairs={{0,3},{1,2},{2,1},{3,0},{4,7},{5,6},{6,5},{7,4},{8,11},{9,10},{10,... | collective-permute-start | bytes 460808 | tf_op jit(solution)/shard_map/ppermute | solution.py:844
  21.8 24.0 %copy-start.32 = (s32[4]{0:T(128)S(1)}, s32[4]{0:T(128)}, u32[]{:S(2)}) copy-start(s32[4]{0:T(128)} %param.17) | copy-start | bytes 52
  32.9 74.5 %all-to-all-start = ((bf16[4,240,1024]{2,1,0:T(8,128)(2,1)}), bf16[4,240,1024]{2,1,0:T(8,128)(2,1)S(1)}, u32[]{:S(2)}, u32[]{:S(2)}) async-start(bf16[4,240,1024]{2,1,0:T(8,128)(2,1)} %convert_element_type.374), calls=%async_computation | async-start | bytes 3932160 | tf_op jit(solution)/shard_map/all_to_all | solution.py:867
  49.4 28.3 %collective-permute-start.3 = (bf16[4,120,640]{2,1,0:T(8,128)(2,1)S(1)}, bf16[4,120,640]{2,1,0:T(8,128)(2,1)S(1)}, u32[]{:S(2)}, u32[]{:S(2)}) collective-permute-start(bf16[4,120,640]{2,1,0:T(8,128)(2,1)S(1)} %pad_maximum_fusion.refs_0_), channel_id=1, source_target_pairs={{0,8},{4,12},{8,0},{12,4},{16,24},{20,28},{24,16},{28,20},{1,9},{5... | collective-permute-start | bytes 1843208 | tf_op jit(solution)/shard_map/ppermute | solution.py:844
  51.0 26.8 %collective-permute-start.4 = (bf16[4,120,640]{2,1,0:T(8,128)(2,1)S(1)}, bf16[4,120,640]{2,1,0:T(8,128)(2,1)}, u32[]{:S(2)}, u32[]{:S(2)}) collective-permute-start(bf16[4,120,640]{2,1,0:T(8,128)(2,1)S(1)} %pad_maximum_fusion.refs_0_), channel_id=1, source_target_pairs={{0,16},{4,20},{8,24},{12,28},{16,0},{20,4},{24,8},{28,12},{1,17},{... | collective-permute-start | bytes 1843208 | tf_op jit(solution)/shard_map/ppermute | solution.py:844
  52.5 36.6 %collective-permute-start.5 = (bf16[4,120,640]{2,1,0:T(8,128)(2,1)S(1)}, bf16[4,120,640]{2,1,0:T(8,128)(2,1)}, u32[]{:S(2)}, u32[]{:S(2)}) collective-permute-start(bf16[4,120,640]{2,1,0:T(8,128)(2,1)S(1)} %pad_maximum_fusion.refs_0_), channel_id=1, source_target_pairs={{0,24},{4,28},{8,16},{12,20},{16,8},{20,12},{24,0},{28,4},{1,25},{... | collective-permute-start | bytes 1843208 | tf_op jit(solution)/shard_map/ppermute | solution.py:844
  77.7 29.7 %copy-start.16 = (bf16[4,120,640]{2,1,0:T(8,128)(2,1)}, bf16[4,120,640]{2,1,0:T(8,128)(2,1)S(1)}, u32[]{:S(2)}) copy-start(bf16[4,120,640]{2,1,0:T(8,128)(2,1)S(1)} %collective-permute-done.3.refs_1_) | copy-start | bytes 1843204
  108.8 72.1 %all-to-all-start.1 = ((bf16[4,240,768]{2,1,0:T(8,128)(2,1)}), bf16[4,240,768]{2,1,0:T(8,128)(2,1)S(1)}, u32[]{:S(2)}, u32[]{:S(2)}) async-start(bf16[4,240,768]{2,1,0:T(8,128)(2,1)} %gather_tokens.1), calls=%async_computation.1 | async-start | bytes 2949120 | tf_op jit(solution)/shard_map/all_to_all | solution.py:867
  112.5 5.9 %collective-permute-start.6 = (bf16[4,120,640]{2,1,0:T(8,128)(2,1)}, bf16[4,120,640]{2,1,0:T(8,128)(2,1)S(1)}, u32[]{:S(2)}, u32[]{:S(2)}) collective-permute-start(bf16[4,120,640]{2,1,0:T(8,128)(2,1)} %copy-done.7), channel_id=1, source_target_pairs={{0,4},{4,0},{8,12},{12,8},{16,20},{20,16},{24,28},{28,24},{1,5},{5... | collective-permute-start | bytes 1843208 | tf_op jit(solution)/shard_map/ppermute | solution.py:838
  112.6 5.8 %collective-permute-start.7 = (bf16[4,120,640]{2,1,0:T(8,128)(2,1)}, bf16[4,120,640]{2,1,0:T(8,128)(2,1)S(1)}, u32[]{:S(2)}, u32[]{:S(2)}) collective-permute-start(bf16[4,120,640]{2,1,0:T(8,128)(2,1)} %copy-done.16), channel_id=1, source_target_pairs={{0,4},{4,0},{8,12},{12,8},{16,20},{20,16},{24,28},{28,24},{1,5},{5... | collective-permute-start | bytes 1843208 | tf_op jit(solution)/shard_map/ppermute | solution.py:838
  113.1 5.3 %collective-permute-start.8 = (bf16[4,120,640]{2,1,0:T(8,128)(2,1)}, bf16[4,120,640]{2,1,0:T(8,128)(2,1)S(1)}, u32[]{:S(2)}, u32[]{:S(2)}) collective-permute-start(bf16[4,120,640]{2,1,0:T(8,128)(2,1)} %collective-permute-done.4.refs_2_), channel_id=1, source_target_pairs={{0,4},{4,0},{8,12},{12,8},{16,20},{20,16},{24,28},{28,24},{1,5},{5... | collective-permute-start | bytes 1843208 | tf_op jit(solution)/shard_map/ppermute | solution.py:838
  113.2 5.2 %collective-permute-start.9 = (bf16[4,120,640]{2,1,0:T(8,128)(2,1)}, bf16[4,120,640]{2,1,0:T(8,128)(2,1)}, u32[]{:S(2)}, u32[]{:S(2)}) collective-permute-start(bf16[4,120,640]{2,1,0:T(8,128)(2,1)} %collective-permute-done.5.refs_3_), channel_id=1, source_target_pairs={{0,4},{4,0},{8,12},{12,8},{16,20},{20,16},{24,28},{28,24},{1,5},{5... | collective-permute-start | bytes 1843208 | tf_op jit(solution)/shard_map/ppermute | solution.py:838
  216.8 20.7 %collective-permute-start.12 = (bf16[4,4,128,640]{3,2,1,0:T(8,128)(2,1)}, bf16[4,4,128,640]{3,2,1,0:T(8,128)(2,1)}, u32[]{:S(2)}, u32[]{:S(2)}) collective-permute-start(bf16[4,4,128,640]{3,2,1,0:T(8,128)(2,1)} %get-tuple-element.215), channel_id=1, source_target_pairs={{0,4},{4,0},{8,12},{12,8},{16,20},{20,16},{24,28},{28,24},{1,5},{5... | collective-permute-start | bytes 7864328 | tf_op jit(solution)/shard_map/ppermute | solution.py:838
  241.1 26.6 %collective-permute-start.13 = (bf16[4,2,240,640]{3,2,1,0:T(8,128)(2,1)}, bf16[4,2,240,640]{3,2,1,0:T(8,128)(2,1)}, u32[]{:S(2)}, u32[]{:S(2)}) collective-permute-start(bf16[4,2,240,640]{3,2,1,0:T(8,128)(2,1)} %get-tuple-element.227), channel_id=1, source_target_pairs={{0,4},{4,0},{8,12},{12,8},{16,20},{20,16},{24,28},{28,24},{1,5},{5... | collective-permute-start | bytes 7372808 | tf_op jit(solution)/shard_map/ppermute | solution.py:838
  241.3 26.4 %copy-start.6 = (bf16[4,2,240,640]{3,2,1,0:T(8,128)(2,1)S(1)}, bf16[4,2,240,640]{3,2,1,0:T(8,128)(2,1)}, u32[]{:S(2)}) copy-start(bf16[4,2,240,640]{3,2,1,0:T(8,128)(2,1)} %get-tuple-element.238) | copy-start | bytes 7372804
  271.0 37.8 %collective-permute-start.17 = (bf16[4,2,240,640]{3,2,1,0:T(8,128)(2,1)}, bf16[4,2,240,640]{3,2,1,0:T(8,128)(2,1)}, u32[]{:S(2)}, u32[]{:S(2)}) collective-permute-start(bf16[4,2,240,640]{3,2,1,0:T(8,128)(2,1)} %get-tuple-element.251), channel_id=1, source_target_pairs={{0,4},{4,0},{8,12},{12,8},{16,20},{20,16},{24,28},{28,24},{1,5},{5... | collective-permute-start | bytes 7372808 | tf_op jit(solution)/shard_map/ppermute | solution.py:838
  271.2 82.6 %all-to-all-start.2 = ((bf16[4,240,768]{2,1,0:T(8,128)(2,1)}), bf16[4,240,768]{2,1,0:T(8,128)(2,1)S(1)}, u32[]{:S(2)}, u32[]{:S(2)}) async-start(bf16[4,240,768]{2,1,0:T(8,128)(2,1)} %bitcast.107), calls=%async_computation.2 | async-start | bytes 2949120 | tf_op jit(solution)/shard_map/all_to_all | solution.py:874
  275.0 17.8 %collective-permute-start.18 = (bf16[4,128,640]{2,1,0:T(8,128)(2,1)}, bf16[4,128,640]{2,1,0:T(8,128)(2,1)S(1)}, u32[]{:S(2)}, u32[]{:S(2)}) collective-permute-start(bf16[4,128,640]{2,1,0:T(8,128)(2,1)} %get-tuple-element.253), channel_id=1, source_target_pairs={{0,8},{4,12},{8,0},{12,4},{16,24},{20,28},{24,16},{28,20},{1,9},{5... | collective-permute-start | bytes 1966088 | tf_op jit(solution)/shard_map/ppermute | solution.py:844
  276.5 30.9 %collective-permute-start.19 = (bf16[4,128,640]{2,1,0:T(8,128)(2,1)}, bf16[4,128,640]{2,1,0:T(8,128)(2,1)S(1)}, u32[]{:S(2)}, u32[]{:S(2)}) collective-permute-start(bf16[4,128,640]{2,1,0:T(8,128)(2,1)} %get-tuple-element.254), channel_id=1, source_target_pairs={{0,16},{4,20},{8,24},{12,28},{16,0},{20,4},{24,8},{28,12},{1,17},{... | collective-permute-start | bytes 1966088 | tf_op jit(solution)/shard_map/ppermute | solution.py:844
  278.0 30.8 %collective-permute-start.20 = (bf16[4,128,640]{2,1,0:T(8,128)(2,1)}, bf16[4,128,640]{2,1,0:T(8,128)(2,1)S(1)}, u32[]{:S(2)}, u32[]{:S(2)}) collective-permute-start(bf16[4,128,640]{2,1,0:T(8,128)(2,1)} %get-tuple-element.255), channel_id=1, source_target_pairs={{0,24},{4,28},{8,16},{12,20},{16,8},{20,12},{24,0},{28,4},{1,25},{... | collective-permute-start | bytes 1966088 | tf_op jit(solution)/shard_map/ppermute | solution.py:844
  278.5 41.5 %collective-permute-start.14 = (bf16[2,240,640]{2,1,0:T(8,128)(2,1)}, bf16[2,240,640]{2,1,0:T(8,128)(2,1)S(1)}, u32[]{:S(2)}, u32[]{:S(2)}) collective-permute-start(bf16[2,240,640]{2,1,0:T(8,128)(2,1)} %get-tuple-element.244), channel_id=1, source_target_pairs={{0,8},{4,12},{8,0},{12,4},{16,24},{20,28},{24,16},{28,20},{1,9},{5... | collective-permute-start | bytes 1843208 | tf_op jit(solution)/shard_map/ppermute | solution.py:844
  292.8 61.1 %collective-permute-start.15 = (bf16[2,240,640]{2,1,0:T(8,128)(2,1)}, bf16[2,240,640]{2,1,0:T(8,128)(2,1)}, u32[]{:S(2)}, u32[]{:S(2)}) collective-permute-start(bf16[2,240,640]{2,1,0:T(8,128)(2,1)} %get-tuple-element.245), channel_id=1, source_target_pairs={{0,16},{4,20},{8,24},{12,28},{16,0},{20,4},{24,8},{28,12},{1,17},{... | collective-permute-start | bytes 1843208 | tf_op jit(solution)/shard_map/ppermute | solution.py:844
  307.4 46.4 %collective-permute-start.16 = (bf16[2,240,640]{2,1,0:T(8,128)(2,1)}, bf16[2,240,640]{2,1,0:T(8,128)(2,1)}, u32[]{:S(2)}, u32[]{:S(2)}) collective-permute-start(bf16[2,240,640]{2,1,0:T(8,128)(2,1)} %get-tuple-element.246), channel_id=1, source_target_pairs={{0,24},{4,28},{8,16},{12,20},{16,8},{20,12},{24,0},{28,4},{1,25},{... | collective-permute-start | bytes 1843208 | tf_op jit(solution)/shard_map/ppermute | solution.py:844
  313.7 40.1 %collective-permute-start.21 = (bf16[128,640]{1,0:T(8,128)(2,1)S(1)}, bf16[128,640]{1,0:T(8,128)(2,1)}, u32[]{:S(2)}, u32[]{:S(2)}) collective-permute-start(bf16[128,640]{1,0:T(8,128)(2,1)S(1)} %get-tuple-element.276), channel_id=1, source_target_pairs={{0,1},{1,0},{2,3},{3,2},{4,5},{5,4},{6,7},{7,6},{8,9},{9,8},{10,11... | collective-permute-start | bytes 491528 | tf_op jit(solution)/shard_map/ppermute | solution.py:844
  315.1 38.8 %collective-permute-start.22 = (bf16[128,640]{1,0:T(8,128)(2,1)S(1)}, bf16[128,640]{1,0:T(8,128)(2,1)}, u32[]{:S(2)}, u32[]{:S(2)}) collective-permute-start(bf16[128,640]{1,0:T(8,128)(2,1)S(1)} %get-tuple-element.277), channel_id=1, source_target_pairs={{0,2},{1,3},{2,0},{3,1},{4,6},{5,7},{6,4},{7,5},{8,10},{9,11},{10,... | collective-permute-start | bytes 491528 | tf_op jit(solution)/shard_map/ppermute | solution.py:844
  320.1 33.8 %collective-permute-start.23 = (bf16[128,640]{1,0:T(8,128)(2,1)S(1)}, bf16[128,640]{1,0:T(8,128)(2,1)}, u32[]{:S(2)}, u32[]{:S(2)}) collective-permute-start(bf16[128,640]{1,0:T(8,128)(2,1)S(1)} %get-tuple-element.278), channel_id=1, source_target_pairs={{0,3},{1,2},{2,1},{3,0},{4,7},{5,6},{6,5},{7,4},{8,11},{9,10},{10,... | collective-permute-start | bytes 491528 | tf_op jit(solution)/shard_map/ppermute | solution.py:844
  356.3 16.9 %collective-permute-start.24 = (bf16[2,240,640]{2,1,0:T(8,128)(2,1)S(1)}, bf16[2,240,640]{2,1,0:T(8,128)(2,1)S(1)}, u32[]{:S(2)}, u32[]{:S(2)}) collective-permute-start(bf16[2,240,640]{2,1,0:T(8,128)(2,1)S(1)} %copy-done.13), channel_id=1, source_target_pairs={{0,8},{4,12},{8,0},{12,4},{16,24},{20,28},{24,16},{28,20},{1,9},{5... | collective-permute-start | bytes 1843208 | tf_op jit(solution)/shard_map/ppermute | solution.py:844
  357.9 26.6 %collective-permute-start.25 = (bf16[2,240,640]{2,1,0:T(8,128)(2,1)S(1)}, bf16[2,240,640]{2,1,0:T(8,128)(2,1)S(1)}, u32[]{:S(2)}, u32[]{:S(2)}) collective-permute-start(bf16[2,240,640]{2,1,0:T(8,128)(2,1)S(1)} %copy-done.12), channel_id=1, source_target_pairs={{0,16},{4,20},{8,24},{12,28},{16,0},{20,4},{24,8},{28,12},{1,17},{... | collective-permute-start | bytes 1843208 | tf_op jit(solution)/shard_map/ppermute | solution.py:844
  359.3 25.2 %collective-permute-start.26 = (bf16[2,240,640]{2,1,0:T(8,128)(2,1)S(1)}, bf16[2,240,640]{2,1,0:T(8,128)(2,1)S(1)}, u32[]{:S(2)}, u32[]{:S(2)}) collective-permute-start(bf16[2,240,640]{2,1,0:T(8,128)(2,1)S(1)} %copy-done.10), channel_id=1, source_target_pairs={{0,24},{4,28},{8,16},{12,20},{16,8},{20,12},{24,0},{28,4},{1,25},{... | collective-permute-start | bytes 1843208 | tf_op jit(solution)/shard_map/ppermute | solution.py:844
  359.9 12.7 %collective-permute-start.27 = (bf16[240,640]{1,0:T(8,128)(2,1)S(1)}, bf16[240,640]{1,0:T(8,128)(2,1)S(1)}, u32[]{:S(2)}, u32[]{:S(2)}) collective-permute-start(bf16[240,640]{1,0:T(8,128)(2,1)S(1)} %get-tuple-element.293), channel_id=1, source_target_pairs={{0,1},{1,0},{2,3},{3,2},{4,5},{5,4},{6,7},{7,6},{8,9},{9,8},{10,11... | collective-permute-start | bytes 921608 | tf_op jit(solution)/shard_map/ppermute | solution.py:844
  385.7 28.5 %collective-permute-start.28 = (bf16[4,4,128,640]{3,2,1,0:T(8,128)(2,1)}, bf16[4,4,128,640]{3,2,1,0:T(8,128)(2,1)S(1)}, u32[]{:S(2)}, u32[]{:S(2)}) collective-permute-start(bf16[4,4,128,640]{3,2,1,0:T(8,128)(2,1)} %get-tuple-element.308), channel_id=1, source_target_pairs={{0,4},{4,0},{8,12},{12,8},{16,20},{20,16},{24,28},{28,24},{1,5},{5... | collective-permute-start | bytes 7864328 | tf_op jit(solution)/shard_map/ppermute | solution.py:838
  388.2 7.9 %collective-permute-start.39 = (bf16[128,320]{1,0:T(8,128)(2,1)}, bf16[128,320]{1,0:T(8,128)(2,1)}, u32[]{:S(2)}, u32[]{:S(2)}) collective-permute-start(bf16[128,320]{1,0:T(8,128)(2,1)} %select_convert_fusion.1), channel_id=1, source_target_pairs={{0,4},{4,0},{8,12},{12,8},{16,20},{20,16},{24,28},{28,24},{1,5},{5... | collective-permute-start | bytes 245768 | tf_op jit(solution)/shard_map/ppermute | solution.py:838
  399.4 31.0 %collective-permute-start.36 = (bf16[240,640]{1,0:T(8,128)(2,1)}, bf16[240,640]{1,0:T(8,128)(2,1)}, u32[]{:S(2)}, u32[]{:S(2)}) collective-permute-start(bf16[240,640]{1,0:T(8,128)(2,1)} %get-tuple-element.328), channel_id=1, source_target_pairs={{0,2},{1,3},{2,0},{3,1},{4,6},{5,7},{6,4},{7,5},{8,10},{9,11},{10,... | collective-permute-start | bytes 921608 | tf_op jit(solution)/shard_map/ppermute | solution.py:844
  399.6 30.8 %collective-permute-start.37 = (bf16[240,640]{1,0:T(8,128)(2,1)}, bf16[240,640]{1,0:T(8,128)(2,1)}, u32[]{:S(2)}, u32[]{:S(2)}) collective-permute-start(bf16[240,640]{1,0:T(8,128)(2,1)} %get-tuple-element.329), channel_id=1, source_target_pairs={{0,3},{1,2},{2,1},{3,0},{4,7},{5,6},{6,5},{7,4},{8,11},{9,10},{10,... | collective-permute-start | bytes 921608 | tf_op jit(solution)/shard_map/ppermute | solution.py:844
  416.4 4.6 collective-permute-start.29
  417.2 67.1 %all-to-all-start.3 = ((bf16[4,240,1024]{2,1,0:T(8,128)(2,1)}), bf16[4,240,1024]{2,1,0:T(8,128)(2,1)S(1)}, u32[]{:S(2)}, u32[]{:S(2)}) async-start(bf16[4,240,1024]{2,1,0:T(8,128)(2,1)} %bitcast.104), calls=%async_computation.3 | async-start | bytes 3932160 | tf_op jit(solution)/shard_map/all_to_all | solution.py:874
  426.0 17.8 %collective-permute-start.30 = (bf16[4,128,640]{2,1,0:T(8,128)(2,1)}, bf16[4,128,640]{2,1,0:T(8,128)(2,1)}, u32[]{:S(2)}, u32[]{:S(2)}) collective-permute-start(bf16[4,128,640]{2,1,0:T(8,128)(2,1)} %get-tuple-element.410), channel_id=1, source_target_pairs={{0,8},{4,12},{8,0},{12,4},{16,24},{20,28},{24,16},{28,20},{1,9},{5... | collective-permute-start | bytes 1966088 | tf_op jit(solution)/shard_map/ppermute | solution.py:844
  427.1 29.7 %collective-permute-start.31 = (bf16[4,128,640]{2,1,0:T(8,128)(2,1)}, bf16[4,128,640]{2,1,0:T(8,128)(2,1)}, u32[]{:S(2)}, u32[]{:S(2)}) collective-permute-start(bf16[4,128,640]{2,1,0:T(8,128)(2,1)} %get-tuple-element.409), channel_id=1, source_target_pairs={{0,16},{4,20},{8,24},{12,28},{16,0},{20,4},{24,8},{28,12},{1,17},{... | collective-permute-start | bytes 1966088 | tf_op jit(solution)/shard_map/ppermute | solution.py:844
  428.1 30.3 %collective-permute-start.32 = (bf16[4,128,640]{2,1,0:T(8,128)(2,1)}, bf16[4,128,640]{2,1,0:T(8,128)(2,1)}, u32[]{:S(2)}, u32[]{:S(2)}) collective-permute-start(bf16[4,128,640]{2,1,0:T(8,128)(2,1)} %get-tuple-element.408), channel_id=1, source_target_pairs={{0,24},{4,28},{8,16},{12,20},{16,8},{20,12},{24,0},{28,4},{1,25},{... | collective-permute-start | bytes 1966088 | tf_op jit(solution)/shard_map/ppermute | solution.py:844
  431.8 32.9 %collective-permute-start.38 = (bf16[120,640]{1,0:T(8,128)(2,1)S(1)}, bf16[120,640]{1,0:T(8,128)(2,1)S(1)}, u32[]{:S(2)}, u32[]{:S(2)}) collective-permute-start(bf16[120,640]{1,0:T(8,128)(2,1)S(1)} %select_convert_fusion), channel_id=1, source_target_pairs={{0,4},{4,0},{8,12},{12,8},{16,20},{20,16},{24,28},{28,24},{1,5},{5... | collective-permute-start | bytes 460808 | tf_op jit(solution)/shard_map/ppermute | solution.py:838
  460.2 12.8 %collective-permute-start.33 = (bf16[128,640]{1,0:T(8,128)(2,1)S(1)}, bf16[128,640]{1,0:T(8,128)(2,1)S(1)}, u32[]{:S(2)}, u32[]{:S(2)}) collective-permute-start(bf16[128,640]{1,0:T(8,128)(2,1)S(1)} %get-tuple-element.426), channel_id=1, source_target_pairs={{0,1},{1,0},{2,3},{3,2},{4,5},{5,4},{6,7},{7,6},{8,9},{9,8},{10,11... | collective-permute-start | bytes 491528 | tf_op jit(solution)/shard_map/ppermute | solution.py:844
  462.0 19.4 %collective-permute-start.34 = (bf16[128,640]{1,0:T(8,128)(2,1)S(1)}, bf16[128,640]{1,0:T(8,128)(2,1)S(1)}, u32[]{:S(2)}, u32[]{:S(2)}) collective-permute-start(bf16[128,640]{1,0:T(8,128)(2,1)S(1)} %get-tuple-element.428), channel_id=1, source_target_pairs={{0,2},{1,3},{2,0},{3,1},{4,6},{5,7},{6,4},{7,5},{8,10},{9,11},{10,... | collective-permute-start | bytes 491528 | tf_op jit(solution)/shard_map/ppermute | solution.py:844
  464.4 17.0 %collective-permute-start.35 = (bf16[128,640]{1,0:T(8,128)(2,1)S(1)}, bf16[128,640]{1,0:T(8,128)(2,1)S(1)}, u32[]{:S(2)}, u32[]{:S(2)}) collective-permute-start(bf16[128,640]{1,0:T(8,128)(2,1)S(1)} %get-tuple-element.427), channel_id=1, source_target_pairs={{0,3},{1,2},{2,1},{3,0},{4,7},{5,6},{6,5},{7,4},{8,11},{9,10},{10,... | collective-permute-start | bytes 491528 | tf_op jit(solution)/shard_map/ppermute | solution.py:844
  (30 other events, 184.6 us)
Sparse Core Ops, SparseCore 0:
  12.5 172.4 all-gather.2

commit v3 on v2

--- a/solution.py
+++ b/solution.py
@@ -347,34 +347,38 @@
     gv_out[...] = gv[...].T.astype(BF)
 
 
-def attend_back(q, k, kt, v, limit, total, grad, mixed, tables_k, tables_q):
-    width, picks = q.shape
+def attend_back(first, count, q, k, kt, v, limit, total, grad, mixed, tables_k, tables_q):
+    picks = q.shape[1]
     length = k.shape[1]
     part = GROUP * HD
     half = HD // 2
-    wide = pl.BlockSpec((part, picks), lambda i: (i, 0))
-    tall = pl.BlockSpec((1, length, HD), lambda i: (i, 0, 0))
-    flat = pl.BlockSpec((HD, length), lambda i: (i, 0))
+    wide = pl.BlockSpec((part, picks), lambda i: (first + i, 0))
+    tall = pl.BlockSpec((1, length, HD), lambda i: (first + i, 0, 0))
+    flat = pl.BlockSpec((HD, length), lambda i: (first + i, 0))
     return pl.pallas_call(
         attend_back_body,
-        grid=(KVH,),
+        grid=(count,),
         in_specs=[
             wide, tall, flat, tall, whole((1, picks)),
-            pl.BlockSpec((1, GROUP, picks), lambda i: (i, 0, 0)),
+            pl.BlockSpec((1, GROUP, picks), lambda i: (first + i, 0, 0)),
             wide, wide,
             whole((half, length)), whole((half, length)),
             whole((half, picks)), whole((half, picks)),
         ],
-        out_specs=[wide, flat, flat],
+        out_specs=[
+            pl.BlockSpec((part, picks), lambda i: (i, 0)),
+            pl.BlockSpec((HD, length), lambda i: (i, 0)),
+            pl.BlockSpec((HD, length), lambda i: (i, 0)),
+        ],
         out_shape=[
-            struct((width, picks), BF),
-            struct((KVH * HD, length), BF),
-            struct((KVH * HD, length), BF),
+            struct((count * part, picks), BF),
+            struct((count * HD, length), BF),
+            struct((count * HD, length), BF),
         ],
         scratch_shapes=[pltpu.VMEM((length, HD), F32), pltpu.VMEM((length, HD), F32)],
         compiler_params=params(),
         cost_estimate=cost(
-            40 * width * length * picks, 8 * width * picks, H * length * picks
+            40 * count * part * length * picks, 8 * count * part * picks, count * GROUP * length * picks
         ),
         name="attend_back",
     )(q, k, kt, v, limit, total, grad, mixed, *tables_k, *tables_q)
@@ -437,13 +441,14 @@
     return -(-part // 32) * 16
 
 
-def ffn_weights(who, first, sources, w_gate, w_up, w_down, done):
+def ffn_weights(who, first, blocks, sources, w_gate, w_up, w_down, done):
     step, steps = pl.program_id(0), pl.num_programs(0)
     slot = lax.rem(step, 2)
     width = w_gate.shape[1]
 
     def copies(step, at):
-        block = (step + first) ^ who[0]
+        turn = blocks - 1 - first - step
+        block = turn ^ who[0]
         if len(sources) == 2:
             some = [
                 (sources[0].at[0, block], w_gate.at[at]),
@@ -458,12 +463,13 @@
             some = []
             for i in range(pairs):
                 place = slice(i * height, (i + 1) * height)
-                some.append((source.at[i, 0, block, :height], w_gate.at[at, place]))
-                some.append((source.at[i, 1, block, :height], w_up.at[at, place]))
+                some.append((source.at[i, 0, turn, :height], w_gate.at[at, place]))
+                some.append((source.at[i, 1, turn, :height], w_up.at[at, place]))
             for c in range(columns):
-                top = slice(c * part, c * part + half)
+                begin = pl.multiple_of((c ^ who[0]) * part, 16)
+                top = pl.ds(begin, half)
                 some.append((source.at[block, 0, c, height : height + half], w_down.at[at, top]))
-                end = slice(c * part + half, (c + 1) * part)
+                end = pl.ds(pl.multiple_of(begin + half, 16), part - half)
                 rest = slice(height + 2 * half - part, height + half)
                 some.append((source.at[block, 1, c, rest], w_down.at[at, end]))
         return [
@@ -498,7 +504,7 @@
     sources, refs = refs[:many], refs[many:]
     gate_out, up_out, active_out, delta, both_out, forward, *buffers = refs
     w_gate, w_up, w_down, _ = buffers
-    slot = ffn_weights(who, 0, sources, *buffers)
+    slot = ffn_weights(who, 0, pl.num_programs(0), sources, *buffers)
 
     @pl.when(pl.program_id(0) == 0)
     def _():
@@ -565,7 +571,7 @@
     here = pairs // blocks
     tile = (columns, down_half(width // columns), hidden // here)
     block = pl.BlockSpec(
-        (here,) + tile, lambda i, who: (i ^ who[0] ^ lax.div(who[1], here), 0, 0, 0)
+        (here,) + tile, lambda i, who: ((blocks - 1 - i) ^ who[0] ^ lax.div(who[1], here), 0, 0, 0)
     )
     return pl.pallas_call(
         down_grad_body,
@@ -585,7 +591,7 @@
     )(who, grad_ffn, active)
 
 
-def ffn_back_body(first, last, many, who, normed, grad_ffn, gate_in, up_in, *refs):
+def ffn_back_body(first, blocks, last, many, who, normed, grad_ffn, gate_in, up_in, *refs):
     sources, refs = refs[:many], refs[many:]
     if first:
         carried, refs = refs[0], refs[1:]
@@ -594,7 +600,7 @@
     keep_pair, send_pair, refs = refs[0], refs[1], refs[2:]
     outs, backward, buffers = refs[:-5], refs[-5], refs[-4:]
     w_gate, w_up, w_down, _ = buffers
-    slot = ffn_weights(who, first, sources, *buffers)
+    slot = ffn_weights(who, first, blocks, sources, *buffers)
     width = normed.shape[0]
     even = who[2] == 0
 
@@ -656,7 +662,7 @@
     extra = ([carried] if first else []) + (list(tail) if last else [])
     extra_specs = ([full] if first else []) + ([full] * 4 + [row] * 2 + [column] * 2 if last else [])
     return pl.pallas_call(
-        functools.partial(ffn_back_body, first, last, len(sources)),
+        functools.partial(ffn_back_body, first, gate.shape[0], last, len(sources)),
         grid_spec=pltpu.PrefetchScalarGridSpec(
             num_scalar_prefetch=1,
             grid=(count,),
@@ -714,29 +720,101 @@
     )(mixed, grad, w)
 
 
-def mixing_grad_body(
-    who, x, rank, gain, gq, gk, gv, gw_out,
-    keep, send, grads_out,
-    normed, gq_full,
-):
+def project_back_body(x, rank, gain, *refs):
+    gq, gk, gv, refs = refs[:2], refs[2:4], refs[4:6], refs[6:]
+    rest, w, out, grads_out, gain_out, gq_full, gkv_full, total = refs
     step = pl.program_id(0)
     width = x.shape[0]
     q_part = width // pl.num_programs(0)
     kv_part = KVH * HD // pl.num_programs(0)
+
+    @pl.when(step == 0)
+    def _():
+        chosen = pick_rows(rank[...], gq[0].shape[1])
+        at = 0
+        for piece in gq:
+            gq_full[at : at + piece.shape[0]] = dot_nn(piece[...], chosen).astype(BF)
+            at += piece.shape[0]
+        for i, pieces in enumerate((gk, gv)):
+            at = 0
+            for piece in pieces:
+                gkv_full[i, at : at + piece.shape[0]] = piece[...]
+                at += piece.shape[0]
+        total[...] = jnp.zeros_like(total)
+
+    q_rows = pl.ds(pl.multiple_of(step * q_part, 8), q_part)
+    kv_rows = pl.ds(pl.multiple_of(step * kv_part, 8), kv_part)
+    grads = jnp.concatenate(
+        [gq_full[q_rows, :], gkv_full[0, kv_rows, :], gkv_full[1, kv_rows, :]], axis=0
+    )
+    grads_out[0] = grads
+    total[...] += dot_nn(w[0, :, : grads.shape[0]], grads)
+
+    @pl.when(step == pl.num_programs(0) - 1)
+    def _():
+        full = x[...].astype(F32)
+        inv = lax.rsqrt(jnp.sum(full * full, axis=0, keepdims=True) / width + EPSILON)
+        grad_norm = total[...]
+        gain_out[...] = jnp.sum(grad_norm * full * inv, axis=1, keepdims=True)
+        unit = grad_norm * gain[...]
+        along = jnp.sum(unit * full, axis=0, keepdims=True) / width
+        chosen = pick_rows(rank[...], rest.shape[1])
+        out[...] = (
+            inv * unit - full * (inv * inv * inv * along) + dot_nn(rest[...], chosen)
+        ).astype(BF)
+
+
+def project_back(x, rank_row, gain, gq, gk, gv, rest, w):
+    width, length = x.shape
+    picks = rest.shape[1]
+    blocks = w.shape[0]
+    kv = KVH * HD
+    part = (width + 2 * kv) // blocks
+    return pl.pallas_call(
+        project_back_body,
+        grid=(blocks,),
+        in_specs=[
+            whole((width, length)),
+            whole((1, length)),
+            whole((width, 1)),
+            *(whole(piece.shape) for piece in (*gq, *gk, *gv)),
+            whole((width, picks)),
+            pl.BlockSpec((1,) + w.shape[1:], lambda i: (i, 0, 0)),
+        ],
+        out_specs=[
+            whole((width, length)),
+            pl.BlockSpec((1, part, length), lambda i: (i, 0, 0)),
+            whole((width, 1)),
+        ],
+        out_shape=[
+            struct((width, length), BF),
+            struct((blocks, part, length), BF),
+            struct((width, 1), F32),
+        ],
+        scratch_shapes=[
+            pltpu.VMEM((width, length), BF),
+            pltpu.VMEM((2, kv, length), BF),
+            pltpu.VMEM((width, length), F32),
+        ],
+        compiler_params=params(),
+        cost_estimate=cost(
+            2 * width * length * (2 * picks + blocks * part), 10 * x.size + 2 * w.size
+        ),
+        name="project_back",
+    )(x, rank_row, gain, *gq, *gk, *gv, rest, w)
+
+
+def mixing_grad_body(who, x, gain, grads, gw_out, keep, send, normed):
+    width = x.shape[0]
     even = who[2] == 0
 
-    @pl.when(step == 0)
+    @pl.when(pl.program_id(0) == 0)
     def _():
         full = x[...].astype(F32)
         inverse = lax.rsqrt(jnp.sum(full * full, axis=0, keepdims=True) / width + EPSILON)
         normed[...] = (full * inverse * gain[...]).astype(BF)
-        gq_full[...] = dot_nn(gq[...], pick_rows(rank[...], gq.shape[1])).astype(BF)
-
-    q_rows = pl.ds(pl.multiple_of(step * q_part, 8), q_part)
-    kv_rows = pl.ds(pl.multiple_of(step * kv_part, 8), kv_part)
-    grads = jnp.concatenate([gq_full[q_rows, :], gk[kv_rows, :], gv[kv_rows, :]], axis=0)
-    grads_out[0] = grads
-    value = dot_nt(normed[...], grads)
+
+    value = dot_nt(normed[...], grads[0])
     value = jnp.concatenate([value, gw_out[0].astype(F32)], axis=1)
     pairs = keep.shape[0]
     rows = width // (2 * pairs)
@@ -747,12 +825,10 @@
         send[pair ^ who[1], 0, :rows] = jnp.where(even, high, low).astype(BF)
 
 
-def mixing_grad(who, x, rank_row, gain, gq, gk, gv, gw_out, pairs):
+def mixing_grad(who, x, gain, grads, gw_out, pairs):
     width, length = x.shape
-    picks = gq.shape[1]
-    blocks, _, out_part = gw_out.shape
-    kv = KVH * HD
-    part = (width + 2 * kv) // blocks
+    blocks, part, _ = grads.shape
+    out_part = gw_out.shape[2]
     rows = width // (2 * pairs) + VECTOR_ROWS
     split = pl.BlockSpec((pairs, 1, rows, part + out_part), lambda i, who: (0, i ^ who[0], 0, 0))
     split_shape = struct((pairs, blocks, rows, part + out_part), BF)
@@ -763,70 +839,18 @@
             grid=(blocks,),
             in_specs=[
                 whole((width, length)),
-                whole((1, length)),
                 whole((width, 1)),
-                whole((width, picks)),
-                whole((kv, length)),
-                whole((kv, length)),
+                pl.BlockSpec((1, part, length), lambda i, who: (i, 0, 0)),
                 pl.BlockSpec((1, width, out_part), lambda i, who: (i, 0, 0)),
             ],
-            out_specs=[split, split, pl.BlockSpec((1, part, length), lambda i, who: (i, 0, 0))],
-            scratch_shapes=[pltpu.VMEM((width, length), BF), pltpu.VMEM((width, length), BF)],
+            out_specs=[split, split],
+            scratch_shapes=[pltpu.VMEM((width, length), BF)],
         ),
-        out_shape=[split_shape, split_shape, struct((blocks, part, length), BF)],
+        out_shape=[split_shape, split_shape],
         compiler_params=params(),
-        cost_estimate=cost(2 * width * length * (picks + width + 2 * kv), 10 * x.size),
+        cost_estimate=cost(2 * width * length * blocks * part, 10 * x.size),
         name="mixing_grad",
-    )(who, x, rank_row, gain, gq, gk, gv, gw_out)
-
-
-def project_back_body(x, rank, gain, grads, rest, w, out, gain_out, total):
-    step = pl.program_id(0)
-    width = x.shape[0]
-    part = grads.shape[1]
-
-    @pl.when(step == 0)
-    def _():
-        total[...] = jnp.zeros_like(total)
-
-    total[...] += dot_nn(w[0, :, :part], grads[0])
-
-    @pl.when(step == pl.num_programs(0) - 1)
-    def _():
-        full = x[...].astype(F32)
-        inv = lax.rsqrt(jnp.sum(full * full, axis=0, keepdims=True) / width + EPSILON)
-        grad_norm = total[...]
-        gain_out[...] = jnp.sum(grad_norm * full * inv, axis=1, keepdims=True)
-        unit = grad_norm * gain[...]
-        along = jnp.sum(unit * full, axis=0, keepdims=True) / width
-        chosen = pick_rows(rank[...], rest.shape[1])
-        out[...] = (
-            inv * unit - full * (inv * inv * inv * along) + dot_nn(rest[...], chosen)
-        ).astype(BF)
-
-
-def project_back(x, rank_row, gain, grads, rest, w):
-    width, length = x.shape
-    picks = rest.shape[1]
-    blocks, part, _ = grads.shape
-    return pl.pallas_call(
-        project_back_body,
-        grid=(blocks,),
-        in_specs=[
-            whole((width, length)),
-            whole((1, length)),
-            whole((width, 1)),
-            pl.BlockSpec((1, part, length), lambda i: (i, 0, 0)),
-            whole((width, picks)),
-            pl.BlockSpec((1,) + w.shape[1:], lambda i: (i, 0, 0)),
-        ],
-        out_specs=[whole((width, length)), whole((width, 1))],
-        out_shape=[struct((width, length), BF), struct((width, 1), F32)],
-        scratch_shapes=[pltpu.VMEM((width, length), F32)],
-        compiler_params=params(),
-        cost_estimate=cost(2 * width * length * (picks + blocks * part), 10 * x.size + 2 * w.size),
-        name="project_back",
-    )(x, rank_row, gain, grads, rest, w)
+    )(who, x, gain, grads, gw_out)
 
 
 def hold(*values):
@@ -854,6 +878,16 @@
 
 def add_up(values):
     return sum(value.astype(F32) for value in values)
+
+
+def pack(first, second):
+    if first.shape[1] == second.shape[1]:
+        return [jnp.concatenate([first, second], axis=0)]
+    return [first, second]
+
+
+def unpack(values, rows):
+    return (values[0][:rows], values[0][rows:]) if len(values) == 1 else tuple(values)
 
 
 def pair_up(keep, got):
@@ -915,10 +949,17 @@
     mine, other = jnp.where(even, low, high), swap(jnp.where(even, high, low))
     down = jnp.concatenate([jnp.where(even, mine, other), jnp.where(even, other, mine)], axis=1)
     mixing = jnp.concatenate([w_query, w_key, w_value, w_out], axis=1)
+    mixing, pair, down = hold(collect(mixing, "col", range(col_count)), pair, down)
+    mixing, x = jnp.stack(mixing), resid.astype(BF)
     if aligned:
-        sources = lax.all_gather(jnp.concatenate([pair, down], axis=0), ("row", "col"), axis=0)
-        sources = (sources.reshape((pairs, 2, col_count) + sources.shape[1:]),)
+        sources = jnp.concatenate([pair, down], axis=0)
+        sources, mixing, x = hold(
+            collect(sources, "col", range(col_count)), collect(mixing, "row", range(pairs)), x
+        )
+        sources = lax.all_gather(jnp.stack(sources), "row", axis=0)
+        sources = (sources.reshape((pairs, 2) + sources.shape[1:]),)
     else:
+        mixing, x = hold(collect(mixing, "row", range(pairs)), x)
         pair_all = lax.all_gather(pair, ("row", "col"), axis=0)
         pair_all = pair_all.reshape(pairs, 2, col_count, 2 * rows, hidden).transpose(1, 2, 0, 3, 4)
         down_all = lax.all_gather(down, ("row", "col"), axis=0)
@@ -930,9 +971,6 @@
             pair_all.reshape(2, col_count, width, hidden),
             down_all.transpose(0, 2, 3, 1, 4).reshape(col_count, width, hidden),
         )
-    mixing, x = hold(collect(mixing, "col", range(col_count)), resid.astype(BF))
-    mixing = jnp.stack(mixing)
-
     every = jnp.arange(length, dtype=jnp.int32)
     chosen_of = chosen[:, 0][slot]
     selected = jnp.any(every[None, :, None] == chosen_of[:, None, :], axis=2)
@@ -949,11 +987,10 @@
     gain_one, gain_two, router = norm1_gain[:, None], norm2_gain[:, None], router[:, None]
     cot = gather_tokens(cotangent, ranks[:, :, None], picks)
 
-    x, mixing, cot, limit, tables_k, tables_q = hold(
-        to_owner(x), collect(mixing, "row", range(pairs)), cot, limit, tables_k, tables_q
+    x, mixing_other, mixing, cot, limit, tables_k, tables_q = hold(
+        to_owner(x), [swap(piece) for piece in mixing], mixing, cot, limit, tables_k, tables_q
     )
     cot = to_owner(cot)
-    mixing_other, mixing = hold([swap(piece) for piece in mixing], mixing)
     if aligned:
         mixing = mixing + mixing_other
     else:
@@ -986,42 +1023,75 @@
     )
     sum_down = pair_up(keep_down, got_down)
     sum_down, send_low, keep_low, carried = hold(sum_down, send_low, keep_low, carried)
-    sum_down = spread(sum_down, "row")
-    got_low, (keep_high, send_high, grad_attn, rest, gain_two_grad, router_grad), keep_low = hold(
-        swap(send_low), ffn_back(who, half, half, True, *back_args, carried, tail), keep_low
+    (
+        got_low, sum_down,
+        (keep_high, send_high, grad_attn, rest, gain_two_grad, router_grad), keep_low,
+    ) = hold(
+        swap(send_low),
+        spread(sum_down, "row"),
+        ffn_back(who, half, half, True, *back_args, carried, tail),
+        keep_low,
     )
     sum_low = pair_up(by_pairs(keep_low), by_pairs(got_low))
-    sum_low, send_high, keep_high, grad_attn = hold(sum_low, send_high, keep_high, grad_attn)
-    got_high, sum_down, (gw_out, grad_mixed), keep_high = hold(
-        swap(send_high), sum_down, merge_back(mixed, grad_attn, mixing), keep_high
+    sum_down = list(add_up(sum_down).astype(BF))
+    sum_low, sum_down, send_high, keep_high, grad_attn = hold(
+        sum_low, sum_down, send_high, keep_high, grad_attn
+    )
+    sum_low = spread(sum_low, "row")
+    got_high, (gw_out, grad_mixed), keep_high = hold(
+        swap(send_high), merge_back(mixed, grad_attn, mixing), keep_high
     )
     sum_high = pair_up(by_pairs(keep_high), by_pairs(got_high))
-    sum_down = list(add_up(sum_down).astype(BF))
-    sum_high, sum_down, grad_mixed = hold(sum_high, sum_down, grad_mixed)
-    sum_low, delta, (gq, gk, gv), sum_high, sum_down = hold(
-        spread(sum_low, "row"),
-        delta,
-        attend_back(q, k, kt, v, limit, mass, grad_mixed, mixed, tables_k, tables_q),
+    sum_high, grad_mixed = hold(sum_high, grad_mixed)
+    heads = (q, k, kt, v, limit, mass, grad_mixed, mixed, tables_k, tables_q)
+    most = (KVH + 1) // 2
+    sum_low, delta, one, sum_high = hold(
+        sum_low, delta, attend_back(0, most, *heads), sum_high
+    )
+    far = [
+        pack(value, sum_down[-1 - i])
+        for i, value in enumerate(add_up(sum_low).astype(BF))
+    ]
+    far, one, grad_mixed = hold(far, one, grad_mixed)
+    far = [
+        [partner(value, "col", col_count - 1 - i) for value in values]
+        for i, values in enumerate(far)
+    ]
+    heads = heads[:6] + (grad_mixed,) + heads[7:]
+    sum_high = spread(sum_high, "row")
+    (two,) = hold(attend_back(most, KVH - most, *heads))
+    gq, gk, gv = zip(one, two)
+    far, sum_high, (back, grads, gain_one_grad) = hold(
+        far,
         sum_high,
-        spread(sum_down, "col"),
-    )
-    sum_low = list(add_up(sum_low).astype(BF))
-    sum_down = add_up(sum_down)
-    sum_low, sum_high, gq = hold(sum_low, sum_high, gq)
-    sum_high, sum_low, (keep_mixing, send_mixing, grads) = hold(
-        spread(sum_high, "row"),
-        spread(sum_low, "col"),
-        mixing_grad(who, x, rank[None, :], gain_one, gq, gk, gv, gw_out, pairs),
-    )
-    sum_high = list(add_up(sum_high).astype(BF))
-    sum_high, send_mixing, keep_mixing, grads = hold(sum_high, send_mixing, keep_mixing, grads)
-    got_mixing, (back, gain_one_grad), keep_mixing = hold(
-        swap(send_mixing),
-        project_back(x, rank[None, :], gain_one, grads, rest, mixing),
-        keep_mixing,
-    )
+        project_back(x, rank[None, :], gain_one, gq, gk, gv, rest, mixing),
+    )
+    *near, sum_pair = add_up(sum_high).astype(BF)
+    near = [pack(value, sum_down[half - 1 - i]) for i, value in enumerate(near)]
+    vectors = jnp.concatenate([gain_one_grad, gain_two_grad, router_grad], axis=1).T.astype(BF)
+    vectors = vectors.reshape(3, col_count, part).transpose(1, 0, 2)
+    vectors = vectors[jnp.arange(col_count) ^ column]
+    vectors = jnp.pad(vectors, ((0, 0), (0, VECTOR_ROWS - 3), (0, mixing_part - part)))
+    vectors = jnp.broadcast_to(vectors[None], (pairs,) + vectors.shape)
+    near, back, grads, vectors = hold(near, back, grads, vectors)
     back = from_owner(back, sequences)
-    sum_pair = add_up(sum_low + [partner(value, "col", half + k) for k, value in enumerate(sum_high)])
+    near, gw_mixing = hold(
+        [
+            [partner(value, "col", half - 1 - i) for value in values]
+            for i, values in enumerate(near)
+        ],
+        mixing_grad(who, x, gain_one, grads, gw_out, pairs),
+    )
+    keep_mixing, send_mixing = (
+        lax.dynamic_update_slice(value, vectors, (0, 0, rows, 0)) for value in gw_mixing
+    )
+    got_mixing, block_out, keep_mixing = hold(
+        swap(send_mixing), scatter_tokens(resid, delta, ranks[:, None, :]), keep_mixing
+    )
+    sum_mixing = add_up(spread(pair_up(keep_mixing, got_mixing), "row")).astype(BF)
+    parts = [unpack(values, 2 * rows) for values in near + far]
+    sum_pair = add_up([sum_pair] + [first for first, _ in parts])
+    sum_down = add_up([sum_down[0]] + [second for _, second in parts])
 
     lanes = sum_down.shape[1] // 2
     first, second = sum_down[:, :lanes], sum_down[:, lanes:]
@@ -1030,20 +1100,6 @@
     top, end = jnp.where(even, mine, other), jnp.where(even, other, mine)
     gw_down = jnp.concatenate([top, end[2 * down_rows_kept - part :]], axis=0).T
 
-    vectors = jnp.concatenate([gain_one_grad, gain_two_grad, router_grad], axis=1).T.astype(BF)
-    vectors = vectors.reshape(3, col_count, part).transpose(1, 0, 2)
-    vectors = vectors[jnp.arange(col_count) ^ column]
-    vectors = jnp.pad(vectors, ((0, 0), (0, VECTOR_ROWS - 3), (0, mixing_part - part)))
-    other = swap(vectors)
-    vectors = jnp.broadcast_to(vectors[None], (pairs,) + vectors.shape)
-    other = jnp.broadcast_to(other[None], vectors.shape)
-    keep_mixing = lax.dynamic_update_slice(keep_mixing, vectors, (0, 0, rows, 0))
-    got_mixing = lax.dynamic_update_slice(got_mixing, other, (0, 0, rows, 0))
-    sum_mixing = pair_up(keep_mixing, got_mixing)
-    sum_mixing, block_out = hold(
-        spread(sum_mixing, "row"), scatter_tokens(resid, delta, ranks[:, None, :])
-    )
-    sum_mixing = add_up(sum_mixing).astype(BF)
     gw_mixing = add_up(spread(list(sum_mixing), "col"))
 
     sum_pair = sum_pair.reshape(2, rows, hidden)

time: 504 us -> 481 us (0.954)
  waiting for transfers between devices: 141 us -> 112 us
  starting transfers between devices: 64.7 us -> 70.7 us
    ppermute x27, waiting for transfers between devices: 110 us -> 81.9 us  [partner(): return lax.ppermute(value, axis, [(i, i ^ far) for i in range(count)])]
    ppermute x27, starting transfers between devices: 37.9 us -> 51.3 us  [partner(): return lax.ppermute(value, axis, [(i, i ^ far) for i in range(count)])]
    all_to_all x2, starting transfers between devices: 16 us -> 7.51 us  [to_owner(): lax.all_to_all(value, 'col', split_axis=0, concat_axis=1, tiled=True)]
    pallas_call x3 -> x4, Pallas kernels: 76.8 us -> 79 us  [the longest x2 46.4 us: ffn_back(): pl.pallas_call(functools.partial(ffn_back_body, first, gate.shape[0], las...]
  transfers between devices with their start and end apart: 45 -> 44, of which waited for: 18 -> 16; matrix products, arithmetic and copies ran while one was open for 9% -> 9% of each run, Pallas kernels for 35% -> 38%
where the time goes in v3:
time: 481 us; the launch traced here: 474 us
  Pallas kernels  210 us (44%)
  waiting for transfers between devices  112 us (23%)
  starting transfers between devices  70.7 us (15%)
  other arithmetic  44.4 us (9%)
  local copies, waits for them, and re-layouts  21.1 us (4%)
  between operations  15.9 us (3%)
    ppermute x27, waiting for transfers between devices, partner(): return lax.ppermute(value, axis, [(i, i ^ far) for i in range(count)])  81.9 us
    ppermute x27, starting transfers between devices, partner(): return lax.ppermute(value, axis, [(i, i ^ far) for i in range(count)])  51.3 us
    pallas_call x2, Pallas kernels, ffn_back(): pl.pallas_call(functools.partial(ffn_back_body, first, gate.shape[0], las...  46.4 us
    pallas_call x2, Pallas kernels, attend_back(): pl.pallas_call(attend_back_body, grid=(count,), in_specs=[wide, tall, fla...  32.6 us
    all_to_all x2, waiting for transfers between devices, to_owner(): lax.all_to_all(value, 'col', split_axis=0, concat_axis=1, tiled=True)  28.3 us
    pallas_call x1, Pallas kernels, attend(): pl.pallas_call(attend_body, grid=(KVH,), in_specs=[pl.BlockSpec((part, pi...  26.1 us
    pallas_call x1, Pallas kernels, ffn(): pl.pallas_call(functools.partial(ffn_body, len(sources)), grid_spec=pltpu...  22.5 us
    pallas_call x1, Pallas kernels, project(): pl.pallas_call(project_body, grid_spec=pltpu.PrefetchScalarGridSpec(num_s...  18 us
  transfers between devices with their start and end apart: 44, of which 16 were waited for; matrix products, arithmetic and copies ran while one was open for 9% of the time, Pallas kernels for 38%

profile of v3, /device:TPU:0, one launch (start us, length us, event | category | flops | bytes accessed | tf_op | source)
XLA Modules:
  0.0 474.0 jit_solution(9799083759641269803)
XLA Ops:
  10.0 5.1 %collective-permute-start.2 = (bf16[120,640]{1,0:T(8,128)(2,1)S(1)}, bf16[120,640]{1,0:T(8,128)(2,1)S(1)}, u32[]{:S(2)}, u32[]{:S(2)}) collective-permute-start(bf16[120,640]{1,0:T(8,128)(2,1)S(1)} %pad_maximum_fusion.7), channel_id=1, source_target_pairs={{0,3},{1,2},{2,1},{3,0},{4,7},{5,6},{6,5},{7,4},{8,11},{9,10},{10,... | collective-permute-start | bytes 460808 | tf_op jit(solution)/shard_map/ppermute | solution.py:868
  20.0 8.1 %collective-permute-done.1 = bf16[120,640]{1,0:T(8,128)(2,1)S(1)} collective-permute-done((bf16[120,640]{1,0:T(8,128)(2,1)S(1)}, bf16[120,640]{1,0:T(8,128)(2,1)S(1)}, u32[]{:S(2)}, u32[]{:S(2)}) %collective-permute-start.1) | collective-permute-done | bytes 153632 | tf_op jit(solution)/shard_map/ppermute | solution.py:868
  28.2 2.6 collective-permute-start.7
  30.9 2.5 collective-permute-start.10
  34.5 9.3 %collective-permute-done.7 = bf16[368,640]{1,0:T(8,128)(2,1)S(1)} collective-permute-done((bf16[368,640]{1,0:T(8,128)(2,1)S(1)}, bf16[368,640]{1,0:T(8,128)(2,1)S(1)}, u32[]{:S(2)}, u32[]{:S(2)}) %collective-permute-start.7) | collective-permute-done | bytes 471072 | tf_op jit(solution)/shard_map/ppermute | solution.py:868
  43.8 18.1 %collective-permute-start.5 = (bf16[368,640]{1,0:T(8,128)(2,1)S(1)}, bf16[368,640]{1,0:T(8,128)(2,1)S(1)}, u32[]{:S(2)}, u32[]{:S(2)}) collective-permute-start(bf16[368,640]{1,0:T(8,128)(2,1)S(1)} %constant_dynamic-update-slice_fusion), channel_id=1, source_target_pairs={{0,1},{1,0},{2,3},{3,2},{4,5},{5,4},{6,7},{7,6},{8,9},{9,8},{10,11... | collective-permute-start | bytes 1413128 | tf_op jit(solution)/shard_map/ppermute | solution.py:868
  63.5 5.9 %collective-permute-done.6 = bf16[368,640]{1,0:T(8,128)(2,1)S(1)} collective-permute-done((bf16[368,640]{1,0:T(8,128)(2,1)S(1)}, bf16[368,640]{1,0:T(8,128)(2,1)S(1)}, u32[]{:S(2)}, u32[]{:S(2)}) %collective-permute-start.6) | collective-permute-done | bytes 471072 | tf_op jit(solution)/shard_map/ppermute | solution.py:868
  69.4 8.6 %collective-permute-done.5 = bf16[368,640]{1,0:T(8,128)(2,1)S(1)} collective-permute-done((bf16[368,640]{1,0:T(8,128)(2,1)S(1)}, bf16[368,640]{1,0:T(8,128)(2,1)S(1)}, u32[]{:S(2)}, u32[]{:S(2)}) %collective-permute-start.5) | collective-permute-done | bytes 471072 | tf_op jit(solution)/shard_map/ppermute | solution.py:868
  79.7 1.6 pad_maximum_fusion
  81.4 3.7 all-to-all-start
  90.9 2.0 copy.90.rank
  92.9 5.9 %gather_tokens.1 = bf16[4,240,768]{2,1,0:T(8,128)(2,1)} custom-call(f32[4,240,1024]{2,1,0:T(8,128)} %values.1, s32[4,1024,1]{2,1,0:T(8,128)} %copy.90.rank), custom_call_target="tpu_custom_call" | custom-call | flops 47185920 | bytes 184320 | tf_op jit(solution)/shard_map/gather_tokens/pallas_call | solution.py:83
  101.2 28.3 %all-to-all-done = bf16[4,240,1024]{2,1,0:T(8,128)(2,1)S(1)} async-done(((bf16[4,240,1024]{2,1,0:T(8,128)(2,1)}), bf16[4,240,1024]{2,1,0:T(8,128)(2,1)S(1)}, u32[]{:S(2)}, u32[]{:S(2)}) %all-to-all-start) | async-done | bytes 1966112 | tf_op jit(solution)/shard_map/all_to_all | solution.py:901
  130.7 3.8 all-to-all-start.1
  139.2 18.0 %project.1 = (bf16[960,768]{1,0:T(8,128)(2,1)}, f32[1,768]{1,0:T(1,128)}, bf16[960,768]{1,0:T(8,128)(2,1)}, bf16[320,1024]{1,0:T(8,128)(2,1)}, bf16[5,1024,64]{2...) custom-call(s32[3]{0:T(128)} %pad_add_fusion.who, ...), custom_call_target="tpu_custom_call" | custom-call | flops 130744320 | bytes 552960 | tf_op jit(solution)/shard_map/project/pallas_call | solution.py:199
  157.9 26.1 %attend.1 = (bf16[960,768]{1,0:T(8,128)(2,1)}, f32[5,3,768]{2,1,0:T(4,128)}) custom-call(bf16[960,768]{1,0:T(8,128)(2,1)} %get-tuple-element.198.q, bf16[5,1024,64]{2,1,0:T(8,128)(2,1)} %get-tuple-element.199.k, bf16[320,1024]{1,0:T(8,128)(2,1)} %get-tuple-element.200.vt, s32[1,768]{1,0:T(1,128)} %max.18.limit), custom_call_target="tpu_custom_call" | custom-call | flops 377487360 | bytes 92160 | tf_op jit(solution)/shard_map/attend/pallas_call | solution.py:291
  184.0 8.1 %merge.1 = (f32[960,768]{1,0:T(8,128)}, f32[1,768]{1,0:T(1,128)}, bf16[960,768]{1,0:T(8,128)(2,1)}) custom-call(bf16[960,768]{1,0:T(8,128)(2,1)} %get-tuple-element.202.mixed, bf16[960,768]{1,0:T(8,128)(2,1)} %get-tuple-element.203.picked.refs_4_, f32[960,1]{1,0:T(8,128)} %copy.94.gain.refs_8_, bf16[4,960,640]{2,1,0:T(8,128)(2,1)} %get-tuple-element.204.w.refs_7_), custom_call_target="tpu_custom_call" | custom-call | flops 44236800 | bytes 476160 | tf_op jit(solution)/shard_map/merge/pallas_call | solution.py:414
  193.7 22.5 %ffn.1 = (bf16[4,640,768]{2,1,0:T(8,128)(2,1)}, bf16[4,640,768]{2,1,0:T(8,128)(2,1)}, bf16[4,640,768]{2,1,0:T(8,128)(2,1)}, bf16[960,768]{1,0:T(8,128)(2,1)}, bf16[960,768]{1,0:T(8,128)(2,1)}) custom-call(s32[3]{0:T(128)} %pad_add_fusion.who, bf16[960,768]{1,0:T(8,128)(2,1)} %get-tuple-element.210.normed, f32[960,768]{1,0:T(8,128)} %get-tuple-element.211.branch.refs_2_, ...), custom_call_target="tpu_custom_call" | custom-call | flops 353894400 | bytes 645120 | tf_op jit(solution)/shard_map/ffn/pallas_call | solution.py:536
  216.2 9.4 %down_grad.1 = (bf16[4,4,128,640]{3,2,1,0:T(8,128)(2,1)}, bf16[4,4,128,640]{3,2,1,0:T(8,128)(2,1)}) custom-call(s32[3]{0:T(128)} %pad_add_fusion.who, bf16[960,768]{1,0:T(8,128)(2,1)} %multiply_convert_fusion.grad_ffn, bf16[4,640,768]{2,1,0:T(8,128)(2,1)} %get-tuple-element.216.active), custom_call_target="tpu_custom_call" | custom-call | flops 117964800 | bytes 460800 | tf_op jit(solution)/shard_map/down_grad/pallas_call | solution.py:576
  225.6 20.5 %ffn_back.2 = (bf16[4,2,240,640]{3,2,1,0:T(8,128)(2,1)}, bf16[4,2,240,640]{3,2,1,0:T(8,128)(2,1)}, f32[960,768]{1,0:T(8,128)}) custom-call(s32[3]{0:T(128)} %pad_add_fusion.who, bf16[960,768]{1,0:T(8,128)(2,1)} %get-tuple-element.210.normed, bf16[960,768]{1,0:T(8,128)(2,1)} %multiply_convert_fusion.grad_ffn, ...), custom_call_target="tpu_custom_call" | custom-call | flops 294912000 | bytes 660480 | tf_op jit(solution)/shard_map/ffn_back/pallas_call | solution.py:664
  246.1 3.4 fusion.10
  251.5 1.8 collective-permute-start.18
  253.5 25.9 %ffn_back.3 = (bf16[4,2,240,640]{3,2,1,0:T(8,128)(2,1)}, bf16[4,2,240,640]{3,2,1,0:T(8,128)(2,1)}, bf16[960,768]{1,0:T(8,128)(2,1)}, bf16[960,768]{1,0:T(8,128)(...) custom-call(s32[3]{0:T(128)} %pad_add_fusion.who, bf16[960,768]{1,0:T(8,128)(2,1)} %get-tuple-element.210.normed, ...), custom_call_target="tpu_custom_call" | custom-call | flops 294912000 | bytes 660480 | tf_op jit(solution)/shard_map/ffn_back/pallas_call | solution.py:664
  279.5 2.8 collective-permute-done.18
  282.3 1.8 add_convert_fusion.4
  284.4 1.7 fusion.18
  286.1 5.3 %all-to-all-start.2 = ((bf16[4,240,768]{2,1,0:T(8,128)(2,1)}), bf16[4,240,768]{2,1,0:T(8,128)(2,1)S(1)}, u32[]{:S(2)}, u32[]{:S(2)}) async-start(bf16[4,240,768]{2,1,0:T(8,128)(2,1)} %bitcast.117), calls=%async_computation.2 | async-start | bytes 2949120 | tf_op jit(solution)/shard_map/all_to_all | solution.py:908
  295.0 9.0 %merge_back.1 = (bf16[4,960,240]{2,1,0:T(8,128)(2,1)}, bf16[960,768]{1,0:T(8,128)(2,1)}) custom-call(bf16[960,768]{1,0:T(8,128)(2,1)} %get-tuple-element.202.mixed, bf16[960,768]{1,0:T(8,128)(2,1)} %get-tuple-element.266.grad, bf16[4,960,640]{2,1,0:T(8,128)(2,1)} %get-tuple-element.204.w.refs_7_), custom_call_target="tpu_custom_call" | custom-call | flops 88473600 | bytes 445440 | tf_op jit(solution)/shard_map/merge_back/pallas_call | solution.py:710
  304.0 3.3 fusion.22
  307.3 18.9 %attend_back.2 = (bf16[576,768]{1,0:T(8,128)(2,1)}, bf16[192,1024]{1,0:T(8,128)(2,1)}, bf16[192,1024]{1,0:T(8,128)(2,1)}) custom-call(bf16[960,768]{1,0:T(8,128)(2,1)} %get-tuple-element.198.q, bf16[5,1024,64]{2,1,0:T(8,128)(2,1)} %get-tuple-element.199.k, bf16[320,1024]{1,0:T(8,128)(2,1)} %get-tuple-element.262.kt, ...), custom_call_target="tpu_custom_call" | custom-call | flops 566231040 | bytes 110592 | tf_op jit(solution)/shard_map/attend_back/pallas_call | solution.py:358
  327.0 2.3 add_convert_fusion.10
  334.6 3.1 collective-permute-start.24
  339.0 13.7 %attend_back.3 = (bf16[384,768]{1,0:T(8,128)(2,1)}, bf16[128,1024]{1,0:T(8,128)(2,1)}, bf16[128,1024]{1,0:T(8,128)(2,1)}) custom-call(bf16[960,768]{1,0:T(8,128)(2,1)} %get-tuple-element.198.q, bf16[5,1024,64]{2,1,0:T(8,128)(2,1)} %get-tuple-element.199.k, bf16[320,1024]{1,0:T(8,128)(2,1)} %get-tuple-element.262.kt, ...), custom_call_target="tpu_custom_call" | custom-call | flops 377487360 | bytes 73728 | tf_op jit(solution)/shard_map/attend_back/pallas_call | solution.py:358
  352.7 15.4 %project_back.1 = (bf16[960,1024]{1,0:T(8,128)(2,1)}, bf16[4,400,1024]{2,1,0:T(8,128)(2,1)}, f32[960,1]{1,0:T(8,128)}) custom-call(bf16[960,1024]{1,0:T(8,128)(2,1)} %bitcast.110, s32[1,1024]{1,0:T(1,128)} %copy-done.19, f32[960,1]{1,0:T(8,128)} %copy.92.gain, bf16[576,768]{1,0:T(8,128)(2,1)} %get-tuple-element.296.refs_0_, ...), custom_call_target="tpu_custom_call" | custom-call | flops 192675840 | bytes 460800 | tf_op jit(solution)/shard_map/project_back/pallas_call | solution.py:773
  368.1 8.7 %collective-permute-done.25 = bf16[368,640]{1,0:T(8,128)(2,1)} collective-permute-done((bf16[368,640]{1,0:T(8,128)(2,1)}, bf16[368,640]{1,0:T(8,128)(2,1)}, u32[]{:S(2)}, u32[]{:S(2)}) %collective-permute-start.25) | collective-permute-done | bytes 471072 | tf_op jit(solution)/shard_map/ppermute | solution.py:868
  380.6 10.2 %mixing_grad.1 = (bf16[4,4,128,640]{3,2,1,0:T(8,128)(2,1)}, bf16[4,4,128,640]{3,2,1,0:T(8,128)(2,1)}) custom-call(s32[3]{0:T(128)} %pad_add_fusion.who, bf16[960,1024]{1,0:T(8,128)(2,1)} %bitcast.111, f32[960,1]{1,0:T(8,128)} %copy.92.gain, bf16[4,400,1024]{2,1,0:T(8,128)(2,1)} %get-tuple-element.318.grads, bf16[4,960,240]{2,1,0:T(8,128)(2,1)} %get-tuple-element.319.gw_out), custom_call_target="tpu_custom_call" | custom-call | flops 98304000 | bytes 307200 | tf_op jit(solution)/shard_map/mixing_grad/pallas_call | solution.py:835
  392.6 3.6 all-to-all-start.3
  396.8 6.1 %scatter_tokens.1 = f32[4,240,1024]{2,1,0:T(8,128)} custom-call(f32[4,240,1024]{2,1,0:T(8,128)} %base.1, bf16[4,240,768]{2,1,0:T(8,128)(2,1)} %copy-done.3, s32[4,1,1024]{2,1,0:T(1,128)} %broadcast_in_dim.67.rank), custom_call_target="tpu_custom_call" | custom-call | flops 47185920 | bytes 307200 | tf_op jit(solution)/shard_map/scatter_tokens/pallas_call | solution.py:106
  406.1 3.1 fusion.12
  410.4 1.7 collective-permute-start.33
  414.6 12.4 %collective-permute-done.31 = bf16[4,128,640]{2,1,0:T(8,128)(2,1)} collective-permute-done((bf16[4,128,640]{2,1,0:T(8,128)(2,1)}, bf16[4,128,640]{2,1,0:T(8,128)(2,1)}, u32[]{:S(2)}, u32[]{:S(2)}) %collective-permute-start.31) | collective-permute-done | bytes 655392 | tf_op jit(solution)/shard_map/ppermute | solution.py:868
  427.0 14.7 %collective-permute-done.33 = bf16[4,128,640]{2,1,0:T(8,128)(2,1)} collective-permute-done((bf16[4,128,640]{2,1,0:T(8,128)(2,1)}, bf16[4,128,640]{2,1,0:T(8,128)(2,1)}, u32[]{:S(2)}, u32[]{:S(2)}) %collective-permute-start.33) | collective-permute-done | bytes 655392 | tf_op jit(solution)/shard_map/ppermute | solution.py:868
  443.0 2.3 fusion.4
  446.0 1.7 collective-permute-start.34
  447.7 2.4 collective-permute-start.36
  450.1 5.0 %convert_add_fusion = f32[4,240,1024]{2,1,0:T(8,128)} fusion(f32[4,240,1024]{2,1,0:T(8,128)} %values.1, bf16[4,240,1024]{2,1,0:T(8,128)(2,1)S(1)} %all-to-all-done.3), kind=kLoop, calls=%fused_computation.6 | loop fusion | flops 1966080 | bytes 9830400 | tf_op jit(solution)/shard_map/add | solution.py:1115
  455.2 3.3 collective-permute-done.36
  458.4 5.3 %collective-permute-done.35 = bf16[128,640]{1,0:T(8,128)(2,1)S(1)} collective-permute-done((bf16[128,640]{1,0:T(8,128)(2,1)S(1)}, bf16[128,640]{1,0:T(8,128)(2,1)S(1)}, u32[]{:S(2)}, u32[]{:S(2)}) %collective-permute-start.35) | collective-permute-done | bytes 163872 | tf_op jit(solution)/shard_map/ppermute | solution.py:868
  (193 shorter events, 59.2 us)
Async XLA Ops:
  7.2 12.3 %copy-start.10 = (bf16[120,640]{1,0:T(8,128)(2,1)S(1)}, bf16[120,640]{1,0:T(8,128)(2,1)}, u32[]{:S(2)}) copy-start(bf16[120,640]{1,0:T(8,128)(2,1)} %param.28) | copy-start | bytes 460804
  7.2 186.5 %all-gather.3.cloned.1.call-start = ((), (), s32[]{:S(2)}) async-start(), calls=%async_computation.4 | async-start | bytes 16957440 | tf_op jit(solution)/shard_map/all_gather | solution.py:959
  10.0 10.0 %collective-permute-start.2 = (bf16[120,640]{1,0:T(8,128)(2,1)S(1)}, bf16[120,640]{1,0:T(8,128)(2,1)S(1)}, u32[]{:S(2)}, u32[]{:S(2)}) collective-permute-start(bf16[120,640]{1,0:T(8,128)(2,1)S(1)} %pad_maximum_fusion.7), channel_id=1, source_target_pairs={{0,3},{1,2},{2,1},{3,0},{4,7},{5,6},{6,5},{7,4},{8,11},{9,10},{10,... | collective-permute-start | bytes 460808 | tf_op jit(solution)/shard_map/ppermute | solution.py:868
  15.1 13.0 %collective-permute-start.1 = (bf16[120,640]{1,0:T(8,128)(2,1)S(1)}, bf16[120,640]{1,0:T(8,128)(2,1)S(1)}, u32[]{:S(2)}, u32[]{:S(2)}) collective-permute-start(bf16[120,640]{1,0:T(8,128)(2,1)S(1)} %pad_maximum_fusion.7), channel_id=1, source_target_pairs={{0,2},{1,3},{2,0},{3,1},{4,6},{5,7},{6,4},{7,5},{8,10},{9,11},{10,... | collective-permute-start | bytes 460808 | tf_op jit(solution)/shard_map/ppermute | solution.py:868
  15.1 13.0 %collective-permute-start = (bf16[120,640]{1,0:T(8,128)(2,1)S(1)}, bf16[120,640]{1,0:T(8,128)(2,1)S(1)}, u32[]{:S(2)}, u32[]{:S(2)}) collective-permute-start(bf16[120,640]{1,0:T(8,128)(2,1)S(1)} %pad_maximum_fusion.7), channel_id=1, source_target_pairs={{0,1},{1,0},{2,3},{3,2},{4,5},{5,4},{6,7},{7,6},{8,9},{9,8},{10,11... | collective-permute-start | bytes 460808 | tf_op jit(solution)/shard_map/ppermute | solution.py:868
  16.9 1.6 collective-permute-start.4
  17.9 1.6 collective-permute-start.3
  18.4 43.5 %copy-start.1 = (f32[4,240,1024]{2,1,0:T(8,128)S(1)}, f32[4,240,1024]{2,1,0:T(8,128)}, u32[]{:S(2)}) copy-start(f32[4,240,1024]{2,1,0:T(8,128)} %base.1) | copy-start | bytes 11796484
  28.2 15.6 %collective-permute-start.7 = (bf16[368,640]{1,0:T(8,128)(2,1)S(1)}, bf16[368,640]{1,0:T(8,128)(2,1)S(1)}, u32[]{:S(2)}, u32[]{:S(2)}) collective-permute-start(bf16[368,640]{1,0:T(8,128)(2,1)S(1)} %constant_dynamic-update-slice_fusion), channel_id=1, source_target_pairs={{0,3},{1,2},{2,1},{3,0},{4,7},{5,6},{6,5},{7,4},{8,11},{9,10},{10,... | collective-permute-start | bytes 1413128 | tf_op jit(solution)/shard_map/ppermute | solution.py:868
  30.9 58.3 %copy-start.8 = (bf16[4,120,640]{2,1,0:T(8,128)(2,1)}, bf16[4,120,640]{2,1,0:T(8,128)(2,1)S(1)}, u32[]{:S(2)}) copy-start(bf16[4,120,640]{2,1,0:T(8,128)(2,1)S(1)} %pad_maximum_fusion.1.refs_0_) | copy-start | bytes 1843204
  30.9 47.1 %collective-permute-start.10 = (bf16[4,120,640]{2,1,0:T(8,128)(2,1)S(1)}, bf16[4,120,640]{2,1,0:T(8,128)(2,1)S(1)}, u32[]{:S(2)}, u32[]{:S(2)}) collective-permute-start(bf16[4,120,640]{2,1,0:T(8,128)(2,1)S(1)} %pad_maximum_fusion.1.refs_0_), channel_id=1, source_target_pairs={{0,24},{4,28},{8,16},{12,20},{16,8},{20,12},{24,0},{28,4},{1,25},{... | collective-permute-start | bytes 1843208 | tf_op jit(solution)/shard_map/ppermute | solution.py:868
  33.4 44.6 %collective-permute-start.9 = (bf16[4,120,640]{2,1,0:T(8,128)(2,1)S(1)}, bf16[4,120,640]{2,1,0:T(8,128)(2,1)S(1)}, u32[]{:S(2)}, u32[]{:S(2)}) collective-permute-start(bf16[4,120,640]{2,1,0:T(8,128)(2,1)S(1)} %pad_maximum_fusion.1.refs_0_), channel_id=1, source_target_pairs={{0,16},{4,20},{8,24},{12,28},{16,0},{20,4},{24,8},{28,12},{1,17},{... | collective-permute-start | bytes 1843208 | tf_op jit(solution)/shard_map/ppermute | solution.py:868
  33.9 44.1 %collective-permute-start.8 = (bf16[4,120,640]{2,1,0:T(8,128)(2,1)S(1)}, bf16[4,120,640]{2,1,0:T(8,128)(2,1)S(1)}, u32[]{:S(2)}, u32[]{:S(2)}) collective-permute-start(bf16[4,120,640]{2,1,0:T(8,128)(2,1)S(1)} %pad_maximum_fusion.1.refs_0_), channel_id=1, source_target_pairs={{0,8},{4,12},{8,0},{12,4},{16,24},{20,28},{24,16},{28,20},{1,9},{5... | collective-permute-start | bytes 1843208 | tf_op jit(solution)/shard_map/ppermute | solution.py:868
  34.5 34.9 %collective-permute-start.6 = (bf16[368,640]{1,0:T(8,128)(2,1)S(1)}, bf16[368,640]{1,0:T(8,128)(2,1)S(1)}, u32[]{:S(2)}, u32[]{:S(2)}) collective-permute-start(bf16[368,640]{1,0:T(8,128)(2,1)S(1)} %constant_dynamic-update-slice_fusion), channel_id=1, source_target_pairs={{0,2},{1,3},{2,0},{3,1},{4,6},{5,7},{6,4},{7,5},{8,10},{9,11},{10,... | collective-permute-start | bytes 1413128 | tf_op jit(solution)/shard_map/ppermute | solution.py:868
  43.8 34.2 %collective-permute-start.5 = (bf16[368,640]{1,0:T(8,128)(2,1)S(1)}, bf16[368,640]{1,0:T(8,128)(2,1)S(1)}, u32[]{:S(2)}, u32[]{:S(2)}) collective-permute-start(bf16[368,640]{1,0:T(8,128)(2,1)S(1)} %constant_dynamic-update-slice_fusion), channel_id=1, source_target_pairs={{0,1},{1,0},{2,3},{3,2},{4,5},{5,4},{6,7},{7,6},{8,9},{9,8},{10,11... | collective-permute-start | bytes 1413128 | tf_op jit(solution)/shard_map/ppermute | solution.py:868
  81.4 48.1 %all-to-all-start = ((bf16[4,240,1024]{2,1,0:T(8,128)(2,1)}), bf16[4,240,1024]{2,1,0:T(8,128)(2,1)S(1)}, u32[]{:S(2)}, u32[]{:S(2)}) async-start(bf16[4,240,1024]{2,1,0:T(8,128)(2,1)} %convert_element_type.378), calls=%async_computation | async-start | bytes 3932160 | tf_op jit(solution)/shard_map/all_to_all | solution.py:901
  89.2 11.9 %collective-permute-start.11 = (bf16[4,120,640]{2,1,0:T(8,128)(2,1)S(1)}, bf16[4,120,640]{2,1,0:T(8,128)(2,1)}, u32[]{:S(2)}, u32[]{:S(2)}) collective-permute-start(bf16[4,120,640]{2,1,0:T(8,128)(2,1)S(1)} %pad_maximum_fusion.1.refs_0_), channel_id=1, source_target_pairs={{0,4},{4,0},{8,12},{12,8},{16,20},{20,16},{24,28},{28,24},{1,5},{5... | collective-permute-start | bytes 1843208 | tf_op jit(solution)/shard_map/ppermute | solution.py:862
  89.3 11.9 %collective-permute-start.12 = (bf16[4,120,640]{2,1,0:T(8,128)(2,1)}, bf16[4,120,640]{2,1,0:T(8,128)(2,1)}, u32[]{:S(2)}, u32[]{:S(2)}) collective-permute-start(bf16[4,120,640]{2,1,0:T(8,128)(2,1)} %copy-done.14), channel_id=1, source_target_pairs={{0,4},{4,0},{8,12},{12,8},{16,20},{20,16},{24,28},{28,24},{1,5},{5... | collective-permute-start | bytes 1843208 | tf_op jit(solution)/shard_map/ppermute | solution.py:862
  89.8 11.4 %collective-permute-start.13 = (bf16[4,120,640]{2,1,0:T(8,128)(2,1)}, bf16[4,120,640]{2,1,0:T(8,128)(2,1)}, u32[]{:S(2)}, u32[]{:S(2)}) collective-permute-start(bf16[4,120,640]{2,1,0:T(8,128)(2,1)} %copy-done.13), channel_id=1, source_target_pairs={{0,4},{4,0},{8,12},{12,8},{16,20},{20,16},{24,28},{28,24},{1,5},{5... | collective-permute-start | bytes 1843208 | tf_op jit(solution)/shard_map/ppermute | solution.py:862
  89.9 11.3 %collective-permute-start.14 = (bf16[4,120,640]{2,1,0:T(8,128)(2,1)S(1)}, bf16[4,120,640]{2,1,0:T(8,128)(2,1)}, u32[]{:S(2)}, u32[]{:S(2)}) collective-permute-start(bf16[4,120,640]{2,1,0:T(8,128)(2,1)S(1)} %collective-permute-done.10.refs_3_), channel_id=1, source_target_pairs={{0,4},{4,0},{8,12},{12,8},{16,20},{20,16},{24,28},{28,24},{1,5},{5... | collective-permute-start | bytes 1843208 | tf_op jit(solution)/shard_map/ppermute | solution.py:862
  130.7 61.4 %all-to-all-start.1 = ((bf16[4,240,768]{2,1,0:T(8,128)(2,1)}), bf16[4,240,768]{2,1,0:T(8,128)(2,1)S(1)}, u32[]{:S(2)}, u32[]{:S(2)}) async-start(bf16[4,240,768]{2,1,0:T(8,128)(2,1)} %gather_tokens.1), calls=%async_computation.1 | async-start | bytes 2949120 | tf_op jit(solution)/shard_map/all_to_all | solution.py:901
  225.6 20.5 %collective-permute-start.15 = (bf16[4,4,128,640]{3,2,1,0:T(8,128)(2,1)}, bf16[4,4,128,640]{3,2,1,0:T(8,128)(2,1)}, u32[]{:S(2)}, u32[]{:S(2)}) collective-permute-start(bf16[4,4,128,640]{3,2,1,0:T(8,128)(2,1)} %get-tuple-element.221), channel_id=1, source_target_pairs={{0,4},{4,0},{8,12},{12,8},{16,20},{20,16},{24,28},{28,24},{1,5},{5... | collective-permute-start | bytes 7864328 | tf_op jit(solution)/shard_map/ppermute | solution.py:862
  225.6 20.5 %copy-start.4 = (bf16[4,4,128,640]{3,2,1,0:T(8,128)(2,1)S(1)}, bf16[4,4,128,640]{3,2,1,0:T(8,128)(2,1)}, u32[]{:S(2)}) copy-start(bf16[4,4,128,640]{3,2,1,0:T(8,128)(2,1)} %get-tuple-element.228) | copy-start | bytes 7864324
  249.6 32.8 %collective-permute-start.16 = (bf16[4,2,240,640]{3,2,1,0:T(8,128)(2,1)}, bf16[4,2,240,640]{3,2,1,0:T(8,128)(2,1)S(1)}, u32[]{:S(2)}, u32[]{:S(2)}) collective-permute-start(bf16[4,2,240,640]{3,2,1,0:T(8,128)(2,1)} %get-tuple-element.233), channel_id=1, source_target_pairs={{0,4},{4,0},{8,12},{12,8},{16,20},{20,16},{24,28},{28,24},{1,5},{5... | collective-permute-start | bytes 7372808 | tf_op jit(solution)/shard_map/ppermute | solution.py:862
  250.1 29.4 %collective-permute-start.17 = (bf16[4,128,640]{2,1,0:T(8,128)(2,1)}, bf16[4,128,640]{2,1,0:T(8,128)(2,1)S(1)}, u32[]{:S(2)}, u32[]{:S(2)}) collective-permute-start(bf16[4,128,640]{2,1,0:T(8,128)(2,1)} %get-tuple-element.235), channel_id=1, source_target_pairs={{0,8},{4,12},{8,0},{12,4},{16,24},{20,28},{24,16},{28,20},{1,9},{5... | collective-permute-start | bytes 1966088 | tf_op jit(solution)/shard_map/ppermute | solution.py:868
  251.5 30.8 %collective-permute-start.18 = (bf16[4,128,640]{2,1,0:T(8,128)(2,1)}, bf16[4,128,640]{2,1,0:T(8,128)(2,1)}, u32[]{:S(2)}, u32[]{:S(2)}) collective-permute-start(bf16[4,128,640]{2,1,0:T(8,128)(2,1)} %get-tuple-element.236), channel_id=1, source_target_pairs={{0,16},{4,20},{8,24},{12,28},{16,0},{20,4},{24,8},{28,12},{1,17},{... | collective-permute-start | bytes 1966088 | tf_op jit(solution)/shard_map/ppermute | solution.py:868
  253.3 29.0 %collective-permute-start.19 = (bf16[4,128,640]{2,1,0:T(8,128)(2,1)}, bf16[4,128,640]{2,1,0:T(8,128)(2,1)}, u32[]{:S(2)}, u32[]{:S(2)}) collective-permute-start(bf16[4,128,640]{2,1,0:T(8,128)(2,1)} %get-tuple-element.237), channel_id=1, source_target_pairs={{0,24},{4,28},{8,16},{12,20},{16,8},{20,12},{24,0},{28,4},{1,25},{... | collective-permute-start | bytes 1966088 | tf_op jit(solution)/shard_map/ppermute | solution.py:868
  286.1 17.9 %collective-permute-start.23 = (bf16[4,2,240,640]{3,2,1,0:T(8,128)(2,1)}, bf16[4,2,240,640]{3,2,1,0:T(8,128)(2,1)}, u32[]{:S(2)}, u32[]{:S(2)}) collective-permute-start(bf16[4,2,240,640]{3,2,1,0:T(8,128)(2,1)} %get-tuple-element.265), channel_id=1, source_target_pairs={{0,4},{4,0},{8,12},{12,8},{16,20},{20,16},{24,28},{28,24},{1,5},{5... | collective-permute-start | bytes 7372808 | tf_op jit(solution)/shard_map/ppermute | solution.py:862
  286.1 40.9 %all-to-all-start.2 = ((bf16[4,240,768]{2,1,0:T(8,128)(2,1)}), bf16[4,240,768]{2,1,0:T(8,128)(2,1)S(1)}, u32[]{:S(2)}, u32[]{:S(2)}) async-start(bf16[4,240,768]{2,1,0:T(8,128)(2,1)} %bitcast.117), calls=%async_computation.2 | async-start | bytes 2949120 | tf_op jit(solution)/shard_map/all_to_all | solution.py:908
  291.5 35.5 %collective-permute-start.20 = (bf16[2,240,640]{2,1,0:T(8,128)(2,1)}, bf16[2,240,640]{2,1,0:T(8,128)(2,1)}, u32[]{:S(2)}, u32[]{:S(2)}) collective-permute-start(bf16[2,240,640]{2,1,0:T(8,128)(2,1)} %get-tuple-element.258), channel_id=1, source_target_pairs={{0,8},{4,12},{8,0},{12,4},{16,24},{20,28},{24,16},{28,20},{1,9},{5... | collective-permute-start | bytes 1843208 | tf_op jit(solution)/shard_map/ppermute | solution.py:868
  292.7 34.2 %collective-permute-start.21 = (bf16[2,240,640]{2,1,0:T(8,128)(2,1)}, bf16[2,240,640]{2,1,0:T(8,128)(2,1)}, u32[]{:S(2)}, u32[]{:S(2)}) collective-permute-start(bf16[2,240,640]{2,1,0:T(8,128)(2,1)} %get-tuple-element.259), channel_id=1, source_target_pairs={{0,16},{4,20},{8,24},{12,28},{16,0},{20,4},{24,8},{28,12},{1,17},{... | collective-permute-start | bytes 1843208 | tf_op jit(solution)/shard_map/ppermute | solution.py:868
  293.6 33.4 %collective-permute-start.22 = (bf16[2,240,640]{2,1,0:T(8,128)(2,1)}, bf16[2,240,640]{2,1,0:T(8,128)(2,1)}, u32[]{:S(2)}, u32[]{:S(2)}) collective-permute-start(bf16[2,240,640]{2,1,0:T(8,128)(2,1)} %get-tuple-element.260), channel_id=1, source_target_pairs={{0,24},{4,28},{8,16},{12,20},{16,8},{20,12},{24,0},{28,4},{1,25},{... | collective-permute-start | bytes 1843208 | tf_op jit(solution)/shard_map/ppermute | solution.py:868
  329.4 47.4 %collective-permute-start.26 = (bf16[2,240,640]{2,1,0:T(8,128)(2,1)}, bf16[2,240,640]{2,1,0:T(8,128)(2,1)S(1)}, u32[]{:S(2)}, u32[]{:S(2)}) collective-permute-start(bf16[2,240,640]{2,1,0:T(8,128)(2,1)} %get-tuple-element.293), channel_id=1, source_target_pairs={{0,8},{4,12},{8,0},{12,4},{16,24},{20,28},{24,16},{28,20},{1,9},{5... | collective-permute-start | bytes 1843208 | tf_op jit(solution)/shard_map/ppermute | solution.py:868
  330.6 46.2 %collective-permute-start.27 = (bf16[2,240,640]{2,1,0:T(8,128)(2,1)}, bf16[2,240,640]{2,1,0:T(8,128)(2,1)S(1)}, u32[]{:S(2)}, u32[]{:S(2)}) collective-permute-start(bf16[2,240,640]{2,1,0:T(8,128)(2,1)} %get-tuple-element.294), channel_id=1, source_target_pairs={{0,16},{4,20},{8,24},{12,28},{16,0},{20,4},{24,8},{28,12},{1,17},{... | collective-permute-start | bytes 1843208 | tf_op jit(solution)/shard_map/ppermute | solution.py:868
  331.5 45.4 %collective-permute-start.28 = (bf16[2,240,640]{2,1,0:T(8,128)(2,1)}, bf16[2,240,640]{2,1,0:T(8,128)(2,1)S(1)}, u32[]{:S(2)}, u32[]{:S(2)}) collective-permute-start(bf16[2,240,640]{2,1,0:T(8,128)(2,1)} %get-tuple-element.295), channel_id=1, source_target_pairs={{0,24},{4,28},{8,16},{12,20},{16,8},{20,12},{24,0},{28,4},{1,25},{... | collective-permute-start | bytes 1843208 | tf_op jit(solution)/shard_map/ppermute | solution.py:868
  334.6 33.5 %collective-permute-start.24 = (bf16[368,640]{1,0:T(8,128)(2,1)}, bf16[368,640]{1,0:T(8,128)(2,1)S(1)}, u32[]{:S(2)}, u32[]{:S(2)}) collective-permute-start(bf16[368,640]{1,0:T(8,128)(2,1)} %pad_maximum_fusion.2), channel_id=1, source_target_pairs={{0,3},{1,2},{2,1},{3,0},{4,7},{5,6},{6,5},{7,4},{8,11},{9,10},{10,... | collective-permute-start | bytes 1413128 | tf_op jit(solution)/shard_map/ppermute | solution.py:868
  337.6 39.2 %collective-permute-start.25 = (bf16[368,640]{1,0:T(8,128)(2,1)}, bf16[368,640]{1,0:T(8,128)(2,1)}, u32[]{:S(2)}, u32[]{:S(2)}) collective-permute-start(bf16[368,640]{1,0:T(8,128)(2,1)} %pad_maximum_fusion.3), channel_id=1, source_target_pairs={{0,2},{1,3},{2,0},{3,1},{4,6},{5,7},{6,4},{7,5},{8,10},{9,11},{10,... | collective-permute-start | bytes 1413128 | tf_op jit(solution)/shard_map/ppermute | solution.py:868
  380.5 11.3 %collective-permute-start.29 = (bf16[368,640]{1,0:T(8,128)(2,1)S(1)}, bf16[368,640]{1,0:T(8,128)(2,1)S(1)}, u32[]{:S(2)}, u32[]{:S(2)}) collective-permute-start(bf16[368,640]{1,0:T(8,128)(2,1)S(1)} %pad_maximum_fusion.4), channel_id=1, source_target_pairs={{0,1},{1,0},{2,3},{3,2},{4,5},{5,4},{6,7},{7,6},{8,9},{9,8},{10,11... | collective-permute-start | bytes 1413128 | tf_op jit(solution)/shard_map/ppermute | solution.py:868
  392.6 13.5 %collective-permute-start.30 = (bf16[4,4,128,640]{3,2,1,0:T(8,128)(2,1)}, bf16[4,4,128,640]{3,2,1,0:T(8,128)(2,1)}, u32[]{:S(2)}, u32[]{:S(2)}) collective-permute-start(bf16[4,4,128,640]{3,2,1,0:T(8,128)(2,1)} %get-tuple-element.434), channel_id=1, source_target_pairs={{0,4},{4,0},{8,12},{12,8},{16,20},{20,16},{24,28},{28,24},{1,5},{5... | collective-permute-start | bytes 7864328 | tf_op jit(solution)/shard_map/ppermute | solution.py:862
  392.6 57.5 %all-to-all-start.3 = ((bf16[4,240,1024]{2,1,0:T(8,128)(2,1)}), bf16[4,240,1024]{2,1,0:T(8,128)(2,1)S(1)}, u32[]{:S(2)}, u32[]{:S(2)}) async-start(bf16[4,240,1024]{2,1,0:T(8,128)(2,1)} %bitcast.114), calls=%async_computation.3 | async-start | bytes 3932160 | tf_op jit(solution)/shard_map/all_to_all | solution.py:908
  404.2 8.5 %collective-permute-start.38 = (bf16[128,320]{1,0:T(8,128)(2,1)S(1)}, bf16[128,320]{1,0:T(8,128)(2,1)S(1)}, u32[]{:S(2)}, u32[]{:S(2)}) collective-permute-start(bf16[128,320]{1,0:T(8,128)(2,1)S(1)} %select_convert_fusion.1), channel_id=1, source_target_pairs={{0,4},{4,0},{8,12},{12,8},{16,20},{20,16},{24,28},{28,24},{1,5},{5... | collective-permute-start | bytes 245768 | tf_op jit(solution)/shard_map/ppermute | solution.py:862
  406.0 7.7 %collective-permute-start.37 = (bf16[120,640]{1,0:T(8,128)(2,1)S(1)}, bf16[120,640]{1,0:T(8,128)(2,1)S(1)}, u32[]{:S(2)}, u32[]{:S(2)}) collective-permute-start(bf16[120,640]{1,0:T(8,128)(2,1)S(1)} %select_convert_fusion), channel_id=1, source_target_pairs={{0,4},{4,0},{8,12},{12,8},{16,20},{20,16},{24,28},{28,24},{1,5},{5... | collective-permute-start | bytes 460808 | tf_op jit(solution)/shard_map/ppermute | solution.py:862
  409.2 17.9 %collective-permute-start.31 = (bf16[4,128,640]{2,1,0:T(8,128)(2,1)}, bf16[4,128,640]{2,1,0:T(8,128)(2,1)}, u32[]{:S(2)}, u32[]{:S(2)}) collective-permute-start(bf16[4,128,640]{2,1,0:T(8,128)(2,1)} %get-tuple-element.396), channel_id=1, source_target_pairs={{0,8},{4,12},{8,0},{12,4},{16,24},{20,28},{24,16},{28,20},{1,9},{5... | collective-permute-start | bytes 1966088 | tf_op jit(solution)/shard_map/ppermute | solution.py:868
  410.4 31.3 %collective-permute-start.33 = (bf16[4,128,640]{2,1,0:T(8,128)(2,1)}, bf16[4,128,640]{2,1,0:T(8,128)(2,1)}, u32[]{:S(2)}, u32[]{:S(2)}) collective-permute-start(bf16[4,128,640]{2,1,0:T(8,128)(2,1)} %get-tuple-element.397), channel_id=1, source_target_pairs={{0,24},{4,28},{8,16},{12,20},{16,8},{20,12},{24,0},{28,4},{1,25},{... | collective-permute-start | bytes 1966088 | tf_op jit(solution)/shard_map/ppermute | solution.py:868
  412.1 30.9 %collective-permute-start.32 = (bf16[4,128,640]{2,1,0:T(8,128)(2,1)}, bf16[4,128,640]{2,1,0:T(8,128)(2,1)}, u32[]{:S(2)}, u32[]{:S(2)}) collective-permute-start(bf16[4,128,640]{2,1,0:T(8,128)(2,1)} %get-tuple-element.398), channel_id=1, source_target_pairs={{0,16},{4,20},{8,24},{12,28},{16,0},{20,4},{24,8},{28,12},{1,17},{... | collective-permute-start | bytes 1966088 | tf_op jit(solution)/shard_map/ppermute | solution.py:868
  446.0 9.1 %collective-permute-start.34 = (bf16[128,640]{1,0:T(8,128)(2,1)}, bf16[128,640]{1,0:T(8,128)(2,1)S(1)}, u32[]{:S(2)}, u32[]{:S(2)}) collective-permute-start(bf16[128,640]{1,0:T(8,128)(2,1)} %get-tuple-element.413), channel_id=1, source_target_pairs={{0,1},{1,0},{2,3},{3,2},{4,5},{5,4},{6,7},{7,6},{8,9},{9,8},{10,11... | collective-permute-start | bytes 491528 | tf_op jit(solution)/shard_map/ppermute | solution.py:868
  447.7 10.7 %collective-permute-start.36 = (bf16[128,640]{1,0:T(8,128)(2,1)S(1)}, bf16[128,640]{1,0:T(8,128)(2,1)S(1)}, u32[]{:S(2)}, u32[]{:S(2)}) collective-permute-start(bf16[128,640]{1,0:T(8,128)(2,1)S(1)} %get-tuple-element.414), channel_id=1, source_target_pairs={{0,3},{1,2},{2,1},{3,0},{4,7},{5,6},{6,5},{7,4},{8,11},{9,10},{10,... | collective-permute-start | bytes 491528 | tf_op jit(solution)/shard_map/ppermute | solution.py:868
  450.1 13.6 %collective-permute-start.35 = (bf16[128,640]{1,0:T(8,128)(2,1)S(1)}, bf16[128,640]{1,0:T(8,128)(2,1)S(1)}, u32[]{:S(2)}, u32[]{:S(2)}) collective-permute-start(bf16[128,640]{1,0:T(8,128)(2,1)S(1)} %get-tuple-element.415), channel_id=1, source_target_pairs={{0,2},{1,3},{2,0},{3,1},{4,6},{5,7},{6,4},{7,5},{8,10},{9,11},{10,... | collective-permute-start | bytes 491528 | tf_op jit(solution)/shard_map/ppermute | solution.py:868
  (22 other events, 123.5 us)
Sparse Core Ops, SparseCore 0:
  81.5 82.4 all-gather.2

commit v4 on v3

--- a/solution.py
+++ b/solution.py
@@ -265,23 +265,29 @@
     return jnp.concatenate([scores[:clear], tail], axis=0) if clear else tail
 
 
+def side_by_side(value, cols):
+    return jnp.concatenate(
+        [value[head * HD : (head + 1) * HD, cols] for head in range(GROUP)], axis=1
+    )
+
+
 def attend_body(q, k, vt, limit, out, total):
     length = k.shape[1]
     picks = q.shape[1]
     for block in range(picks // QBLOCK):
-        at = block * QBLOCK
+        cols = slice(block * QBLOCK, (block + 1) * QBLOCK)
         reach = reach_of(block, length, picks)
+        limits = jnp.concatenate([limit[:, cols]] * GROUP, axis=1)
+        scores = block_scores(side_by_side(q, cols), k[0], limits, block, reach)
+        top = jnp.max(scores, axis=0, keepdims=True)
+        weight = jnp.exp(scores - top)
+        mass = jnp.sum(weight, axis=0, keepdims=True)
+        mixed = (dot_nn(vt[:, :reach], weight.astype(BF)) / mass).astype(BF)
+        logs = top + jnp.log(mass)
         for head in range(GROUP):
-            rows = slice(head * HD, (head + 1) * HD)
-            scores = block_scores(
-                q[rows, at : at + QBLOCK], k[0], limit[:, at : at + QBLOCK], block, reach
-            )
-            top = jnp.max(scores, axis=0, keepdims=True)
-            weight = jnp.exp(scores - top)
-            mass = jnp.sum(weight, axis=0, keepdims=True)
-            mixed = dot_nn(vt[:, :reach], weight.astype(BF))
-            out[rows, at : at + QBLOCK] = (mixed / mass).astype(BF)
-            total[0, head : head + 1, at : at + QBLOCK] = top + jnp.log(mass)
+            part = slice(head * QBLOCK, (head + 1) * QBLOCK)
+            out[head * HD : (head + 1) * HD, cols] = mixed[:, part]
+            total[0, head : head + 1, cols] = logs[:, part]
 
 
 def attend(q, k, vt, limit):
@@ -320,26 +326,26 @@
     gk[...] = jnp.zeros_like(gk)
     gv[...] = jnp.zeros_like(gv)
     for block in range(picks // QBLOCK):
-        at = block * QBLOCK
-        cols = slice(at, at + QBLOCK)
+        cols = slice(block * QBLOCK, (block + 1) * QBLOCK)
         reach = reach_of(block, length, picks)
+        limits = jnp.concatenate([limit[:, cols]] * GROUP, axis=1)
+        q_part, g_part = side_by_side(q, cols), side_by_side(grad, cols)
+        scores = block_scores(q_part, k[0], limits, block, reach)
+        logs = jnp.concatenate([total[0, head : head + 1, cols] for head in range(GROUP)], axis=1)
+        weight = jnp.exp(scores - logs)
+        delta = jnp.sum(
+            g_part.astype(F32) * side_by_side(mixed, cols).astype(F32), axis=0, keepdims=True
+        )
+        pull = dot_nn(v[0, :reach], g_part)
+        back = (weight * (pull - delta)).astype(BF)
+        gq = dot_nn(kt[:, :reach], back) * HD ** (-0.5)
+        gk[:reach] += dot_nt(back, q_part)
+        gv[:reach] += dot_nt(weight.astype(BF), g_part)
         for head in range(GROUP):
-            rows = slice(head * HD, (head + 1) * HD)
-            q_part = q[rows, cols]
-            g_part = grad[rows, cols]
-            scores = block_scores(q_part, k[0], limit[:, cols], block, reach)
-            weight = jnp.exp(scores - total[0, head : head + 1, cols])
-            delta = jnp.sum(
-                g_part.astype(F32) * mixed[rows, cols].astype(F32), axis=0, keepdims=True
-            )
-            pull = dot_nn(v[0, :reach], g_part)
-            back = (weight * (pull - delta)).astype(BF)
-            gq = dot_nn(kt[:, :reach], back) * HD ** (-0.5)
-            a, b = turn(gq[:half], gq[half:], cos_q[:, cols], sin_q[:, cols], -1.0)
+            part = slice(head * QBLOCK, (head + 1) * QBLOCK)
+            a, b = turn(gq[:half, part], gq[half:, part], cos_q[:, cols], sin_q[:, cols], -1.0)
             gq_out[head * HD : head * HD + half, cols] = a.astype(BF)
             gq_out[head * HD + half : (head + 1) * HD, cols] = b.astype(BF)
-            gk[:reach] += dot_nt(back, q_part)
-            gv[:reach] += dot_nt(weight.astype(BF), g_part)
     turned = gk[...].T
     a, b = turn(turned[:half], turned[half:], cos_k[...], sin_k[...], -1.0)
     gk_out[:half] = a.astype(BF)
@@ -441,18 +447,18 @@
     return -(-part // 32) * 16
 
 
-def ffn_weights(who, first, blocks, sources, w_gate, w_up, w_down, done):
+def ffn_weights(who, first, blocks, sources, w_pair, w_down, done):
     step, steps = pl.program_id(0), pl.num_programs(0)
     slot = lax.rem(step, 2)
-    width = w_gate.shape[1]
+    width, hidden = w_pair.shape[1], w_down.shape[2]
+    gates, ups = slice(0, hidden), slice(hidden, 2 * hidden)
 
     def copies(step, at):
         turn = blocks - 1 - first - step
         block = turn ^ who[0]
         if len(sources) == 2:
             some = [
-                (sources[0].at[0, block], w_gate.at[at]),
-                (sources[0].at[1, block], w_up.at[at]),
+                (sources[0].at[block], w_pair.at[at]),
                 (sources[1].at[block], w_down.at[at]),
             ]
         else:
@@ -463,8 +469,8 @@
             some = []
             for i in range(pairs):
                 place = slice(i * height, (i + 1) * height)
-                some.append((source.at[i, 0, turn, :height], w_gate.at[at, place]))
-                some.append((source.at[i, 1, turn, :height], w_up.at[at, place]))
+                some.append((source.at[i, 0, turn, :height], w_pair.at[at, place, gates]))
+                some.append((source.at[i, 1, turn, :height], w_pair.at[at, place, ups]))
             for c in range(columns):
                 begin = pl.multiple_of((c ^ who[0]) * part, 16)
                 top = pl.ds(begin, half)
@@ -493,17 +499,22 @@
 
 
 def ffn_scratch(width, sources):
-    hidden = sources[0].shape[-1]
-    count = 3
+    hidden = sources[-1].shape[-1]
+    count = 2
     if len(sources) == 1:
         count = 2 * (sources[0].shape[0] + sources[0].shape[2])
-    return [pltpu.VMEM((2, width, hidden), BF)] * 3 + [pltpu.SemaphoreType.DMA((2, count))]
+    return [
+        pltpu.VMEM((2, width, 2 * hidden), BF),
+        pltpu.VMEM((2, width, hidden), BF),
+        pltpu.SemaphoreType.DMA((2, count)),
+    ]
 
 
 def ffn_body(many, who, normed, branch, prob, *refs):
     sources, refs = refs[:many], refs[many:]
     gate_out, up_out, active_out, delta, both_out, forward, *buffers = refs
-    w_gate, w_up, w_down, _ = buffers
+    w_pair, w_down, _ = buffers
+    hidden = w_down.shape[2]
     slot = ffn_weights(who, 0, pl.num_programs(0), sources, *buffers)
 
     @pl.when(pl.program_id(0) == 0)
@@ -511,8 +522,8 @@
         forward[...] = branch[...]
 
     tokens = normed[...]
-    gate = dot_tn(w_gate[slot], tokens)
-    up = dot_tn(w_up[slot], tokens)
+    pair = dot_tn(w_pair[slot], tokens)
+    gate, up = pair[:hidden], pair[hidden:]
     active = (gate * jax.nn.sigmoid(gate) * up).astype(BF)
     gate_out[0] = gate.astype(BF)
     up_out[0] = up.astype(BF)
@@ -598,8 +609,9 @@
     if last:
         (branch, both_in, picked, cot, prob, inverse, gain, router), refs = refs[:8], refs[8:]
     keep_pair, send_pair, refs = refs[0], refs[1], refs[2:]
-    outs, backward, buffers = refs[:-5], refs[-5], refs[-4:]
-    w_gate, w_up, w_down, _ = buffers
+    outs, backward, buffers = refs[:-4], refs[-4], refs[-3:]
+    w_pair, w_down, _ = buffers
+    hidden = w_down.shape[2]
     slot = ffn_weights(who, first, blocks, sources, *buffers)
     width = normed.shape[0]
     even = who[2] == 0
@@ -614,10 +626,11 @@
     silu = gate * sigmoid
     grad_gate = (pull * up_in[0].astype(F32) * (sigmoid + silu * (1.0 - sigmoid))).astype(BF)
     grad_up = (pull * silu).astype(BF)
-    backward[...] += dot_nn(w_gate[slot], grad_gate) + dot_nn(w_up[slot], grad_up)
     tokens = normed[...]
-    for_gate = dot_nt(tokens, grad_gate).astype(BF)
-    for_up = dot_nt(tokens, grad_up).astype(BF)
+    grads = jnp.concatenate([grad_gate, grad_up], axis=0)
+    backward[...] += dot_nn(w_pair[slot], grads)
+    for_pair = dot_nt(tokens, grads).astype(BF)
+    for_gate, for_up = for_pair[:, :hidden], for_pair[:, hidden:]
     pieces, _, height, _ = keep_pair.shape
     for i in range(pieces):
         place = slice(i * height, (i + 1) * height)
@@ -638,13 +651,13 @@
         )
         token = picked[...].astype(F32)
         router_out[...] = jnp.sum(slope * token, axis=1, keepdims=True)
-        hidden = token + branch[...]
+        merged = token + branch[...]
         inv = inverse[...]
         grad_norm = backward[...]
-        gain_out[...] = jnp.sum(grad_norm * hidden * inv, axis=1, keepdims=True)
+        gain_out[...] = jnp.sum(grad_norm * merged * inv, axis=1, keepdims=True)
         unit = grad_norm * gain[...]
-        along = jnp.sum(unit * hidden, axis=0, keepdims=True) / width
-        grad_hidden = inv * unit - hidden * (inv * inv * inv * along)
+        along = jnp.sum(unit * merged, axis=0, keepdims=True) / width
+        grad_hidden = inv * unit - merged * (inv * inv * inv * along)
         grad_attn[...] = (grad_hidden + share * cot_full).astype(BF)
         rest_out[...] = (grad_hidden + slope * router[...]).astype(BF)
 
@@ -936,7 +949,7 @@
     core = lax.axis_index("row") & 1
     even = core == 0
     who = jnp.stack([column, own_pair_index, core]).astype(jnp.int32)
-    aligned = 2 * rows % 16 == 0
+    aligned = 2 * rows % 16 == 0 and hidden % 128 == 0
 
     half = col_count // 2
 
@@ -961,14 +974,14 @@
     else:
         mixing, x = hold(collect(mixing, "row", range(pairs)), x)
         pair_all = lax.all_gather(pair, ("row", "col"), axis=0)
-        pair_all = pair_all.reshape(pairs, 2, col_count, 2 * rows, hidden).transpose(1, 2, 0, 3, 4)
+        pair_all = pair_all.reshape(pairs, 2, col_count, 2 * rows, hidden).transpose(2, 0, 3, 1, 4)
         down_all = lax.all_gather(down, ("row", "col"), axis=0)
         down_all = down_all.reshape((col_count, pairs // col_count, 2, col_count) + down.shape)
         down_all = jnp.concatenate(
             [down_all[:, :, 0], down_all[:, :, 1, :, 2 * down_rows_kept - part :]], axis=3
         )
         sources = (
-            pair_all.reshape(2, col_count, width, hidden),
+            pair_all.reshape(col_count, width, 2 * hidden),
             down_all.transpose(0, 2, 3, 1, 4).reshape(col_count, width, hidden),
         )
     every = jnp.arange(length, dtype=jnp.int32)

time: 481 us -> 467 us (0.971)
  Pallas kernels: 210 us -> 195 us
    pallas_call x1, Pallas kernels: 26.1 us -> 16.4 us  [attend(): pl.pallas_call(attend_body, grid=(KVH,), in_specs=[pl.BlockSpec((part, pi...]
  transfers between devices with their start and end apart: 44 -> 44, of which waited for: 16 -> 16; matrix products, arithmetic and copies ran while one was open for 9% -> 9% of each run, Pallas kernels for 38% -> 36%
where the time goes in v4:
time: 467 us; the launch traced here: 460 us
  Pallas kernels  195 us (42%)
  waiting for transfers between devices  113 us (24%)
  starting transfers between devices  70.3 us (15%)
  other arithmetic  44.4 us (10%)
  local copies, waits for them, and re-layouts  21.1 us (5%)
  between operations  15.6 us (3%)
    ppermute x27, waiting for transfers between devices, partner(): return lax.ppermute(value, axis, [(i, i ^ far) for i in range(count)])  82 us
    ppermute x27, starting transfers between devices, partner(): return lax.ppermute(value, axis, [(i, i ^ far) for i in range(count)])  50.5 us
    pallas_call x2, Pallas kernels, ffn_back(): pl.pallas_call(functools.partial(ffn_back_body, first, gate.shape[0], las...  43.4 us
    pallas_call x2, Pallas kernels, attend_back(): pl.pallas_call(attend_back_body, grid=(count,), in_specs=[wide, tall, fla...  31 us
    all_to_all x2, waiting for transfers between devices, to_owner(): lax.all_to_all(value, 'col', split_axis=0, concat_axis=1, tiled=True)  28.3 us
    pallas_call x1, Pallas kernels, ffn(): pl.pallas_call(functools.partial(ffn_body, len(sources)), grid_spec=pltpu...  22.4 us
    pallas_call x1, Pallas kernels, project(): pl.pallas_call(project_body, grid_spec=pltpu.PrefetchScalarGridSpec(num_s...  17.9 us
    pallas_call x1, Pallas kernels, attend(): pl.pallas_call(attend_body, grid=(KVH,), in_specs=[pl.BlockSpec((part, pi...  16.4 us
  transfers between devices with their start and end apart: 44, of which 16 were waited for; matrix products, arithmetic and copies ran while one was open for 9% of the time, Pallas kernels for 36%

profile of v4, /device:TPU:0, one launch (start us, length us, event | category | flops | bytes accessed | tf_op | source)
XLA Modules:
  0.0 459.8 jit_solution(2016150905924945951)
XLA Ops:
  10.0 5.1 %collective-permute-start.2 = (bf16[120,640]{1,0:T(8,128)(2,1)S(1)}, bf16[120,640]{1,0:T(8,128)(2,1)S(1)}, u32[]{:S(2)}, u32[]{:S(2)}) collective-permute-start(bf16[120,640]{1,0:T(8,128)(2,1)S(1)} %pad_maximum_fusion.7), channel_id=1, source_target_pairs={{0,3},{1,2},{2,1},{3,0},{4,7},{5,6},{6,5},{7,4},{8,11},{9,10},{10,... | collective-permute-start | bytes 460808 | tf_op jit(solution)/shard_map/ppermute | solution.py:881
  20.0 8.1 %collective-permute-done.1 = bf16[120,640]{1,0:T(8,128)(2,1)S(1)} collective-permute-done((bf16[120,640]{1,0:T(8,128)(2,1)S(1)}, bf16[120,640]{1,0:T(8,128)(2,1)S(1)}, u32[]{:S(2)}, u32[]{:S(2)}) %collective-permute-start.1) | collective-permute-done | bytes 153632 | tf_op jit(solution)/shard_map/ppermute | solution.py:881
  28.2 2.6 collective-permute-start.7
  30.9 2.5 collective-permute-start.10
  34.5 9.3 %collective-permute-done.7 = bf16[368,640]{1,0:T(8,128)(2,1)S(1)} collective-permute-done((bf16[368,640]{1,0:T(8,128)(2,1)S(1)}, bf16[368,640]{1,0:T(8,128)(2,1)S(1)}, u32[]{:S(2)}, u32[]{:S(2)}) %collective-permute-start.7) | collective-permute-done | bytes 471072 | tf_op jit(solution)/shard_map/ppermute | solution.py:881
  43.8 18.1 %collective-permute-start.5 = (bf16[368,640]{1,0:T(8,128)(2,1)S(1)}, bf16[368,640]{1,0:T(8,128)(2,1)S(1)}, u32[]{:S(2)}, u32[]{:S(2)}) collective-permute-start(bf16[368,640]{1,0:T(8,128)(2,1)S(1)} %constant_dynamic-update-slice_fusion), channel_id=1, source_target_pairs={{0,1},{1,0},{2,3},{3,2},{4,5},{5,4},{6,7},{7,6},{8,9},{9,8},{10,11... | collective-permute-start | bytes 1413128 | tf_op jit(solution)/shard_map/ppermute | solution.py:881
  63.5 5.9 %collective-permute-done.6 = bf16[368,640]{1,0:T(8,128)(2,1)S(1)} collective-permute-done((bf16[368,640]{1,0:T(8,128)(2,1)S(1)}, bf16[368,640]{1,0:T(8,128)(2,1)S(1)}, u32[]{:S(2)}, u32[]{:S(2)}) %collective-permute-start.6) | collective-permute-done | bytes 471072 | tf_op jit(solution)/shard_map/ppermute | solution.py:881
  69.4 8.6 %collective-permute-done.5 = bf16[368,640]{1,0:T(8,128)(2,1)S(1)} collective-permute-done((bf16[368,640]{1,0:T(8,128)(2,1)S(1)}, bf16[368,640]{1,0:T(8,128)(2,1)S(1)}, u32[]{:S(2)}, u32[]{:S(2)}) %collective-permute-start.5) | collective-permute-done | bytes 471072 | tf_op jit(solution)/shard_map/ppermute | solution.py:881
  81.4 3.7 all-to-all-start
  90.9 2.0 copy.90.rank
  92.9 5.9 %gather_tokens.1 = bf16[4,240,768]{2,1,0:T(8,128)(2,1)} custom-call(f32[4,240,1024]{2,1,0:T(8,128)} %values.1, s32[4,1024,1]{2,1,0:T(8,128)} %copy.90.rank), custom_call_target="tpu_custom_call" | custom-call | flops 47185920 | bytes 184320 | tf_op jit(solution)/shard_map/gather_tokens/pallas_call | solution.py:83
  101.2 28.3 %all-to-all-done = bf16[4,240,1024]{2,1,0:T(8,128)(2,1)S(1)} async-done(((bf16[4,240,1024]{2,1,0:T(8,128)(2,1)}), bf16[4,240,1024]{2,1,0:T(8,128)(2,1)S(1)}, u32[]{:S(2)}, u32[]{:S(2)}) %all-to-all-start) | async-done | bytes 1966112 | tf_op jit(solution)/shard_map/all_to_all | solution.py:914
  130.7 3.7 all-to-all-start.1
  139.2 17.9 %project.1 = (bf16[960,768]{1,0:T(8,128)(2,1)}, f32[1,768]{1,0:T(1,128)}, bf16[960,768]{1,0:T(8,128)(2,1)}, bf16[320,1024]{1,0:T(8,128)(2,1)}, bf16[5,1024,64]{2...) custom-call(s32[3]{0:T(128)} %pad_add_fusion.who, ...), custom_call_target="tpu_custom_call" | custom-call | flops 130744320 | bytes 552960 | tf_op jit(solution)/shard_map/project/pallas_call | solution.py:199
  157.8 16.4 %attend.1 = (bf16[960,768]{1,0:T(8,128)(2,1)}, f32[5,3,768]{2,1,0:T(4,128)}) custom-call(bf16[960,768]{1,0:T(8,128)(2,1)} %get-tuple-element.198.q, bf16[5,1024,64]{2,1,0:T(8,128)(2,1)} %get-tuple-element.199.k, bf16[320,1024]{1,0:T(8,128)(2,1)} %get-tuple-element.200.vt, s32[1,768]{1,0:T(1,128)} %max.18.limit), custom_call_target="tpu_custom_call" | custom-call | flops 377487360 | bytes 92160 | tf_op jit(solution)/shard_map/attend/pallas_call | solution.py:297
  174.2 8.1 %merge.1 = (f32[960,768]{1,0:T(8,128)}, f32[1,768]{1,0:T(1,128)}, bf16[960,768]{1,0:T(8,128)(2,1)}) custom-call(bf16[960,768]{1,0:T(8,128)(2,1)} %get-tuple-element.202.mixed, bf16[960,768]{1,0:T(8,128)(2,1)} %get-tuple-element.203.picked.refs_4_, f32[960,1]{1,0:T(8,128)} %copy.94.gain.refs_8_, bf16[4,960,640]{2,1,0:T(8,128)(2,1)} %get-tuple-element.204.w.refs_7_), custom_call_target="tpu_custom_call" | custom-call | flops 44236800 | bytes 476160 | tf_op jit(solution)/shard_map/merge/pallas_call | solution.py:420
  183.9 22.4 %ffn.1 = (bf16[4,640,768]{2,1,0:T(8,128)(2,1)}, bf16[4,640,768]{2,1,0:T(8,128)(2,1)}, bf16[4,640,768]{2,1,0:T(8,128)(2,1)}, bf16[960,768]{1,0:T(8,128)(2,1)}, bf16[960,768]{1,0:T(8,128)(2,1)}) custom-call(s32[3]{0:T(128)} %pad_add_fusion.who, bf16[960,768]{1,0:T(8,128)(2,1)} %get-tuple-element.210.normed, f32[960,768]{1,0:T(8,128)} %get-tuple-element.211.branch.refs_2_, ...), custom_call_target="tpu_custom_call" | custom-call | flops 353894400 | bytes 645120 | tf_op jit(solution)/shard_map/ffn/pallas_call | solution.py:547
  206.3 9.4 %down_grad.1 = (bf16[4,4,128,640]{3,2,1,0:T(8,128)(2,1)}, bf16[4,4,128,640]{3,2,1,0:T(8,128)(2,1)}) custom-call(s32[3]{0:T(128)} %pad_add_fusion.who, bf16[960,768]{1,0:T(8,128)(2,1)} %multiply_convert_fusion.grad_ffn, bf16[4,640,768]{2,1,0:T(8,128)(2,1)} %get-tuple-element.216.active), custom_call_target="tpu_custom_call" | custom-call | flops 117964800 | bytes 460800 | tf_op jit(solution)/shard_map/down_grad/pallas_call | solution.py:587
  215.8 18.9 %ffn_back.2 = (bf16[4,2,240,640]{3,2,1,0:T(8,128)(2,1)}, bf16[4,2,240,640]{3,2,1,0:T(8,128)(2,1)}, f32[960,768]{1,0:T(8,128)}) custom-call(s32[3]{0:T(128)} %pad_add_fusion.who, bf16[960,768]{1,0:T(8,128)(2,1)} %get-tuple-element.210.normed, bf16[960,768]{1,0:T(8,128)(2,1)} %multiply_convert_fusion.grad_ffn, ...), custom_call_target="tpu_custom_call" | custom-call | flops 294912000 | bytes 660480 | tf_op jit(solution)/shard_map/ffn_back/pallas_call | solution.py:677
  234.6 3.4 fusion.10
  240.1 1.8 collective-permute-start.18
  242.1 24.5 %ffn_back.3 = (bf16[4,2,240,640]{3,2,1,0:T(8,128)(2,1)}, bf16[4,2,240,640]{3,2,1,0:T(8,128)(2,1)}, bf16[960,768]{1,0:T(8,128)(2,1)}, bf16[960,768]{1,0:T(8,128)(...) custom-call(s32[3]{0:T(128)} %pad_add_fusion.who, bf16[960,768]{1,0:T(8,128)(2,1)} %get-tuple-element.210.normed, ...), custom_call_target="tpu_custom_call" | custom-call | flops 294912000 | bytes 660480 | tf_op jit(solution)/shard_map/ffn_back/pallas_call | solution.py:677
  266.6 4.3 collective-permute-done.18
  270.9 1.8 add_convert_fusion.4
  273.0 1.7 fusion.18
  274.7 5.3 %all-to-all-start.2 = ((bf16[4,240,768]{2,1,0:T(8,128)(2,1)}), bf16[4,240,768]{2,1,0:T(8,128)(2,1)S(1)}, u32[]{:S(2)}, u32[]{:S(2)}) async-start(bf16[4,240,768]{2,1,0:T(8,128)(2,1)} %bitcast.117), calls=%async_computation.2 | async-start | bytes 2949120 | tf_op jit(solution)/shard_map/all_to_all | solution.py:921
  283.5 9.0 %merge_back.1 = (bf16[4,960,240]{2,1,0:T(8,128)(2,1)}, bf16[960,768]{1,0:T(8,128)(2,1)}) custom-call(bf16[960,768]{1,0:T(8,128)(2,1)} %get-tuple-element.202.mixed, bf16[960,768]{1,0:T(8,128)(2,1)} %get-tuple-element.266.grad, bf16[4,960,640]{2,1,0:T(8,128)(2,1)} %get-tuple-element.204.w.refs_7_), custom_call_target="tpu_custom_call" | custom-call | flops 88473600 | bytes 445440 | tf_op jit(solution)/shard_map/merge_back/pallas_call | solution.py:723
  292.5 3.3 fusion.22
  295.8 17.9 %attend_back.2 = (bf16[576,768]{1,0:T(8,128)(2,1)}, bf16[192,1024]{1,0:T(8,128)(2,1)}, bf16[192,1024]{1,0:T(8,128)(2,1)}) custom-call(bf16[960,768]{1,0:T(8,128)(2,1)} %get-tuple-element.198.q, bf16[5,1024,64]{2,1,0:T(8,128)(2,1)} %get-tuple-element.199.k, bf16[320,1024]{1,0:T(8,128)(2,1)} %get-tuple-element.262.kt, ...), custom_call_target="tpu_custom_call" | custom-call | flops 566231040 | bytes 110592 | tf_op jit(solution)/shard_map/attend_back/pallas_call | solution.py:364
  313.7 1.7 all-to-all-done.2.values
  315.5 2.3 add_convert_fusion.10
  323.0 2.1 collective-permute-start.24
  326.5 13.0 %attend_back.3 = (bf16[384,768]{1,0:T(8,128)(2,1)}, bf16[128,1024]{1,0:T(8,128)(2,1)}, bf16[128,1024]{1,0:T(8,128)(2,1)}) custom-call(bf16[960,768]{1,0:T(8,128)(2,1)} %get-tuple-element.198.q, bf16[5,1024,64]{2,1,0:T(8,128)(2,1)} %get-tuple-element.199.k, bf16[320,1024]{1,0:T(8,128)(2,1)} %get-tuple-element.262.kt, ...), custom_call_target="tpu_custom_call" | custom-call | flops 377487360 | bytes 73728 | tf_op jit(solution)/shard_map/attend_back/pallas_call | solution.py:364
  339.5 15.4 %project_back.1 = (bf16[960,1024]{1,0:T(8,128)(2,1)}, bf16[4,400,1024]{2,1,0:T(8,128)(2,1)}, f32[960,1]{1,0:T(8,128)}) custom-call(bf16[960,1024]{1,0:T(8,128)(2,1)} %bitcast.110, s32[1,1024]{1,0:T(1,128)} %copy-done.19, f32[960,1]{1,0:T(8,128)} %copy.92.gain, bf16[576,768]{1,0:T(8,128)(2,1)} %get-tuple-element.296.refs_0_, ...), custom_call_target="tpu_custom_call" | custom-call | flops 192675840 | bytes 460800 | tf_op jit(solution)/shard_map/project_back/pallas_call | solution.py:786
  355.0 9.4 %collective-permute-done.25 = bf16[368,640]{1,0:T(8,128)(2,1)} collective-permute-done((bf16[368,640]{1,0:T(8,128)(2,1)}, bf16[368,640]{1,0:T(8,128)(2,1)}, u32[]{:S(2)}, u32[]{:S(2)}) %collective-permute-start.25) | collective-permute-done | bytes 471072 | tf_op jit(solution)/shard_map/ppermute | solution.py:881
  368.1 10.2 %mixing_grad.1 = (bf16[4,4,128,640]{3,2,1,0:T(8,128)(2,1)}, bf16[4,4,128,640]{3,2,1,0:T(8,128)(2,1)}) custom-call(s32[3]{0:T(128)} %pad_add_fusion.who, bf16[960,1024]{1,0:T(8,128)(2,1)} %bitcast.111, f32[960,1]{1,0:T(8,128)} %copy.92.gain, bf16[4,400,1024]{2,1,0:T(8,128)(2,1)} %get-tuple-element.318.grads, bf16[4,960,240]{2,1,0:T(8,128)(2,1)} %get-tuple-element.319.gw_out), custom_call_target="tpu_custom_call" | custom-call | flops 98304000 | bytes 307200 | tf_op jit(solution)/shard_map/mixing_grad/pallas_call | solution.py:848
  379.2 4.2 all-to-all-start.3
  384.0 6.1 %scatter_tokens.1 = f32[4,240,1024]{2,1,0:T(8,128)} custom-call(f32[4,240,1024]{2,1,0:T(8,128)} %base.1, bf16[4,240,768]{2,1,0:T(8,128)(2,1)} %copy-done.3, s32[4,1,1024]{2,1,0:T(1,128)} %broadcast_in_dim.67.rank), custom_call_target="tpu_custom_call" | custom-call | flops 47185920 | bytes 307200 | tf_op jit(solution)/shard_map/scatter_tokens/pallas_call | solution.py:106
  393.2 3.1 fusion.12
  397.6 1.8 collective-permute-start.33
  401.7 12.4 %collective-permute-done.31 = bf16[4,128,640]{2,1,0:T(8,128)(2,1)} collective-permute-done((bf16[4,128,640]{2,1,0:T(8,128)(2,1)}, bf16[4,128,640]{2,1,0:T(8,128)(2,1)}, u32[]{:S(2)}, u32[]{:S(2)}) %collective-permute-start.31) | collective-permute-done | bytes 655392 | tf_op jit(solution)/shard_map/ppermute | solution.py:881
  414.2 14.5 %collective-permute-done.33 = bf16[4,128,640]{2,1,0:T(8,128)(2,1)} collective-permute-done((bf16[4,128,640]{2,1,0:T(8,128)(2,1)}, bf16[4,128,640]{2,1,0:T(8,128)(2,1)}, u32[]{:S(2)}, u32[]{:S(2)}) %collective-permute-start.33) | collective-permute-done | bytes 655392 | tf_op jit(solution)/shard_map/ppermute | solution.py:881
  430.0 2.3 fusion.4
  433.0 1.8 collective-permute-start.34
  434.8 2.4 collective-permute-start.36
  437.2 5.0 %convert_add_fusion = f32[4,240,1024]{2,1,0:T(8,128)} fusion(f32[4,240,1024]{2,1,0:T(8,128)} %values.1, bf16[4,240,1024]{2,1,0:T(8,128)(2,1)S(1)} %all-to-all-done.3), kind=kLoop, calls=%fused_computation.6 | loop fusion | flops 1966080 | bytes 9830400 | tf_op jit(solution)/shard_map/add | solution.py:1128
  442.2 2.3 collective-permute-done.36
  444.5 5.3 %collective-permute-done.35 = bf16[128,640]{1,0:T(8,128)(2,1)S(1)} collective-permute-done((bf16[128,640]{1,0:T(8,128)(2,1)S(1)}, bf16[128,640]{1,0:T(8,128)(2,1)S(1)}, u32[]{:S(2)}, u32[]{:S(2)}) %collective-permute-start.35) | collective-permute-done | bytes 163872 | tf_op jit(solution)/shard_map/ppermute | solution.py:881
  (193 shorter events, 59.0 us)
Async XLA Ops:
  7.2 12.3 %copy-start.10 = (bf16[120,640]{1,0:T(8,128)(2,1)S(1)}, bf16[120,640]{1,0:T(8,128)(2,1)}, u32[]{:S(2)}) copy-start(bf16[120,640]{1,0:T(8,128)(2,1)} %param.28) | copy-start | bytes 460804
  7.2 176.7 %all-gather.3.cloned.1.call-start = ((), (), s32[]{:S(2)}) async-start(), calls=%async_computation.4 | async-start | bytes 16957440 | tf_op jit(solution)/shard_map/all_gather | solution.py:972
  10.0 10.0 %collective-permute-start.2 = (bf16[120,640]{1,0:T(8,128)(2,1)S(1)}, bf16[120,640]{1,0:T(8,128)(2,1)S(1)}, u32[]{:S(2)}, u32[]{:S(2)}) collective-permute-start(bf16[120,640]{1,0:T(8,128)(2,1)S(1)} %pad_maximum_fusion.7), channel_id=1, source_target_pairs={{0,3},{1,2},{2,1},{3,0},{4,7},{5,6},{6,5},{7,4},{8,11},{9,10},{10,... | collective-permute-start | bytes 460808 | tf_op jit(solution)/shard_map/ppermute | solution.py:881
  15.1 13.0 %collective-permute-start.1 = (bf16[120,640]{1,0:T(8,128)(2,1)S(1)}, bf16[120,640]{1,0:T(8,128)(2,1)S(1)}, u32[]{:S(2)}, u32[]{:S(2)}) collective-permute-start(bf16[120,640]{1,0:T(8,128)(2,1)S(1)} %pad_maximum_fusion.7), channel_id=1, source_target_pairs={{0,2},{1,3},{2,0},{3,1},{4,6},{5,7},{6,4},{7,5},{8,10},{9,11},{10,... | collective-permute-start | bytes 460808 | tf_op jit(solution)/shard_map/ppermute | solution.py:881
  15.1 13.0 %collective-permute-start = (bf16[120,640]{1,0:T(8,128)(2,1)S(1)}, bf16[120,640]{1,0:T(8,128)(2,1)S(1)}, u32[]{:S(2)}, u32[]{:S(2)}) collective-permute-start(bf16[120,640]{1,0:T(8,128)(2,1)S(1)} %pad_maximum_fusion.7), channel_id=1, source_target_pairs={{0,1},{1,0},{2,3},{3,2},{4,5},{5,4},{6,7},{7,6},{8,9},{9,8},{10,11... | collective-permute-start | bytes 460808 | tf_op jit(solution)/shard_map/ppermute | solution.py:881
  16.9 1.6 collective-permute-start.4
  17.9 1.6 collective-permute-start.3
  18.4 43.5 %copy-start.1 = (f32[4,240,1024]{2,1,0:T(8,128)S(1)}, f32[4,240,1024]{2,1,0:T(8,128)}, u32[]{:S(2)}) copy-start(f32[4,240,1024]{2,1,0:T(8,128)} %base.1) | copy-start | bytes 11796484
  28.2 15.6 %collective-permute-start.7 = (bf16[368,640]{1,0:T(8,128)(2,1)S(1)}, bf16[368,640]{1,0:T(8,128)(2,1)S(1)}, u32[]{:S(2)}, u32[]{:S(2)}) collective-permute-start(bf16[368,640]{1,0:T(8,128)(2,1)S(1)} %constant_dynamic-update-slice_fusion), channel_id=1, source_target_pairs={{0,3},{1,2},{2,1},{3,0},{4,7},{5,6},{6,5},{7,4},{8,11},{9,10},{10,... | collective-permute-start | bytes 1413128 | tf_op jit(solution)/shard_map/ppermute | solution.py:881
  30.9 58.3 %copy-start.8 = (bf16[4,120,640]{2,1,0:T(8,128)(2,1)}, bf16[4,120,640]{2,1,0:T(8,128)(2,1)S(1)}, u32[]{:S(2)}) copy-start(bf16[4,120,640]{2,1,0:T(8,128)(2,1)S(1)} %pad_maximum_fusion.1.refs_0_) | copy-start | bytes 1843204
  30.9 47.1 %collective-permute-start.10 = (bf16[4,120,640]{2,1,0:T(8,128)(2,1)S(1)}, bf16[4,120,640]{2,1,0:T(8,128)(2,1)S(1)}, u32[]{:S(2)}, u32[]{:S(2)}) collective-permute-start(bf16[4,120,640]{2,1,0:T(8,128)(2,1)S(1)} %pad_maximum_fusion.1.refs_0_), channel_id=1, source_target_pairs={{0,24},{4,28},{8,16},{12,20},{16,8},{20,12},{24,0},{28,4},{1,25},{... | collective-permute-start | bytes 1843208 | tf_op jit(solution)/shard_map/ppermute | solution.py:881
  33.4 44.6 %collective-permute-start.9 = (bf16[4,120,640]{2,1,0:T(8,128)(2,1)S(1)}, bf16[4,120,640]{2,1,0:T(8,128)(2,1)S(1)}, u32[]{:S(2)}, u32[]{:S(2)}) collective-permute-start(bf16[4,120,640]{2,1,0:T(8,128)(2,1)S(1)} %pad_maximum_fusion.1.refs_0_), channel_id=1, source_target_pairs={{0,16},{4,20},{8,24},{12,28},{16,0},{20,4},{24,8},{28,12},{1,17},{... | collective-permute-start | bytes 1843208 | tf_op jit(solution)/shard_map/ppermute | solution.py:881
  33.9 44.1 %collective-permute-start.8 = (bf16[4,120,640]{2,1,0:T(8,128)(2,1)S(1)}, bf16[4,120,640]{2,1,0:T(8,128)(2,1)S(1)}, u32[]{:S(2)}, u32[]{:S(2)}) collective-permute-start(bf16[4,120,640]{2,1,0:T(8,128)(2,1)S(1)} %pad_maximum_fusion.1.refs_0_), channel_id=1, source_target_pairs={{0,8},{4,12},{8,0},{12,4},{16,24},{20,28},{24,16},{28,20},{1,9},{5... | collective-permute-start | bytes 1843208 | tf_op jit(solution)/shard_map/ppermute | solution.py:881
  34.5 34.9 %collective-permute-start.6 = (bf16[368,640]{1,0:T(8,128)(2,1)S(1)}, bf16[368,640]{1,0:T(8,128)(2,1)S(1)}, u32[]{:S(2)}, u32[]{:S(2)}) collective-permute-start(bf16[368,640]{1,0:T(8,128)(2,1)S(1)} %constant_dynamic-update-slice_fusion), channel_id=1, source_target_pairs={{0,2},{1,3},{2,0},{3,1},{4,6},{5,7},{6,4},{7,5},{8,10},{9,11},{10,... | collective-permute-start | bytes 1413128 | tf_op jit(solution)/shard_map/ppermute | solution.py:881
  43.8 34.2 %collective-permute-start.5 = (bf16[368,640]{1,0:T(8,128)(2,1)S(1)}, bf16[368,640]{1,0:T(8,128)(2,1)S(1)}, u32[]{:S(2)}, u32[]{:S(2)}) collective-permute-start(bf16[368,640]{1,0:T(8,128)(2,1)S(1)} %constant_dynamic-update-slice_fusion), channel_id=1, source_target_pairs={{0,1},{1,0},{2,3},{3,2},{4,5},{5,4},{6,7},{7,6},{8,9},{9,8},{10,11... | collective-permute-start | bytes 1413128 | tf_op jit(solution)/shard_map/ppermute | solution.py:881
  81.4 48.1 %all-to-all-start = ((bf16[4,240,1024]{2,1,0:T(8,128)(2,1)}), bf16[4,240,1024]{2,1,0:T(8,128)(2,1)S(1)}, u32[]{:S(2)}, u32[]{:S(2)}) async-start(bf16[4,240,1024]{2,1,0:T(8,128)(2,1)} %convert_element_type.378), calls=%async_computation | async-start | bytes 3932160 | tf_op jit(solution)/shard_map/all_to_all | solution.py:914
  89.2 11.9 %collective-permute-start.11 = (bf16[4,120,640]{2,1,0:T(8,128)(2,1)S(1)}, bf16[4,120,640]{2,1,0:T(8,128)(2,1)}, u32[]{:S(2)}, u32[]{:S(2)}) collective-permute-start(bf16[4,120,640]{2,1,0:T(8,128)(2,1)S(1)} %pad_maximum_fusion.1.refs_0_), channel_id=1, source_target_pairs={{0,4},{4,0},{8,12},{12,8},{16,20},{20,16},{24,28},{28,24},{1,5},{5... | collective-permute-start | bytes 1843208 | tf_op jit(solution)/shard_map/ppermute | solution.py:875
  89.3 11.9 %collective-permute-start.12 = (bf16[4,120,640]{2,1,0:T(8,128)(2,1)}, bf16[4,120,640]{2,1,0:T(8,128)(2,1)}, u32[]{:S(2)}, u32[]{:S(2)}) collective-permute-start(bf16[4,120,640]{2,1,0:T(8,128)(2,1)} %copy-done.14), channel_id=1, source_target_pairs={{0,4},{4,0},{8,12},{12,8},{16,20},{20,16},{24,28},{28,24},{1,5},{5... | collective-permute-start | bytes 1843208 | tf_op jit(solution)/shard_map/ppermute | solution.py:875
  89.8 11.4 %collective-permute-start.13 = (bf16[4,120,640]{2,1,0:T(8,128)(2,1)}, bf16[4,120,640]{2,1,0:T(8,128)(2,1)}, u32[]{:S(2)}, u32[]{:S(2)}) collective-permute-start(bf16[4,120,640]{2,1,0:T(8,128)(2,1)} %copy-done.13), channel_id=1, source_target_pairs={{0,4},{4,0},{8,12},{12,8},{16,20},{20,16},{24,28},{28,24},{1,5},{5... | collective-permute-start | bytes 1843208 | tf_op jit(solution)/shard_map/ppermute | solution.py:875
  89.9 11.3 %collective-permute-start.14 = (bf16[4,120,640]{2,1,0:T(8,128)(2,1)S(1)}, bf16[4,120,640]{2,1,0:T(8,128)(2,1)}, u32[]{:S(2)}, u32[]{:S(2)}) collective-permute-start(bf16[4,120,640]{2,1,0:T(8,128)(2,1)S(1)} %collective-permute-done.10.refs_3_), channel_id=1, source_target_pairs={{0,4},{4,0},{8,12},{12,8},{16,20},{20,16},{24,28},{28,24},{1,5},{5... | collective-permute-start | bytes 1843208 | tf_op jit(solution)/shard_map/ppermute | solution.py:875
  130.7 51.6 %all-to-all-start.1 = ((bf16[4,240,768]{2,1,0:T(8,128)(2,1)}), bf16[4,240,768]{2,1,0:T(8,128)(2,1)S(1)}, u32[]{:S(2)}, u32[]{:S(2)}) async-start(bf16[4,240,768]{2,1,0:T(8,128)(2,1)} %gather_tokens.1), calls=%async_computation.1 | async-start | bytes 2949120 | tf_op jit(solution)/shard_map/all_to_all | solution.py:914
  215.7 18.9 %collective-permute-start.15 = (bf16[4,4,128,640]{3,2,1,0:T(8,128)(2,1)}, bf16[4,4,128,640]{3,2,1,0:T(8,128)(2,1)}, u32[]{:S(2)}, u32[]{:S(2)}) collective-permute-start(bf16[4,4,128,640]{3,2,1,0:T(8,128)(2,1)} %get-tuple-element.221), channel_id=1, source_target_pairs={{0,4},{4,0},{8,12},{12,8},{16,20},{20,16},{24,28},{28,24},{1,5},{5... | collective-permute-start | bytes 7864328 | tf_op jit(solution)/shard_map/ppermute | solution.py:875
  215.7 18.9 %copy-start.4 = (bf16[4,4,128,640]{3,2,1,0:T(8,128)(2,1)S(1)}, bf16[4,4,128,640]{3,2,1,0:T(8,128)(2,1)}, u32[]{:S(2)}) copy-start(bf16[4,4,128,640]{3,2,1,0:T(8,128)(2,1)} %get-tuple-element.228) | copy-start | bytes 7864324
  238.1 32.8 %collective-permute-start.16 = (bf16[4,2,240,640]{3,2,1,0:T(8,128)(2,1)}, bf16[4,2,240,640]{3,2,1,0:T(8,128)(2,1)S(1)}, u32[]{:S(2)}, u32[]{:S(2)}) collective-permute-start(bf16[4,2,240,640]{3,2,1,0:T(8,128)(2,1)} %get-tuple-element.233), channel_id=1, source_target_pairs={{0,4},{4,0},{8,12},{12,8},{16,20},{20,16},{24,28},{28,24},{1,5},{5... | collective-permute-start | bytes 7372808 | tf_op jit(solution)/shard_map/ppermute | solution.py:875
  238.6 28.0 %collective-permute-start.17 = (bf16[4,128,640]{2,1,0:T(8,128)(2,1)}, bf16[4,128,640]{2,1,0:T(8,128)(2,1)S(1)}, u32[]{:S(2)}, u32[]{:S(2)}) collective-permute-start(bf16[4,128,640]{2,1,0:T(8,128)(2,1)} %get-tuple-element.235), channel_id=1, source_target_pairs={{0,8},{4,12},{8,0},{12,4},{16,24},{20,28},{24,16},{28,20},{1,9},{5... | collective-permute-start | bytes 1966088 | tf_op jit(solution)/shard_map/ppermute | solution.py:881
  240.1 30.8 %collective-permute-start.18 = (bf16[4,128,640]{2,1,0:T(8,128)(2,1)}, bf16[4,128,640]{2,1,0:T(8,128)(2,1)}, u32[]{:S(2)}, u32[]{:S(2)}) collective-permute-start(bf16[4,128,640]{2,1,0:T(8,128)(2,1)} %get-tuple-element.236), channel_id=1, source_target_pairs={{0,16},{4,20},{8,24},{12,28},{16,0},{20,4},{24,8},{28,12},{1,17},{... | collective-permute-start | bytes 1966088 | tf_op jit(solution)/shard_map/ppermute | solution.py:881
  241.9 29.0 %collective-permute-start.19 = (bf16[4,128,640]{2,1,0:T(8,128)(2,1)}, bf16[4,128,640]{2,1,0:T(8,128)(2,1)}, u32[]{:S(2)}, u32[]{:S(2)}) collective-permute-start(bf16[4,128,640]{2,1,0:T(8,128)(2,1)} %get-tuple-element.237), channel_id=1, source_target_pairs={{0,24},{4,28},{8,16},{12,20},{16,8},{20,12},{24,0},{28,4},{1,25},{... | collective-permute-start | bytes 1966088 | tf_op jit(solution)/shard_map/ppermute | solution.py:881
  274.7 17.8 %collective-permute-start.23 = (bf16[4,2,240,640]{3,2,1,0:T(8,128)(2,1)}, bf16[4,2,240,640]{3,2,1,0:T(8,128)(2,1)}, u32[]{:S(2)}, u32[]{:S(2)}) collective-permute-start(bf16[4,2,240,640]{3,2,1,0:T(8,128)(2,1)} %get-tuple-element.265), channel_id=1, source_target_pairs={{0,4},{4,0},{8,12},{12,8},{16,20},{20,16},{24,28},{28,24},{1,5},{5... | collective-permute-start | bytes 7372808 | tf_op jit(solution)/shard_map/ppermute | solution.py:875
  274.7 40.8 %all-to-all-start.2 = ((bf16[4,240,768]{2,1,0:T(8,128)(2,1)}), bf16[4,240,768]{2,1,0:T(8,128)(2,1)S(1)}, u32[]{:S(2)}, u32[]{:S(2)}) async-start(bf16[4,240,768]{2,1,0:T(8,128)(2,1)} %bitcast.117), calls=%async_computation.2 | async-start | bytes 2949120 | tf_op jit(solution)/shard_map/all_to_all | solution.py:921
  279.9 35.5 %collective-permute-start.20 = (bf16[2,240,640]{2,1,0:T(8,128)(2,1)}, bf16[2,240,640]{2,1,0:T(8,128)(2,1)}, u32[]{:S(2)}, u32[]{:S(2)}) collective-permute-start(bf16[2,240,640]{2,1,0:T(8,128)(2,1)} %get-tuple-element.258), channel_id=1, source_target_pairs={{0,8},{4,12},{8,0},{12,4},{16,24},{20,28},{24,16},{28,20},{1,9},{5... | collective-permute-start | bytes 1843208 | tf_op jit(solution)/shard_map/ppermute | solution.py:881
  281.3 34.2 %collective-permute-start.21 = (bf16[2,240,640]{2,1,0:T(8,128)(2,1)}, bf16[2,240,640]{2,1,0:T(8,128)(2,1)}, u32[]{:S(2)}, u32[]{:S(2)}) collective-permute-start(bf16[2,240,640]{2,1,0:T(8,128)(2,1)} %get-tuple-element.259), channel_id=1, source_target_pairs={{0,16},{4,20},{8,24},{12,28},{16,0},{20,4},{24,8},{28,12},{1,17},{... | collective-permute-start | bytes 1843208 | tf_op jit(solution)/shard_map/ppermute | solution.py:881
  282.1 33.4 %collective-permute-start.22 = (bf16[2,240,640]{2,1,0:T(8,128)(2,1)}, bf16[2,240,640]{2,1,0:T(8,128)(2,1)}, u32[]{:S(2)}, u32[]{:S(2)}) collective-permute-start(bf16[2,240,640]{2,1,0:T(8,128)(2,1)} %get-tuple-element.260), channel_id=1, source_target_pairs={{0,24},{4,28},{8,16},{12,20},{16,8},{20,12},{24,0},{28,4},{1,25},{... | collective-permute-start | bytes 1843208 | tf_op jit(solution)/shard_map/ppermute | solution.py:881
  317.8 46.5 %collective-permute-start.26 = (bf16[2,240,640]{2,1,0:T(8,128)(2,1)}, bf16[2,240,640]{2,1,0:T(8,128)(2,1)S(1)}, u32[]{:S(2)}, u32[]{:S(2)}) collective-permute-start(bf16[2,240,640]{2,1,0:T(8,128)(2,1)} %get-tuple-element.293), channel_id=1, source_target_pairs={{0,8},{4,12},{8,0},{12,4},{16,24},{20,28},{24,16},{28,20},{1,9},{5... | collective-permute-start | bytes 1843208 | tf_op jit(solution)/shard_map/ppermute | solution.py:881
  319.2 45.2 %collective-permute-start.27 = (bf16[2,240,640]{2,1,0:T(8,128)(2,1)}, bf16[2,240,640]{2,1,0:T(8,128)(2,1)S(1)}, u32[]{:S(2)}, u32[]{:S(2)}) collective-permute-start(bf16[2,240,640]{2,1,0:T(8,128)(2,1)} %get-tuple-element.294), channel_id=1, source_target_pairs={{0,16},{4,20},{8,24},{12,28},{16,0},{20,4},{24,8},{28,12},{1,17},{... | collective-permute-start | bytes 1843208 | tf_op jit(solution)/shard_map/ppermute | solution.py:881
  320.0 44.3 %collective-permute-start.28 = (bf16[2,240,640]{2,1,0:T(8,128)(2,1)}, bf16[2,240,640]{2,1,0:T(8,128)(2,1)S(1)}, u32[]{:S(2)}, u32[]{:S(2)}) collective-permute-start(bf16[2,240,640]{2,1,0:T(8,128)(2,1)} %get-tuple-element.295), channel_id=1, source_target_pairs={{0,24},{4,28},{8,16},{12,20},{16,8},{20,12},{24,0},{28,4},{1,25},{... | collective-permute-start | bytes 1843208 | tf_op jit(solution)/shard_map/ppermute | solution.py:881
  323.0 31.9 %collective-permute-start.24 = (bf16[368,640]{1,0:T(8,128)(2,1)}, bf16[368,640]{1,0:T(8,128)(2,1)S(1)}, u32[]{:S(2)}, u32[]{:S(2)}) collective-permute-start(bf16[368,640]{1,0:T(8,128)(2,1)} %pad_maximum_fusion.2), channel_id=1, source_target_pairs={{0,3},{1,2},{2,1},{3,0},{4,7},{5,6},{6,5},{7,4},{8,11},{9,10},{10,... | collective-permute-start | bytes 1413128 | tf_op jit(solution)/shard_map/ppermute | solution.py:881
  325.2 39.2 %collective-permute-start.25 = (bf16[368,640]{1,0:T(8,128)(2,1)}, bf16[368,640]{1,0:T(8,128)(2,1)}, u32[]{:S(2)}, u32[]{:S(2)}) collective-permute-start(bf16[368,640]{1,0:T(8,128)(2,1)} %pad_maximum_fusion.3), channel_id=1, source_target_pairs={{0,2},{1,3},{2,0},{3,1},{4,6},{5,7},{6,4},{7,5},{8,10},{9,11},{10,... | collective-permute-start | bytes 1413128 | tf_op jit(solution)/shard_map/ppermute | solution.py:881
  368.0 10.3 %collective-permute-start.29 = (bf16[368,640]{1,0:T(8,128)(2,1)S(1)}, bf16[368,640]{1,0:T(8,128)(2,1)S(1)}, u32[]{:S(2)}, u32[]{:S(2)}) collective-permute-start(bf16[368,640]{1,0:T(8,128)(2,1)S(1)} %pad_maximum_fusion.4), channel_id=1, source_target_pairs={{0,1},{1,0},{2,3},{3,2},{4,5},{5,4},{6,7},{7,6},{8,9},{9,8},{10,11... | collective-permute-start | bytes 1413128 | tf_op jit(solution)/shard_map/ppermute | solution.py:881
  379.2 14.0 %collective-permute-start.30 = (bf16[4,4,128,640]{3,2,1,0:T(8,128)(2,1)}, bf16[4,4,128,640]{3,2,1,0:T(8,128)(2,1)}, u32[]{:S(2)}, u32[]{:S(2)}) collective-permute-start(bf16[4,4,128,640]{3,2,1,0:T(8,128)(2,1)} %get-tuple-element.434), channel_id=1, source_target_pairs={{0,4},{4,0},{8,12},{12,8},{16,20},{20,16},{24,28},{28,24},{1,5},{5... | collective-permute-start | bytes 7864328 | tf_op jit(solution)/shard_map/ppermute | solution.py:875
  379.2 58.0 %all-to-all-start.3 = ((bf16[4,240,1024]{2,1,0:T(8,128)(2,1)}), bf16[4,240,1024]{2,1,0:T(8,128)(2,1)S(1)}, u32[]{:S(2)}, u32[]{:S(2)}) async-start(bf16[4,240,1024]{2,1,0:T(8,128)(2,1)} %bitcast.114), calls=%async_computation.3 | async-start | bytes 3932160 | tf_op jit(solution)/shard_map/all_to_all | solution.py:921
  391.3 8.4 %collective-permute-start.38 = (bf16[128,320]{1,0:T(8,128)(2,1)S(1)}, bf16[128,320]{1,0:T(8,128)(2,1)S(1)}, u32[]{:S(2)}, u32[]{:S(2)}) collective-permute-start(bf16[128,320]{1,0:T(8,128)(2,1)S(1)} %select_convert_fusion.1), channel_id=1, source_target_pairs={{0,4},{4,0},{8,12},{12,8},{16,20},{20,16},{24,28},{28,24},{1,5},{5... | collective-permute-start | bytes 245768 | tf_op jit(solution)/shard_map/ppermute | solution.py:875
  392.9 8.0 %collective-permute-start.37 = (bf16[120,640]{1,0:T(8,128)(2,1)S(1)}, bf16[120,640]{1,0:T(8,128)(2,1)S(1)}, u32[]{:S(2)}, u32[]{:S(2)}) collective-permute-start(bf16[120,640]{1,0:T(8,128)(2,1)S(1)} %select_convert_fusion), channel_id=1, source_target_pairs={{0,4},{4,0},{8,12},{12,8},{16,20},{20,16},{24,28},{28,24},{1,5},{5... | collective-permute-start | bytes 460808 | tf_op jit(solution)/shard_map/ppermute | solution.py:875
  396.3 17.9 %collective-permute-start.31 = (bf16[4,128,640]{2,1,0:T(8,128)(2,1)}, bf16[4,128,640]{2,1,0:T(8,128)(2,1)}, u32[]{:S(2)}, u32[]{:S(2)}) collective-permute-start(bf16[4,128,640]{2,1,0:T(8,128)(2,1)} %get-tuple-element.396), channel_id=1, source_target_pairs={{0,8},{4,12},{8,0},{12,4},{16,24},{20,28},{24,16},{28,20},{1,9},{5... | collective-permute-start | bytes 1966088 | tf_op jit(solution)/shard_map/ppermute | solution.py:881
  397.6 31.1 %collective-permute-start.33 = (bf16[4,128,640]{2,1,0:T(8,128)(2,1)}, bf16[4,128,640]{2,1,0:T(8,128)(2,1)}, u32[]{:S(2)}, u32[]{:S(2)}) collective-permute-start(bf16[4,128,640]{2,1,0:T(8,128)(2,1)} %get-tuple-element.397), channel_id=1, source_target_pairs={{0,24},{4,28},{8,16},{12,20},{16,8},{20,12},{24,0},{28,4},{1,25},{... | collective-permute-start | bytes 1966088 | tf_op jit(solution)/shard_map/ppermute | solution.py:881
  399.3 30.7 %collective-permute-start.32 = (bf16[4,128,640]{2,1,0:T(8,128)(2,1)}, bf16[4,128,640]{2,1,0:T(8,128)(2,1)}, u32[]{:S(2)}, u32[]{:S(2)}) collective-permute-start(bf16[4,128,640]{2,1,0:T(8,128)(2,1)} %get-tuple-element.398), channel_id=1, source_target_pairs={{0,16},{4,20},{8,24},{12,28},{16,0},{20,4},{24,8},{28,12},{1,17},{... | collective-permute-start | bytes 1966088 | tf_op jit(solution)/shard_map/ppermute | solution.py:881
  433.0 9.2 %collective-permute-start.34 = (bf16[128,640]{1,0:T(8,128)(2,1)}, bf16[128,640]{1,0:T(8,128)(2,1)S(1)}, u32[]{:S(2)}, u32[]{:S(2)}) collective-permute-start(bf16[128,640]{1,0:T(8,128)(2,1)} %get-tuple-element.413), channel_id=1, source_target_pairs={{0,1},{1,0},{2,3},{3,2},{4,5},{5,4},{6,7},{7,6},{8,9},{9,8},{10,11... | collective-permute-start | bytes 491528 | tf_op jit(solution)/shard_map/ppermute | solution.py:881
  434.8 9.7 %collective-permute-start.36 = (bf16[128,640]{1,0:T(8,128)(2,1)S(1)}, bf16[128,640]{1,0:T(8,128)(2,1)S(1)}, u32[]{:S(2)}, u32[]{:S(2)}) collective-permute-start(bf16[128,640]{1,0:T(8,128)(2,1)S(1)} %get-tuple-element.414), channel_id=1, source_target_pairs={{0,3},{1,2},{2,1},{3,0},{4,7},{5,6},{6,5},{7,4},{8,11},{9,10},{10,... | collective-permute-start | bytes 491528 | tf_op jit(solution)/shard_map/ppermute | solution.py:881
  437.2 12.6 %collective-permute-start.35 = (bf16[128,640]{1,0:T(8,128)(2,1)S(1)}, bf16[128,640]{1,0:T(8,128)(2,1)S(1)}, u32[]{:S(2)}, u32[]{:S(2)}) collective-permute-start(bf16[128,640]{1,0:T(8,128)(2,1)S(1)} %get-tuple-element.415), channel_id=1, source_target_pairs={{0,2},{1,3},{2,0},{3,1},{4,6},{5,7},{6,4},{7,5},{8,10},{9,11},{10,... | collective-permute-start | bytes 491528 | tf_op jit(solution)/shard_map/ppermute | solution.py:881
  (22 other events, 123.7 us)
Sparse Core Ops, SparseCore 0:
  81.5 82.4 all-gather.2

commit v5 on v4

--- a/solution.py
+++ b/solution.py
@@ -18,6 +18,7 @@
 ROPE_BASE = 10000.0
 NEG = -1e30
 VECTOR_ROWS = 8
+LANES = 128
 
 BF = jnp.bfloat16
 F32 = jnp.float32
@@ -95,72 +96,99 @@
     )(values, rank_column)
 
 
-def scatter_body(base, values, rank, out):
-    chosen = pick_rows(rank[0], values.shape[2])
-    out[0] = base[0] + dot_nn(values[0], chosen)
-
-
-def scatter_tokens(base, values, rank_row):
+def scatter_body(who, base, rank, *refs):
+    *pieces, out = refs
+    chosen = pick_rows(rank[0], pieces[0].shape[1])
+    count = len(pieces)
+    for k, piece in enumerate(pieces):
+
+        @pl.when((pl.program_id(0) ^ lax.rem(who[0], count)) == k)
+        def _():
+            out[0] = base[0] + dot_nn(piece[...], chosen)
+
+
+def scatter_tokens(who, base, pieces, rank_row):
     count, width, length = base.shape
-    picks = values.shape[2]
+    picks = pieces[0].shape[1]
     return pl.pallas_call(
         scatter_body,
-        grid=(count,),
-        in_specs=[
-            pl.BlockSpec((1, width, length), lambda i: (i, 0, 0)),
-            pl.BlockSpec((1, width, picks), lambda i: (i, 0, 0)),
-            pl.BlockSpec((1, 1, length), lambda i: (i, 0, 0)),
-        ],
-        out_specs=pl.BlockSpec((1, width, length), lambda i: (i, 0, 0)),
+        grid_spec=pltpu.PrefetchScalarGridSpec(
+            num_scalar_prefetch=1,
+            grid=(count,),
+            in_specs=[
+                pl.BlockSpec((1, width, length), lambda i, who: (i, 0, 0)),
+                pl.BlockSpec((1, 1, length), lambda i, who: (i, 0, 0)),
+            ]
+            + [whole((width, picks))] * count,
+            out_specs=pl.BlockSpec((1, width, length), lambda i, who: (i, 0, 0)),
+        ),
         out_shape=struct(base.shape, F32),
         compiler_params=params(),
         cost_estimate=cost(2 * count * width * length * picks, 10 * base.size),
         name="scatter_tokens",
-    )(base, values, rank_row)
-
-
-def project_body(who, x, rank, gain, router, cos_k, sin_k, cos_q, sin_q, *refs):
-    pieces = refs[:-12]
-    (
-        picked, prob, q_out, kt_out, k_out, vt_out, v_out, w,
-        normed, normed_picked, q_raw, kv_raw,
-    ) = refs[-12:]
+    )(who, base, rank_row, *pieces)
+
+
+def join_body(who, *refs):
+    *pieces, w = refs
+    even = who[2] == 0
+    count = len(pieces) // 2
+    for k, (own, other) in enumerate(zip(pieces[:count], pieces[count:])):
+        first, second = own[0].astype(F32), other[0].astype(F32)
+        both = [jnp.where(even, first, second), jnp.where(even, second, first)]
+        height = 2 * first.shape[0]
+        place = pl.ds(pl.multiple_of((who[1] ^ k) * height, 16), height)
+        w[0, place] = jnp.concatenate(both, axis=0).astype(BF)
+
+
+def join(who, own, other):
+    blocks, height, part = own[0].shape
+    width = 2 * len(own) * height
+    piece = pl.BlockSpec((1, height, part), lambda i, who: (i, 0, 0))
+    return pl.pallas_call(
+        join_body,
+        grid_spec=pltpu.PrefetchScalarGridSpec(
+            num_scalar_prefetch=1,
+            grid=(blocks,),
+            in_specs=[piece] * (2 * len(own)),
+            out_specs=pl.BlockSpec((1, width, part), lambda i, who: (i ^ who[0], 0, 0)),
+        ),
+        out_shape=struct((blocks, width, part), BF),
+        compiler_params=params(),
+        cost_estimate=cost(0, 4 * blocks * width * part),
+        name="join",
+    )(who, *own, *other)
+
+
+def project_body(
+    x, rank, gain, router, cos_k, sin_k, cos_q, sin_q, w,
+    picked, prob, q_out, kt_out, k_out, vt_out, v_out,
+    normed, normed_picked, q_raw, kv_raw,
+):
     step = pl.program_id(0)
-    block = step ^ who[0]
     width = x.shape[0]
     q_part = width // pl.num_programs(0)
     kv_part = KVH * HD // pl.num_programs(0)
-    if len(pieces) == 1:
-        w[0] = pieces[0][0]
-    else:
-        even = who[2] == 0
-        count = len(pieces) // 2
-        for k, (own, other) in enumerate(zip(pieces[:count], pieces[count:])):
-            first, second = own[0].astype(F32), other[0].astype(F32)
-            both = [jnp.where(even, first, second), jnp.where(even, second, first)]
-            height = 2 * first.shape[0]
-            place = pl.ds(pl.multiple_of((who[1] ^ k) * height, 16), height)
-            w[0, place] = jnp.concatenate(both, axis=0).astype(BF)
 
     @pl.when(step == 0)
     def _():
         full = x[...].astype(F32)
         inverse = lax.rsqrt(jnp.sum(full * full, axis=0, keepdims=True) / width + EPSILON)
-        normed[...] = (full * inverse * gain[...]).astype(BF)
-        chosen = pick_columns(rank[...], picked.shape[1])
+        normed[...] = (full * inverse * gain[:, :1]).astype(BF)
+        chosen = pick_columns(rank[:, :1], picked.shape[1])
         part = dot_nn(x[...], chosen)
         picked[...] = part.astype(BF)
         inverse = lax.rsqrt(jnp.sum(part * part, axis=0, keepdims=True) / width + EPSILON)
-        normed_picked[...] = (part * inverse * gain[...]).astype(BF)
-        logit = jnp.sum(part * router[...], axis=0, keepdims=True)
+        normed_picked[...] = (part * inverse * gain[:, :1]).astype(BF)
+        logit = jnp.sum(part * router[:, :1], axis=0, keepdims=True)
         prob[...] = jax.nn.sigmoid(logit)
 
-    q_raw[pl.ds(pl.multiple_of(block * q_part, 8), q_part)] = dot_tn(
+    q_raw[pl.ds(pl.multiple_of(step * q_part, 8), q_part)] = dot_tn(
         w[0, :, :q_part], normed_picked[...]
     ).astype(BF)
     kv = dot_tn(w[0, :, q_part : q_part + 2 * kv_part], normed[...]).astype(BF)
-    kv_raw[0, pl.ds(pl.multiple_of(block * kv_part, 8), kv_part)] = kv[:kv_part]
-    kv_raw[1, pl.ds(pl.multiple_of(block * kv_part, 8), kv_part)] = kv[kv_part:]
+    kv_raw[0, pl.ds(pl.multiple_of(step * kv_part, 8), kv_part)] = kv[:kv_part]
+    kv_raw[1, pl.ds(pl.multiple_of(step * kv_part, 8), kv_part)] = kv[kv_part:]
 
     @pl.when(step == pl.num_programs(0) - 1)
     def _():
@@ -190,28 +218,26 @@
             v_out[head] = value.astype(F32).T.astype(BF)
 
 
-def project(who, x, rank_column, gain, router, tables_k, tables_q, pieces):
+def project(x, rank_column, gain, router, tables_k, tables_q, w):
     width, length = x.shape
     picks = tables_q[0].shape[1]
-    blocks, height, part = pieces[0].shape
+    blocks, _, part = w.shape
     kv = KVH * HD
     half = HD // 2
     return pl.pallas_call(
         project_body,
-        grid_spec=pltpu.PrefetchScalarGridSpec(
-        num_scalar_prefetch=1,
         grid=(blocks,),
         in_specs=[
             whole((width, length)),
-            whole((length, 1)),
-            whole((width, 1)),
-            whole((width, 1)),
+            whole((length, LANES)),
+            whole((width, LANES)),
+            whole((width, LANES)),
             whole((half, length)),
             whole((half, length)),
             whole((half, picks)),
             whole((half, picks)),
-        ]
-        + [pl.BlockSpec((1, height, part), lambda i, who: (i, 0, 0))] * len(pieces),
+            pl.BlockSpec((1, width, part), lambda i: (i, 0, 0)),
+        ],
         out_specs=[
             whole((width, picks)),
             whole((1, picks)),
@@ -220,7 +246,6 @@
             whole((KVH, length, HD)),
             whole((kv, length)),
             whole((KVH, length, HD)),
-            pl.BlockSpec((1, width, part), lambda i, who: (i ^ who[0], 0, 0)),
         ],
         scratch_shapes=[
             pltpu.VMEM((width, length), BF),
@@ -228,7 +253,6 @@
             pltpu.VMEM((width, picks), BF),
             pltpu.VMEM((2, kv, length), BF),
         ],
-        ),
         out_shape=[
             struct((width, picks), BF),
             struct((1, picks), F32),
@@ -237,7 +261,6 @@
             struct((KVH, length, HD), BF),
             struct((kv, length), BF),
             struct((KVH, length, HD), BF),
-            struct((blocks, width, part), BF),
         ],
         compiler_params=params(),
         cost_estimate=cost(
@@ -245,7 +268,7 @@
             2 * (2 * blocks * width * part + 4 * x.size),
         ),
         name="project",
-    )(who, x, rank_column, gain, router, *tables_k, *tables_q, *pieces)
+    )(x, rank_column, gain, router, *tables_k, *tables_q, w)
 
 
 def reach_of(block, length, picks):
@@ -410,7 +433,7 @@
     def _():
         inverse = lax.rsqrt(square[...] / width + EPSILON)
         inverse_out[...] = inverse
-        normed[...] = (hidden[...] * inverse * gain[...]).astype(BF)
+        normed[...] = (hidden[...] * inverse * gain[:, :1]).astype(BF)
 
 
 def merge(mixed, picked, gain, w):
@@ -423,7 +446,7 @@
         in_specs=[
             whole((width, picks)),
             whole((width, picks)),
-            whole((width, 1)),
+            whole((width, LANES)),
             pl.BlockSpec((1, width, wide), lambda i: (i, 0, 0)),
         ],
         out_specs=[
@@ -655,11 +678,11 @@
         inv = inverse[...]
         grad_norm = backward[...]
         gain_out[...] = jnp.sum(grad_norm * merged * inv, axis=1, keepdims=True)
-        unit = grad_norm * gain[...]
+        unit = grad_norm * gain[:, :1]
         along = jnp.sum(unit * merged, axis=0, keepdims=True) / width
         grad_hidden = inv * unit - merged * (inv * inv * inv * along)
         grad_attn[...] = (grad_hidden + share * cot_full).astype(BF)
-        rest_out[...] = (grad_hidden + slope * router[...]).astype(BF)
+        rest_out[...] = (grad_hidden + slope * router[:, :1]).astype(BF)
 
 
 def ffn_back(who, first, count, last, pieces, normed, grad_ffn, gate, up, sources, carried, tail):
@@ -673,7 +696,7 @@
     tall_shape = struct((pieces, count, height, hidden), BF)
     low, thin = struct((width, picks), BF), struct((width, 1), F32)
     extra = ([carried] if first else []) + (list(tail) if last else [])
-    extra_specs = ([full] if first else []) + ([full] * 4 + [row] * 2 + [column] * 2 if last else [])
+    extra_specs = ([full] if first else []) + ([full] * 4 + [row] * 2 + [whole((width, LANES))] * 2 if last else [])
     return pl.pallas_call(
         functools.partial(ffn_back_body, first, gate.shape[0], last, len(sources)),
         grid_spec=pltpu.PrefetchScalarGridSpec(
@@ -733,16 +756,22 @@
     )(mixed, grad, w)
 
 
-def project_back_body(x, rank, gain, *refs):
+def mixing_grad_body(
+    who, x, rank, gain, *refs
+):
     gq, gk, gv, refs = refs[:2], refs[2:4], refs[4:6], refs[6:]
-    rest, w, out, grads_out, gain_out, gq_full, gkv_full, total = refs
+    gw_out, w, keep, send, grads_out, gain_out, normed, gq_full, gkv_full = refs
     step = pl.program_id(0)
     width = x.shape[0]
     q_part = width // pl.num_programs(0)
     kv_part = KVH * HD // pl.num_programs(0)
+    even = who[2] == 0
 
     @pl.when(step == 0)
     def _():
+        full = x[...].astype(F32)
+        inverse = lax.rsqrt(jnp.sum(full * full, axis=0, keepdims=True) / width + EPSILON)
+        normed[...] = (full * inverse * gain[:, :1]).astype(BF)
         chosen = pick_rows(rank[...], gq[0].shape[1])
         at = 0
         for piece in gq:
@@ -753,7 +782,6 @@
             for piece in pieces:
                 gkv_full[i, at : at + piece.shape[0]] = piece[...]
                 at += piece.shape[0]
-        total[...] = jnp.zeros_like(total)
 
     q_rows = pl.ds(pl.multiple_of(step * q_part, 8), q_part)
     kv_rows = pl.ds(pl.multiple_of(step * kv_part, 8), kv_part)
@@ -761,73 +789,11 @@
         [gq_full[q_rows, :], gkv_full[0, kv_rows, :], gkv_full[1, kv_rows, :]], axis=0
     )
     grads_out[0] = grads
-    total[...] += dot_nn(w[0, :, : grads.shape[0]], grads)
-
-    @pl.when(step == pl.num_programs(0) - 1)
-    def _():
-        full = x[...].astype(F32)
-        inv = lax.rsqrt(jnp.sum(full * full, axis=0, keepdims=True) / width + EPSILON)
-        grad_norm = total[...]
-        gain_out[...] = jnp.sum(grad_norm * full * inv, axis=1, keepdims=True)
-        unit = grad_norm * gain[...]
-        along = jnp.sum(unit * full, axis=0, keepdims=True) / width
-        chosen = pick_rows(rank[...], rest.shape[1])
-        out[...] = (
-            inv * unit - full * (inv * inv * inv * along) + dot_nn(rest[...], chosen)
-        ).astype(BF)
-
-
-def project_back(x, rank_row, gain, gq, gk, gv, rest, w):
-    width, length = x.shape
-    picks = rest.shape[1]
-    blocks = w.shape[0]
-    kv = KVH * HD
-    part = (width + 2 * kv) // blocks
-    return pl.pallas_call(
-        project_back_body,
-        grid=(blocks,),
-        in_specs=[
-            whole((width, length)),
-            whole((1, length)),
-            whole((width, 1)),
-            *(whole(piece.shape) for piece in (*gq, *gk, *gv)),
-            whole((width, picks)),
-            pl.BlockSpec((1,) + w.shape[1:], lambda i: (i, 0, 0)),
-        ],
-        out_specs=[
-            whole((width, length)),
-            pl.BlockSpec((1, part, length), lambda i: (i, 0, 0)),
-            whole((width, 1)),
-        ],
-        out_shape=[
-            struct((width, length), BF),
-            struct((blocks, part, length), BF),
-            struct((width, 1), F32),
-        ],
-        scratch_shapes=[
-            pltpu.VMEM((width, length), BF),
-            pltpu.VMEM((2, kv, length), BF),
-            pltpu.VMEM((width, length), F32),
-        ],
-        compiler_params=params(),
-        cost_estimate=cost(
-            2 * width * length * (2 * picks + blocks * part), 10 * x.size + 2 * w.size
-        ),
-        name="project_back",
-    )(x, rank_row, gain, *gq, *gk, *gv, rest, w)
-
-
-def mixing_grad_body(who, x, gain, grads, gw_out, keep, send, normed):
-    width = x.shape[0]
-    even = who[2] == 0
-
-    @pl.when(pl.program_id(0) == 0)
-    def _():
-        full = x[...].astype(F32)
-        inverse = lax.rsqrt(jnp.sum(full * full, axis=0, keepdims=True) / width + EPSILON)
-        normed[...] = (full * inverse * gain[...]).astype(BF)
-
-    value = dot_nt(normed[...], grads[0])
+    value = dot_nt(normed[...], grads)
+    share = jnp.sum(
+        value * w[0, :, : grads.shape[0]].astype(F32), axis=1, keepdims=True
+    ) / gain[:, :1]
+    gain_out[...] = jnp.where(step == 0, share, gain_out[...] + share)
     value = jnp.concatenate([value, gw_out[0].astype(F32)], axis=1)
     pairs = keep.shape[0]
     rows = width // (2 * pairs)
@@ -838,10 +804,12 @@
         send[pair ^ who[1], 0, :rows] = jnp.where(even, high, low).astype(BF)
 
 
-def mixing_grad(who, x, gain, grads, gw_out, pairs):
+def mixing_grad(who, x, rank_row, gain, gq, gk, gv, gw_out, w, pairs):
     width, length = x.shape
-    blocks, part, _ = grads.shape
-    out_part = gw_out.shape[2]
+    picks = gq[0].shape[1]
+    blocks, _, out_part = gw_out.shape
+    kv = KVH * HD
+    part = (width + 2 * kv) // blocks
     rows = width // (2 * pairs) + VECTOR_ROWS
     split = pl.BlockSpec((pairs, 1, rows, part + out_part), lambda i, who: (0, i ^ who[0], 0, 0))
     split_shape = struct((pairs, blocks, rows, part + out_part), BF)
@@ -852,18 +820,86 @@
             grid=(blocks,),
             in_specs=[
                 whole((width, length)),
+                whole((1, length)),
+                whole((width, LANES)),
+                *(whole(piece.shape) for piece in (*gq, *gk, *gv)),
+                pl.BlockSpec((1, width, out_part), lambda i, who: (i, 0, 0)),
+                pl.BlockSpec((1,) + w.shape[1:], lambda i, who: (i, 0, 0)),
+            ],
+            out_specs=[
+                split,
+                split,
+                pl.BlockSpec((1, part, length), lambda i, who: (i, 0, 0)),
                 whole((width, 1)),
-                pl.BlockSpec((1, part, length), lambda i, who: (i, 0, 0)),
-                pl.BlockSpec((1, width, out_part), lambda i, who: (i, 0, 0)),
             ],
-            out_specs=[split, split],
-            scratch_shapes=[pltpu.VMEM((width, length), BF)],
+            scratch_shapes=[
+                pltpu.VMEM((width, length), BF),
+                pltpu.VMEM((width, length), BF),
+                pltpu.VMEM((2, kv, length), BF),
+            ],
         ),
-        out_shape=[split_shape, split_shape],
+        out_shape=[
+            split_shape,
+            split_shape,
+            struct((blocks, part, length), BF),
+            struct((width, 1), F32),
+        ],
         compiler_params=params(),
-        cost_estimate=cost(2 * width * length * blocks * part, 10 * x.size),
+        cost_estimate=cost(2 * width * length * (picks + width + 2 * kv), 10 * x.size),
         name="mixing_grad",
-    )(who, x, gain, grads, gw_out)
+    )(who, x, rank_row, gain, *gq, *gk, *gv, gw_out, w)
+
+
+def project_back_body(x, rank, gain, grads, rest, w, out, total):
+    step = pl.program_id(0)
+    width = x.shape[0]
+    part = grads.shape[1]
+
+    @pl.when(step == 0)
+    def _():
+        total[...] = jnp.zeros_like(total)
+
+    total[...] += dot_nn(w[0, :, :part], grads[0])
+
+    @pl.when(step == pl.num_programs(0) - 1)
+    def _():
+        full = x[...].astype(F32)
+        inv = lax.rsqrt(jnp.sum(full * full, axis=0, keepdims=True) / width + EPSILON)
+        grad_norm = total[...]
+        unit = grad_norm * gain[:, :1]
+        along = jnp.sum(unit * full, axis=0, keepdims=True) / width
+        chosen = pick_rows(rank[...], rest.shape[1])
+        out[...] = (
+            inv * unit - full * (inv * inv * inv * along) + dot_nn(rest[...], chosen)
+        ).astype(BF)
+
+
+def project_back(x, rank_row, gain, grads, rest, w):
+    width, length = x.shape
+    picks = rest.shape[1]
+    blocks, part, _ = grads.shape
+    return pl.pallas_call(
+        project_back_body,
+        grid=(blocks,),
+        in_specs=[
+            whole((width, length)),
+            whole((1, length)),
+            whole((width, LANES)),
+            pl.BlockSpec((1, part, length), lambda i: (i, 0, 0)),
+            whole((width, picks)),
+            pl.BlockSpec((1,) + w.shape[1:], lambda i: (i, 0, 0)),
+        ],
+        out_specs=whole((width, length)),
+        out_shape=struct((width, length), BF),
+        scratch_shapes=[pltpu.VMEM((width, length), F32)],
+        compiler_params=params(),
+        cost_estimate=cost(2 * width * length * (picks + blocks * part), 10 * x.size + 2 * w.size),
+        name="project_back",
+    )(x, rank_row, gain, grads, rest, w)
+
+
+def columns(value):
+    return jnp.broadcast_to(value[:, None], (value.shape[0], LANES))
 
 
 def hold(*values):
@@ -997,21 +1033,27 @@
     limit = jnp.maximum(spot, prefix_len - 1)[None, :]
     tables_k = rope_tables(every)
     tables_q = rope_tables(spot)
-    gain_one, gain_two, router = norm1_gain[:, None], norm2_gain[:, None], router[:, None]
+    gain_one, gain_two, router = columns(norm1_gain), columns(norm2_gain), columns(router)
     cot = gather_tokens(cotangent, ranks[:, :, None], picks)
 
-    x, mixing_other, mixing, cot, limit, tables_k, tables_q = hold(
-        to_owner(x), [swap(piece) for piece in mixing], mixing, cot, limit, tables_k, tables_q
-    )
-    cot = to_owner(cot)
+    mixing_other, mixing, rank_column, gain_one, gain_two, router = hold(
+        [swap(piece) for piece in mixing], mixing, columns(rank), gain_one, gain_two, router
+    )
     if aligned:
-        mixing = mixing + mixing_other
+        mixing = join(who, mixing, mixing_other)
     else:
         order = jnp.arange(pairs) ^ own_pair_index
         mixing = jnp.stack([jnp.stack(mixing), jnp.stack(mixing_other)])[jnp.stack([core, 1 - core])]
-        mixing = [mixing[:, order].transpose(2, 1, 0, 3, 4).reshape(col_count, width, mixing_part)]
-    picked, prob, q, kt, k, vt, v, mixing = project(
-        who, x, rank[:, None], gain_one, router, tables_k, tables_q, mixing
+        mixing = mixing[:, order].transpose(2, 1, 0, 3, 4).reshape(col_count, width, mixing_part)
+        mixing = mixing[jnp.arange(col_count) ^ column]
+    (
+        x, mixing, cot, limit, tables_k, tables_q, rank_column, gain_one, gain_two, router,
+    ) = hold(
+        to_owner(x), mixing, cot, limit, tables_k, tables_q, rank_column, gain_one, gain_two, router
+    )
+    cot = to_owner(cot)
+    picked, prob, q, kt, k, vt, v = project(
+        x, rank_column, gain_one, router, tables_k, tables_q, mixing
     )
     mixed, mass = attend(q, k, vt, limit)
     (branch, inverse, normed), cot = hold(merge(mixed, picked, gain_two, mixing), cot)
@@ -1020,7 +1062,11 @@
     (keep_down, send_down), delta, gate = hold(
         down_grad(who, grad_ffn, active, pairs, col_count), delta, gate
     )
-    delta = from_owner(delta, sequences)
+    delta = [
+        lax.dynamic_slice_in_dim(delta, (column ^ k) * part, part, 0) for k in range(sequences)
+    ]
+    delta, keep_down, send_down = hold(delta, keep_down, send_down)
+    delta = [partner(value, "col", k) if k else value for k, value in enumerate(delta)]
     pieces = pairs if aligned else 1
     back_args = (pieces, normed, grad_ffn, gate, up, sources)
     tail = (branch, both, picked, cot, prob, inverse, gain_two, router)
@@ -1031,17 +1077,22 @@
         value = value[0].reshape(half, pairs, 2 * rows, hidden).transpose(1, 0, 2, 3)
         return value[jnp.arange(pairs) ^ own_pair_index]
 
-    got_down, (keep_low, send_low, carried), keep_down = hold(
-        swap(send_down), ffn_back(who, 0, half, False, *back_args, None, None), keep_down
-    )
+    got_down, (keep_low, send_low, carried), keep_down, near = hold(
+        swap(send_down),
+        ffn_back(who, 0, half, False, *back_args, None, None),
+        keep_down,
+        delta[1:-1],
+    )
+    delta[1:-1] = near
     sum_down = pair_up(keep_down, got_down)
     sum_down, send_low, keep_low, carried = hold(sum_down, send_low, keep_low, carried)
     (
-        got_low, sum_down,
+        got_low, sum_down, delta,
         (keep_high, send_high, grad_attn, rest, gain_two_grad, router_grad), keep_low,
     ) = hold(
         swap(send_low),
         spread(sum_down, "row"),
+        delta,
         ffn_back(who, half, half, True, *back_args, carried, tail),
         keep_low,
     )
@@ -1058,26 +1109,23 @@
     sum_high, grad_mixed = hold(sum_high, grad_mixed)
     heads = (q, k, kt, v, limit, mass, grad_mixed, mixed, tables_k, tables_q)
     most = (KVH + 1) // 2
-    sum_low, delta, one, sum_high = hold(
-        sum_low, delta, attend_back(0, most, *heads), sum_high
-    )
-    far = [
-        pack(value, sum_down[-1 - i])
-        for i, value in enumerate(add_up(sum_low).astype(BF))
-    ]
+    down_far, sum_low, one, sum_high = hold(
+        [partner(sum_down[k], "col", k) for k in range(half, col_count)],
+        sum_low,
+        attend_back(0, most, *heads),
+        sum_high,
+    )
+    far = list(add_up(sum_low).astype(BF))
     far, one, grad_mixed = hold(far, one, grad_mixed)
-    far = [
-        [partner(value, "col", col_count - 1 - i) for value in values]
-        for i, values in enumerate(far)
-    ]
+    far = [partner(value, "col", col_count - 1 - i) for i, value in enumerate(far)]
     heads = heads[:6] + (grad_mixed,) + heads[7:]
     sum_high = spread(sum_high, "row")
     (two,) = hold(attend_back(most, KVH - most, *heads))
     gq, gk, gv = zip(one, two)
-    far, sum_high, (back, grads, gain_one_grad) = hold(
+    far, sum_high, (*gw_mixing, grads, gain_one_grad) = hold(
         far,
         sum_high,
-        project_back(x, rank[None, :], gain_one, gq, gk, gv, rest, mixing),
+        mixing_grad(who, x, rank[None, :], gain_one, gq, gk, gv, gw_out, mixing, pairs),
     )
     *near, sum_pair = add_up(sum_high).astype(BF)
     near = [pack(value, sum_down[half - 1 - i]) for i, value in enumerate(near)]
@@ -1086,25 +1134,30 @@
     vectors = vectors[jnp.arange(col_count) ^ column]
     vectors = jnp.pad(vectors, ((0, 0), (0, VECTOR_ROWS - 3), (0, mixing_part - part)))
     vectors = jnp.broadcast_to(vectors[None], (pairs,) + vectors.shape)
-    near, back, grads, vectors = hold(near, back, grads, vectors)
-    back = from_owner(back, sequences)
-    near, gw_mixing = hold(
+    keep_mixing, send_mixing = (
+        lax.dynamic_update_slice(value, vectors, (0, 0, rows, 0)) for value in gw_mixing
+    )
+    near, keep_mixing, send_mixing, grads = hold(near, keep_mixing, send_mixing, grads)
+    got_mixing, near, back, keep_mixing = hold(
+        swap(send_mixing),
         [
             [partner(value, "col", half - 1 - i) for value in values]
             for i, values in enumerate(near)
         ],
-        mixing_grad(who, x, gain_one, grads, gw_out, pairs),
-    )
-    keep_mixing, send_mixing = (
-        lax.dynamic_update_slice(value, vectors, (0, 0, rows, 0)) for value in gw_mixing
-    )
-    got_mixing, block_out, keep_mixing = hold(
-        swap(send_mixing), scatter_tokens(resid, delta, ranks[:, None, :]), keep_mixing
-    )
-    sum_mixing = add_up(spread(pair_up(keep_mixing, got_mixing), "row")).astype(BF)
-    parts = [unpack(values, 2 * rows) for values in near + far]
-    sum_pair = add_up([sum_pair] + [first for first, _ in parts])
-    sum_down = add_up([sum_down[0]] + [second for _, second in parts])
+        project_back(x, rank[None, :], gain_one, grads, rest, mixing),
+        keep_mixing,
+    )
+    back = from_owner(back, sequences)
+    sum_mixing = pair_up(keep_mixing, got_mixing)
+    sum_mixing, near, delta, sum_pair = hold(sum_mixing, near, delta, sum_pair)
+    block_out = scatter_tokens(who, resid, delta, ranks[:, None, :])
+    sum_mixing, block_out, near, sum_pair, far = hold(
+        spread(sum_mixing, "row"), block_out, near, sum_pair, far
+    )
+    sum_mixing = add_up(sum_mixing).astype(BF)
+    parts = [unpack(values, 2 * rows) for values in near]
+    sum_pair = add_up([sum_pair] + [first for first, _ in parts] + far)
+    sum_down = add_up([sum_down[0]] + [second for _, second in parts] + down_far)
 
     lanes = sum_down.shape[1] // 2
     first, second = sum_down[:, :lanes], sum_down[:, lanes:]

time: 467 us -> 458 us (0.981)
  waiting for transfers between devices: 113 us -> 95 us
  Pallas kernels: 195 us -> 202 us
  other arithmetic: 44.4 us -> 38.2 us
    all_to_all x2, waiting for transfers between devices: 28.3 us -> 17.3 us  [to_owner(): lax.all_to_all(value, 'col', split_axis=0, concat_axis=1, tiled=True)]
    ppermute x27 -> x32, starting transfers between devices: 50.5 us -> 59.9 us  [partner(): return lax.ppermute(value, axis, [(i, i ^ far) for i in range(count)])]
    pallas_call x2 -> x3, Pallas kernels: 24 us -> 29.6 us  [the longest x1 15.2 us: project(): pl.pallas_call(project_body, grid=(blocks,), in_specs=[whole((width, leng...]
    all_to_all x2 -> x1, starting transfers between devices: 9.45 us -> 3.89 us  [from_owner(): lax.all_to_all(value, 'col', split_axis=0, concat_axis=0, tiled=True)]
    ppermute x27 -> x32, waiting for transfers between devices: 82 us -> 76.8 us  [partner(): return lax.ppermute(value, axis, [(i, i ^ far) for i in range(count)])]
    pallas_call x1, Pallas kernels: 10.2 us -> 15 us  [mixing_grad(): pl.pallas_call(mixing_grad_body, grid_spec=pltpu.PrefetchScalarGridSpec(n...]
    unnamed x60 -> x86, local copies, waits for them, and re-layouts: 8.45 us -> 10.9 us
  transfers between devices with their start and end apart: 44 -> 48, of which waited for: 16 -> 15; matrix products, arithmetic and copies ran while one was open for 9% -> 8% of each run, Pallas kernels for 36% -> 38%
where the time goes in v5:
time: 458 us; the launch traced here: 451 us
  Pallas kernels  202 us (44%)
  waiting for transfers between devices  95 us (21%)
  starting transfers between devices  73.6 us (16%)
  other arithmetic  38.2 us (8%)
  local copies, waits for them, and re-layouts  25 us (5%)
  between operations  16 us (3%)
    ppermute x32, waiting for transfers between devices, partner(): return lax.ppermute(value, axis, [(i, i ^ far) for i in range(count)])  76.8 us
    ppermute x32, starting transfers between devices, partner(): return lax.ppermute(value, axis, [(i, i ^ far) for i in range(count)])  59.9 us
    pallas_call x2, Pallas kernels, ffn_back(): pl.pallas_call(functools.partial(ffn_back_body, first, gate.shape[0], las...  43.1 us
    pallas_call x2, Pallas kernels, attend_back(): pl.pallas_call(attend_back_body, grid=(count,), in_specs=[wide, tall, fla...  31 us
    pallas_call x1, Pallas kernels, ffn(): pl.pallas_call(functools.partial(ffn_body, len(sources)), grid_spec=pltpu...  22.6 us
    all_to_all x2, waiting for transfers between devices, to_owner(): lax.all_to_all(value, 'col', split_axis=0, concat_axis=1, tiled=True)  17.3 us
    pallas_call x1, Pallas kernels, attend(): pl.pallas_call(attend_body, grid=(KVH,), in_specs=[pl.BlockSpec((part, pi...  16.4 us
    pallas_call x1, Pallas kernels, project(): pl.pallas_call(project_body, grid=(blocks,), in_specs=[whole((width, leng...  15.2 us
  transfers between devices with their start and end apart: 48, of which 15 were waited for; matrix products, arithmetic and copies ran while one was open for 8% of the time, Pallas kernels for 38%

profile of v5, /device:TPU:0, one launch (start us, length us, event | category | flops | bytes accessed | tf_op | source)
XLA Modules:
  0.0 450.6 jit_solution(7036071832550101386)
XLA Ops:
  10.0 5.1 %collective-permute-start.2 = (bf16[120,640]{1,0:T(8,128)(2,1)S(1)}, bf16[120,640]{1,0:T(8,128)(2,1)S(1)}, u32[]{:S(2)}, u32[]{:S(2)}) collective-permute-start(bf16[120,640]{1,0:T(8,128)(2,1)S(1)} %pad_maximum_fusion.5), channel_id=1, source_target_pairs={{0,3},{1,2},{2,1},{3,0},{4,7},{5,6},{6,5},{7,4},{8,11},{9,10},{10,... | collective-permute-start | bytes 460808 | tf_op jit(solution)/shard_map/ppermute | solution.py:917
  20.0 8.1 %collective-permute-done.1 = bf16[120,640]{1,0:T(8,128)(2,1)S(1)} collective-permute-done((bf16[120,640]{1,0:T(8,128)(2,1)S(1)}, bf16[120,640]{1,0:T(8,128)(2,1)S(1)}, u32[]{:S(2)}, u32[]{:S(2)}) %collective-permute-start.1) | collective-permute-done | bytes 153632 | tf_op jit(solution)/shard_map/ppermute | solution.py:917
  28.2 2.6 collective-permute-start.7
  30.9 2.5 collective-permute-start.10
  34.5 9.3 %collective-permute-done.7 = bf16[368,640]{1,0:T(8,128)(2,1)S(1)} collective-permute-done((bf16[368,640]{1,0:T(8,128)(2,1)S(1)}, bf16[368,640]{1,0:T(8,128)(2,1)S(1)}, u32[]{:S(2)}, u32[]{:S(2)}) %collective-permute-start.7) | collective-permute-done | bytes 471072 | tf_op jit(solution)/shard_map/ppermute | solution.py:917
  43.8 18.1 %collective-permute-start.5 = (bf16[368,640]{1,0:T(8,128)(2,1)S(1)}, bf16[368,640]{1,0:T(8,128)(2,1)S(1)}, u32[]{:S(2)}, u32[]{:S(2)}) collective-permute-start(bf16[368,640]{1,0:T(8,128)(2,1)S(1)} %constant_dynamic-update-slice_fusion), channel_id=1, source_target_pairs={{0,1},{1,0},{2,3},{3,2},{4,5},{5,4},{6,7},{7,6},{8,9},{9,8},{10,11... | collective-permute-start | bytes 1413128 | tf_op jit(solution)/shard_map/ppermute | solution.py:917
  63.5 5.9 %collective-permute-done.6 = bf16[368,640]{1,0:T(8,128)(2,1)S(1)} collective-permute-done((bf16[368,640]{1,0:T(8,128)(2,1)S(1)}, bf16[368,640]{1,0:T(8,128)(2,1)S(1)}, u32[]{:S(2)}, u32[]{:S(2)}) %collective-permute-start.6) | collective-permute-done | bytes 471072 | tf_op jit(solution)/shard_map/ppermute | solution.py:917
  69.4 8.6 %collective-permute-done.5 = bf16[368,640]{1,0:T(8,128)(2,1)S(1)} collective-permute-done((bf16[368,640]{1,0:T(8,128)(2,1)S(1)}, bf16[368,640]{1,0:T(8,128)(2,1)S(1)}, u32[]{:S(2)}, u32[]{:S(2)}) %collective-permute-start.5) | collective-permute-done | bytes 471072 | tf_op jit(solution)/shard_map/ppermute | solution.py:917
  81.4 3.7 all-to-all-start
  91.6 2.0 copy.69.rank
  93.5 6.0 %gather_tokens.1 = bf16[4,240,768]{2,1,0:T(8,128)(2,1)} custom-call(f32[4,240,1024]{2,1,0:T(8,128)} %values.1, s32[4,1024,1]{2,1,0:T(8,128)} %copy.69.rank), custom_call_target="tpu_custom_call" | custom-call | flops 47185920 | bytes 184320 | tf_op jit(solution)/shard_map/gather_tokens/pallas_call | solution.py:84
  105.9 6.3 %join.1.w.refs_7_ = bf16[4,960,640]{2,1,0:T(8,128)(2,1)} custom-call(s32[3]{0:T(128)} %pad_add_fusion.who, bf16[4,120,640]{2,1,0:T(8,128)(2,1)} %copy-done.6, bf16[4,120,640]{2,1,0:T(8,128)(2,1)} %copy-done.15, bf16[4,120,640]{2,1,0:T(8,128)(2,1)} %copy-done.14, bf16[4,120,640]{2,1,0:T(8,128)(2,1)} %copy-done.13, ...), custom_call_target="tpu_custom_call" | custom-call | bytes 307200 | tf_op jit(solution)/shard_map/join/pallas_call | solution.py:148
  112.2 17.3 %all-to-all-done = bf16[4,240,1024]{2,1,0:T(8,128)(2,1)S(1)} async-done(((bf16[4,240,1024]{2,1,0:T(8,128)(2,1)}), bf16[4,240,1024]{2,1,0:T(8,128)(2,1)S(1)}, u32[]{:S(2)}, u32[]{:S(2)}) %all-to-all-start) | async-done | bytes 1966112 | tf_op jit(solution)/shard_map/all_to_all | solution.py:950
  130.7 3.8 all-to-all-start.1
  134.5 15.2 %project.1 = (bf16[960,768]{1,0:T(8,128)(2,1)}, f32[1,768]{1,0:T(1,128)}, bf16[960,768]{1,0:T(8,128)(2,1)}, bf16[320,1024]{1,0:T(8,128)(2,1)}, bf16[5,1024,64]{2...) custom-call(bf16[960,1024]{1,0:T(8,128)(2,1)} %bitcast.97, ...), custom_call_target="tpu_custom_call" | custom-call | flops 130744320 | bytes 552960 | tf_op jit(solution)/shard_map/project/pallas_call | solution.py:227
  150.5 16.4 %attend.1 = (bf16[960,768]{1,0:T(8,128)(2,1)}, f32[5,3,768]{2,1,0:T(4,128)}) custom-call(bf16[960,768]{1,0:T(8,128)(2,1)} %get-tuple-element.244.q, bf16[5,1024,64]{2,1,0:T(8,128)(2,1)} %get-tuple-element.245.k, bf16[320,1024]{1,0:T(8,128)(2,1)} %get-tuple-element.246.vt, s32[1,768]{1,0:T(1,128)} %max.18.limit), custom_call_target="tpu_custom_call" | custom-call | flops 377487360 | bytes 92160 | tf_op jit(solution)/shard_map/attend/pallas_call | solution.py:320
  166.9 8.1 %merge.1 = (f32[960,768]{1,0:T(8,128)}, f32[1,768]{1,0:T(1,128)}, bf16[960,768]{1,0:T(8,128)(2,1)}) custom-call(bf16[960,768]{1,0:T(8,128)(2,1)} %get-tuple-element.248.mixed, bf16[960,768]{1,0:T(8,128)(2,1)} %get-tuple-element.249.picked.refs_4_, f32[960,128]{1,0:T(8,128)} %broadcast_in_dim.39.gain.refs_8_, bf16[4,960,640]{2,1,0:T(8,128)(2,1)} %join.1.w.refs_7_), custom_call_target="tpu_custom_call" | custom-call | flops 44236800 | bytes 476160 | tf_op jit(solution)/shard_map/merge/pallas_call | solution.py:443
  176.6 22.6 %ffn.1 = (bf16[4,640,768]{2,1,0:T(8,128)(2,1)}, bf16[4,640,768]{2,1,0:T(8,128)(2,1)}, bf16[4,640,768]{2,1,0:T(8,128)(2,1)}, bf16[960,768]{1,0:T(8,128)(2,1)}, bf16[960,768]{1,0:T(8,128)(2,1)}) custom-call(s32[3]{0:T(128)} %pad_add_fusion.who, bf16[960,768]{1,0:T(8,128)(2,1)} %get-tuple-element.256.normed, f32[960,768]{1,0:T(8,128)} %get-tuple-element.257.branch.refs_2_, ...), custom_call_target="tpu_custom_call" | custom-call | flops 353894400 | bytes 645120 | tf_op jit(solution)/shard_map/ffn/pallas_call | solution.py:570
  199.2 9.6 %down_grad.1 = (bf16[4,4,128,640]{3,2,1,0:T(8,128)(2,1)}, bf16[4,4,128,640]{3,2,1,0:T(8,128)(2,1)}) custom-call(s32[3]{0:T(128)} %pad_add_fusion.who, bf16[960,768]{1,0:T(8,128)(2,1)} %multiply_convert_fusion.grad_ffn, bf16[4,640,768]{2,1,0:T(8,128)(2,1)} %get-tuple-element.262.active), custom_call_target="tpu_custom_call" | custom-call | flops 117964800 | bytes 460800 | tf_op jit(solution)/shard_map/down_grad/pallas_call | solution.py:610
  209.8 2.1 collective-permute-start.16
  211.8 2.4 collective-permute-start.17
  214.2 18.9 %ffn_back.2 = (bf16[4,2,240,640]{3,2,1,0:T(8,128)(2,1)}, bf16[4,2,240,640]{3,2,1,0:T(8,128)(2,1)}, f32[960,768]{1,0:T(8,128)}) custom-call(s32[3]{0:T(128)} %pad_add_fusion.who, bf16[960,768]{1,0:T(8,128)(2,1)} %get-tuple-element.256.normed, bf16[960,768]{1,0:T(8,128)(2,1)} %multiply_convert_fusion.grad_ffn, ...), custom_call_target="tpu_custom_call" | custom-call | flops 294912000 | bytes 660480 | tf_op jit(solution)/shard_map/ffn_back/pallas_call | solution.py:700
  233.9 3.4 fusion.7
  238.8 1.8 collective-permute-start.20
  241.4 24.3 %ffn_back.3 = (bf16[4,2,240,640]{3,2,1,0:T(8,128)(2,1)}, bf16[4,2,240,640]{3,2,1,0:T(8,128)(2,1)}, bf16[960,768]{1,0:T(8,128)(2,1)}, bf16[960,768]{1,0:T(8,128)(...) custom-call(s32[3]{0:T(128)} %pad_add_fusion.who, bf16[960,768]{1,0:T(8,128)(2,1)} %get-tuple-element.256.normed, ...), custom_call_target="tpu_custom_call" | custom-call | flops 294912000 | bytes 660480 | tf_op jit(solution)/shard_map/ffn_back/pallas_call | solution.py:700
  265.7 3.7 collective-permute-done.20
  270.1 1.8 add_convert_fusion.5
  272.6 1.7 fusion.15
  278.4 9.0 %merge_back.1 = (bf16[4,960,240]{2,1,0:T(8,128)(2,1)}, bf16[960,768]{1,0:T(8,128)(2,1)}) custom-call(bf16[960,768]{1,0:T(8,128)(2,1)} %get-tuple-element.248.mixed, bf16[960,768]{1,0:T(8,128)(2,1)} %get-tuple-element.322.grad, bf16[4,960,640]{2,1,0:T(8,128)(2,1)} %join.1.w.refs_7_), custom_call_target="tpu_custom_call" | custom-call | flops 88473600 | bytes 445440 | tf_op jit(solution)/shard_map/merge_back/pallas_call | solution.py:746
  287.4 2.4 collective-permute-start.24
  291.4 18.2 %attend_back.2 = (bf16[576,768]{1,0:T(8,128)(2,1)}, bf16[192,1024]{1,0:T(8,128)(2,1)}, bf16[192,1024]{1,0:T(8,128)(2,1)}) custom-call(bf16[960,768]{1,0:T(8,128)(2,1)} %get-tuple-element.244.q, bf16[5,1024,64]{2,1,0:T(8,128)(2,1)} %get-tuple-element.245.k, bf16[320,1024]{1,0:T(8,128)(2,1)} %get-tuple-element.318.kt, ...), custom_call_target="tpu_custom_call" | custom-call | flops 566231040 | bytes 110592 | tf_op jit(solution)/shard_map/attend_back/pallas_call | solution.py:387
  313.2 1.7 add_convert_fusion.11
  317.4 12.8 %attend_back.3 = (bf16[384,768]{1,0:T(8,128)(2,1)}, bf16[128,1024]{1,0:T(8,128)(2,1)}, bf16[128,1024]{1,0:T(8,128)(2,1)}) custom-call(bf16[960,768]{1,0:T(8,128)(2,1)} %get-tuple-element.244.q, bf16[5,1024,64]{2,1,0:T(8,128)(2,1)} %get-tuple-element.245.k, bf16[320,1024]{1,0:T(8,128)(2,1)} %get-tuple-element.318.kt, ...), custom_call_target="tpu_custom_call" | custom-call | flops 377487360 | bytes 73728 | tf_op jit(solution)/shard_map/attend_back/pallas_call | solution.py:387
  330.2 15.0 %mixing_grad.1 = (bf16[4,4,128,640]{3,2,1,0:T(8,128)(2,1)}, bf16[4,4,128,640]{3,2,1,0:T(8,128)(2,1)}, bf16[4,400,1024]{2,1,0:T(8,128)(2,1)}, f32[960,1]{1,0:T(8,128)}) custom-call(s32[3]{0:T(128)} %pad_add_fusion.who, bf16[960,1024]{1,0:T(8,128)(2,1)} %bitcast.98, s32[1,1024]{1,0:T(1,128)} %copy-done.32, f32[960,128]{1,0:T(8,128)} %broadcast_in_dim.38.gain, ...), custom_call_target="tpu_custom_call" | custom-call | flops 145489920 | bytes 307200 | tf_op jit(solution)/shard_map/mixing_grad/pallas_call | solution.py:816
  346.0 1.8 add_convert_fusion.10
  350.5 2.4 collective-permute-start.35
  353.0 12.0 %project_back.1 = bf16[960,1024]{1,0:T(8,128)(2,1)} custom-call(bf16[960,1024]{1,0:T(8,128)(2,1)} %bitcast.99, s32[1,1024]{1,0:T(1,128)} %copy-done.32, f32[960,128]{1,0:T(8,128)} %broadcast_in_dim.38.gain, bf16[4,400,1024]{2,1,0:T(8,128)(2,1)} %get-tuple-element.375.grads, bf16[960,768]{1,0:T(8,128)(2,1)} %get-tuple-element.376.rest, ...), custom_call_target="tpu_custom_call" | custom-call | flops 145489920 | bytes 460800 | tf_op jit(solution)/shard_map/project_back/pallas_call | solution.py:881
  365.0 2.0 fusion.11
  371.0 3.9 all-to-all-start.2
  375.0 8.1 %scatter_tokens.1 = f32[4,240,1024]{2,1,0:T(8,128)} custom-call(s32[3]{0:T(128)} %pad_add_fusion.who, f32[4,240,1024]{2,1,0:T(8,128)} %base.1, s32[4,1,1024]{2,1,0:T(1,128)} %broadcast_in_dim.45.rank, bf16[240,768]{1,0:T(8,128)(2,1)} %get-tuple-element.389.refs_0_, bf16[240,768]{1,0:T(8,128)(2,1)} %copy-done.22, bf16[240,768]{1,0:T(8,128)(2,1)} %copy-done.23, ...), custom_call_target="tpu_custom_call" | custom-call | flops 47185920 | bytes 307200 | tf_op jit(solution)/shard_map/scatter_tokens/pallas_call | solution.py:113
  383.0 1.7 collective-permute-done.36
  384.7 13.0 %collective-permute-done.37 = bf16[4,128,640]{2,1,0:T(8,128)(2,1)} collective-permute-done((bf16[4,128,640]{2,1,0:T(8,128)(2,1)}, bf16[4,128,640]{2,1,0:T(8,128)(2,1)}, u32[]{:S(2)}, u32[]{:S(2)}) %collective-permute-start.37) | collective-permute-done | bytes 655392 | tf_op jit(solution)/shard_map/ppermute | solution.py:917
  397.7 1.6 collective-permute-done.38
  401.0 1.6 add_convert_fusion
  407.9 1.9 copy.76
  411.5 7.8 %collective-permute-done.41 = bf16[128,640]{1,0:T(8,128)(2,1)} collective-permute-done((bf16[128,640]{1,0:T(8,128)(2,1)}, bf16[128,640]{1,0:T(8,128)(2,1)}, u32[]{:S(2)}, u32[]{:S(2)}) %collective-permute-start.41) | collective-permute-done | bytes 163872 | tf_op jit(solution)/shard_map/ppermute | solution.py:917
  419.3 15.0 %collective-permute-done.40 = bf16[128,640]{1,0:T(8,128)(2,1)} collective-permute-done((bf16[128,640]{1,0:T(8,128)(2,1)}, bf16[128,640]{1,0:T(8,128)(2,1)}, u32[]{:S(2)}, u32[]{:S(2)}) %collective-permute-start.40) | collective-permute-done | bytes 163872 | tf_op jit(solution)/shard_map/ppermute | solution.py:917
  438.2 5.0 %convert_add_fusion = f32[4,240,1024]{2,1,0:T(8,128)} fusion(f32[4,240,1024]{2,1,0:T(8,128)} %values.1, bf16[4,240,1024]{2,1,0:T(8,128)(2,1)S(1)} %all-to-all-done.2), kind=kLoop, calls=%fused_computation.6 | loop fusion | flops 1966080 | bytes 9830400 | tf_op jit(solution)/shard_map/add | solution.py:1181
  (225 shorter events, 66.6 us)
Async XLA Ops:
  7.2 169.4 %all-gather.3.cloned.1.call-start = ((), (), s32[]{:S(2)}) async-start(), calls=%async_computation.3 | async-start | bytes 16957440 | tf_op jit(solution)/shard_map/all_gather | solution.py:1008
  10.0 10.0 %collective-permute-start.2 = (bf16[120,640]{1,0:T(8,128)(2,1)S(1)}, bf16[120,640]{1,0:T(8,128)(2,1)S(1)}, u32[]{:S(2)}, u32[]{:S(2)}) collective-permute-start(bf16[120,640]{1,0:T(8,128)(2,1)S(1)} %pad_maximum_fusion.5), channel_id=1, source_target_pairs={{0,3},{1,2},{2,1},{3,0},{4,7},{5,6},{6,5},{7,4},{8,11},{9,10},{10,... | collective-permute-start | bytes 460808 | tf_op jit(solution)/shard_map/ppermute | solution.py:917
  15.1 13.0 %collective-permute-start.1 = (bf16[120,640]{1,0:T(8,128)(2,1)S(1)}, bf16[120,640]{1,0:T(8,128)(2,1)S(1)}, u32[]{:S(2)}, u32[]{:S(2)}) collective-permute-start(bf16[120,640]{1,0:T(8,128)(2,1)S(1)} %pad_maximum_fusion.5), channel_id=1, source_target_pairs={{0,2},{1,3},{2,0},{3,1},{4,6},{5,7},{6,4},{7,5},{8,10},{9,11},{10,... | collective-permute-start | bytes 460808 | tf_op jit(solution)/shard_map/ppermute | solution.py:917
  15.1 13.0 %collective-permute-start = (bf16[120,640]{1,0:T(8,128)(2,1)S(1)}, bf16[120,640]{1,0:T(8,128)(2,1)S(1)}, u32[]{:S(2)}, u32[]{:S(2)}) collective-permute-start(bf16[120,640]{1,0:T(8,128)(2,1)S(1)} %pad_maximum_fusion.5), channel_id=1, source_target_pairs={{0,1},{1,0},{2,3},{3,2},{4,5},{5,4},{6,7},{7,6},{8,9},{9,8},{10,11... | collective-permute-start | bytes 460808 | tf_op jit(solution)/shard_map/ppermute | solution.py:917
  16.9 1.6 collective-permute-start.4
  17.9 1.6 collective-permute-start.3
  28.2 15.6 %collective-permute-start.7 = (bf16[368,640]{1,0:T(8,128)(2,1)S(1)}, bf16[368,640]{1,0:T(8,128)(2,1)S(1)}, u32[]{:S(2)}, u32[]{:S(2)}) collective-permute-start(bf16[368,640]{1,0:T(8,128)(2,1)S(1)} %constant_dynamic-update-slice_fusion), channel_id=1, source_target_pairs={{0,3},{1,2},{2,1},{3,0},{4,7},{5,6},{6,5},{7,4},{8,11},{9,10},{10,... | collective-permute-start | bytes 1413128 | tf_op jit(solution)/shard_map/ppermute | solution.py:917
  30.9 47.1 %collective-permute-start.10 = (bf16[4,120,640]{2,1,0:T(8,128)(2,1)S(1)}, bf16[4,120,640]{2,1,0:T(8,128)(2,1)S(1)}, u32[]{:S(2)}, u32[]{:S(2)}) collective-permute-start(bf16[4,120,640]{2,1,0:T(8,128)(2,1)S(1)} %pad_maximum_fusion.1.refs_0_), channel_id=1, source_target_pairs={{0,24},{4,28},{8,16},{12,20},{16,8},{20,12},{24,0},{28,4},{1,25},{... | collective-permute-start | bytes 1843208 | tf_op jit(solution)/shard_map/ppermute | solution.py:917
  33.4 44.6 %collective-permute-start.9 = (bf16[4,120,640]{2,1,0:T(8,128)(2,1)S(1)}, bf16[4,120,640]{2,1,0:T(8,128)(2,1)S(1)}, u32[]{:S(2)}, u32[]{:S(2)}) collective-permute-start(bf16[4,120,640]{2,1,0:T(8,128)(2,1)S(1)} %pad_maximum_fusion.1.refs_0_), channel_id=1, source_target_pairs={{0,16},{4,20},{8,24},{12,28},{16,0},{20,4},{24,8},{28,12},{1,17},{... | collective-permute-start | bytes 1843208 | tf_op jit(solution)/shard_map/ppermute | solution.py:917
  33.9 44.1 %collective-permute-start.8 = (bf16[4,120,640]{2,1,0:T(8,128)(2,1)S(1)}, bf16[4,120,640]{2,1,0:T(8,128)(2,1)S(1)}, u32[]{:S(2)}, u32[]{:S(2)}) collective-permute-start(bf16[4,120,640]{2,1,0:T(8,128)(2,1)S(1)} %pad_maximum_fusion.1.refs_0_), channel_id=1, source_target_pairs={{0,8},{4,12},{8,0},{12,4},{16,24},{20,28},{24,16},{28,20},{1,9},{5... | collective-permute-start | bytes 1843208 | tf_op jit(solution)/shard_map/ppermute | solution.py:917
  34.5 34.9 %collective-permute-start.6 = (bf16[368,640]{1,0:T(8,128)(2,1)S(1)}, bf16[368,640]{1,0:T(8,128)(2,1)S(1)}, u32[]{:S(2)}, u32[]{:S(2)}) collective-permute-start(bf16[368,640]{1,0:T(8,128)(2,1)S(1)} %constant_dynamic-update-slice_fusion), channel_id=1, source_target_pairs={{0,2},{1,3},{2,0},{3,1},{4,6},{5,7},{6,4},{7,5},{8,10},{9,11},{10,... | collective-permute-start | bytes 1413128 | tf_op jit(solution)/shard_map/ppermute | solution.py:917
  43.8 34.2 %collective-permute-start.5 = (bf16[368,640]{1,0:T(8,128)(2,1)S(1)}, bf16[368,640]{1,0:T(8,128)(2,1)S(1)}, u32[]{:S(2)}, u32[]{:S(2)}) collective-permute-start(bf16[368,640]{1,0:T(8,128)(2,1)S(1)} %constant_dynamic-update-slice_fusion), channel_id=1, source_target_pairs={{0,1},{1,0},{2,3},{3,2},{4,5},{5,4},{6,7},{7,6},{8,9},{9,8},{10,11... | collective-permute-start | bytes 1413128 | tf_op jit(solution)/shard_map/ppermute | solution.py:917
  81.4 48.1 %all-to-all-start = ((bf16[4,240,1024]{2,1,0:T(8,128)(2,1)}), bf16[4,240,1024]{2,1,0:T(8,128)(2,1)S(1)}, u32[]{:S(2)}, u32[]{:S(2)}) async-start(bf16[4,240,1024]{2,1,0:T(8,128)(2,1)} %convert_element_type.374), calls=%async_computation | async-start | bytes 3932160 | tf_op jit(solution)/shard_map/all_to_all | solution.py:950
  89.2 12.7 %collective-permute-start.11 = (bf16[4,120,640]{2,1,0:T(8,128)(2,1)S(1)}, bf16[4,120,640]{2,1,0:T(8,128)(2,1)}, u32[]{:S(2)}, u32[]{:S(2)}) collective-permute-start(bf16[4,120,640]{2,1,0:T(8,128)(2,1)S(1)} %pad_maximum_fusion.1.refs_0_), channel_id=1, source_target_pairs={{0,4},{4,0},{8,12},{12,8},{16,20},{20,16},{24,28},{28,24},{1,5},{5... | collective-permute-start | bytes 1843208 | tf_op jit(solution)/shard_map/ppermute | solution.py:911
  89.3 12.6 %collective-permute-start.12 = (bf16[4,120,640]{2,1,0:T(8,128)(2,1)}, bf16[4,120,640]{2,1,0:T(8,128)(2,1)}, u32[]{:S(2)}, u32[]{:S(2)}) collective-permute-start(bf16[4,120,640]{2,1,0:T(8,128)(2,1)} %copy-done.15), channel_id=1, source_target_pairs={{0,4},{4,0},{8,12},{12,8},{16,20},{20,16},{24,28},{28,24},{1,5},{5... | collective-permute-start | bytes 1843208 | tf_op jit(solution)/shard_map/ppermute | solution.py:911
  89.8 12.1 %collective-permute-start.13 = (bf16[4,120,640]{2,1,0:T(8,128)(2,1)}, bf16[4,120,640]{2,1,0:T(8,128)(2,1)}, u32[]{:S(2)}, u32[]{:S(2)}) collective-permute-start(bf16[4,120,640]{2,1,0:T(8,128)(2,1)} %copy-done.14), channel_id=1, source_target_pairs={{0,4},{4,0},{8,12},{12,8},{16,20},{20,16},{24,28},{28,24},{1,5},{5... | collective-permute-start | bytes 1843208 | tf_op jit(solution)/shard_map/ppermute | solution.py:911
  89.9 12.0 %collective-permute-start.14 = (bf16[4,120,640]{2,1,0:T(8,128)(2,1)S(1)}, bf16[4,120,640]{2,1,0:T(8,128)(2,1)}, u32[]{:S(2)}, u32[]{:S(2)}) collective-permute-start(bf16[4,120,640]{2,1,0:T(8,128)(2,1)S(1)} %collective-permute-done.10.refs_3_), channel_id=1, source_target_pairs={{0,4},{4,0},{8,12},{12,8},{16,20},{20,16},{24,28},{28,24},{1,5},{5... | collective-permute-start | bytes 1843208 | tf_op jit(solution)/shard_map/ppermute | solution.py:911
  130.7 44.2 %all-to-all-start.1 = ((bf16[4,240,768]{2,1,0:T(8,128)(2,1)}), bf16[4,240,768]{2,1,0:T(8,128)(2,1)S(1)}, u32[]{:S(2)}, u32[]{:S(2)}) async-start(bf16[4,240,768]{2,1,0:T(8,128)(2,1)} %gather_tokens.1), calls=%async_computation.1 | async-start | bytes 2949120 | tf_op jit(solution)/shard_map/all_to_all | solution.py:950
  209.8 23.3 %collective-permute-start.15 = (bf16[4,4,128,640]{3,2,1,0:T(8,128)(2,1)}, bf16[4,4,128,640]{3,2,1,0:T(8,128)(2,1)}, u32[]{:S(2)}, u32[]{:S(2)}) collective-permute-start(bf16[4,4,128,640]{3,2,1,0:T(8,128)(2,1)} %get-tuple-element.270), channel_id=1, source_target_pairs={{0,4},{4,0},{8,12},{12,8},{16,20},{20,16},{24,28},{28,24},{1,5},{5... | collective-permute-start | bytes 7864328 | tf_op jit(solution)/shard_map/ppermute | solution.py:911
  209.8 23.3 %collective-permute-start.16 = (bf16[240,768]{1,0:T(8,128)(2,1)S(1)}, bf16[240,768]{1,0:T(8,128)(2,1)S(1)}, u32[]{:S(2)}, u32[]{:S(2)}) collective-permute-start(bf16[240,768]{1,0:T(8,128)(2,1)S(1)} %get-tuple-element.277), channel_id=1, source_target_pairs={{0,1},{1,0},{2,3},{3,2},{4,5},{5,4},{6,7},{7,6},{8,9},{9,8},{10,11... | collective-permute-start | bytes 1105928 | tf_op jit(solution)/shard_map/ppermute | solution.py:917
  211.8 21.3 %collective-permute-start.17 = (bf16[240,768]{1,0:T(8,128)(2,1)S(1)}, bf16[240,768]{1,0:T(8,128)(2,1)S(1)}, u32[]{:S(2)}, u32[]{:S(2)}) collective-permute-start(bf16[240,768]{1,0:T(8,128)(2,1)S(1)} %get-tuple-element.278), channel_id=1, source_target_pairs={{0,2},{1,3},{2,0},{3,1},{4,6},{5,7},{6,4},{7,5},{8,10},{9,11},{10,... | collective-permute-start | bytes 1105928 | tf_op jit(solution)/shard_map/ppermute | solution.py:917
  237.4 32.7 %collective-permute-start.18 = (bf16[4,2,240,640]{3,2,1,0:T(8,128)(2,1)}, bf16[4,2,240,640]{3,2,1,0:T(8,128)(2,1)S(1)}, u32[]{:S(2)}, u32[]{:S(2)}) collective-permute-start(bf16[4,2,240,640]{3,2,1,0:T(8,128)(2,1)} %get-tuple-element.284), channel_id=1, source_target_pairs={{0,4},{4,0},{8,12},{12,8},{16,20},{20,16},{24,28},{28,24},{1,5},{5... | collective-permute-start | bytes 7372808 | tf_op jit(solution)/shard_map/ppermute | solution.py:911
  237.4 28.3 %collective-permute-start.19 = (bf16[4,128,640]{2,1,0:T(8,128)(2,1)}, bf16[4,128,640]{2,1,0:T(8,128)(2,1)S(1)}, u32[]{:S(2)}, u32[]{:S(2)}) collective-permute-start(bf16[4,128,640]{2,1,0:T(8,128)(2,1)} %get-tuple-element.286), channel_id=1, source_target_pairs={{0,8},{4,12},{8,0},{12,4},{16,24},{20,28},{24,16},{28,20},{1,9},{5... | collective-permute-start | bytes 1966088 | tf_op jit(solution)/shard_map/ppermute | solution.py:917
  238.8 30.5 %collective-permute-start.20 = (bf16[4,128,640]{2,1,0:T(8,128)(2,1)}, bf16[4,128,640]{2,1,0:T(8,128)(2,1)}, u32[]{:S(2)}, u32[]{:S(2)}) collective-permute-start(bf16[4,128,640]{2,1,0:T(8,128)(2,1)} %get-tuple-element.287), channel_id=1, source_target_pairs={{0,16},{4,20},{8,24},{12,28},{16,0},{20,4},{24,8},{28,12},{1,17},{... | collective-permute-start | bytes 1966088 | tf_op jit(solution)/shard_map/ppermute | solution.py:917
  240.6 29.5 %collective-permute-start.21 = (bf16[4,128,640]{2,1,0:T(8,128)(2,1)}, bf16[4,128,640]{2,1,0:T(8,128)(2,1)}, u32[]{:S(2)}, u32[]{:S(2)}) collective-permute-start(bf16[4,128,640]{2,1,0:T(8,128)(2,1)} %get-tuple-element.288), channel_id=1, source_target_pairs={{0,24},{4,28},{8,16},{12,20},{16,8},{20,12},{24,0},{28,4},{1,25},{... | collective-permute-start | bytes 1966088 | tf_op jit(solution)/shard_map/ppermute | solution.py:917
  240.9 24.8 %collective-permute-start.22 = (bf16[240,768]{1,0:T(8,128)(2,1)}, bf16[240,768]{1,0:T(8,128)(2,1)}, u32[]{:S(2)}, u32[]{:S(2)}) collective-permute-start(bf16[240,768]{1,0:T(8,128)(2,1)} %get-tuple-element.292), channel_id=1, source_target_pairs={{0,3},{1,2},{2,1},{3,0},{4,7},{5,6},{6,5},{7,4},{8,11},{9,10},{10,... | collective-permute-start | bytes 1105928 | tf_op jit(solution)/shard_map/ppermute | solution.py:917
  274.3 13.1 %collective-permute-start.28 = (bf16[4,2,240,640]{3,2,1,0:T(8,128)(2,1)}, bf16[4,2,240,640]{3,2,1,0:T(8,128)(2,1)S(1)}, u32[]{:S(2)}, u32[]{:S(2)}) collective-permute-start(bf16[4,2,240,640]{3,2,1,0:T(8,128)(2,1)} %get-tuple-element.321), channel_id=1, source_target_pairs={{0,4},{4,0},{8,12},{12,8},{16,20},{20,16},{24,28},{28,24},{1,5},{5... | collective-permute-start | bytes 7372808 | tf_op jit(solution)/shard_map/ppermute | solution.py:911
  274.3 35.3 %collective-permute-start.25 = (bf16[2,240,640]{2,1,0:T(8,128)(2,1)}, bf16[2,240,640]{2,1,0:T(8,128)(2,1)S(1)}, u32[]{:S(2)}, u32[]{:S(2)}) collective-permute-start(bf16[2,240,640]{2,1,0:T(8,128)(2,1)} %get-tuple-element.315), channel_id=1, source_target_pairs={{0,8},{4,12},{8,0},{12,4},{16,24},{20,28},{24,16},{28,20},{1,9},{5... | collective-permute-start | bytes 1843208 | tf_op jit(solution)/shard_map/ppermute | solution.py:917
  275.7 33.9 %collective-permute-start.26 = (bf16[2,240,640]{2,1,0:T(8,128)(2,1)}, bf16[2,240,640]{2,1,0:T(8,128)(2,1)}, u32[]{:S(2)}, u32[]{:S(2)}) collective-permute-start(bf16[2,240,640]{2,1,0:T(8,128)(2,1)} %get-tuple-element.316), channel_id=1, source_target_pairs={{0,16},{4,20},{8,24},{12,28},{16,0},{20,4},{24,8},{28,12},{1,17},{... | collective-permute-start | bytes 1843208 | tf_op jit(solution)/shard_map/ppermute | solution.py:917
  276.6 33.1 %collective-permute-start.27 = (bf16[2,240,640]{2,1,0:T(8,128)(2,1)}, bf16[2,240,640]{2,1,0:T(8,128)(2,1)}, u32[]{:S(2)}, u32[]{:S(2)}) collective-permute-start(bf16[2,240,640]{2,1,0:T(8,128)(2,1)} %get-tuple-element.317), channel_id=1, source_target_pairs={{0,24},{4,28},{8,16},{12,20},{16,8},{20,12},{24,0},{28,4},{1,25},{... | collective-permute-start | bytes 1843208 | tf_op jit(solution)/shard_map/ppermute | solution.py:917
  277.8 31.8 %collective-permute-start.23 = (bf16[128,640]{1,0:T(8,128)(2,1)S(1)}, bf16[128,640]{1,0:T(8,128)(2,1)S(1)}, u32[]{:S(2)}, u32[]{:S(2)}) collective-permute-start(bf16[128,640]{1,0:T(8,128)(2,1)S(1)} %get-tuple-element.312), channel_id=1, source_target_pairs={{0,2},{1,3},{2,0},{3,1},{4,6},{5,7},{6,4},{7,5},{8,10},{9,11},{10,... | collective-permute-start | bytes 491528 | tf_op jit(solution)/shard_map/ppermute | solution.py:917
  287.4 22.2 %collective-permute-start.24 = (bf16[128,640]{1,0:T(8,128)(2,1)S(1)}, bf16[128,640]{1,0:T(8,128)(2,1)S(1)}, u32[]{:S(2)}, u32[]{:S(2)}) collective-permute-start(bf16[128,640]{1,0:T(8,128)(2,1)S(1)} %get-tuple-element.313), channel_id=1, source_target_pairs={{0,3},{1,2},{2,1},{3,0},{4,7},{5,6},{6,5},{7,4},{8,11},{9,10},{10,... | collective-permute-start | bytes 491528 | tf_op jit(solution)/shard_map/ppermute | solution.py:917
  309.7 35.6 %collective-permute-start.31 = (bf16[2,240,640]{2,1,0:T(8,128)(2,1)}, bf16[2,240,640]{2,1,0:T(8,128)(2,1)}, u32[]{:S(2)}, u32[]{:S(2)}) collective-permute-start(bf16[2,240,640]{2,1,0:T(8,128)(2,1)} %get-tuple-element.347), channel_id=1, source_target_pairs={{0,8},{4,12},{8,0},{12,4},{16,24},{20,28},{24,16},{28,20},{1,9},{5... | collective-permute-start | bytes 1843208 | tf_op jit(solution)/shard_map/ppermute | solution.py:917
  311.2 34.1 %collective-permute-start.32 = (bf16[2,240,640]{2,1,0:T(8,128)(2,1)}, bf16[2,240,640]{2,1,0:T(8,128)(2,1)}, u32[]{:S(2)}, u32[]{:S(2)}) collective-permute-start(bf16[2,240,640]{2,1,0:T(8,128)(2,1)} %get-tuple-element.348), channel_id=1, source_target_pairs={{0,16},{4,20},{8,24},{12,28},{16,0},{20,4},{24,8},{28,12},{1,17},{... | collective-permute-start | bytes 1843208 | tf_op jit(solution)/shard_map/ppermute | solution.py:917
  312.0 33.3 %collective-permute-start.33 = (bf16[2,240,640]{2,1,0:T(8,128)(2,1)S(1)}, bf16[2,240,640]{2,1,0:T(8,128)(2,1)}, u32[]{:S(2)}, u32[]{:S(2)}) collective-permute-start(bf16[2,240,640]{2,1,0:T(8,128)(2,1)S(1)} %get-tuple-element.349), channel_id=1, source_target_pairs={{0,24},{4,28},{8,16},{12,20},{16,8},{20,12},{24,0},{28,4},{1,25},{... | collective-permute-start | bytes 1843208 | tf_op jit(solution)/shard_map/ppermute | solution.py:917
  315.1 30.2 %collective-permute-start.29 = (bf16[240,640]{1,0:T(8,128)(2,1)S(1)}, bf16[240,640]{1,0:T(8,128)(2,1)S(1)}, u32[]{:S(2)}, u32[]{:S(2)}) collective-permute-start(bf16[240,640]{1,0:T(8,128)(2,1)S(1)} %get-tuple-element.344), channel_id=1, source_target_pairs={{0,3},{1,2},{2,1},{3,0},{4,7},{5,6},{6,5},{7,4},{8,11},{9,10},{10,... | collective-permute-start | bytes 921608 | tf_op jit(solution)/shard_map/ppermute | solution.py:917
  316.5 28.7 %collective-permute-start.30 = (bf16[240,640]{1,0:T(8,128)(2,1)S(1)}, bf16[240,640]{1,0:T(8,128)(2,1)S(1)}, u32[]{:S(2)}, u32[]{:S(2)}) collective-permute-start(bf16[240,640]{1,0:T(8,128)(2,1)S(1)} %get-tuple-element.345), channel_id=1, source_target_pairs={{0,2},{1,3},{2,0},{3,1},{4,6},{5,7},{6,4},{7,5},{8,10},{9,11},{10,... | collective-permute-start | bytes 921608 | tf_op jit(solution)/shard_map/ppermute | solution.py:917
  350.5 14.4 %collective-permute-start.34 = (bf16[4,4,128,640]{3,2,1,0:T(8,128)(2,1)}, bf16[4,4,128,640]{3,2,1,0:T(8,128)(2,1)S(1)}, u32[]{:S(2)}, u32[]{:S(2)}) collective-permute-start(bf16[4,4,128,640]{3,2,1,0:T(8,128)(2,1)} %get-tuple-element.373), channel_id=1, source_target_pairs={{0,4},{4,0},{8,12},{12,8},{16,20},{20,16},{24,28},{28,24},{1,5},{5... | collective-permute-start | bytes 7864328 | tf_op jit(solution)/shard_map/ppermute | solution.py:911
  350.5 14.4 %collective-permute-start.35 = (bf16[368,640]{1,0:T(8,128)(2,1)S(1)}, bf16[368,640]{1,0:T(8,128)(2,1)S(1)}, u32[]{:S(2)}, u32[]{:S(2)}) collective-permute-start(bf16[368,640]{1,0:T(8,128)(2,1)S(1)} %pad_maximum_fusion.2), channel_id=1, source_target_pairs={{0,1},{1,0},{2,3},{3,2},{4,5},{5,4},{6,7},{7,6},{8,9},{9,8},{10,11... | collective-permute-start | bytes 1413128 | tf_op jit(solution)/shard_map/ppermute | solution.py:917
  366.9 17.8 %collective-permute-start.36 = (bf16[4,128,640]{2,1,0:T(8,128)(2,1)}, bf16[4,128,640]{2,1,0:T(8,128)(2,1)S(1)}, u32[]{:S(2)}, u32[]{:S(2)}) collective-permute-start(bf16[4,128,640]{2,1,0:T(8,128)(2,1)} %get-tuple-element.386), channel_id=1, source_target_pairs={{0,8},{4,12},{8,0},{12,4},{16,24},{20,28},{24,16},{28,20},{1,9},{5... | collective-permute-start | bytes 1966088 | tf_op jit(solution)/shard_map/ppermute | solution.py:917
  368.4 29.3 %collective-permute-start.37 = (bf16[4,128,640]{2,1,0:T(8,128)(2,1)}, bf16[4,128,640]{2,1,0:T(8,128)(2,1)}, u32[]{:S(2)}, u32[]{:S(2)}) collective-permute-start(bf16[4,128,640]{2,1,0:T(8,128)(2,1)} %get-tuple-element.387), channel_id=1, source_target_pairs={{0,16},{4,20},{8,24},{12,28},{16,0},{20,4},{24,8},{28,12},{1,17},{... | collective-permute-start | bytes 1966088 | tf_op jit(solution)/shard_map/ppermute | solution.py:917
  369.2 30.1 %collective-permute-start.38 = (bf16[4,128,640]{2,1,0:T(8,128)(2,1)}, bf16[4,128,640]{2,1,0:T(8,128)(2,1)}, u32[]{:S(2)}, u32[]{:S(2)}) collective-permute-start(bf16[4,128,640]{2,1,0:T(8,128)(2,1)} %get-tuple-element.388), channel_id=1, source_target_pairs={{0,24},{4,28},{8,16},{12,20},{16,8},{20,12},{24,0},{28,4},{1,25},{... | collective-permute-start | bytes 1966088 | tf_op jit(solution)/shard_map/ppermute | solution.py:917
  371.0 67.2 %all-to-all-start.2 = ((bf16[4,240,1024]{2,1,0:T(8,128)(2,1)}), bf16[4,240,1024]{2,1,0:T(8,128)(2,1)S(1)}, u32[]{:S(2)}, u32[]{:S(2)}) async-start(bf16[4,240,1024]{2,1,0:T(8,128)(2,1)} %bitcast.102), calls=%async_computation.2 | async-start | bytes 3932160 | tf_op jit(solution)/shard_map/all_to_all | solution.py:957
  399.6 7.4 %collective-permute-start.43 = (bf16[128,320]{1,0:T(8,128)(2,1)S(1)}, bf16[128,320]{1,0:T(8,128)(2,1)S(1)}, u32[]{:S(2)}, u32[]{:S(2)}) collective-permute-start(bf16[128,320]{1,0:T(8,128)(2,1)S(1)} %select_convert_fusion.1), channel_id=1, source_target_pairs={{0,4},{4,0},{8,12},{12,8},{16,20},{20,16},{24,28},{28,24},{1,5},{5... | collective-permute-start | bytes 245768 | tf_op jit(solution)/shard_map/ppermute | solution.py:911
  400.5 9.2 %collective-permute-start.42 = (bf16[120,640]{1,0:T(8,128)(2,1)}, bf16[120,640]{1,0:T(8,128)(2,1)S(1)}, u32[]{:S(2)}, u32[]{:S(2)}) collective-permute-start(bf16[120,640]{1,0:T(8,128)(2,1)} %select_convert_fusion), channel_id=1, source_target_pairs={{0,4},{4,0},{8,12},{12,8},{16,20},{20,16},{24,28},{28,24},{1,5},{5... | collective-permute-start | bytes 460808 | tf_op jit(solution)/shard_map/ppermute | solution.py:911
  403.4 8.1 %collective-permute-start.39 = (bf16[128,640]{1,0:T(8,128)(2,1)}, bf16[128,640]{1,0:T(8,128)(2,1)S(1)}, u32[]{:S(2)}, u32[]{:S(2)}) collective-permute-start(bf16[128,640]{1,0:T(8,128)(2,1)} %get-tuple-element.494), channel_id=1, source_target_pairs={{0,1},{1,0},{2,3},{3,2},{4,5},{5,4},{6,7},{7,6},{8,9},{9,8},{10,11... | collective-permute-start | bytes 491528 | tf_op jit(solution)/shard_map/ppermute | solution.py:917
  404.1 15.2 %collective-permute-start.41 = (bf16[128,640]{1,0:T(8,128)(2,1)}, bf16[128,640]{1,0:T(8,128)(2,1)}, u32[]{:S(2)}, u32[]{:S(2)}) collective-permute-start(bf16[128,640]{1,0:T(8,128)(2,1)} %get-tuple-element.495), channel_id=1, source_target_pairs={{0,3},{1,2},{2,1},{3,0},{4,7},{5,6},{6,5},{7,4},{8,11},{9,10},{10,... | collective-permute-start | bytes 491528 | tf_op jit(solution)/shard_map/ppermute | solution.py:917
  405.6 28.7 %collective-permute-start.40 = (bf16[128,640]{1,0:T(8,128)(2,1)}, bf16[128,640]{1,0:T(8,128)(2,1)}, u32[]{:S(2)}, u32[]{:S(2)}) collective-permute-start(bf16[128,640]{1,0:T(8,128)(2,1)} %get-tuple-element.496), channel_id=1, source_target_pairs={{0,2},{1,3},{2,0},{3,1},{4,6},{5,7},{6,4},{7,5},{8,10},{9,11},{10,... | collective-permute-start | bytes 491528 | tf_op jit(solution)/shard_map/ppermute | solution.py:917
  (39 other events, 393.4 us)
Sparse Core Ops, SparseCore 0:
  81.4 82.4 all-gather.2

commit v6 on v5

--- a/solution.py
+++ b/solution.py
@@ -97,14 +97,15 @@
 
 
 def scatter_body(who, base, rank, *refs):
-    *pieces, out = refs
-    chosen = pick_rows(rank[0], pieces[0].shape[1])
+    *pieces, out, values = refs
     count = len(pieces)
     for k, piece in enumerate(pieces):
 
         @pl.when((pl.program_id(0) ^ lax.rem(who[0], count)) == k)
         def _():
-            out[0] = base[0] + dot_nn(piece[...], chosen)
+            values[...] = piece[...]
+
+    out[0] = base[0] + dot_nn(values[...], pick_rows(rank[0], values.shape[1]))
 
 
 def scatter_tokens(who, base, pieces, rank_row):
@@ -121,6 +122,7 @@
             ]
             + [whole((width, picks))] * count,
             out_specs=pl.BlockSpec((1, width, length), lambda i, who: (i, 0, 0)),
+            scratch_shapes=[pltpu.VMEM((width, picks), BF)],
         ),
         out_shape=struct(base.shape, F32),
         compiler_params=params(),
@@ -923,6 +925,17 @@
 
 def spread(values, axis):
     return [values[0]] + [partner(value, axis, k) for k, value in enumerate(values) if k]
+
+
+def scatter_col(value, other):
+    while value.shape[0] > 1:
+        keep, send = value[0::2], value[1::2]
+        step = lax.axis_size("col") // value.shape[0]
+        got, other = hold(partner(send, "col", step), other)
+        value = add_up((keep, got))
+        if value.shape[0] > 1:
+            value = value.astype(BF)
+    return value[0], other
 
 
 def add_up(values):
@@ -1166,7 +1179,7 @@
     top, end = jnp.where(even, mine, other), jnp.where(even, other, mine)
     gw_down = jnp.concatenate([top, end[2 * down_rows_kept - part :]], axis=0).T
 
-    gw_mixing = add_up(spread(list(sum_mixing), "col"))
+    gw_mixing, resid_grad = scatter_col(sum_mixing, cotangent + back.astype(F32))
 
     sum_pair = sum_pair.reshape(2, rows, hidden)
     mine = jnp.where(even, sum_pair[0], sum_pair[1])
@@ -1178,7 +1191,6 @@
             a / copies for a in (gw_gate, gw_up, gw_down, gw_mixing)
         )
 
-    resid_grad = cotangent + back.astype(F32)
     kv_part = w_key.shape[1]
     ends = (part, part + kv_part, part + 2 * kv_part)
     return (

time: 458 us -> 449 us (0.980)
  waiting for transfers between devices: 95 us -> 89.2 us
    ppermute x32 -> x31, waiting for transfers between devices: 76.8 us -> 68.8 us  [partner(): return lax.ppermute(value, axis, [(i, i ^ far) for i in range(count)])]
    ppermute x32 -> x31, starting transfers between devices: 59.9 us -> 58.2 us  [partner(): return lax.ppermute(value, axis, [(i, i ^ far) for i in range(count)])]
    unnamed x86 -> x74, local copies, waits for them, and re-layouts: 10.9 us -> 11 us
  transfers between devices with their start and end apart: 48 -> 47, of which waited for: 15 -> 15; matrix products, arithmetic and copies ran while one was open for 8% -> 9% of each run, Pallas kernels for 38% -> 38%
where the time goes in v6:
time: 449 us; the launch traced here: 442 us
  Pallas kernels  201 us (45%)
  waiting for transfers between devices  89.2 us (20%)
  starting transfers between devices  72 us (16%)
  other arithmetic  38.5 us (9%)
  local copies, waits for them, and re-layouts  24.6 us (5%)
  between operations  16 us (4%)
    ppermute x31, waiting for transfers between devices, partner(): return lax.ppermute(value, axis, [(i, i ^ far) for i in range(count)])  68.8 us
    ppermute x31, starting transfers between devices, partner(): return lax.ppermute(value, axis, [(i, i ^ far) for i in range(count)])  58.2 us
    pallas_call x2, Pallas kernels, ffn_back(): pl.pallas_call(functools.partial(ffn_back_body, first, gate.shape[0], las...  43.1 us
    pallas_call x2, Pallas kernels, attend_back(): pl.pallas_call(attend_back_body, grid=(count,), in_specs=[wide, tall, fla...  31 us
    pallas_call x1, Pallas kernels, ffn(): pl.pallas_call(functools.partial(ffn_body, len(sources)), grid_spec=pltpu...  22.6 us
    all_to_all x2, waiting for transfers between devices, to_owner(): lax.all_to_all(value, 'col', split_axis=0, concat_axis=1, tiled=True)  17.3 us
    pallas_call x1, Pallas kernels, attend(): pl.pallas_call(attend_body, grid=(KVH,), in_specs=[pl.BlockSpec((part, pi...  16.4 us
    pallas_call x1, Pallas kernels, project(): pl.pallas_call(project_body, grid=(blocks,), in_specs=[whole((width, leng...  15.2 us
  transfers between devices with their start and end apart: 47, of which 15 were waited for; matrix products, arithmetic and copies ran while one was open for 9% of the time, Pallas kernels for 38%

profile of v6, /device:TPU:0, one launch (start us, length us, event | category | flops | bytes accessed | tf_op | source)
XLA Modules:
  0.0 441.7 jit_solution(7160456833432985368)
XLA Ops:
  10.0 5.1 %collective-permute-start.2 = (bf16[120,640]{1,0:T(8,128)(2,1)S(1)}, bf16[120,640]{1,0:T(8,128)(2,1)S(1)}, u32[]{:S(2)}, u32[]{:S(2)}) collective-permute-start(bf16[120,640]{1,0:T(8,128)(2,1)S(1)} %pad_maximum_fusion.5), channel_id=1, source_target_pairs={{0,3},{1,2},{2,1},{3,0},{4,7},{5,6},{6,5},{7,4},{8,11},{9,10},{10,... | collective-permute-start | bytes 460808 | tf_op jit(solution)/shard_map/ppermute | solution.py:919
  20.0 8.1 %collective-permute-done.1 = bf16[120,640]{1,0:T(8,128)(2,1)S(1)} collective-permute-done((bf16[120,640]{1,0:T(8,128)(2,1)S(1)}, bf16[120,640]{1,0:T(8,128)(2,1)S(1)}, u32[]{:S(2)}, u32[]{:S(2)}) %collective-permute-start.1) | collective-permute-done | bytes 153632 | tf_op jit(solution)/shard_map/ppermute | solution.py:919
  28.2 2.6 collective-permute-start.7
  30.9 2.5 collective-permute-start.10
  34.5 9.3 %collective-permute-done.7 = bf16[368,640]{1,0:T(8,128)(2,1)S(1)} collective-permute-done((bf16[368,640]{1,0:T(8,128)(2,1)S(1)}, bf16[368,640]{1,0:T(8,128)(2,1)S(1)}, u32[]{:S(2)}, u32[]{:S(2)}) %collective-permute-start.7) | collective-permute-done | bytes 471072 | tf_op jit(solution)/shard_map/ppermute | solution.py:919
  43.8 18.1 %collective-permute-start.5 = (bf16[368,640]{1,0:T(8,128)(2,1)S(1)}, bf16[368,640]{1,0:T(8,128)(2,1)S(1)}, u32[]{:S(2)}, u32[]{:S(2)}) collective-permute-start(bf16[368,640]{1,0:T(8,128)(2,1)S(1)} %constant_dynamic-update-slice_fusion), channel_id=1, source_target_pairs={{0,1},{1,0},{2,3},{3,2},{4,5},{5,4},{6,7},{7,6},{8,9},{9,8},{10,11... | collective-permute-start | bytes 1413128 | tf_op jit(solution)/shard_map/ppermute | solution.py:919
  63.5 5.9 %collective-permute-done.6 = bf16[368,640]{1,0:T(8,128)(2,1)S(1)} collective-permute-done((bf16[368,640]{1,0:T(8,128)(2,1)S(1)}, bf16[368,640]{1,0:T(8,128)(2,1)S(1)}, u32[]{:S(2)}, u32[]{:S(2)}) %collective-permute-start.6) | collective-permute-done | bytes 471072 | tf_op jit(solution)/shard_map/ppermute | solution.py:919
  69.4 8.6 %collective-permute-done.5 = bf16[368,640]{1,0:T(8,128)(2,1)S(1)} collective-permute-done((bf16[368,640]{1,0:T(8,128)(2,1)S(1)}, bf16[368,640]{1,0:T(8,128)(2,1)S(1)}, u32[]{:S(2)}, u32[]{:S(2)}) %collective-permute-start.5) | collective-permute-done | bytes 471072 | tf_op jit(solution)/shard_map/ppermute | solution.py:919
  81.4 3.7 all-to-all-start
  91.5 2.0 copy.69.rank
  93.5 6.0 %gather_tokens.1 = bf16[4,240,768]{2,1,0:T(8,128)(2,1)} custom-call(f32[4,240,1024]{2,1,0:T(8,128)} %values.1, s32[4,1024,1]{2,1,0:T(8,128)} %copy.69.rank), custom_call_target="tpu_custom_call" | custom-call | flops 47185920 | bytes 184320 | tf_op jit(solution)/shard_map/gather_tokens/pallas_call | solution.py:84
  105.9 6.3 %join.1.w.refs_7_ = bf16[4,960,640]{2,1,0:T(8,128)(2,1)} custom-call(s32[3]{0:T(128)} %pad_add_fusion.who, bf16[4,120,640]{2,1,0:T(8,128)(2,1)} %copy-done.4, bf16[4,120,640]{2,1,0:T(8,128)(2,1)} %copy-done.10, bf16[4,120,640]{2,1,0:T(8,128)(2,1)} %copy-done.9, bf16[4,120,640]{2,1,0:T(8,128)(2,1)} %copy-done.8, ...), custom_call_target="tpu_custom_call" | custom-call | bytes 307200 | tf_op jit(solution)/shard_map/join/pallas_call | solution.py:150
  112.2 17.3 %all-to-all-done = bf16[4,240,1024]{2,1,0:T(8,128)(2,1)S(1)} async-done(((bf16[4,240,1024]{2,1,0:T(8,128)(2,1)}), bf16[4,240,1024]{2,1,0:T(8,128)(2,1)S(1)}, u32[]{:S(2)}, u32[]{:S(2)}) %all-to-all-start) | async-done | bytes 1966112 | tf_op jit(solution)/shard_map/all_to_all | solution.py:963
  130.8 3.8 all-to-all-start.1
  134.6 15.2 %project.1 = (bf16[960,768]{1,0:T(8,128)(2,1)}, f32[1,768]{1,0:T(1,128)}, bf16[960,768]{1,0:T(8,128)(2,1)}, bf16[320,1024]{1,0:T(8,128)(2,1)}, bf16[5,1024,64]{2...) custom-call(bf16[960,1024]{1,0:T(8,128)(2,1)} %bitcast.88, ...), custom_call_target="tpu_custom_call" | custom-call | flops 130744320 | bytes 552960 | tf_op jit(solution)/shard_map/project/pallas_call | solution.py:229
  150.5 16.4 %attend.1 = (bf16[960,768]{1,0:T(8,128)(2,1)}, f32[5,3,768]{2,1,0:T(4,128)}) custom-call(bf16[960,768]{1,0:T(8,128)(2,1)} %get-tuple-element.248.q, bf16[5,1024,64]{2,1,0:T(8,128)(2,1)} %get-tuple-element.249.k, bf16[320,1024]{1,0:T(8,128)(2,1)} %get-tuple-element.250.vt, s32[1,768]{1,0:T(1,128)} %max.18.limit), custom_call_target="tpu_custom_call" | custom-call | flops 377487360 | bytes 92160 | tf_op jit(solution)/shard_map/attend/pallas_call | solution.py:322
  166.9 8.1 %merge.1 = (f32[960,768]{1,0:T(8,128)}, f32[1,768]{1,0:T(1,128)}, bf16[960,768]{1,0:T(8,128)(2,1)}) custom-call(bf16[960,768]{1,0:T(8,128)(2,1)} %get-tuple-element.252.mixed, bf16[960,768]{1,0:T(8,128)(2,1)} %get-tuple-element.253.picked.refs_4_, f32[960,128]{1,0:T(8,128)} %broadcast_in_dim.39.gain.refs_8_, bf16[4,960,640]{2,1,0:T(8,128)(2,1)} %join.1.w.refs_7_), custom_call_target="tpu_custom_call" | custom-call | flops 44236800 | bytes 476160 | tf_op jit(solution)/shard_map/merge/pallas_call | solution.py:445
  176.6 22.6 %ffn.1 = (bf16[4,640,768]{2,1,0:T(8,128)(2,1)}, bf16[4,640,768]{2,1,0:T(8,128)(2,1)}, bf16[4,640,768]{2,1,0:T(8,128)(2,1)}, bf16[960,768]{1,0:T(8,128)(2,1)}, bf16[960,768]{1,0:T(8,128)(2,1)}) custom-call(s32[3]{0:T(128)} %pad_add_fusion.who, bf16[960,768]{1,0:T(8,128)(2,1)} %get-tuple-element.260.normed, f32[960,768]{1,0:T(8,128)} %get-tuple-element.261.branch.refs_2_, ...), custom_call_target="tpu_custom_call" | custom-call | flops 353894400 | bytes 645120 | tf_op jit(solution)/shard_map/ffn/pallas_call | solution.py:572
  199.3 9.6 %down_grad.1 = (bf16[4,4,128,640]{3,2,1,0:T(8,128)(2,1)}, bf16[4,4,128,640]{3,2,1,0:T(8,128)(2,1)}) custom-call(s32[3]{0:T(128)} %pad_add_fusion.who, bf16[960,768]{1,0:T(8,128)(2,1)} %multiply_convert_fusion.grad_ffn, bf16[4,640,768]{2,1,0:T(8,128)(2,1)} %get-tuple-element.266.active), custom_call_target="tpu_custom_call" | custom-call | flops 117964800 | bytes 460800 | tf_op jit(solution)/shard_map/down_grad/pallas_call | solution.py:612
  209.8 2.0 collective-permute-start.16
  211.8 2.3 collective-permute-start.17
  214.2 18.9 %ffn_back.2 = (bf16[4,2,240,640]{3,2,1,0:T(8,128)(2,1)}, bf16[4,2,240,640]{3,2,1,0:T(8,128)(2,1)}, f32[960,768]{1,0:T(8,128)}) custom-call(s32[3]{0:T(128)} %pad_add_fusion.who, bf16[960,768]{1,0:T(8,128)(2,1)} %get-tuple-element.260.normed, bf16[960,768]{1,0:T(8,128)(2,1)} %multiply_convert_fusion.grad_ffn, ...), custom_call_target="tpu_custom_call" | custom-call | flops 294912000 | bytes 660480 | tf_op jit(solution)/shard_map/ffn_back/pallas_call | solution.py:702
  233.9 3.4 fusion.7
  238.9 1.7 collective-permute-start.20
  241.4 24.3 %ffn_back.3 = (bf16[4,2,240,640]{3,2,1,0:T(8,128)(2,1)}, bf16[4,2,240,640]{3,2,1,0:T(8,128)(2,1)}, bf16[960,768]{1,0:T(8,128)(2,1)}, bf16[960,768]{1,0:T(8,128)(...) custom-call(s32[3]{0:T(128)} %pad_add_fusion.who, bf16[960,768]{1,0:T(8,128)(2,1)} %get-tuple-element.260.normed, ...), custom_call_target="tpu_custom_call" | custom-call | flops 294912000 | bytes 660480 | tf_op jit(solution)/shard_map/ffn_back/pallas_call | solution.py:702
  265.7 3.7 collective-permute-done.20
  270.1 1.8 add_convert_fusion.5
  278.0 9.0 %merge_back.1 = (bf16[4,960,240]{2,1,0:T(8,128)(2,1)}, bf16[960,768]{1,0:T(8,128)(2,1)}) custom-call(bf16[960,768]{1,0:T(8,128)(2,1)} %get-tuple-element.252.mixed, bf16[960,768]{1,0:T(8,128)(2,1)} %get-tuple-element.326.grad, bf16[4,960,640]{2,1,0:T(8,128)(2,1)} %join.1.w.refs_7_), custom_call_target="tpu_custom_call" | custom-call | flops 88473600 | bytes 445440 | tf_op jit(solution)/shard_map/merge_back/pallas_call | solution.py:748
  286.9 2.4 collective-permute-start.24
  289.4 1.7 fusion.19
  291.1 18.2 %attend_back.2 = (bf16[576,768]{1,0:T(8,128)(2,1)}, bf16[192,1024]{1,0:T(8,128)(2,1)}, bf16[192,1024]{1,0:T(8,128)(2,1)}) custom-call(bf16[960,768]{1,0:T(8,128)(2,1)} %get-tuple-element.248.q, bf16[5,1024,64]{2,1,0:T(8,128)(2,1)} %get-tuple-element.249.k, bf16[320,1024]{1,0:T(8,128)(2,1)} %get-tuple-element.322.kt, ...), custom_call_target="tpu_custom_call" | custom-call | flops 566231040 | bytes 110592 | tf_op jit(solution)/shard_map/attend_back/pallas_call | solution.py:389
  312.9 1.7 add_convert_fusion.11
  317.1 12.8 %attend_back.3 = (bf16[384,768]{1,0:T(8,128)(2,1)}, bf16[128,1024]{1,0:T(8,128)(2,1)}, bf16[128,1024]{1,0:T(8,128)(2,1)}) custom-call(bf16[960,768]{1,0:T(8,128)(2,1)} %get-tuple-element.248.q, bf16[5,1024,64]{2,1,0:T(8,128)(2,1)} %get-tuple-element.249.k, bf16[320,1024]{1,0:T(8,128)(2,1)} %get-tuple-element.322.kt, ...), custom_call_target="tpu_custom_call" | custom-call | flops 377487360 | bytes 73728 | tf_op jit(solution)/shard_map/attend_back/pallas_call | solution.py:389
  329.9 15.0 %mixing_grad.1 = (bf16[4,4,128,640]{3,2,1,0:T(8,128)(2,1)}, bf16[4,4,128,640]{3,2,1,0:T(8,128)(2,1)}, bf16[4,400,1024]{2,1,0:T(8,128)(2,1)}, f32[960,1]{1,0:T(8,128)}) custom-call(s32[3]{0:T(128)} %pad_add_fusion.who, bf16[960,1024]{1,0:T(8,128)(2,1)} %bitcast.89, s32[1,1024]{1,0:T(1,128)} %copy-done.26, f32[960,128]{1,0:T(8,128)} %broadcast_in_dim.38.gain, ...), custom_call_target="tpu_custom_call" | custom-call | flops 145489920 | bytes 307200 | tf_op jit(solution)/shard_map/mixing_grad/pallas_call | solution.py:818
  345.6 1.8 add_convert_fusion.10
  349.2 2.4 collective-permute-start.35
  351.6 12.1 %project_back.1 = bf16[960,1024]{1,0:T(8,128)(2,1)} custom-call(bf16[960,1024]{1,0:T(8,128)(2,1)} %bitcast.90, s32[1,1024]{1,0:T(1,128)} %copy-done.26, f32[960,128]{1,0:T(8,128)} %broadcast_in_dim.38.gain, bf16[4,400,1024]{2,1,0:T(8,128)(2,1)} %get-tuple-element.379.grads, bf16[960,768]{1,0:T(8,128)(2,1)} %get-tuple-element.380.rest, ...), custom_call_target="tpu_custom_call" | custom-call | flops 145489920 | bytes 460800 | tf_op jit(solution)/shard_map/project_back/pallas_call | solution.py:883
  363.7 3.9 all-to-all-start.2
  367.6 4.1 fusion.11
  375.8 6.9 %scatter_tokens.1 = f32[4,240,1024]{2,1,0:T(8,128)} custom-call(s32[3]{0:T(128)} %pad_add_fusion.who, f32[4,240,1024]{2,1,0:T(8,128)} %base.1, s32[4,1,1024]{2,1,0:T(1,128)} %broadcast_in_dim.45.rank, bf16[240,768]{1,0:T(8,128)(2,1)} %get-tuple-element.393.refs_0_, bf16[240,768]{1,0:T(8,128)(2,1)} %copy-done.18, bf16[240,768]{1,0:T(8,128)(2,1)} %copy-done.19, ...), custom_call_target="tpu_custom_call" | custom-call | flops 47185920 | bytes 307200 | tf_op jit(solution)/shard_map/scatter_tokens/pallas_call | solution.py:114
  382.7 6.8 %collective-permute-done.36 = bf16[4,128,640]{2,1,0:T(8,128)(2,1)S(1)} collective-permute-done((bf16[4,128,640]{2,1,0:T(8,128)(2,1)}, bf16[4,128,640]{2,1,0:T(8,128)(2,1)S(1)}, u32[]{:S(2)}, u32[]{:S(2)}) %collective-permute-start.36) | collective-permute-done | bytes 655392 | tf_op jit(solution)/shard_map/ppermute | solution.py:919
  389.5 12.7 %collective-permute-done.37 = bf16[4,128,640]{2,1,0:T(8,128)(2,1)S(1)} collective-permute-done((bf16[4,128,640]{2,1,0:T(8,128)(2,1)S(1)}, bf16[4,128,640]{2,1,0:T(8,128)(2,1)S(1)}, u32[]{:S(2)}, u32[]{:S(2)}) %collective-permute-start.37) | collective-permute-done | bytes 655392 | tf_op jit(solution)/shard_map/ppermute | solution.py:919
  402.1 1.9 collective-permute-done.38
  409.7 1.9 copy.76
  411.6 2.1 all-to-all-done.2
  413.7 5.0 %convert_add_fusion = f32[4,240,1024]{2,1,0:T(8,128)} fusion(f32[4,240,1024]{2,1,0:T(8,128)} %values.1, bf16[4,240,1024]{2,1,0:T(8,128)(2,1)S(1)} %all-to-all-done.2), kind=kLoop, calls=%fused_computation.6 | loop fusion | flops 1966080 | bytes 9830400 | tf_op jit(solution)/shard_map/add | solution.py:1182
  418.8 2.0 collective-permute-done.39
  422.8 8.6 %collective-permute-done.40 = bf16[1,128,640]{2,1,0:T(8,128)(2,1)S(1)} collective-permute-done((bf16[1,128,640]{2,1,0:T(8,128)(2,1)S(1)}, bf16[1,128,640]{2,1,0:T(8,128)(2,1)S(1)}, u32[]{:S(2)}, u32[]{:S(2)}) %collective-permute-start.40) | collective-permute-done | bytes 163872 | tf_op jit(solution)/shard_map/ppermute | solution.py:919
  (213 shorter events, 63.5 us)
Async XLA Ops:
  7.2 169.4 %all-gather.3.cloned.1.call-start = ((), (), s32[]{:S(2)}) async-start(), calls=%async_computation.3 | async-start | bytes 16957440 | tf_op jit(solution)/shard_map/all_gather | solution.py:1021
  10.0 10.0 %collective-permute-start.2 = (bf16[120,640]{1,0:T(8,128)(2,1)S(1)}, bf16[120,640]{1,0:T(8,128)(2,1)S(1)}, u32[]{:S(2)}, u32[]{:S(2)}) collective-permute-start(bf16[120,640]{1,0:T(8,128)(2,1)S(1)} %pad_maximum_fusion.5), channel_id=1, source_target_pairs={{0,3},{1,2},{2,1},{3,0},{4,7},{5,6},{6,5},{7,4},{8,11},{9,10},{10,... | collective-permute-start | bytes 460808 | tf_op jit(solution)/shard_map/ppermute | solution.py:919
  15.1 13.0 %collective-permute-start.1 = (bf16[120,640]{1,0:T(8,128)(2,1)S(1)}, bf16[120,640]{1,0:T(8,128)(2,1)S(1)}, u32[]{:S(2)}, u32[]{:S(2)}) collective-permute-start(bf16[120,640]{1,0:T(8,128)(2,1)S(1)} %pad_maximum_fusion.5), channel_id=1, source_target_pairs={{0,2},{1,3},{2,0},{3,1},{4,6},{5,7},{6,4},{7,5},{8,10},{9,11},{10,... | collective-permute-start | bytes 460808 | tf_op jit(solution)/shard_map/ppermute | solution.py:919
  15.1 13.0 %collective-permute-start = (bf16[120,640]{1,0:T(8,128)(2,1)S(1)}, bf16[120,640]{1,0:T(8,128)(2,1)S(1)}, u32[]{:S(2)}, u32[]{:S(2)}) collective-permute-start(bf16[120,640]{1,0:T(8,128)(2,1)S(1)} %pad_maximum_fusion.5), channel_id=1, source_target_pairs={{0,1},{1,0},{2,3},{3,2},{4,5},{5,4},{6,7},{7,6},{8,9},{9,8},{10,11... | collective-permute-start | bytes 460808 | tf_op jit(solution)/shard_map/ppermute | solution.py:919
  16.9 1.6 collective-permute-start.4
  17.9 1.6 collective-permute-start.3
  28.2 15.6 %collective-permute-start.7 = (bf16[368,640]{1,0:T(8,128)(2,1)S(1)}, bf16[368,640]{1,0:T(8,128)(2,1)S(1)}, u32[]{:S(2)}, u32[]{:S(2)}) collective-permute-start(bf16[368,640]{1,0:T(8,128)(2,1)S(1)} %constant_dynamic-update-slice_fusion), channel_id=1, source_target_pairs={{0,3},{1,2},{2,1},{3,0},{4,7},{5,6},{6,5},{7,4},{8,11},{9,10},{10,... | collective-permute-start | bytes 1413128 | tf_op jit(solution)/shard_map/ppermute | solution.py:919
  30.9 58.3 %copy-start.4 = (bf16[4,120,640]{2,1,0:T(8,128)(2,1)}, bf16[4,120,640]{2,1,0:T(8,128)(2,1)S(1)}, u32[]{:S(2)}) copy-start(bf16[4,120,640]{2,1,0:T(8,128)(2,1)S(1)} %pad_maximum_fusion.1.refs_0_) | copy-start | bytes 1843204
  30.9 47.1 %collective-permute-start.10 = (bf16[4,120,640]{2,1,0:T(8,128)(2,1)S(1)}, bf16[4,120,640]{2,1,0:T(8,128)(2,1)S(1)}, u32[]{:S(2)}, u32[]{:S(2)}) collective-permute-start(bf16[4,120,640]{2,1,0:T(8,128)(2,1)S(1)} %pad_maximum_fusion.1.refs_0_), channel_id=1, source_target_pairs={{0,24},{4,28},{8,16},{12,20},{16,8},{20,12},{24,0},{28,4},{1,25},{... | collective-permute-start | bytes 1843208 | tf_op jit(solution)/shard_map/ppermute | solution.py:919
  33.4 44.6 %collective-permute-start.9 = (bf16[4,120,640]{2,1,0:T(8,128)(2,1)S(1)}, bf16[4,120,640]{2,1,0:T(8,128)(2,1)S(1)}, u32[]{:S(2)}, u32[]{:S(2)}) collective-permute-start(bf16[4,120,640]{2,1,0:T(8,128)(2,1)S(1)} %pad_maximum_fusion.1.refs_0_), channel_id=1, source_target_pairs={{0,16},{4,20},{8,24},{12,28},{16,0},{20,4},{24,8},{28,12},{1,17},{... | collective-permute-start | bytes 1843208 | tf_op jit(solution)/shard_map/ppermute | solution.py:919
  33.9 44.1 %collective-permute-start.8 = (bf16[4,120,640]{2,1,0:T(8,128)(2,1)S(1)}, bf16[4,120,640]{2,1,0:T(8,128)(2,1)S(1)}, u32[]{:S(2)}, u32[]{:S(2)}) collective-permute-start(bf16[4,120,640]{2,1,0:T(8,128)(2,1)S(1)} %pad_maximum_fusion.1.refs_0_), channel_id=1, source_target_pairs={{0,8},{4,12},{8,0},{12,4},{16,24},{20,28},{24,16},{28,20},{1,9},{5... | collective-permute-start | bytes 1843208 | tf_op jit(solution)/shard_map/ppermute | solution.py:919
  34.5 34.9 %collective-permute-start.6 = (bf16[368,640]{1,0:T(8,128)(2,1)S(1)}, bf16[368,640]{1,0:T(8,128)(2,1)S(1)}, u32[]{:S(2)}, u32[]{:S(2)}) collective-permute-start(bf16[368,640]{1,0:T(8,128)(2,1)S(1)} %constant_dynamic-update-slice_fusion), channel_id=1, source_target_pairs={{0,2},{1,3},{2,0},{3,1},{4,6},{5,7},{6,4},{7,5},{8,10},{9,11},{10,... | collective-permute-start | bytes 1413128 | tf_op jit(solution)/shard_map/ppermute | solution.py:919
  43.8 34.2 %collective-permute-start.5 = (bf16[368,640]{1,0:T(8,128)(2,1)S(1)}, bf16[368,640]{1,0:T(8,128)(2,1)S(1)}, u32[]{:S(2)}, u32[]{:S(2)}) collective-permute-start(bf16[368,640]{1,0:T(8,128)(2,1)S(1)} %constant_dynamic-update-slice_fusion), channel_id=1, source_target_pairs={{0,1},{1,0},{2,3},{3,2},{4,5},{5,4},{6,7},{7,6},{8,9},{9,8},{10,11... | collective-permute-start | bytes 1413128 | tf_op jit(solution)/shard_map/ppermute | solution.py:919
  81.4 48.1 %all-to-all-start = ((bf16[4,240,1024]{2,1,0:T(8,128)(2,1)}), bf16[4,240,1024]{2,1,0:T(8,128)(2,1)S(1)}, u32[]{:S(2)}, u32[]{:S(2)}) async-start(bf16[4,240,1024]{2,1,0:T(8,128)(2,1)} %convert_element_type.374), calls=%async_computation | async-start | bytes 3932160 | tf_op jit(solution)/shard_map/all_to_all | solution.py:963
  89.3 12.6 %collective-permute-start.11 = (bf16[4,120,640]{2,1,0:T(8,128)(2,1)S(1)}, bf16[4,120,640]{2,1,0:T(8,128)(2,1)}, u32[]{:S(2)}, u32[]{:S(2)}) collective-permute-start(bf16[4,120,640]{2,1,0:T(8,128)(2,1)S(1)} %pad_maximum_fusion.1.refs_0_), channel_id=1, source_target_pairs={{0,4},{4,0},{8,12},{12,8},{16,20},{20,16},{24,28},{28,24},{1,5},{5... | collective-permute-start | bytes 1843208 | tf_op jit(solution)/shard_map/ppermute | solution.py:913
  89.3 12.5 %collective-permute-start.12 = (bf16[4,120,640]{2,1,0:T(8,128)(2,1)}, bf16[4,120,640]{2,1,0:T(8,128)(2,1)}, u32[]{:S(2)}, u32[]{:S(2)}) collective-permute-start(bf16[4,120,640]{2,1,0:T(8,128)(2,1)} %copy-done.10), channel_id=1, source_target_pairs={{0,4},{4,0},{8,12},{12,8},{16,20},{20,16},{24,28},{28,24},{1,5},{5... | collective-permute-start | bytes 1843208 | tf_op jit(solution)/shard_map/ppermute | solution.py:913
  89.8 12.0 %collective-permute-start.13 = (bf16[4,120,640]{2,1,0:T(8,128)(2,1)}, bf16[4,120,640]{2,1,0:T(8,128)(2,1)}, u32[]{:S(2)}, u32[]{:S(2)}) collective-permute-start(bf16[4,120,640]{2,1,0:T(8,128)(2,1)} %copy-done.9), channel_id=1, source_target_pairs={{0,4},{4,0},{8,12},{12,8},{16,20},{20,16},{24,28},{28,24},{1,5},{5... | collective-permute-start | bytes 1843208 | tf_op jit(solution)/shard_map/ppermute | solution.py:913
  89.9 11.9 %collective-permute-start.14 = (bf16[4,120,640]{2,1,0:T(8,128)(2,1)S(1)}, bf16[4,120,640]{2,1,0:T(8,128)(2,1)}, u32[]{:S(2)}, u32[]{:S(2)}) collective-permute-start(bf16[4,120,640]{2,1,0:T(8,128)(2,1)S(1)} %collective-permute-done.10.refs_3_), channel_id=1, source_target_pairs={{0,4},{4,0},{8,12},{12,8},{16,20},{20,16},{24,28},{28,24},{1,5},{5... | collective-permute-start | bytes 1843208 | tf_op jit(solution)/shard_map/ppermute | solution.py:913
  130.8 44.2 %all-to-all-start.1 = ((bf16[4,240,768]{2,1,0:T(8,128)(2,1)}), bf16[4,240,768]{2,1,0:T(8,128)(2,1)S(1)}, u32[]{:S(2)}, u32[]{:S(2)}) async-start(bf16[4,240,768]{2,1,0:T(8,128)(2,1)} %gather_tokens.1), calls=%async_computation.1 | async-start | bytes 2949120 | tf_op jit(solution)/shard_map/all_to_all | solution.py:963
  209.8 23.3 %collective-permute-start.15 = (bf16[4,4,128,640]{3,2,1,0:T(8,128)(2,1)}, bf16[4,4,128,640]{3,2,1,0:T(8,128)(2,1)}, u32[]{:S(2)}, u32[]{:S(2)}) collective-permute-start(bf16[4,4,128,640]{3,2,1,0:T(8,128)(2,1)} %get-tuple-element.274), channel_id=1, source_target_pairs={{0,4},{4,0},{8,12},{12,8},{16,20},{20,16},{24,28},{28,24},{1,5},{5... | collective-permute-start | bytes 7864328 | tf_op jit(solution)/shard_map/ppermute | solution.py:913
  209.8 23.3 %collective-permute-start.16 = (bf16[240,768]{1,0:T(8,128)(2,1)S(1)}, bf16[240,768]{1,0:T(8,128)(2,1)S(1)}, u32[]{:S(2)}, u32[]{:S(2)}) collective-permute-start(bf16[240,768]{1,0:T(8,128)(2,1)S(1)} %get-tuple-element.281), channel_id=1, source_target_pairs={{0,1},{1,0},{2,3},{3,2},{4,5},{5,4},{6,7},{7,6},{8,9},{9,8},{10,11... | collective-permute-start | bytes 1105928 | tf_op jit(solution)/shard_map/ppermute | solution.py:919
  211.8 21.3 %collective-permute-start.17 = (bf16[240,768]{1,0:T(8,128)(2,1)S(1)}, bf16[240,768]{1,0:T(8,128)(2,1)S(1)}, u32[]{:S(2)}, u32[]{:S(2)}) collective-permute-start(bf16[240,768]{1,0:T(8,128)(2,1)S(1)} %get-tuple-element.282), channel_id=1, source_target_pairs={{0,2},{1,3},{2,0},{3,1},{4,6},{5,7},{6,4},{7,5},{8,10},{9,11},{10,... | collective-permute-start | bytes 1105928 | tf_op jit(solution)/shard_map/ppermute | solution.py:919
  237.4 32.7 %collective-permute-start.18 = (bf16[4,2,240,640]{3,2,1,0:T(8,128)(2,1)}, bf16[4,2,240,640]{3,2,1,0:T(8,128)(2,1)S(1)}, u32[]{:S(2)}, u32[]{:S(2)}) collective-permute-start(bf16[4,2,240,640]{3,2,1,0:T(8,128)(2,1)} %get-tuple-element.288), channel_id=1, source_target_pairs={{0,4},{4,0},{8,12},{12,8},{16,20},{20,16},{24,28},{28,24},{1,5},{5... | collective-permute-start | bytes 7372808 | tf_op jit(solution)/shard_map/ppermute | solution.py:913
  237.4 28.3 %collective-permute-start.19 = (bf16[4,128,640]{2,1,0:T(8,128)(2,1)}, bf16[4,128,640]{2,1,0:T(8,128)(2,1)S(1)}, u32[]{:S(2)}, u32[]{:S(2)}) collective-permute-start(bf16[4,128,640]{2,1,0:T(8,128)(2,1)} %get-tuple-element.290), channel_id=1, source_target_pairs={{0,8},{4,12},{8,0},{12,4},{16,24},{20,28},{24,16},{28,20},{1,9},{5... | collective-permute-start | bytes 1966088 | tf_op jit(solution)/shard_map/ppermute | solution.py:919
  238.9 30.5 %collective-permute-start.20 = (bf16[4,128,640]{2,1,0:T(8,128)(2,1)}, bf16[4,128,640]{2,1,0:T(8,128)(2,1)}, u32[]{:S(2)}, u32[]{:S(2)}) collective-permute-start(bf16[4,128,640]{2,1,0:T(8,128)(2,1)} %get-tuple-element.291), channel_id=1, source_target_pairs={{0,16},{4,20},{8,24},{12,28},{16,0},{20,4},{24,8},{28,12},{1,17},{... | collective-permute-start | bytes 1966088 | tf_op jit(solution)/shard_map/ppermute | solution.py:919
  240.6 29.5 %collective-permute-start.21 = (bf16[4,128,640]{2,1,0:T(8,128)(2,1)}, bf16[4,128,640]{2,1,0:T(8,128)(2,1)}, u32[]{:S(2)}, u32[]{:S(2)}) collective-permute-start(bf16[4,128,640]{2,1,0:T(8,128)(2,1)} %get-tuple-element.292), channel_id=1, source_target_pairs={{0,24},{4,28},{8,16},{12,20},{16,8},{20,12},{24,0},{28,4},{1,25},{... | collective-permute-start | bytes 1966088 | tf_op jit(solution)/shard_map/ppermute | solution.py:919
  240.8 24.8 %collective-permute-start.22 = (bf16[240,768]{1,0:T(8,128)(2,1)}, bf16[240,768]{1,0:T(8,128)(2,1)}, u32[]{:S(2)}, u32[]{:S(2)}) collective-permute-start(bf16[240,768]{1,0:T(8,128)(2,1)} %get-tuple-element.296), channel_id=1, source_target_pairs={{0,3},{1,2},{2,1},{3,0},{4,7},{5,6},{6,5},{7,4},{8,11},{9,10},{10,... | collective-permute-start | bytes 1105928 | tf_op jit(solution)/shard_map/ppermute | solution.py:919
  273.9 13.1 %collective-permute-start.28 = (bf16[4,2,240,640]{3,2,1,0:T(8,128)(2,1)}, bf16[4,2,240,640]{3,2,1,0:T(8,128)(2,1)S(1)}, u32[]{:S(2)}, u32[]{:S(2)}) collective-permute-start(bf16[4,2,240,640]{3,2,1,0:T(8,128)(2,1)} %get-tuple-element.325), channel_id=1, source_target_pairs={{0,4},{4,0},{8,12},{12,8},{16,20},{20,16},{24,28},{28,24},{1,5},{5... | collective-permute-start | bytes 7372808 | tf_op jit(solution)/shard_map/ppermute | solution.py:913
  273.9 35.4 %collective-permute-start.25 = (bf16[2,240,640]{2,1,0:T(8,128)(2,1)}, bf16[2,240,640]{2,1,0:T(8,128)(2,1)S(1)}, u32[]{:S(2)}, u32[]{:S(2)}) collective-permute-start(bf16[2,240,640]{2,1,0:T(8,128)(2,1)} %get-tuple-element.319), channel_id=1, source_target_pairs={{0,8},{4,12},{8,0},{12,4},{16,24},{20,28},{24,16},{28,20},{1,9},{5... | collective-permute-start | bytes 1843208 | tf_op jit(solution)/shard_map/ppermute | solution.py:919
  275.3 34.0 %collective-permute-start.26 = (bf16[2,240,640]{2,1,0:T(8,128)(2,1)}, bf16[2,240,640]{2,1,0:T(8,128)(2,1)}, u32[]{:S(2)}, u32[]{:S(2)}) collective-permute-start(bf16[2,240,640]{2,1,0:T(8,128)(2,1)} %get-tuple-element.320), channel_id=1, source_target_pairs={{0,16},{4,20},{8,24},{12,28},{16,0},{20,4},{24,8},{28,12},{1,17},{... | collective-permute-start | bytes 1843208 | tf_op jit(solution)/shard_map/ppermute | solution.py:919
  276.1 33.2 %collective-permute-start.27 = (bf16[2,240,640]{2,1,0:T(8,128)(2,1)}, bf16[2,240,640]{2,1,0:T(8,128)(2,1)}, u32[]{:S(2)}, u32[]{:S(2)}) collective-permute-start(bf16[2,240,640]{2,1,0:T(8,128)(2,1)} %get-tuple-element.321), channel_id=1, source_target_pairs={{0,24},{4,28},{8,16},{12,20},{16,8},{20,12},{24,0},{28,4},{1,25},{... | collective-permute-start | bytes 1843208 | tf_op jit(solution)/shard_map/ppermute | solution.py:919
  277.4 31.9 %collective-permute-start.23 = (bf16[128,640]{1,0:T(8,128)(2,1)S(1)}, bf16[128,640]{1,0:T(8,128)(2,1)S(1)}, u32[]{:S(2)}, u32[]{:S(2)}) collective-permute-start(bf16[128,640]{1,0:T(8,128)(2,1)S(1)} %get-tuple-element.316), channel_id=1, source_target_pairs={{0,2},{1,3},{2,0},{3,1},{4,6},{5,7},{6,4},{7,5},{8,10},{9,11},{10,... | collective-permute-start | bytes 491528 | tf_op jit(solution)/shard_map/ppermute | solution.py:919
  286.9 22.3 %collective-permute-start.24 = (bf16[128,640]{1,0:T(8,128)(2,1)S(1)}, bf16[128,640]{1,0:T(8,128)(2,1)S(1)}, u32[]{:S(2)}, u32[]{:S(2)}) collective-permute-start(bf16[128,640]{1,0:T(8,128)(2,1)S(1)} %get-tuple-element.317), channel_id=1, source_target_pairs={{0,3},{1,2},{2,1},{3,0},{4,7},{5,6},{6,5},{7,4},{8,11},{9,10},{10,... | collective-permute-start | bytes 491528 | tf_op jit(solution)/shard_map/ppermute | solution.py:919
  309.3 35.6 %collective-permute-start.31 = (bf16[2,240,640]{2,1,0:T(8,128)(2,1)}, bf16[2,240,640]{2,1,0:T(8,128)(2,1)}, u32[]{:S(2)}, u32[]{:S(2)}) collective-permute-start(bf16[2,240,640]{2,1,0:T(8,128)(2,1)} %get-tuple-element.351), channel_id=1, source_target_pairs={{0,8},{4,12},{8,0},{12,4},{16,24},{20,28},{24,16},{28,20},{1,9},{5... | collective-permute-start | bytes 1843208 | tf_op jit(solution)/shard_map/ppermute | solution.py:919
  310.8 34.1 %collective-permute-start.32 = (bf16[2,240,640]{2,1,0:T(8,128)(2,1)}, bf16[2,240,640]{2,1,0:T(8,128)(2,1)}, u32[]{:S(2)}, u32[]{:S(2)}) collective-permute-start(bf16[2,240,640]{2,1,0:T(8,128)(2,1)} %get-tuple-element.352), channel_id=1, source_target_pairs={{0,16},{4,20},{8,24},{12,28},{16,0},{20,4},{24,8},{28,12},{1,17},{... | collective-permute-start | bytes 1843208 | tf_op jit(solution)/shard_map/ppermute | solution.py:919
  311.6 33.3 %collective-permute-start.33 = (bf16[2,240,640]{2,1,0:T(8,128)(2,1)}, bf16[2,240,640]{2,1,0:T(8,128)(2,1)}, u32[]{:S(2)}, u32[]{:S(2)}) collective-permute-start(bf16[2,240,640]{2,1,0:T(8,128)(2,1)} %get-tuple-element.353), channel_id=1, source_target_pairs={{0,24},{4,28},{8,16},{12,20},{16,8},{20,12},{24,0},{28,4},{1,25},{... | collective-permute-start | bytes 1843208 | tf_op jit(solution)/shard_map/ppermute | solution.py:919
  314.7 30.2 %collective-permute-start.29 = (bf16[240,640]{1,0:T(8,128)(2,1)S(1)}, bf16[240,640]{1,0:T(8,128)(2,1)S(1)}, u32[]{:S(2)}, u32[]{:S(2)}) collective-permute-start(bf16[240,640]{1,0:T(8,128)(2,1)S(1)} %get-tuple-element.348), channel_id=1, source_target_pairs={{0,3},{1,2},{2,1},{3,0},{4,7},{5,6},{6,5},{7,4},{8,11},{9,10},{10,... | collective-permute-start | bytes 921608 | tf_op jit(solution)/shard_map/ppermute | solution.py:919
  316.3 28.6 %collective-permute-start.30 = (bf16[240,640]{1,0:T(8,128)(2,1)S(1)}, bf16[240,640]{1,0:T(8,128)(2,1)S(1)}, u32[]{:S(2)}, u32[]{:S(2)}) collective-permute-start(bf16[240,640]{1,0:T(8,128)(2,1)S(1)} %get-tuple-element.349), channel_id=1, source_target_pairs={{0,2},{1,3},{2,0},{3,1},{4,6},{5,7},{6,4},{7,5},{8,10},{9,11},{10,... | collective-permute-start | bytes 921608 | tf_op jit(solution)/shard_map/ppermute | solution.py:919
  349.2 14.5 %collective-permute-start.34 = (bf16[4,4,128,640]{3,2,1,0:T(8,128)(2,1)}, bf16[4,4,128,640]{3,2,1,0:T(8,128)(2,1)}, u32[]{:S(2)}, u32[]{:S(2)}) collective-permute-start(bf16[4,4,128,640]{3,2,1,0:T(8,128)(2,1)} %get-tuple-element.377), channel_id=1, source_target_pairs={{0,4},{4,0},{8,12},{12,8},{16,20},{20,16},{24,28},{28,24},{1,5},{5... | collective-permute-start | bytes 7864328 | tf_op jit(solution)/shard_map/ppermute | solution.py:913
  349.2 14.5 %collective-permute-start.35 = (bf16[368,640]{1,0:T(8,128)(2,1)S(1)}, bf16[368,640]{1,0:T(8,128)(2,1)S(1)}, u32[]{:S(2)}, u32[]{:S(2)}) collective-permute-start(bf16[368,640]{1,0:T(8,128)(2,1)S(1)} %pad_maximum_fusion.2), channel_id=1, source_target_pairs={{0,1},{1,0},{2,3},{3,2},{4,5},{5,4},{6,7},{7,6},{8,9},{9,8},{10,11... | collective-permute-start | bytes 1413128 | tf_op jit(solution)/shard_map/ppermute | solution.py:919
  363.7 50.0 %all-to-all-start.2 = ((bf16[4,240,1024]{2,1,0:T(8,128)(2,1)}), bf16[4,240,1024]{2,1,0:T(8,128)(2,1)S(1)}, u32[]{:S(2)}, u32[]{:S(2)}) async-start(bf16[4,240,1024]{2,1,0:T(8,128)(2,1)} %bitcast.93), calls=%async_computation.2 | async-start | bytes 3932160 | tf_op jit(solution)/shard_map/all_to_all | solution.py:970
  371.7 17.8 %collective-permute-start.36 = (bf16[4,128,640]{2,1,0:T(8,128)(2,1)}, bf16[4,128,640]{2,1,0:T(8,128)(2,1)S(1)}, u32[]{:S(2)}, u32[]{:S(2)}) collective-permute-start(bf16[4,128,640]{2,1,0:T(8,128)(2,1)} %get-tuple-element.390), channel_id=1, source_target_pairs={{0,8},{4,12},{8,0},{12,4},{16,24},{20,28},{24,16},{28,20},{1,9},{5... | collective-permute-start | bytes 1966088 | tf_op jit(solution)/shard_map/ppermute | solution.py:919
  373.1 29.0 %collective-permute-start.37 = (bf16[4,128,640]{2,1,0:T(8,128)(2,1)S(1)}, bf16[4,128,640]{2,1,0:T(8,128)(2,1)S(1)}, u32[]{:S(2)}, u32[]{:S(2)}) collective-permute-start(bf16[4,128,640]{2,1,0:T(8,128)(2,1)S(1)} %get-tuple-element.391), channel_id=1, source_target_pairs={{0,16},{4,20},{8,24},{12,28},{16,0},{20,4},{24,8},{28,12},{1,17},{... | collective-permute-start | bytes 1966088 | tf_op jit(solution)/shard_map/ppermute | solution.py:919
  373.9 30.0 %collective-permute-start.38 = (bf16[4,128,640]{2,1,0:T(8,128)(2,1)S(1)}, bf16[4,128,640]{2,1,0:T(8,128)(2,1)S(1)}, u32[]{:S(2)}, u32[]{:S(2)}) collective-permute-start(bf16[4,128,640]{2,1,0:T(8,128)(2,1)S(1)} %get-tuple-element.392), channel_id=1, source_target_pairs={{0,24},{4,28},{8,16},{12,20},{16,8},{20,12},{24,0},{28,4},{1,25},{... | collective-permute-start | bytes 1966088 | tf_op jit(solution)/shard_map/ppermute | solution.py:919
  404.2 4.6 %collective-permute-start.42 = (bf16[128,320]{1,0:T(8,128)(2,1)S(1)}, bf16[128,320]{1,0:T(8,128)(2,1)S(1)}, u32[]{:S(2)}, u32[]{:S(2)}) collective-permute-start(bf16[128,320]{1,0:T(8,128)(2,1)S(1)} %select_convert_fusion.1), channel_id=1, source_target_pairs={{0,4},{4,0},{8,12},{12,8},{16,20},{20,16},{24,28},{28,24},{1,5},{5... | collective-permute-start | bytes 245768 | tf_op jit(solution)/shard_map/ppermute | solution.py:913
  405.4 16.5 %collective-permute-start.41 = (bf16[120,640]{1,0:T(8,128)(2,1)S(1)}, bf16[120,640]{1,0:T(8,128)(2,1)S(1)}, u32[]{:S(2)}, u32[]{:S(2)}) collective-permute-start(bf16[120,640]{1,0:T(8,128)(2,1)S(1)} %select_convert_fusion), channel_id=1, source_target_pairs={{0,4},{4,0},{8,12},{12,8},{16,20},{20,16},{24,28},{28,24},{1,5},{5... | collective-permute-start | bytes 460808 | tf_op jit(solution)/shard_map/ppermute | solution.py:913
  407.1 13.7 %collective-permute-start.39 = (bf16[2,128,640]{2,1,0:T(8,128)(2,1)}, bf16[2,128,640]{2,1,0:T(8,128)(2,1)}, u32[]{:S(2)}, u32[]{:S(2)}) collective-permute-start(bf16[2,128,640]{2,1,0:T(8,128)(2,1)} %slice.69), channel_id=1, source_target_pairs={{0,1},{1,0},{2,3},{3,2},{4,5},{5,4},{6,7},{7,6},{8,9},{9,8},{10,11... | collective-permute-start | bytes 983048 | tf_op jit(solution)/shard_map/ppermute | solution.py:919
  421.9 9.6 %collective-permute-start.40 = (bf16[1,128,640]{2,1,0:T(8,128)(2,1)S(1)}, bf16[1,128,640]{2,1,0:T(8,128)(2,1)S(1)}, u32[]{:S(2)}, u32[]{:S(2)}) collective-permute-start(bf16[1,128,640]{2,1,0:T(8,128)(2,1)S(1)} %slice.92), channel_id=1, source_target_pairs={{0,2},{1,3},{2,0},{3,1},{4,6},{5,7},{6,4},{7,5},{8,10},{9,11},{10,... | collective-permute-start | bytes 491528 | tf_op jit(solution)/shard_map/ppermute | solution.py:919
  (32 other events, 326.0 us)
Sparse Core Ops, SparseCore 0:
  81.5 82.4 all-gather.2

commit v7 on v6

--- a/solution.py
+++ b/solution.py
@@ -195,28 +195,30 @@
     @pl.when(step == pl.num_programs(0) - 1)
     def _():
         half = HD // 2
-        for head in range(H):
-            at = head * HD
+
+        @pl.loop(0, H)
+        def _(head):
+            at = pl.multiple_of(head * HD, HD)
+            low, high = pl.ds(at, half), pl.ds(pl.multiple_of(at + half, half), half)
             a, b = turn(
-                q_raw[at : at + half].astype(F32),
-                q_raw[at + half : at + HD].astype(F32),
-                cos_q[...], sin_q[...], 1.0,
+                q_raw[low].astype(F32), q_raw[high].astype(F32), cos_q[...], sin_q[...], 1.0
             )
             scale = HD ** (-0.5)
-            q_out[at : at + half] = (a.astype(BF).astype(F32) * scale).astype(BF)
-            q_out[at + half : at + HD] = (b.astype(BF).astype(F32) * scale).astype(BF)
-        for head in range(KVH):
-            at = head * HD
+            q_out[low] = (a.astype(BF).astype(F32) * scale).astype(BF)
+            q_out[high] = (b.astype(BF).astype(F32) * scale).astype(BF)
+
+        @pl.loop(0, KVH)
+        def _(head):
+            at = pl.multiple_of(head * HD, HD)
+            low, high = pl.ds(at, half), pl.ds(pl.multiple_of(at + half, half), half)
             a, b = turn(
-                kv_raw[0, at : at + half].astype(F32),
-                kv_raw[0, at + half : at + HD].astype(F32),
-                cos_k[...], sin_k[...], 1.0,
+                kv_raw[0, low].astype(F32), kv_raw[0, high].astype(F32), cos_k[...], sin_k[...], 1.0
             )
             turned = jnp.concatenate([a, b], axis=0)
-            kt_out[at : at + HD] = turned.astype(BF)
+            kt_out[pl.ds(at, HD)] = turned.astype(BF)
             k_out[head] = turned.T.astype(BF)
-            value = kv_raw[1, at : at + HD]
-            vt_out[at : at + HD] = value
+            value = kv_raw[1, pl.ds(at, HD)]
+            vt_out[pl.ds(at, HD)] = value
             v_out[head] = value.astype(F32).T.astype(BF)
 
 
@@ -535,9 +537,9 @@
     ]
 
 
-def ffn_body(many, who, normed, branch, prob, *refs):
+def ffn_body(many, who, normed, branch, prob, cot, *refs):
     sources, refs = refs[:many], refs[many:]
-    gate_out, up_out, active_out, delta, both_out, forward, *buffers = refs
+    gate_out, up_out, active_out, delta, both_out, grad_ffn, forward, *buffers = refs
     w_pair, w_down, _ = buffers
     hidden = w_down.shape[2]
     slot = ffn_weights(who, 0, pl.num_programs(0), sources, *buffers)
@@ -545,6 +547,7 @@
     @pl.when(pl.program_id(0) == 0)
     def _():
         forward[...] = branch[...]
+        grad_ffn[...] = (prob[...] * cot[...].astype(F32)).astype(BF)
 
     tokens = normed[...]
     pair = dot_tn(w_pair[slot], tokens)
@@ -562,7 +565,7 @@
         both_out[...] = both.astype(BF)
 
 
-def ffn(who, normed, branch, prob, blocks, hidden, sources):
+def ffn(who, normed, branch, prob, cot, blocks, hidden, sources):
     width, picks = normed.shape
     full, row = whole((width, picks)), whole((1, picks))
     far = pl.BlockSpec(memory_space=pl.ANY)
@@ -574,17 +577,17 @@
         grid_spec=pltpu.PrefetchScalarGridSpec(
             num_scalar_prefetch=1,
             grid=(blocks,),
-            in_specs=[full, full, row] + [far] * len(sources),
-            out_specs=[kept] * 3 + [full, full],
+            in_specs=[full, full, row, full] + [far] * len(sources),
+            out_specs=[kept] * 3 + [full] * 3,
             scratch_shapes=[pltpu.VMEM((width, picks), F32)] + ffn_scratch(width, sources),
         ),
-        out_shape=[kept_shape] * 3 + [low, low],
+        out_shape=[kept_shape] * 3 + [low] * 3,
         compiler_params=params(60),
         cost_estimate=cost(
             6 * width * hidden * blocks * picks, 6 * width * hidden * blocks + 8 * width * picks
         ),
         name="ffn",
-    )(who, normed, branch, prob, *sources)
+    )(who, normed, branch, prob, cot, *sources)
 
 
 def down_grad_body(who, grad_ffn, active, keep, send):
@@ -1070,8 +1073,9 @@
     )
     mixed, mass = attend(q, k, vt, limit)
     (branch, inverse, normed), cot = hold(merge(mixed, picked, gain_two, mixing), cot)
-    gate, up, active, delta, both = ffn(who, normed, branch, prob, col_count, hidden, sources)
-    grad_ffn = (prob * cot.astype(F32)).astype(BF)
+    gate, up, active, delta, both, grad_ffn = ffn(
+        who, normed, branch, prob, cot, col_count, hidden, sources
+    )
     (keep_down, send_down), delta, gate = hold(
         down_grad(who, grad_ffn, active, pairs, col_count), delta, gate
     )

time: 449 us -> 449 us (level)
  transfers between devices with their start and end apart: 47 -> 47, of which waited for: 15 -> 14; matrix products, arithmetic and copies ran while one was open for 9% -> 8% of each run, Pallas kernels for 38% -> 38%
where the time goes in v7:
time: 449 us; the launch traced here: 442 us
  Pallas kernels  202 us (45%)
  waiting for transfers between devices  89.1 us (20%)
  starting transfers between devices  72 us (16%)
  other arithmetic  36.2 us (8%)
  local copies, waits for them, and re-layouts  25.6 us (6%)
  between operations  16 us (4%)
    ppermute x31, waiting for transfers between devices, partner(): return lax.ppermute(value, axis, [(i, i ^ far) for i in range(count)])  68.5 us
    ppermute x31, starting transfers between devices, partner(): return lax.ppermute(value, axis, [(i, i ^ far) for i in range(count)])  58.2 us
    pallas_call x2, Pallas kernels, ffn_back(): pl.pallas_call(functools.partial(ffn_back_body, first, gate.shape[0], las...  43.1 us
    pallas_call x2, Pallas kernels, attend_back(): pl.pallas_call(attend_back_body, grid=(count,), in_specs=[wide, tall, fla...  31 us
    pallas_call x1, Pallas kernels, ffn(): pl.pallas_call(functools.partial(ffn_body, len(sources)), grid_spec=pltpu...  23.4 us
    all_to_all x2, waiting for transfers between devices, to_owner(): lax.all_to_all(value, 'col', split_axis=0, concat_axis=1, tiled=True)  17.4 us
    pallas_call x1, Pallas kernels, attend(): pl.pallas_call(attend_body, grid=(KVH,), in_specs=[pl.BlockSpec((part, pi...  16.4 us
    pallas_call x1, Pallas kernels, project(): pl.pallas_call(project_body, grid=(blocks,), in_specs=[whole((width, leng...  15.3 us
  transfers between devices with their start and end apart: 47, of which 14 were waited for; matrix products, arithmetic and copies ran while one was open for 8% of the time, Pallas kernels for 38%

profile of v7, /device:TPU:0, one launch (start us, length us, event | category | flops | bytes accessed | tf_op | source)
XLA Modules:
  0.0 441.6 jit_solution(6954657924274120166)
XLA Ops:
  10.0 5.1 %collective-permute-start.2 = (bf16[120,640]{1,0:T(8,128)(2,1)S(1)}, bf16[120,640]{1,0:T(8,128)(2,1)S(1)}, u32[]{:S(2)}, u32[]{:S(2)}) collective-permute-start(bf16[120,640]{1,0:T(8,128)(2,1)S(1)} %pad_maximum_fusion.5), channel_id=1, source_target_pairs={{0,3},{1,2},{2,1},{3,0},{4,7},{5,6},{6,5},{7,4},{8,11},{9,10},{10,... | collective-permute-start | bytes 460808 | tf_op jit(solution)/shard_map/ppermute | solution.py:922
  20.0 8.1 %collective-permute-done.1 = bf16[120,640]{1,0:T(8,128)(2,1)S(1)} collective-permute-done((bf16[120,640]{1,0:T(8,128)(2,1)S(1)}, bf16[120,640]{1,0:T(8,128)(2,1)S(1)}, u32[]{:S(2)}, u32[]{:S(2)}) %collective-permute-start.1) | collective-permute-done | bytes 153632 | tf_op jit(solution)/shard_map/ppermute | solution.py:922
  28.2 2.6 collective-permute-start.7
  30.9 2.5 collective-permute-start.10
  34.5 9.3 %collective-permute-done.7 = bf16[368,640]{1,0:T(8,128)(2,1)S(1)} collective-permute-done((bf16[368,640]{1,0:T(8,128)(2,1)S(1)}, bf16[368,640]{1,0:T(8,128)(2,1)S(1)}, u32[]{:S(2)}, u32[]{:S(2)}) %collective-permute-start.7) | collective-permute-done | bytes 471072 | tf_op jit(solution)/shard_map/ppermute | solution.py:922
  43.8 18.1 %collective-permute-start.5 = (bf16[368,640]{1,0:T(8,128)(2,1)S(1)}, bf16[368,640]{1,0:T(8,128)(2,1)S(1)}, u32[]{:S(2)}, u32[]{:S(2)}) collective-permute-start(bf16[368,640]{1,0:T(8,128)(2,1)S(1)} %constant_dynamic-update-slice_fusion), channel_id=1, source_target_pairs={{0,1},{1,0},{2,3},{3,2},{4,5},{5,4},{6,7},{7,6},{8,9},{9,8},{10,11... | collective-permute-start | bytes 1413128 | tf_op jit(solution)/shard_map/ppermute | solution.py:922
  63.5 5.9 %collective-permute-done.6 = bf16[368,640]{1,0:T(8,128)(2,1)S(1)} collective-permute-done((bf16[368,640]{1,0:T(8,128)(2,1)S(1)}, bf16[368,640]{1,0:T(8,128)(2,1)S(1)}, u32[]{:S(2)}, u32[]{:S(2)}) %collective-permute-start.6) | collective-permute-done | bytes 471072 | tf_op jit(solution)/shard_map/ppermute | solution.py:922
  69.4 8.6 %collective-permute-done.5 = bf16[368,640]{1,0:T(8,128)(2,1)S(1)} collective-permute-done((bf16[368,640]{1,0:T(8,128)(2,1)S(1)}, bf16[368,640]{1,0:T(8,128)(2,1)S(1)}, u32[]{:S(2)}, u32[]{:S(2)}) %collective-permute-start.5) | collective-permute-done | bytes 471072 | tf_op jit(solution)/shard_map/ppermute | solution.py:922
  81.4 3.7 all-to-all-start
  91.6 2.0 copy.69.rank
  93.5 6.0 %gather_tokens.1 = bf16[4,240,768]{2,1,0:T(8,128)(2,1)} custom-call(f32[4,240,1024]{2,1,0:T(8,128)} %values.1, s32[4,1024,1]{2,1,0:T(8,128)} %copy.69.rank), custom_call_target="tpu_custom_call" | custom-call | flops 47185920 | bytes 184320 | tf_op jit(solution)/shard_map/gather_tokens/pallas_call | solution.py:84
  105.8 6.3 %join.1.w.refs_7_ = bf16[4,960,640]{2,1,0:T(8,128)(2,1)} custom-call(s32[3]{0:T(128)} %pad_add_fusion.who, bf16[4,120,640]{2,1,0:T(8,128)(2,1)} %copy-done.4, bf16[4,120,640]{2,1,0:T(8,128)(2,1)} %copy-done.10, bf16[4,120,640]{2,1,0:T(8,128)(2,1)} %copy-done.9, bf16[4,120,640]{2,1,0:T(8,128)(2,1)} %copy-done.8, ...), custom_call_target="tpu_custom_call" | custom-call | bytes 307200 | tf_op jit(solution)/shard_map/join/pallas_call | solution.py:150
  112.1 17.3 %all-to-all-done = bf16[4,240,1024]{2,1,0:T(8,128)(2,1)S(1)} async-done(((bf16[4,240,1024]{2,1,0:T(8,128)(2,1)}), bf16[4,240,1024]{2,1,0:T(8,128)(2,1)S(1)}, u32[]{:S(2)}, u32[]{:S(2)}) %all-to-all-start) | async-done | bytes 1966112 | tf_op jit(solution)/shard_map/all_to_all | solution.py:966
  130.8 3.8 all-to-all-start.1
  134.6 15.3 %project.1 = (bf16[960,768]{1,0:T(8,128)(2,1)}, f32[1,768]{1,0:T(1,128)}, bf16[960,768]{1,0:T(8,128)(2,1)}, bf16[320,1024]{1,0:T(8,128)(2,1)}, bf16[5,1024,64]{2...) custom-call(bf16[960,1024]{1,0:T(8,128)(2,1)} %bitcast.88, ...), custom_call_target="tpu_custom_call" | custom-call | flops 130744320 | bytes 552960 | tf_op jit(solution)/shard_map/project/pallas_call | solution.py:231
  149.8 16.4 %attend.1 = (bf16[960,768]{1,0:T(8,128)(2,1)}, f32[5,3,768]{2,1,0:T(4,128)}) custom-call(bf16[960,768]{1,0:T(8,128)(2,1)} %get-tuple-element.248.q, bf16[5,1024,64]{2,1,0:T(8,128)(2,1)} %get-tuple-element.249.k, bf16[320,1024]{1,0:T(8,128)(2,1)} %get-tuple-element.250.vt, s32[1,768]{1,0:T(1,128)} %max.18.limit), custom_call_target="tpu_custom_call" | custom-call | flops 377487360 | bytes 92160 | tf_op jit(solution)/shard_map/attend/pallas_call | solution.py:324
  166.3 8.1 %merge.1 = (f32[960,768]{1,0:T(8,128)}, f32[1,768]{1,0:T(1,128)}, bf16[960,768]{1,0:T(8,128)(2,1)}) custom-call(bf16[960,768]{1,0:T(8,128)(2,1)} %get-tuple-element.252.mixed, bf16[960,768]{1,0:T(8,128)(2,1)} %get-tuple-element.253.picked.refs_4_, f32[960,128]{1,0:T(8,128)} %broadcast_in_dim.39.gain.refs_8_, bf16[4,960,640]{2,1,0:T(8,128)(2,1)} %join.1.w.refs_7_), custom_call_target="tpu_custom_call" | custom-call | flops 44236800 | bytes 476160 | tf_op jit(solution)/shard_map/merge/pallas_call | solution.py:447
  175.5 23.4 %ffn.1 = (bf16[4,640,768]{2,1,0:T(8,128)(2,1)}, bf16[4,640,768]{2,1,0:T(8,128)(2,1)}, bf16[4,640,768]{2,1,0:T(8,128)(2,1)}, bf16[960,768]{1,0:T(8,128)(2,1)}, bf...) custom-call(s32[3]{0:T(128)} %pad_add_fusion.who, bf16[960,768]{1,0:T(8,128)(2,1)} %get-tuple-element.259.normed, ...), custom_call_target="tpu_custom_call" | custom-call | flops 353894400 | bytes 645120 | tf_op jit(solution)/shard_map/ffn/pallas_call | solution.py:575
  198.9 10.0 %down_grad.1 = (bf16[4,4,128,640]{3,2,1,0:T(8,128)(2,1)}, bf16[4,4,128,640]{3,2,1,0:T(8,128)(2,1)}) custom-call(s32[3]{0:T(128)} %pad_add_fusion.who, bf16[960,768]{1,0:T(8,128)(2,1)} %get-tuple-element.267.grad_ffn, bf16[4,640,768]{2,1,0:T(8,128)(2,1)} %get-tuple-element.268.active), custom_call_target="tpu_custom_call" | custom-call | flops 117964800 | bytes 460800 | tf_op jit(solution)/shard_map/down_grad/pallas_call | solution.py:615
  209.8 2.0 collective-permute-start.16
  211.8 2.3 collective-permute-start.17
  214.2 18.8 %ffn_back.2 = (bf16[4,2,240,640]{3,2,1,0:T(8,128)(2,1)}, bf16[4,2,240,640]{3,2,1,0:T(8,128)(2,1)}, f32[960,768]{1,0:T(8,128)}) custom-call(s32[3]{0:T(128)} %pad_add_fusion.who, bf16[960,768]{1,0:T(8,128)(2,1)} %get-tuple-element.259.normed, bf16[960,768]{1,0:T(8,128)(2,1)} %get-tuple-element.267.grad_ffn, bf16[4,640,768]{2,1,0:T(8,128)(2,1)} %get-tuple-element.277.gate_in, ...), custom_call_target="tpu_custom_call" | custom-call | flops 294912000 | bytes 660480 | tf_op jit(solution)/shard_map/ffn_back/pallas_call | solution.py:705
  233.9 3.4 fusion.7
  241.4 24.3 %ffn_back.3 = (bf16[4,2,240,640]{3,2,1,0:T(8,128)(2,1)}, bf16[4,2,240,640]{3,2,1,0:T(8,128)(2,1)}, bf16[960,768]{1,0:T(8,128)(2,1)}, bf16[960,768]{1,0:T(8,128)(...) custom-call(s32[3]{0:T(128)} %pad_add_fusion.who, bf16[960,768]{1,0:T(8,128)(2,1)} %get-tuple-element.259.normed, ...), custom_call_target="tpu_custom_call" | custom-call | flops 294912000 | bytes 660480 | tf_op jit(solution)/shard_map/ffn_back/pallas_call | solution.py:705
  265.7 4.4 collective-permute-done.20
  270.1 1.8 add_convert_fusion.5
  272.2 1.7 fusion.15
  278.0 9.0 %merge_back.1 = (bf16[4,960,240]{2,1,0:T(8,128)(2,1)}, bf16[960,768]{1,0:T(8,128)(2,1)}) custom-call(bf16[960,768]{1,0:T(8,128)(2,1)} %get-tuple-element.252.mixed, bf16[960,768]{1,0:T(8,128)(2,1)} %get-tuple-element.328.grad, bf16[4,960,640]{2,1,0:T(8,128)(2,1)} %join.1.w.refs_7_), custom_call_target="tpu_custom_call" | custom-call | flops 88473600 | bytes 445440 | tf_op jit(solution)/shard_map/merge_back/pallas_call | solution.py:751
  287.0 2.4 collective-permute-start.24
  289.3 1.7 fusion.19
  291.1 18.2 %attend_back.2 = (bf16[576,768]{1,0:T(8,128)(2,1)}, bf16[192,1024]{1,0:T(8,128)(2,1)}, bf16[192,1024]{1,0:T(8,128)(2,1)}) custom-call(bf16[960,768]{1,0:T(8,128)(2,1)} %get-tuple-element.248.q, bf16[5,1024,64]{2,1,0:T(8,128)(2,1)} %get-tuple-element.249.k, bf16[320,1024]{1,0:T(8,128)(2,1)} %get-tuple-element.324.kt, ...), custom_call_target="tpu_custom_call" | custom-call | flops 566231040 | bytes 110592 | tf_op jit(solution)/shard_map/attend_back/pallas_call | solution.py:391
  312.9 1.7 add_convert_fusion.11
  317.1 12.8 %attend_back.3 = (bf16[384,768]{1,0:T(8,128)(2,1)}, bf16[128,1024]{1,0:T(8,128)(2,1)}, bf16[128,1024]{1,0:T(8,128)(2,1)}) custom-call(bf16[960,768]{1,0:T(8,128)(2,1)} %get-tuple-element.248.q, bf16[5,1024,64]{2,1,0:T(8,128)(2,1)} %get-tuple-element.249.k, bf16[320,1024]{1,0:T(8,128)(2,1)} %get-tuple-element.324.kt, ...), custom_call_target="tpu_custom_call" | custom-call | flops 377487360 | bytes 73728 | tf_op jit(solution)/shard_map/attend_back/pallas_call | solution.py:391
  329.9 15.0 %mixing_grad.1 = (bf16[4,4,128,640]{3,2,1,0:T(8,128)(2,1)}, bf16[4,4,128,640]{3,2,1,0:T(8,128)(2,1)}, bf16[4,400,1024]{2,1,0:T(8,128)(2,1)}, f32[960,1]{1,0:T(8,128)}) custom-call(s32[3]{0:T(128)} %pad_add_fusion.who, bf16[960,1024]{1,0:T(8,128)(2,1)} %bitcast.89, s32[1,1024]{1,0:T(1,128)} %copy-done.26, f32[960,128]{1,0:T(8,128)} %broadcast_in_dim.38.gain, ...), custom_call_target="tpu_custom_call" | custom-call | flops 145489920 | bytes 307200 | tf_op jit(solution)/shard_map/mixing_grad/pallas_call | solution.py:821
  345.6 1.8 add_convert_fusion.10
  349.2 2.4 collective-permute-start.35
  351.6 12.1 %project_back.1 = bf16[960,1024]{1,0:T(8,128)(2,1)} custom-call(bf16[960,1024]{1,0:T(8,128)(2,1)} %bitcast.90, s32[1,1024]{1,0:T(1,128)} %copy-done.26, f32[960,128]{1,0:T(8,128)} %broadcast_in_dim.38.gain, bf16[4,400,1024]{2,1,0:T(8,128)(2,1)} %get-tuple-element.381.grads, bf16[960,768]{1,0:T(8,128)(2,1)} %get-tuple-element.382.rest, ...), custom_call_target="tpu_custom_call" | custom-call | flops 145489920 | bytes 460800 | tf_op jit(solution)/shard_map/project_back/pallas_call | solution.py:886
  363.7 3.9 all-to-all-start.2
  367.6 4.1 fusion.11
  375.8 6.9 %scatter_tokens.1 = f32[4,240,1024]{2,1,0:T(8,128)} custom-call(s32[3]{0:T(128)} %pad_add_fusion.who, f32[4,240,1024]{2,1,0:T(8,128)} %base.1, s32[4,1,1024]{2,1,0:T(1,128)} %broadcast_in_dim.45.rank, bf16[240,768]{1,0:T(8,128)(2,1)} %get-tuple-element.395.refs_0_, bf16[240,768]{1,0:T(8,128)(2,1)} %copy-done.18, bf16[240,768]{1,0:T(8,128)(2,1)} %copy-done.19, ...), custom_call_target="tpu_custom_call" | custom-call | flops 47185920 | bytes 307200 | tf_op jit(solution)/shard_map/scatter_tokens/pallas_call | solution.py:114
  382.7 6.8 %collective-permute-done.36 = bf16[4,128,640]{2,1,0:T(8,128)(2,1)S(1)} collective-permute-done((bf16[4,128,640]{2,1,0:T(8,128)(2,1)}, bf16[4,128,640]{2,1,0:T(8,128)(2,1)S(1)}, u32[]{:S(2)}, u32[]{:S(2)}) %collective-permute-start.36) | collective-permute-done | bytes 655392 | tf_op jit(solution)/shard_map/ppermute | solution.py:922
  390.0 13.8 %collective-permute-done.38 = bf16[4,128,640]{2,1,0:T(8,128)(2,1)S(1)} collective-permute-done((bf16[4,128,640]{2,1,0:T(8,128)(2,1)S(1)}, bf16[4,128,640]{2,1,0:T(8,128)(2,1)S(1)}, u32[]{:S(2)}, u32[]{:S(2)}) %collective-permute-start.38) | collective-permute-done | bytes 655392 | tf_op jit(solution)/shard_map/ppermute | solution.py:922
  406.9 1.7 collective-permute-start.39
  409.5 1.9 copy.76
  411.4 2.4 all-to-all-done.2
  413.7 5.0 %convert_add_fusion = f32[4,240,1024]{2,1,0:T(8,128)} fusion(f32[4,240,1024]{2,1,0:T(8,128)} %values.1, bf16[4,240,1024]{2,1,0:T(8,128)(2,1)S(1)} %all-to-all-done.2), kind=kLoop, calls=%fused_computation.6 | loop fusion | flops 1966080 | bytes 9830400 | tf_op jit(solution)/shard_map/add | solution.py:1186
  418.8 2.0 collective-permute-done.39
  422.8 8.6 %collective-permute-done.40 = bf16[1,128,640]{2,1,0:T(8,128)(2,1)S(1)} collective-permute-done((bf16[1,128,640]{2,1,0:T(8,128)(2,1)S(1)}, bf16[1,128,640]{2,1,0:T(8,128)(2,1)S(1)}, u32[]{:S(2)}, u32[]{:S(2)}) %collective-permute-start.40) | collective-permute-done | bytes 163872 | tf_op jit(solution)/shard_map/ppermute | solution.py:922
  (211 shorter events, 60.4 us)
Async XLA Ops:
  7.2 167.2 %all-gather.3.cloned.1.call-start = ((), (), s32[]{:S(2)}) async-start(), calls=%async_computation.3 | async-start | bytes 16957440 | tf_op jit(solution)/shard_map/all_gather | solution.py:1024
  10.0 10.0 %collective-permute-start.2 = (bf16[120,640]{1,0:T(8,128)(2,1)S(1)}, bf16[120,640]{1,0:T(8,128)(2,1)S(1)}, u32[]{:S(2)}, u32[]{:S(2)}) collective-permute-start(bf16[120,640]{1,0:T(8,128)(2,1)S(1)} %pad_maximum_fusion.5), channel_id=1, source_target_pairs={{0,3},{1,2},{2,1},{3,0},{4,7},{5,6},{6,5},{7,4},{8,11},{9,10},{10,... | collective-permute-start | bytes 460808 | tf_op jit(solution)/shard_map/ppermute | solution.py:922
  15.1 13.0 %collective-permute-start.1 = (bf16[120,640]{1,0:T(8,128)(2,1)S(1)}, bf16[120,640]{1,0:T(8,128)(2,1)S(1)}, u32[]{:S(2)}, u32[]{:S(2)}) collective-permute-start(bf16[120,640]{1,0:T(8,128)(2,1)S(1)} %pad_maximum_fusion.5), channel_id=1, source_target_pairs={{0,2},{1,3},{2,0},{3,1},{4,6},{5,7},{6,4},{7,5},{8,10},{9,11},{10,... | collective-permute-start | bytes 460808 | tf_op jit(solution)/shard_map/ppermute | solution.py:922
  15.1 13.0 %collective-permute-start = (bf16[120,640]{1,0:T(8,128)(2,1)S(1)}, bf16[120,640]{1,0:T(8,128)(2,1)S(1)}, u32[]{:S(2)}, u32[]{:S(2)}) collective-permute-start(bf16[120,640]{1,0:T(8,128)(2,1)S(1)} %pad_maximum_fusion.5), channel_id=1, source_target_pairs={{0,1},{1,0},{2,3},{3,2},{4,5},{5,4},{6,7},{7,6},{8,9},{9,8},{10,11... | collective-permute-start | bytes 460808 | tf_op jit(solution)/shard_map/ppermute | solution.py:922
  16.9 1.6 collective-permute-start.4
  17.9 1.6 collective-permute-start.3
  28.2 15.6 %collective-permute-start.7 = (bf16[368,640]{1,0:T(8,128)(2,1)S(1)}, bf16[368,640]{1,0:T(8,128)(2,1)S(1)}, u32[]{:S(2)}, u32[]{:S(2)}) collective-permute-start(bf16[368,640]{1,0:T(8,128)(2,1)S(1)} %constant_dynamic-update-slice_fusion), channel_id=1, source_target_pairs={{0,3},{1,2},{2,1},{3,0},{4,7},{5,6},{6,5},{7,4},{8,11},{9,10},{10,... | collective-permute-start | bytes 1413128 | tf_op jit(solution)/shard_map/ppermute | solution.py:922
  30.9 58.3 %copy-start.4 = (bf16[4,120,640]{2,1,0:T(8,128)(2,1)}, bf16[4,120,640]{2,1,0:T(8,128)(2,1)S(1)}, u32[]{:S(2)}) copy-start(bf16[4,120,640]{2,1,0:T(8,128)(2,1)S(1)} %pad_maximum_fusion.1.refs_0_) | copy-start | bytes 1843204
  30.9 47.1 %collective-permute-start.10 = (bf16[4,120,640]{2,1,0:T(8,128)(2,1)S(1)}, bf16[4,120,640]{2,1,0:T(8,128)(2,1)S(1)}, u32[]{:S(2)}, u32[]{:S(2)}) collective-permute-start(bf16[4,120,640]{2,1,0:T(8,128)(2,1)S(1)} %pad_maximum_fusion.1.refs_0_), channel_id=1, source_target_pairs={{0,24},{4,28},{8,16},{12,20},{16,8},{20,12},{24,0},{28,4},{1,25},{... | collective-permute-start | bytes 1843208 | tf_op jit(solution)/shard_map/ppermute | solution.py:922
  33.4 44.6 %collective-permute-start.9 = (bf16[4,120,640]{2,1,0:T(8,128)(2,1)S(1)}, bf16[4,120,640]{2,1,0:T(8,128)(2,1)S(1)}, u32[]{:S(2)}, u32[]{:S(2)}) collective-permute-start(bf16[4,120,640]{2,1,0:T(8,128)(2,1)S(1)} %pad_maximum_fusion.1.refs_0_), channel_id=1, source_target_pairs={{0,16},{4,20},{8,24},{12,28},{16,0},{20,4},{24,8},{28,12},{1,17},{... | collective-permute-start | bytes 1843208 | tf_op jit(solution)/shard_map/ppermute | solution.py:922
  33.9 44.1 %collective-permute-start.8 = (bf16[4,120,640]{2,1,0:T(8,128)(2,1)S(1)}, bf16[4,120,640]{2,1,0:T(8,128)(2,1)S(1)}, u32[]{:S(2)}, u32[]{:S(2)}) collective-permute-start(bf16[4,120,640]{2,1,0:T(8,128)(2,1)S(1)} %pad_maximum_fusion.1.refs_0_), channel_id=1, source_target_pairs={{0,8},{4,12},{8,0},{12,4},{16,24},{20,28},{24,16},{28,20},{1,9},{5... | collective-permute-start | bytes 1843208 | tf_op jit(solution)/shard_map/ppermute | solution.py:922
  34.5 34.9 %collective-permute-start.6 = (bf16[368,640]{1,0:T(8,128)(2,1)S(1)}, bf16[368,640]{1,0:T(8,128)(2,1)S(1)}, u32[]{:S(2)}, u32[]{:S(2)}) collective-permute-start(bf16[368,640]{1,0:T(8,128)(2,1)S(1)} %constant_dynamic-update-slice_fusion), channel_id=1, source_target_pairs={{0,2},{1,3},{2,0},{3,1},{4,6},{5,7},{6,4},{7,5},{8,10},{9,11},{10,... | collective-permute-start | bytes 1413128 | tf_op jit(solution)/shard_map/ppermute | solution.py:922
  43.8 34.2 %collective-permute-start.5 = (bf16[368,640]{1,0:T(8,128)(2,1)S(1)}, bf16[368,640]{1,0:T(8,128)(2,1)S(1)}, u32[]{:S(2)}, u32[]{:S(2)}) collective-permute-start(bf16[368,640]{1,0:T(8,128)(2,1)S(1)} %constant_dynamic-update-slice_fusion), channel_id=1, source_target_pairs={{0,1},{1,0},{2,3},{3,2},{4,5},{5,4},{6,7},{7,6},{8,9},{9,8},{10,11... | collective-permute-start | bytes 1413128 | tf_op jit(solution)/shard_map/ppermute | solution.py:922
  81.4 48.1 %all-to-all-start = ((bf16[4,240,1024]{2,1,0:T(8,128)(2,1)}), bf16[4,240,1024]{2,1,0:T(8,128)(2,1)S(1)}, u32[]{:S(2)}, u32[]{:S(2)}) async-start(bf16[4,240,1024]{2,1,0:T(8,128)(2,1)} %convert_element_type.368), calls=%async_computation | async-start | bytes 3932160 | tf_op jit(solution)/shard_map/all_to_all | solution.py:966
  89.3 12.6 %collective-permute-start.11 = (bf16[4,120,640]{2,1,0:T(8,128)(2,1)S(1)}, bf16[4,120,640]{2,1,0:T(8,128)(2,1)}, u32[]{:S(2)}, u32[]{:S(2)}) collective-permute-start(bf16[4,120,640]{2,1,0:T(8,128)(2,1)S(1)} %pad_maximum_fusion.1.refs_0_), channel_id=1, source_target_pairs={{0,4},{4,0},{8,12},{12,8},{16,20},{20,16},{24,28},{28,24},{1,5},{5... | collective-permute-start | bytes 1843208 | tf_op jit(solution)/shard_map/ppermute | solution.py:916
  89.3 12.5 %collective-permute-start.12 = (bf16[4,120,640]{2,1,0:T(8,128)(2,1)}, bf16[4,120,640]{2,1,0:T(8,128)(2,1)}, u32[]{:S(2)}, u32[]{:S(2)}) collective-permute-start(bf16[4,120,640]{2,1,0:T(8,128)(2,1)} %copy-done.10), channel_id=1, source_target_pairs={{0,4},{4,0},{8,12},{12,8},{16,20},{20,16},{24,28},{28,24},{1,5},{5... | collective-permute-start | bytes 1843208 | tf_op jit(solution)/shard_map/ppermute | solution.py:916
  89.8 12.0 %collective-permute-start.13 = (bf16[4,120,640]{2,1,0:T(8,128)(2,1)}, bf16[4,120,640]{2,1,0:T(8,128)(2,1)}, u32[]{:S(2)}, u32[]{:S(2)}) collective-permute-start(bf16[4,120,640]{2,1,0:T(8,128)(2,1)} %copy-done.9), channel_id=1, source_target_pairs={{0,4},{4,0},{8,12},{12,8},{16,20},{20,16},{24,28},{28,24},{1,5},{5... | collective-permute-start | bytes 1843208 | tf_op jit(solution)/shard_map/ppermute | solution.py:916
  89.9 11.9 %collective-permute-start.14 = (bf16[4,120,640]{2,1,0:T(8,128)(2,1)S(1)}, bf16[4,120,640]{2,1,0:T(8,128)(2,1)}, u32[]{:S(2)}, u32[]{:S(2)}) collective-permute-start(bf16[4,120,640]{2,1,0:T(8,128)(2,1)S(1)} %collective-permute-done.10.refs_3_), channel_id=1, source_target_pairs={{0,4},{4,0},{8,12},{12,8},{16,20},{20,16},{24,28},{28,24},{1,5},{5... | collective-permute-start | bytes 1843208 | tf_op jit(solution)/shard_map/ppermute | solution.py:916
  130.8 43.6 %all-to-all-start.1 = ((bf16[4,240,768]{2,1,0:T(8,128)(2,1)}), bf16[4,240,768]{2,1,0:T(8,128)(2,1)S(1)}, u32[]{:S(2)}, u32[]{:S(2)}) async-start(bf16[4,240,768]{2,1,0:T(8,128)(2,1)} %gather_tokens.1), calls=%async_computation.1 | async-start | bytes 2949120 | tf_op jit(solution)/shard_map/all_to_all | solution.py:966
  209.8 23.2 %collective-permute-start.15 = (bf16[4,4,128,640]{3,2,1,0:T(8,128)(2,1)}, bf16[4,4,128,640]{3,2,1,0:T(8,128)(2,1)}, u32[]{:S(2)}, u32[]{:S(2)}) collective-permute-start(bf16[4,4,128,640]{3,2,1,0:T(8,128)(2,1)} %get-tuple-element.276), channel_id=1, source_target_pairs={{0,4},{4,0},{8,12},{12,8},{16,20},{20,16},{24,28},{28,24},{1,5},{5... | collective-permute-start | bytes 7864328 | tf_op jit(solution)/shard_map/ppermute | solution.py:916
  209.8 23.2 %collective-permute-start.16 = (bf16[240,768]{1,0:T(8,128)(2,1)S(1)}, bf16[240,768]{1,0:T(8,128)(2,1)S(1)}, u32[]{:S(2)}, u32[]{:S(2)}) collective-permute-start(bf16[240,768]{1,0:T(8,128)(2,1)S(1)} %get-tuple-element.283), channel_id=1, source_target_pairs={{0,1},{1,0},{2,3},{3,2},{4,5},{5,4},{6,7},{7,6},{8,9},{9,8},{10,11... | collective-permute-start | bytes 1105928 | tf_op jit(solution)/shard_map/ppermute | solution.py:922
  211.8 21.2 %collective-permute-start.17 = (bf16[240,768]{1,0:T(8,128)(2,1)S(1)}, bf16[240,768]{1,0:T(8,128)(2,1)S(1)}, u32[]{:S(2)}, u32[]{:S(2)}) collective-permute-start(bf16[240,768]{1,0:T(8,128)(2,1)S(1)} %get-tuple-element.284), channel_id=1, source_target_pairs={{0,2},{1,3},{2,0},{3,1},{4,6},{5,7},{6,4},{7,5},{8,10},{9,11},{10,... | collective-permute-start | bytes 1105928 | tf_op jit(solution)/shard_map/ppermute | solution.py:922
  237.3 32.8 %collective-permute-start.18 = (bf16[4,2,240,640]{3,2,1,0:T(8,128)(2,1)}, bf16[4,2,240,640]{3,2,1,0:T(8,128)(2,1)S(1)}, u32[]{:S(2)}, u32[]{:S(2)}) collective-permute-start(bf16[4,2,240,640]{3,2,1,0:T(8,128)(2,1)} %get-tuple-element.290), channel_id=1, source_target_pairs={{0,4},{4,0},{8,12},{12,8},{16,20},{20,16},{24,28},{28,24},{1,5},{5... | collective-permute-start | bytes 7372808 | tf_op jit(solution)/shard_map/ppermute | solution.py:916
  237.3 28.4 %collective-permute-start.19 = (bf16[4,128,640]{2,1,0:T(8,128)(2,1)}, bf16[4,128,640]{2,1,0:T(8,128)(2,1)S(1)}, u32[]{:S(2)}, u32[]{:S(2)}) collective-permute-start(bf16[4,128,640]{2,1,0:T(8,128)(2,1)} %get-tuple-element.292), channel_id=1, source_target_pairs={{0,8},{4,12},{8,0},{12,4},{16,24},{20,28},{24,16},{28,20},{1,9},{5... | collective-permute-start | bytes 1966088 | tf_op jit(solution)/shard_map/ppermute | solution.py:922
  238.9 31.2 %collective-permute-start.20 = (bf16[4,128,640]{2,1,0:T(8,128)(2,1)}, bf16[4,128,640]{2,1,0:T(8,128)(2,1)}, u32[]{:S(2)}, u32[]{:S(2)}) collective-permute-start(bf16[4,128,640]{2,1,0:T(8,128)(2,1)} %get-tuple-element.293), channel_id=1, source_target_pairs={{0,16},{4,20},{8,24},{12,28},{16,0},{20,4},{24,8},{28,12},{1,17},{... | collective-permute-start | bytes 1966088 | tf_op jit(solution)/shard_map/ppermute | solution.py:922
  240.4 29.6 %collective-permute-start.21 = (bf16[4,128,640]{2,1,0:T(8,128)(2,1)}, bf16[4,128,640]{2,1,0:T(8,128)(2,1)}, u32[]{:S(2)}, u32[]{:S(2)}) collective-permute-start(bf16[4,128,640]{2,1,0:T(8,128)(2,1)} %get-tuple-element.294), channel_id=1, source_target_pairs={{0,24},{4,28},{8,16},{12,20},{16,8},{20,12},{24,0},{28,4},{1,25},{... | collective-permute-start | bytes 1966088 | tf_op jit(solution)/shard_map/ppermute | solution.py:922
  240.8 24.9 %collective-permute-start.22 = (bf16[240,768]{1,0:T(8,128)(2,1)}, bf16[240,768]{1,0:T(8,128)(2,1)}, u32[]{:S(2)}, u32[]{:S(2)}) collective-permute-start(bf16[240,768]{1,0:T(8,128)(2,1)} %get-tuple-element.298), channel_id=1, source_target_pairs={{0,3},{1,2},{2,1},{3,0},{4,7},{5,6},{6,5},{7,4},{8,11},{9,10},{10,... | collective-permute-start | bytes 1105928 | tf_op jit(solution)/shard_map/ppermute | solution.py:922
  273.8 13.1 %collective-permute-start.28 = (bf16[4,2,240,640]{3,2,1,0:T(8,128)(2,1)}, bf16[4,2,240,640]{3,2,1,0:T(8,128)(2,1)S(1)}, u32[]{:S(2)}, u32[]{:S(2)}) collective-permute-start(bf16[4,2,240,640]{3,2,1,0:T(8,128)(2,1)} %get-tuple-element.327), channel_id=1, source_target_pairs={{0,4},{4,0},{8,12},{12,8},{16,20},{20,16},{24,28},{28,24},{1,5},{5... | collective-permute-start | bytes 7372808 | tf_op jit(solution)/shard_map/ppermute | solution.py:916
  273.9 35.4 %collective-permute-start.25 = (bf16[2,240,640]{2,1,0:T(8,128)(2,1)}, bf16[2,240,640]{2,1,0:T(8,128)(2,1)S(1)}, u32[]{:S(2)}, u32[]{:S(2)}) collective-permute-start(bf16[2,240,640]{2,1,0:T(8,128)(2,1)} %get-tuple-element.321), channel_id=1, source_target_pairs={{0,8},{4,12},{8,0},{12,4},{16,24},{20,28},{24,16},{28,20},{1,9},{5... | collective-permute-start | bytes 1843208 | tf_op jit(solution)/shard_map/ppermute | solution.py:922
  275.1 34.2 %collective-permute-start.26 = (bf16[2,240,640]{2,1,0:T(8,128)(2,1)}, bf16[2,240,640]{2,1,0:T(8,128)(2,1)}, u32[]{:S(2)}, u32[]{:S(2)}) collective-permute-start(bf16[2,240,640]{2,1,0:T(8,128)(2,1)} %get-tuple-element.322), channel_id=1, source_target_pairs={{0,16},{4,20},{8,24},{12,28},{16,0},{20,4},{24,8},{28,12},{1,17},{... | collective-permute-start | bytes 1843208 | tf_op jit(solution)/shard_map/ppermute | solution.py:922
  276.0 33.4 %collective-permute-start.27 = (bf16[2,240,640]{2,1,0:T(8,128)(2,1)}, bf16[2,240,640]{2,1,0:T(8,128)(2,1)}, u32[]{:S(2)}, u32[]{:S(2)}) collective-permute-start(bf16[2,240,640]{2,1,0:T(8,128)(2,1)} %get-tuple-element.323), channel_id=1, source_target_pairs={{0,24},{4,28},{8,16},{12,20},{16,8},{20,12},{24,0},{28,4},{1,25},{... | collective-permute-start | bytes 1843208 | tf_op jit(solution)/shard_map/ppermute | solution.py:922
  277.3 31.9 %collective-permute-start.23 = (bf16[128,640]{1,0:T(8,128)(2,1)S(1)}, bf16[128,640]{1,0:T(8,128)(2,1)S(1)}, u32[]{:S(2)}, u32[]{:S(2)}) collective-permute-start(bf16[128,640]{1,0:T(8,128)(2,1)S(1)} %get-tuple-element.318), channel_id=1, source_target_pairs={{0,2},{1,3},{2,0},{3,1},{4,6},{5,7},{6,4},{7,5},{8,10},{9,11},{10,... | collective-permute-start | bytes 491528 | tf_op jit(solution)/shard_map/ppermute | solution.py:922
  287.0 22.3 %collective-permute-start.24 = (bf16[128,640]{1,0:T(8,128)(2,1)S(1)}, bf16[128,640]{1,0:T(8,128)(2,1)S(1)}, u32[]{:S(2)}, u32[]{:S(2)}) collective-permute-start(bf16[128,640]{1,0:T(8,128)(2,1)S(1)} %get-tuple-element.319), channel_id=1, source_target_pairs={{0,3},{1,2},{2,1},{3,0},{4,7},{5,6},{6,5},{7,4},{8,11},{9,10},{10,... | collective-permute-start | bytes 491528 | tf_op jit(solution)/shard_map/ppermute | solution.py:922
  309.3 35.6 %collective-permute-start.31 = (bf16[2,240,640]{2,1,0:T(8,128)(2,1)}, bf16[2,240,640]{2,1,0:T(8,128)(2,1)}, u32[]{:S(2)}, u32[]{:S(2)}) collective-permute-start(bf16[2,240,640]{2,1,0:T(8,128)(2,1)} %get-tuple-element.353), channel_id=1, source_target_pairs={{0,8},{4,12},{8,0},{12,4},{16,24},{20,28},{24,16},{28,20},{1,9},{5... | collective-permute-start | bytes 1843208 | tf_op jit(solution)/shard_map/ppermute | solution.py:922
  310.6 34.3 %collective-permute-start.32 = (bf16[2,240,640]{2,1,0:T(8,128)(2,1)}, bf16[2,240,640]{2,1,0:T(8,128)(2,1)}, u32[]{:S(2)}, u32[]{:S(2)}) collective-permute-start(bf16[2,240,640]{2,1,0:T(8,128)(2,1)} %get-tuple-element.354), channel_id=1, source_target_pairs={{0,16},{4,20},{8,24},{12,28},{16,0},{20,4},{24,8},{28,12},{1,17},{... | collective-permute-start | bytes 1843208 | tf_op jit(solution)/shard_map/ppermute | solution.py:922
  311.5 33.4 %collective-permute-start.33 = (bf16[2,240,640]{2,1,0:T(8,128)(2,1)}, bf16[2,240,640]{2,1,0:T(8,128)(2,1)}, u32[]{:S(2)}, u32[]{:S(2)}) collective-permute-start(bf16[2,240,640]{2,1,0:T(8,128)(2,1)} %get-tuple-element.355), channel_id=1, source_target_pairs={{0,24},{4,28},{8,16},{12,20},{16,8},{20,12},{24,0},{28,4},{1,25},{... | collective-permute-start | bytes 1843208 | tf_op jit(solution)/shard_map/ppermute | solution.py:922
  314.7 30.2 %collective-permute-start.29 = (bf16[240,640]{1,0:T(8,128)(2,1)S(1)}, bf16[240,640]{1,0:T(8,128)(2,1)S(1)}, u32[]{:S(2)}, u32[]{:S(2)}) collective-permute-start(bf16[240,640]{1,0:T(8,128)(2,1)S(1)} %get-tuple-element.350), channel_id=1, source_target_pairs={{0,3},{1,2},{2,1},{3,0},{4,7},{5,6},{6,5},{7,4},{8,11},{9,10},{10,... | collective-permute-start | bytes 921608 | tf_op jit(solution)/shard_map/ppermute | solution.py:922
  316.3 28.6 %collective-permute-start.30 = (bf16[240,640]{1,0:T(8,128)(2,1)S(1)}, bf16[240,640]{1,0:T(8,128)(2,1)S(1)}, u32[]{:S(2)}, u32[]{:S(2)}) collective-permute-start(bf16[240,640]{1,0:T(8,128)(2,1)S(1)} %get-tuple-element.351), channel_id=1, source_target_pairs={{0,2},{1,3},{2,0},{3,1},{4,6},{5,7},{6,4},{7,5},{8,10},{9,11},{10,... | collective-permute-start | bytes 921608 | tf_op jit(solution)/shard_map/ppermute | solution.py:922
  349.2 14.5 %collective-permute-start.34 = (bf16[4,4,128,640]{3,2,1,0:T(8,128)(2,1)}, bf16[4,4,128,640]{3,2,1,0:T(8,128)(2,1)}, u32[]{:S(2)}, u32[]{:S(2)}) collective-permute-start(bf16[4,4,128,640]{3,2,1,0:T(8,128)(2,1)} %get-tuple-element.379), channel_id=1, source_target_pairs={{0,4},{4,0},{8,12},{12,8},{16,20},{20,16},{24,28},{28,24},{1,5},{5... | collective-permute-start | bytes 7864328 | tf_op jit(solution)/shard_map/ppermute | solution.py:916
  349.2 14.5 %collective-permute-start.35 = (bf16[368,640]{1,0:T(8,128)(2,1)S(1)}, bf16[368,640]{1,0:T(8,128)(2,1)S(1)}, u32[]{:S(2)}, u32[]{:S(2)}) collective-permute-start(bf16[368,640]{1,0:T(8,128)(2,1)S(1)} %pad_maximum_fusion.2), channel_id=1, source_target_pairs={{0,1},{1,0},{2,3},{3,2},{4,5},{5,4},{6,7},{7,6},{8,9},{9,8},{10,11... | collective-permute-start | bytes 1413128 | tf_op jit(solution)/shard_map/ppermute | solution.py:922
  363.7 50.0 %all-to-all-start.2 = ((bf16[4,240,1024]{2,1,0:T(8,128)(2,1)}), bf16[4,240,1024]{2,1,0:T(8,128)(2,1)S(1)}, u32[]{:S(2)}, u32[]{:S(2)}) async-start(bf16[4,240,1024]{2,1,0:T(8,128)(2,1)} %bitcast.93), calls=%async_computation.2 | async-start | bytes 3932160 | tf_op jit(solution)/shard_map/all_to_all | solution.py:973
  371.7 17.8 %collective-permute-start.36 = (bf16[4,128,640]{2,1,0:T(8,128)(2,1)}, bf16[4,128,640]{2,1,0:T(8,128)(2,1)S(1)}, u32[]{:S(2)}, u32[]{:S(2)}) collective-permute-start(bf16[4,128,640]{2,1,0:T(8,128)(2,1)} %get-tuple-element.392), channel_id=1, source_target_pairs={{0,8},{4,12},{8,0},{12,4},{16,24},{20,28},{24,16},{28,20},{1,9},{5... | collective-permute-start | bytes 1966088 | tf_op jit(solution)/shard_map/ppermute | solution.py:922
  372.9 17.1 %collective-permute-start.37 = (bf16[4,128,640]{2,1,0:T(8,128)(2,1)S(1)}, bf16[4,128,640]{2,1,0:T(8,128)(2,1)S(1)}, u32[]{:S(2)}, u32[]{:S(2)}) collective-permute-start(bf16[4,128,640]{2,1,0:T(8,128)(2,1)S(1)} %get-tuple-element.393), channel_id=1, source_target_pairs={{0,16},{4,20},{8,24},{12,28},{16,0},{20,4},{24,8},{28,12},{1,17},{... | collective-permute-start | bytes 1966088 | tf_op jit(solution)/shard_map/ppermute | solution.py:922
  373.8 30.0 %collective-permute-start.38 = (bf16[4,128,640]{2,1,0:T(8,128)(2,1)S(1)}, bf16[4,128,640]{2,1,0:T(8,128)(2,1)S(1)}, u32[]{:S(2)}, u32[]{:S(2)}) collective-permute-start(bf16[4,128,640]{2,1,0:T(8,128)(2,1)S(1)} %get-tuple-element.394), channel_id=1, source_target_pairs={{0,24},{4,28},{8,16},{12,20},{16,8},{20,12},{24,0},{28,4},{1,25},{... | collective-permute-start | bytes 1966088 | tf_op jit(solution)/shard_map/ppermute | solution.py:922
  404.0 4.6 %collective-permute-start.42 = (bf16[128,320]{1,0:T(8,128)(2,1)S(1)}, bf16[128,320]{1,0:T(8,128)(2,1)S(1)}, u32[]{:S(2)}, u32[]{:S(2)}) collective-permute-start(bf16[128,320]{1,0:T(8,128)(2,1)S(1)} %select_convert_fusion.1), channel_id=1, source_target_pairs={{0,4},{4,0},{8,12},{12,8},{16,20},{20,16},{24,28},{28,24},{1,5},{5... | collective-permute-start | bytes 245768 | tf_op jit(solution)/shard_map/ppermute | solution.py:916
  405.2 16.7 %collective-permute-start.41 = (bf16[120,640]{1,0:T(8,128)(2,1)S(1)}, bf16[120,640]{1,0:T(8,128)(2,1)S(1)}, u32[]{:S(2)}, u32[]{:S(2)}) collective-permute-start(bf16[120,640]{1,0:T(8,128)(2,1)S(1)} %select_convert_fusion), channel_id=1, source_target_pairs={{0,4},{4,0},{8,12},{12,8},{16,20},{20,16},{24,28},{28,24},{1,5},{5... | collective-permute-start | bytes 460808 | tf_op jit(solution)/shard_map/ppermute | solution.py:916
  406.9 13.9 %collective-permute-start.39 = (bf16[2,128,640]{2,1,0:T(8,128)(2,1)}, bf16[2,128,640]{2,1,0:T(8,128)(2,1)}, u32[]{:S(2)}, u32[]{:S(2)}) collective-permute-start(bf16[2,128,640]{2,1,0:T(8,128)(2,1)} %slice.69), channel_id=1, source_target_pairs={{0,1},{1,0},{2,3},{3,2},{4,5},{5,4},{6,7},{7,6},{8,9},{9,8},{10,11... | collective-permute-start | bytes 983048 | tf_op jit(solution)/shard_map/ppermute | solution.py:922
  421.8 9.6 %collective-permute-start.40 = (bf16[1,128,640]{2,1,0:T(8,128)(2,1)S(1)}, bf16[1,128,640]{2,1,0:T(8,128)(2,1)S(1)}, u32[]{:S(2)}, u32[]{:S(2)}) collective-permute-start(bf16[1,128,640]{2,1,0:T(8,128)(2,1)S(1)} %slice.92), channel_id=1, source_target_pairs={{0,2},{1,3},{2,0},{3,1},{4,6},{5,7},{6,4},{7,5},{8,10},{9,11},{10,... | collective-permute-start | bytes 491528 | tf_op jit(solution)/shard_map/ppermute | solution.py:922
  (32 other events, 324.8 us)
Sparse Core Ops, SparseCore 0:
  81.5 82.4 all-gather.2
